TPU v7x, 32 devices: a whole 2x2x4 slice. The times are simulated.
32 devices in a mesh: dp: 8 (over z, x), ctx: 4 (over y, core).
Axes of the slice: x: 2, y: 2, z: 4, core: 2. Of those that a mesh axis runs over, the one named last changes fastest.
Arguments:
- features: bfloat16 [8, 2048, 768], P('dp', 'ctx'), may hold values from -24 to 24
- bases: int32 [8, 2048], P('dp', 'ctx'), may hold values from 0 to 3
- dna_table: bfloat16 [4, 768], replicated, may hold values from -6 to 6
- norm_gain: bfloat16 [768], replicated, may hold values from 0.099609375 to 1.8984375
- w_conv: bfloat16 [5, 768, 768], replicated, may hold values from -0.09375 to 0.09375
- w_query: bfloat16 [768, 768], replicated, may hold values from -0.21875 to 0.21875
- w_key: bfloat16 [768, 768], replicated, may hold values from -0.21875 to 0.21875
- w_value: bfloat16 [768, 768], replicated, may hold values from -0.21875 to 0.21875
- w_out: bfloat16 [768, 768], replicated, may hold values from -0.21875 to 0.21875
- cotangent: bfloat16 [8, 128, 768], P('dp', 'ctx'), may hold values from -48 to 48
Outputs:
- grad_features: bfloat16 [8, 2048, 768], P('dp', 'ctx')
- grad_conv: float32 [768, 5, 768], P('ctx', None, 'dp')
All inputs are finite; a program needn't handle non-finite values.
Results may differ from a plain program's by a relative error of at most 0.025.
The roundings to bfloat16 on the way count: a program that leaves them out, or rounds other values in their place, can miss the bound.
Values may be sent and summed in bfloat16 or wider, within the bound.
No kernel may reach another device: no remote copies, remote signals or barrier semaphores. Data moves between devices by JAX's collectives and lax.ppermute only.
A program may use at most 128 MiB of HBM per device.

v0:
```python
import functools

import jax
import jax.numpy as jnp
from jax import lax
from jax.experimental import pallas as pl
from jax.experimental.pallas import tpu as pltpu
from jax.sharding import PartitionSpec as P


HEADS = 6
DH = 128

EPSILON = 1e-06
GELU_SCALE = 0.7978845608028654
CUBIC = 0.044715
F32 = jnp.float32
BF16 = jnp.bfloat16
VMEM_LIMIT = 20 << 20
GATHER = 4


def dot_nn(left, right):
    return lax.dot_general(left, right, (((1,), (0,)), ((), ())), preferred_element_type=F32)


def dot_nt(left, right):
    return lax.dot_general(left, right, (((1,), (1,)), ((), ())), preferred_element_type=F32)


def dot_tn(left, right):
    return lax.dot_general(left, right, (((0,), (0,)), ((), ())), preferred_element_type=F32)


def split2(value):
    high = value.astype(BF16)
    return high, (value - high.astype(F32)).astype(BF16)


def iota(shape, dim):
    return lax.broadcasted_iota(jnp.int32, shape, dim)


def normed_of(summed):
    inv_rms = lax.rsqrt(jnp.mean(summed * summed, axis=-1, keepdims=True) + EPSILON)
    return inv_rms, summed * inv_rms


def gelu_of(u):
    tanh_val = jnp.tanh(GELU_SCALE * (u + CUBIC * (u * u * u)))
    return tanh_val, 0.5 * u * (1.0 + tanh_val)


def pick(index, values):
    out = jnp.int32(values[0])
    for at, value in enumerate(values[1:], 1):
        out = jnp.where(index == at, jnp.int32(value), out)
    return out


def edge_kernel(half, feat, base, table, near, far, rows_buf, base_buf, table_buf, sems):
    length = feat.shape[0]
    edge = rows_buf.shape[1]
    copies = [
        pltpu.make_async_copy(feat.at[pl.ds(0, edge)], rows_buf.at[0], sems.at[0]),
        pltpu.make_async_copy(feat.at[pl.ds(length - edge, edge)], rows_buf.at[1], sems.at[1]),
        pltpu.make_async_copy(base, base_buf, sems.at[2]),
        pltpu.make_async_copy(table, table_buf, sems.at[3]),
    ]
    for copy in copies:
        copy.start()
    for copy in copies:
        copy.wait()
    odd = lax.axis_index("ctx") % 2 == 1
    table_f = table_buf[...].astype(F32)
    kinds = table_f.shape[0]

    def row(values, at, position):
        code = base_buf[:, position : position + 1]
        out = values[at : at + 1, :]
        for b in range(kinds):
            out = out + jnp.where(code == b, table_f[b : b + 1, :], 0.0)
        return out

    top, bottom = rows_buf[0].astype(F32), rows_buf[1].astype(F32)
    for i in range(half):
        first = row(top, i, i)
        last = row(bottom, edge - half + i, length - half + i)
        near[i : i + 1, :] = jnp.where(odd, first, last)
        far[i : i + 1, :] = jnp.where(odd, last, first)


def act_kernel(
    kernel, pool, tok_rows, feat, base, table, gain,
    taps, sums, slope_out, normed_out, act_buf, high_buf, low_buf,
):
    half = kernel // 2
    rows, channels = feat.shape
    block = act_buf.shape[0]
    gain_f = gain[...].reshape(1, channels).astype(F32)
    taps[...] = jnp.zeros_like(taps)
    sums[...] = jnp.zeros_like(sums)
    chunk = 32

    @pl.loop(0, rows // block)
    def _(step):
        start = pl.multiple_of(step * block, block)
        onehot = (iota((table.shape[0], block), 0) == base[:, pl.ds(start, block)]).astype(BF16)
        embed = dot_tn(onehot, table[...])
        for begin in range(0, block, chunk):
            part = slice(begin, begin + chunk)
            here = pl.ds(start + begin, chunk)
            summed = feat[here, :].astype(F32) + embed[part, :]
            inv_rms, normed = normed_of(summed)
            u = normed * gain_f
            tanh_val, value = gelu_of(u)
            slopes = 0.5 * (1.0 + tanh_val) + 0.5 * u * (1.0 - tanh_val * tanh_val) * GELU_SCALE * (
                1.0 + 3.0 * CUBIC * (u * u)
            )
            act_buf[part, :] = value.astype(BF16)
            high_buf[part, :], low_buf[part, :] = split2(summed)
            slope_out[here, :] = inv_rms * (slopes * gain_f)
            normed_out[here, :] = normed
        shape = (kernel * tok_rows, block)
        row = iota(shape, 0)
        tap = sum((row >= tok_rows * j).astype(jnp.int32) for j in range(1, kernel))
        token = row - tap * tok_rows
        offset = iota(shape, 1) + start - tap + half - token * pool
        spread = ((offset >= 0) & (offset < pool)).astype(BF16)
        taps[...] += dot_nn(spread, act_buf[...])
        plain = spread[half * tok_rows : (half + 1) * tok_rows, :]
        sums[...] += dot_nn(plain, high_buf[...]) + dot_nn(plain, low_buf[...])


def taps_kernel(kernel, tok_rows, blocks, taps, gain, near, far, pairs, *rest):
    outs, turn = rest[:blocks], rest[blocks]
    half = kernel // 2
    me = lax.axis_index("ctx")
    odd = me % 2 == 1
    channels = taps.shape[1]
    gain_f = gain[...].reshape(1, channels).astype(F32)
    edges = []
    for edge in (near, far):
        _, normed = normed_of(edge[...])
        edges.append(gelu_of(normed * gain_f)[1].astype(BF16).astype(F32))
    before = jnp.where(odd, edges[0], edges[1])
    after = jnp.where(odd, edges[1], edges[0])
    row = iota((tok_rows, channels), 0)
    highs = []
    for j in range(kernel):
        value = taps[j * tok_rows : (j + 1) * tok_rows, :]
        if j < half:
            extra = jnp.sum(before[j:, :], axis=0, keepdims=True)
            value = value + jnp.where(row == 0, extra, 0.0)
        if j > half:
            extra = jnp.sum(after[: j - half, :], axis=0, keepdims=True)
            value = value + jnp.where(row == tok_rows - 1, extra, 0.0)
        high, low = split2(value)
        highs.append(high)
        pairs[j] = jnp.concatenate([high, low], axis=0)
    width = channels // blocks
    for b in range(blocks):
        turn[b ^ me] = jnp.concatenate([h[:, b * width : (b + 1) * width] for h in highs], axis=1)
    for b in range(blocks):
        outs[b][...] = turn[b]


def pool_kernel(pool, pairs, sums, weights, cot, rows):
    tok_rows = sums.shape[0]
    total = dot_nn(pairs[0], weights[0])
    for j in range(1, pairs.shape[0]):
        total = total + dot_nn(pairs[j], weights[j])
    conv = total[:tok_rows] + total[tok_rows:]
    rows[0] = ((sums[...] + conv) * (1.0 / pool)).astype(BF16)
    rows[1] = cot[...]


def pack_kernel(*refs):
    *parts, out = refs
    at = 0
    for part in parts:
        out[at : at + part.shape[0], :] = part[...]
        at += part.shape[0]


def attention_kernel(pool, blocks, late, *refs):
    parts, refs = refs[:blocks], refs[blocks:]
    weights, refs = refs[:4], refs[4:]
    g_out, refs = refs[0], refs[1:]
    gts, refs = refs[:GATHER], refs[GATHER:]
    p_buf, c_buf, q_buf, k_buf, v_buf, ga_buf, gq_buf, gk_buf, gv_buf, turn = refs
    size = parts[0].shape[1]
    for at, part in enumerate(parts):
        p_buf[at * size : (at + 1) * size, :] = part[0]
        c_buf[at * size : (at + 1) * size, :] = part[1]
    for i, dst in enumerate((q_buf, k_buf, v_buf)):
        dst[...] = dot_nn(p_buf[...], weights[i][...]).astype(BF16)
    ga_buf[...] = dot_nt(c_buf[...], weights[3][...]).astype(BF16)
    scale = 1.0 / DH**0.5
    for h in range(HEADS):
        cols = slice(h * DH, (h + 1) * DH)
        q, k, v, ga = q_buf[:, cols], k_buf[:, cols], v_buf[:, cols], ga_buf[:, cols]
        scores = dot_nt(q, k) * scale
        expo = jnp.exp(scores - jnp.max(scores, axis=-1, keepdims=True))
        probs = expo / jnp.sum(expo, axis=-1, keepdims=True)
        probs_b = probs.astype(BF16)
        out = dot_nn(probs_b, v).astype(BF16)
        delta = jnp.sum(ga.astype(F32) * out.astype(F32), axis=-1, keepdims=True)
        grad_score = (probs * (dot_nt(ga, v) - delta) * scale).astype(BF16)
        gq_buf[:, cols] = dot_nn(grad_score, k).astype(BF16)
        gk_buf[:, cols] = dot_tn(grad_score, q).astype(BF16)
        gv_buf[:, cols] = dot_tn(probs_b, ga).astype(BF16)
    grad = c_buf[...].astype(F32)
    for i, src in enumerate((gq_buf, gk_buf, gv_buf)):
        grad = grad + dot_nt(src[...], weights[i][...])
    g = (grad * (1.0 / pool)).astype(BF16)
    g_out[...] = g
    tokens = g.shape[0]
    eye = (iota((tokens, tokens), 0) == iota((tokens, tokens), 1)).astype(BF16)
    turned = dot_tn(g, eye).astype(BF16)
    count = turn.shape[0]
    span = turned.shape[0] // count
    me = lax.axis_index("dp")
    for o in range(count):
        turn[o ^ me] = turned[o * span : (o + 1) * span, :]
    for r in range(GATHER):
        for at, rel in enumerate(late):
            gts[r][at * span : (at + 1) * span, :] = turn[r ^ rel]


def spread_kernel(kernel, tok_rows, befores, afters, g_ref, weights, highs, lows, near):
    tokens = g_ref.shape[0]
    padded = near.shape[0]
    me = lax.axis_index("ctx")
    row = iota((padded, tokens), 0)
    source = jnp.where(
        row == 0, pick(me, befores), jnp.where(row == tok_rows + 1, pick(me, afters), row - 1)
    )
    source = jnp.where(row > tok_rows + 1, -1, source)
    chosen = (source == iota((padded, tokens), 1)).astype(BF16)
    rows = dot_nn(chosen, g_ref[...]).astype(BF16)
    near[...] = rows
    for j in range(kernel):
        part = slice(j * padded, (j + 1) * padded)
        highs[part, :], lows[part, :] = split2(dot_nt(rows, weights[j]))


def input_grad_kernel(kernel, pool, highs, lows, near, slope, normed, out):
    half = kernel // 2
    rows = out.shape[0]
    padded = near.shape[0]
    start = pl.program_id(0) * rows
    here = pl.ds(pl.multiple_of(start, rows), rows)
    shape = (rows, kernel * padded)
    col = iota(shape, 1)
    tap = sum((col >= padded * j).astype(jnp.int32) for j in range(1, kernel))
    token = col - tap * padded - 1
    offset = iota(shape, 0) + start - tap + half - token * pool
    spread = ((offset >= 0) & (offset < pool)).astype(BF16)
    grad_act = dot_nn(spread, highs[...]) + dot_nn(spread, lows[...])
    plain = spread[:, half * padded : (half + 1) * padded]
    grad_rows = dot_nn(plain, near[...])
    scaled = grad_act * slope[here, :]
    unit = normed[here, :]
    mean = jnp.mean(scaled * unit, axis=-1, keepdims=True)
    out[...] = (grad_rows + scaled - unit * mean).astype(BF16)


def kernel_grad_kernel(factor, *refs):
    acts, gts, (mine, theirs) = refs[:GATHER], refs[GATHER : 2 * GATHER], refs[2 * GATHER :]
    total = None
    for act, gt in zip(acts, gts):
        term = dot_nn(gt[...], act[...])
        total = term if total is None else total + term
    total = total * factor
    span = mine.shape[0]
    mine[...] = total[:span, :]
    theirs[...] = total[span:, :].astype(BF16)


def fold_kernel(mine, other, kept, sent):
    span = kept.shape[0]
    kept[...] = mine[:span, :] + other[:span, :].astype(F32)
    sent[...] = (mine[span:, :] + other[span:, :].astype(F32)).astype(BF16)


def join_kernel(kernel, mine, other, out):
    width = out.shape[1]
    total = jnp.transpose(mine[...] + other[...].astype(F32))
    for j in range(kernel):
        out[j] = total[j * width : (j + 1) * width, :]


def xor_order(count):
    order = [0]
    bit = count // 2
    while bit:
        order = order + [v ^ bit for v in order]
        bit //= 2
    return order


def swap(value, axis, bit):
    count = lax.axis_size(axis)
    return lax.ppermute(value, axis, [(i, i ^ bit) for i in range(count)])


WHOLE = pl.BlockSpec(memory_space=pltpu.VMEM)


def call(body, args, outs, scratch=(), **options):
    options.setdefault("in_specs", [WHOLE] * len(args))
    options.setdefault("out_specs", [WHOLE] * len(outs))
    return pl.pallas_call(
        body,
        out_shape=list(outs),
        scratch_shapes=list(scratch),
        compiler_params=pltpu.CompilerParams(vmem_limit_bytes=VMEM_LIMIT),
        **options,
    )(*args)


def held(value):
    return pltpu.with_memory_space_constraint(value, pltpu.VMEM)


def per_device(
    features, bases, dna_table, norm_gain, w_conv, w_query, w_key, w_value, w_out, cotangent
):
    feat, cot = features[0], cotangent[0]
    kernel = w_conv.shape[0]
    half = kernel // 2
    length, channels = feat.shape
    tok_rows = cot.shape[0]
    pool = length // tok_rows
    n_ctx, n_dp = lax.axis_size("ctx"), lax.axis_size("dp")
    tokens = n_ctx * tok_rows
    width = channels // n_ctx
    narrow = channels // n_dp
    late = list(range(0, n_dp, GATHER))

    order = xor_order(n_ctx)
    place = {rel: at for at, rel in enumerate(order)}
    befores = [-1] + [place[c ^ (c - 1)] * tok_rows + tok_rows - 1 for c in range(1, n_ctx)]
    afters = [place[c ^ (c + 1)] * tok_rows for c in range(n_ctx - 1)] + [-1]

    feat_v = held(feat)
    w_conv_v = held(w_conv)
    squares = [held(w) for w in (w_query, w_key, w_value, w_out)]

    edge = 16
    hbm = pl.BlockSpec(memory_space=pltpu.HBM)
    near, far = call(
        functools.partial(edge_kernel, half),
        (feat, bases, dna_table),
        [pltpu.VMEM((half, channels), F32)] * 2,
        [
            pltpu.VMEM((2, edge, channels), BF16),
            pltpu.VMEM(bases.shape, jnp.int32),
            pltpu.VMEM(dna_table.shape, BF16),
            pltpu.SemaphoreType.DMA((4,)),
        ],
        in_specs=[hbm] * 3,
    )
    near = swap(near, "ctx", 1)
    links = [(i, i + 1) for i in range(1, n_ctx - 1, 2)]
    far = lax.ppermute(far, "ctx", links + [(b, a) for a, b in links])

    block = 128
    taps, sums, slope, normed = call(
        functools.partial(act_kernel, kernel, pool, tok_rows),
        (feat_v, bases, dna_table, norm_gain),
        [
            pltpu.VMEM((kernel * tok_rows, channels), F32),
            pltpu.VMEM((tok_rows, channels), F32),
            pltpu.VMEM((length, channels), F32),
            pltpu.VMEM((length, channels), F32),
        ],
        [pltpu.VMEM((block, channels), BF16)] * 3,
    )
    pairs, *acts = call(
        functools.partial(taps_kernel, kernel, tok_rows, n_ctx),
        (taps, norm_gain, near, far),
        [pltpu.VMEM((kernel, 2 * tok_rows, channels), BF16)]
        + [pltpu.VMEM((tok_rows, kernel * width), BF16)] * n_ctx,
        [pltpu.VMEM((n_ctx, tok_rows, kernel * width), BF16)],
    )
    acts = [acts[0]] + [swap(acts[rel], "ctx", rel) for rel in order[1:]]
    rows = list(
        call(
            functools.partial(pool_kernel, pool),
            (pairs, sums, w_conv_v, cot),
            [pltpu.VMEM((2, tok_rows, channels), BF16)],
        )
    )
    bit = n_ctx // 2
    while bit:
        rows = rows + [swap(value, "ctx", bit) for value in rows]
        bit //= 2

    act = call(pack_kernel, acts, [pltpu.VMEM((tokens, kernel * width), BF16)])[0]

    act_z = swap(act, "dp", 2)
    act_x = swap(act, "dp", 1)

    g_all, *gts = call(
        functools.partial(attention_kernel, pool, n_ctx, late),
        (*rows, *squares),
        [pltpu.VMEM((tokens, channels), BF16)]
        + [pltpu.VMEM((len(late) * narrow, tokens), BF16)] * GATHER,
        [pltpu.VMEM((tokens, channels), BF16)] * 9 + [pltpu.VMEM((n_dp, narrow, tokens), BF16)],
    )

    act_zx = swap(act_z, "dp", 1)
    gts = [gts[0]] + [swap(gts[rel], "dp", rel) for rel in range(1, GATHER)]

    padded = -(-(tok_rows + 2) // 8) * 8
    highs, lows, near_g = call(
        functools.partial(spread_kernel, kernel, tok_rows, befores, afters),
        (g_all, w_conv_v),
        [pltpu.VMEM((kernel * padded, channels), BF16)] * 2
        + [pltpu.VMEM((padded, channels), BF16)],
    )
    factor = 1.0 / (n_dp * length * n_ctx) ** 0.5
    kept = len(late) // 2
    mine, theirs = call(
        functools.partial(kernel_grad_kernel, factor),
        (act, act_x, act_z, act_zx, *gts),
        [
            pltpu.VMEM((kept * narrow, kernel * width), F32),
            pltpu.VMEM((kept * narrow, kernel * width), BF16),
        ],
    )
    other = swap(theirs, "dp", GATHER * kept)
    while kept > 1:
        kept //= 2
        mine, theirs = call(
            fold_kernel,
            (mine, other),
            [
                pltpu.VMEM((kept * narrow, kernel * width), F32),
                pltpu.VMEM((kept * narrow, kernel * width), BF16),
            ],
        )
        other = swap(theirs, "dp", GATHER * kept)

    by_rows = pl.BlockSpec((block, channels), lambda i: (i, 0))
    grad_in = call(
        functools.partial(input_grad_kernel, kernel, pool),
        (highs, lows, near_g, slope, normed),
        [jax.ShapeDtypeStruct((length, channels), BF16)],
        grid=(length // block,),
        out_specs=[by_rows],
    )[0]
    grad_conv = call(
        functools.partial(join_kernel, kernel),
        (mine, other),
        [jax.ShapeDtypeStruct((kernel, width, narrow), F32)],
    )[0]
    return grad_in[None], jnp.transpose(grad_conv, (1, 0, 2))


def solution(mesh):
    in_specs = (
        P("dp", "ctx", None),
        P("dp", "ctx"),
        P(),
        P(),
        P(),
        P(),
        P(),
        P(),
        P(),
        P("dp", "ctx", None),
    )
    out_specs = (P("dp", "ctx", None), P("ctx", None, "dp"))
    return jax.shard_map(
        per_device, mesh=mesh, in_specs=in_specs, out_specs=out_specs, check_vma=False
    )
```

profile of v0, /device:TPU:0, one launch (start us, length us, event | category | flops | bytes accessed | tf_op | source)
XLA Modules:
  0.0 54.4 jit_solution(17151995466444019214)
XLA Ops:
  0.6 1.1 %copy-done.2 = bf16[1,512,768]{2,1,0:T(8,128)(2,1)S(1)} copy-done((bf16[1,512,768]{2,1,0:T(8,128)(2,1)S(1)}, bf16[1,512,768]{2,1,0:T(8,128)(2,1)}, u32[]{:S(2)}) %copy-start.2) | copy-done | bytes 786456
  1.8 0.7 %copy-done.8 = bf16[4,768]{1,0:T(4,128)(2,1)S(1)} copy-done((bf16[4,768]{1,0:T(4,128)(2,1)S(1)}, bf16[4,768]{1,0:T(4,128)(2,1)}, u32[]{:S(2)}) %copy-start.8) | copy-done | bytes 6168
  2.5 0.7 %copy-done.9 = s32[1,512]{1,0:T(1,128)S(1)} copy-done((s32[1,512]{1,0:T(1,128)S(1)}, s32[1,512]{1,0:T(1,128)}, u32[]{:S(2)}) %copy-start.9) | copy-done | bytes 2072
  3.1 0.2 shard_map.114
  3.4 0.6 %collective-permute-start = (f32[2,768]{1,0:T(2,128)S(1)}, f32[2,768]{1,0:T(2,128)S(1)}, u32[]{:S(2)}, u32[]{:S(2)}) collective-permute-start(f32[2,768]{1,0:T(2,128)S(1)} %get-tuple-element.24), channel_id=1, source_target_pairs={{0,1},{1,0},{2,3},{3,2},{4,5},{5,4},{6,7},{7,6},{8,9},{9,8},{10,11... | collective-permute-start | bytes 18440 | tf_op jit(solution)/shard_map/ppermute | solution.py:305
  3.9 0.6 %collective-permute-start.1 = (f32[2,768]{1,0:T(2,128)S(1)}, f32[2,768]{1,0:T(2,128)S(1)}, u32[]{:S(2)}, u32[]{:S(2)}) collective-permute-start(f32[2,768]{1,0:T(2,128)S(1)} %get-tuple-element.25), channel_id=1, source_target_pairs={{1,2},{2,1},{5,6},{6,5},{9,10},{10,9},{13,14},{14,13},{17,18},{18,... | collective-permute-start | bytes 18440 | tf_op jit(solution)/shard_map/ppermute | solution.py:367
  4.6 0.0 copy-start.10
  4.6 0.7 %copy-done.10 = bf16[768]{0:T(1024)(128)(2,1)S(1)} copy-done((bf16[768]{0:T(1024)(128)(2,1)S(1)}, bf16[768]{0:T(1024)(128)(2,1)}, u32[]{:S(2)}) %copy-start.10) | copy-done | bytes 1560
  5.3 3.5 %shard_map.113 = (f32[160,768]{1,0:T(8,128)S(1)}, f32[32,768]{1,0:T(8,128)S(1)}, f32[512,768]{1,0:T(8,128)S(1)}, f32[512,768]{1,0:T(8,128)S(1)}) custom-call(bf16[512,768]{1,0:T(8,128)(2,1)S(1)} %bitcast.5, s32[1,512]{1,0:T(1,128)S(1)} %copy-done.9, bf16[4,768]{1,0:T(4,128)(2,1)S(1)} %copy-done.8, bf16[768]{0:T(1024)(128)(2,1)S(1)} %copy-done.10), custom_call_target="tpu_custom_call" | custom-call | tf_op jit(solution)/shard_map/pallas_call | solution.py:314
  8.8 0.0 collective-permute-done.near
  8.8 0.0 collective-permute-done.1.far
  8.8 0.2 shard_map.115
  9.1 3.9 %collective-permute-start.5 = (bf16[32,960]{1,0:T(8,128)(2,1)S(1)}, bf16[32,960]{1,0:T(8,128)(2,1)S(1)}, u32[]{:S(2)}, u32[]{:S(2)}) collective-permute-start(bf16[32,960]{1,0:T(8,128)(2,1)S(1)} %get-tuple-element.35), channel_id=1, source_target_pairs={{0,2},{1,3},{2,0},{3,1},{4,6},{5,7},{6,4},{7,5},{8,10},{9,11},{10,... | collective-permute-start | bytes 184328 | tf_op jit(solution)/shard_map/ppermute | solution.py:305
  12.9 0.2 collective-permute-start.6
  13.1 1.3 %collective-permute-start.7 = (bf16[32,960]{1,0:T(8,128)(2,1)S(1)}, bf16[32,960]{1,0:T(8,128)(2,1)S(1)}, u32[]{:S(2)}, u32[]{:S(2)}) collective-permute-start(bf16[32,960]{1,0:T(8,128)(2,1)S(1)} %get-tuple-element.37), channel_id=1, source_target_pairs={{0,3},{1,2},{2,1},{3,0},{4,7},{5,6},{6,5},{7,4},{8,11},{9,10},{10,... | collective-permute-start | bytes 184328 | tf_op jit(solution)/shard_map/ppermute | solution.py:305
  14.4 0.8 %collective-permute-done.5.refs_1_ = bf16[32,960]{1,0:T(8,128)(2,1)S(1)} collective-permute-done((bf16[32,960]{1,0:T(8,128)(2,1)S(1)}, bf16[32,960]{1,0:T(8,128)(2,1)S(1)}, u32[]{:S(2)}, u32[]{:S(2)}) %collective-permute-start.5) | collective-permute-done | bytes 61472 | tf_op jit(solution)/shard_map/ppermute | solution.py:305
  15.2 0.0 collective-permute-done.6.refs_2_
  15.2 2.3 %collective-permute-done.7.refs_3_ = bf16[32,960]{1,0:T(8,128)(2,1)S(1)} collective-permute-done((bf16[32,960]{1,0:T(8,128)(2,1)S(1)}, bf16[32,960]{1,0:T(8,128)(2,1)S(1)}, u32[]{:S(2)}, u32[]{:S(2)}) %collective-permute-start.7) | collective-permute-done | bytes 61472 | tf_op jit(solution)/shard_map/ppermute | solution.py:305
  17.5 1.4 %collective-permute-start.9 = (bf16[128,960]{1,0:T(8,128)(2,1)S(1)}, bf16[128,960]{1,0:T(8,128)(2,1)S(1)}, u32[]{:S(2)}, u32[]{:S(2)}) collective-permute-start(bf16[128,960]{1,0:T(8,128)(2,1)S(1)} %shard_map.120.refs_0_), channel_id=1, source_target_pairs={{0,8},{4,12},{8,0},{12,4},{16,24},{20,28},{24,16},{28,20},{1,9},{5... | collective-permute-start | bytes 737288 | tf_op jit(solution)/shard_map/ppermute | solution.py:305
  18.9 2.7 %copy-done = bf16[5,768,768]{2,1,0:T(8,128)(2,1)S(1)} copy-done((bf16[5,768,768]{2,1,0:T(8,128)(2,1)S(1)}, bf16[5,768,768]{2,1,0:T(8,128)(2,1)}, u32[]{:S(2)}) %copy-start) | copy-done | bytes 5898264
  21.6 1.1 %shard_map.116.refs_0_ = bf16[2,32,768]{2,1,0:T(8,128)(2,1)S(1)} custom-call(bf16[5,64,768]{2,1,0:T(8,128)(2,1)S(1)} %get-tuple-element.26.pairs, f32[32,768]{1,0:T(8,128)S(1)} %get-tuple-element.27.sums, bf16[5,768,768]{2,1,0:T(8,128)(2,1)S(1)} %copy-done, bf16[32,768]{1,0:T(8,128)(2,1)S(1)} %bitcast.6), custom_call_target="tpu_custom_call" | custom-call | tf_op jit(solution)/shard_map/pallas_call | solution.py:314
  22.7 1.9 %collective-permute-start.2 = (bf16[2,32,768]{2,1,0:T(8,128)(2,1)S(1)}, bf16[2,32,768]{2,1,0:T(8,128)(2,1)S(1)}, u32[]{:S(2)}, u32[]{:S(2)}) collective-permute-start(bf16[2,32,768]{2,1,0:T(8,128)(2,1)S(1)} %shard_map.116.refs_0_), channel_id=1, source_target_pairs={{0,2},{1,3},{2,0},{3,1},{4,6},{5,7},{6,4},{7,5},{8,10},{9,11},{10,... | collective-permute-start | bytes 294920 | tf_op jit(solution)/shard_map/ppermute | solution.py:305
  24.6 1.5 %collective-permute-start.8 = (bf16[128,960]{1,0:T(8,128)(2,1)S(1)}, bf16[128,960]{1,0:T(8,128)(2,1)S(1)}, u32[]{:S(2)}, u32[]{:S(2)}) collective-permute-start(bf16[128,960]{1,0:T(8,128)(2,1)S(1)} %shard_map.120.refs_0_), channel_id=1, source_target_pairs={{0,4},{4,0},{8,12},{12,8},{16,20},{20,16},{24,28},{28,24},{1,5},{5... | collective-permute-start | bytes 737288 | tf_op jit(solution)/shard_map/ppermute | solution.py:305
  26.1 0.0 collective-permute-done.9.refs_2_
  26.1 1.4 %collective-permute-start.10 = (bf16[128,960]{1,0:T(8,128)(2,1)S(1)}, bf16[128,960]{1,0:T(8,128)(2,1)S(1)}, u32[]{:S(2)}, u32[]{:S(2)}) collective-permute-start(bf16[128,960]{1,0:T(8,128)(2,1)S(1)} %collective-permute-done.9.refs_2_), channel_id=1, source_target_pairs={{0,4},{4,0},{8,12},{12,8},{16,20},{20,16},{24,28},{28,24},{1,5},{5... | collective-permute-start | bytes 737288 | tf_op jit(solution)/shard_map/ppermute | solution.py:305
  27.5 0.0 collective-permute-start.3
  27.5 0.2 collective-permute-done.2.refs_1_
  27.7 0.3 collective-permute-start.4
  28.0 0.8 %collective-permute-done.3.refs_2_ = bf16[2,32,768]{2,1,0:T(8,128)(2,1)S(1)} collective-permute-done((bf16[2,32,768]{2,1,0:T(8,128)(2,1)S(1)}, bf16[2,32,768]{2,1,0:T(8,128)(2,1)S(1)}, u32[]{:S(2)}, u32[]{:S(2)}) %collective-permute-start.3) | collective-permute-done | bytes 98336 | tf_op jit(solution)/shard_map/ppermute | solution.py:305
  28.8 0.2 collective-permute-done.4.refs_3_
  29.0 0.0 copy-done.4
  29.0 0.0 copy-start.1
  29.1 5.9 %shard_map.117 = (bf16[128,768]{1,0:T(8,128)(2,1)S(1)}, bf16[192,128]{1,0:T(8,128)(2,1)S(1)}, bf16[192,128]{1,0:T(8,128)(2,1)S(1)}, bf16[192,128]{1,0:T(8,128)(2,1)S(1)}, bf16[192,128]{1,0:T(8,128)(2,1)S(1)}) custom-call(bf16[2,32,768]{2,1,0:T(8,128)(2,1)S(1)} %shard_map.116.refs_0_, bf16[2,32,768]{2,1,0:T(8,128)(2,1)S(1)} %collective-permute-done.2.refs_1_, ...), custom_call_target="tpu_custom_call" | custom-call | tf_op jit(solution)/shard_map/pallas_call | solution.py:314
  34.9 1.6 %collective-permute-start.11 = (bf16[192,128]{1,0:T(8,128)(2,1)S(1)}, bf16[192,128]{1,0:T(8,128)(2,1)S(1)}, u32[]{:S(2)}, u32[]{:S(2)}) collective-permute-start(bf16[192,128]{1,0:T(8,128)(2,1)S(1)} %get-tuple-element.39), channel_id=1, source_target_pairs={{0,4},{4,0},{8,12},{12,8},{16,20},{20,16},{24,28},{28,24},{1,5},{5... | collective-permute-start | bytes 147464 | tf_op jit(solution)/shard_map/ppermute | solution.py:305
  36.5 0.6 %collective-permute-start.12 = (bf16[192,128]{1,0:T(8,128)(2,1)S(1)}, bf16[192,128]{1,0:T(8,128)(2,1)S(1)}, u32[]{:S(2)}, u32[]{:S(2)}) collective-permute-start(bf16[192,128]{1,0:T(8,128)(2,1)S(1)} %get-tuple-element.40), channel_id=1, source_target_pairs={{0,8},{4,12},{8,0},{12,4},{16,24},{20,28},{24,16},{28,20},{1,9},{5... | collective-permute-start | bytes 147464 | tf_op jit(solution)/shard_map/ppermute | solution.py:305
  37.0 1.4 %collective-permute-start.13 = (bf16[192,128]{1,0:T(8,128)(2,1)S(1)}, bf16[192,128]{1,0:T(8,128)(2,1)S(1)}, u32[]{:S(2)}, u32[]{:S(2)}) collective-permute-start(bf16[192,128]{1,0:T(8,128)(2,1)S(1)} %get-tuple-element.41), channel_id=1, source_target_pairs={{0,12},{4,8},{8,4},{12,0},{16,28},{20,24},{24,20},{28,16},{1,13},{... | collective-permute-start | bytes 147464 | tf_op jit(solution)/shard_map/ppermute | solution.py:305
  38.5 0.6 %collective-permute-done.11.refs_5_ = bf16[192,128]{1,0:T(8,128)(2,1)S(1)} collective-permute-done((bf16[192,128]{1,0:T(8,128)(2,1)S(1)}, bf16[192,128]{1,0:T(8,128)(2,1)S(1)}, u32[]{:S(2)}, u32[]{:S(2)}) %collective-permute-start.11) | collective-permute-done | bytes 49184 | tf_op jit(solution)/shard_map/ppermute | solution.py:305
  39.1 1.7 %collective-permute-done.12.refs_6_ = bf16[192,128]{1,0:T(8,128)(2,1)S(1)} collective-permute-done((bf16[192,128]{1,0:T(8,128)(2,1)S(1)}, bf16[192,128]{1,0:T(8,128)(2,1)S(1)}, u32[]{:S(2)}, u32[]{:S(2)}) %collective-permute-start.12) | collective-permute-done | bytes 49184 | tf_op jit(solution)/shard_map/ppermute | solution.py:305
  40.8 1.3 %collective-permute-done.13.refs_7_ = bf16[192,128]{1,0:T(8,128)(2,1)S(1)} collective-permute-done((bf16[192,128]{1,0:T(8,128)(2,1)S(1)}, bf16[192,128]{1,0:T(8,128)(2,1)S(1)}, u32[]{:S(2)}, u32[]{:S(2)}) %collective-permute-start.13) | collective-permute-done | bytes 49184 | tf_op jit(solution)/shard_map/ppermute | solution.py:305
  42.0 0.0 collective-permute-done.8.refs_1_
  42.0 0.0 collective-permute-done.10.refs_3_
  42.0 0.6 %shard_map.121 = (f32[96,960]{1,0:T(8,128)S(1)}, bf16[96,960]{1,0:T(8,128)(2,1)S(1)}) custom-call(bf16[128,960]{1,0:T(8,128)(2,1)S(1)} %shard_map.120.refs_0_, bf16[128,960]{1,0:T(8,128)(2,1)S(1)} %collective-permute-done.8.refs_1_, bf16[128,960]{1,0:T(8,128)(2,1)S(1)} %collective-permute-done.9.refs_2_, ...), custom_call_target="tpu_custom_call" | custom-call | tf_op jit(solution)/shard_map/pallas_call | solution.py:314
  42.6 2.7 %collective-permute-start.14 = (bf16[96,960]{1,0:T(8,128)(2,1)S(1)}, bf16[96,960]{1,0:T(8,128)(2,1)S(1)}, u32[]{:S(2)}, u32[]{:S(2)}) collective-permute-start(bf16[96,960]{1,0:T(8,128)(2,1)S(1)} %get-tuple-element.43), channel_id=1, source_target_pairs={{0,16},{4,20},{8,24},{12,28},{16,0},{20,4},{24,8},{28,12},{1,17},{... | collective-permute-start | bytes 552968 | tf_op jit(solution)/shard_map/ppermute | solution.py:305
  45.3 0.0 copy-done.1
  45.3 1.8 %shard_map.118 = (bf16[200,768]{1,0:T(8,128)(2,1)S(1)}, bf16[200,768]{1,0:T(8,128)(2,1)S(1)}, bf16[40,768]{1,0:T(8,128)(2,1)S(1)}) custom-call(bf16[128,768]{1,0:T(8,128)(2,1)S(1)} %get-tuple-element.28.g_ref, bf16[5,768,768]{2,1,0:T(8,128)(2,1)S(1)} %copy-done.1), custom_call_target="tpu_custom_call" | custom-call | tf_op jit(solution)/shard_map/pallas_call | solution.py:314
  47.0 2.5 %shard_map.119 = bf16[512,768]{1,0:T(8,128)(2,1)} custom-call(bf16[200,768]{1,0:T(8,128)(2,1)S(1)} %get-tuple-element.29.highs, bf16[200,768]{1,0:T(8,128)(2,1)S(1)} %get-tuple-element.30.lows, bf16[40,768]{1,0:T(8,128)(2,1)S(1)} %get-tuple-element.31.near, f32[512,768]{1,0:T(8,128)S(1)} %get-tuple-element.32.slope, f32[512,768]{1,0:T(8,128)S(1)} %get-tuple-element.33.normed), custom_call_target="tpu_custom_call" | custom-call | tf_op jit(solution)/shard_map/pallas_call | solution.py:314
  49.6 3.9 %collective-permute-done.14.other = bf16[96,960]{1,0:T(8,128)(2,1)S(1)} collective-permute-done((bf16[96,960]{1,0:T(8,128)(2,1)S(1)}, bf16[96,960]{1,0:T(8,128)(2,1)S(1)}, u32[]{:S(2)}, u32[]{:S(2)}) %collective-permute-start.14) | collective-permute-done | bytes 184352 | tf_op jit(solution)/shard_map/ppermute | solution.py:305
  53.4 1.0 %shard_map.122 = f32[5,192,96]{2,1,0:T(8,128)} custom-call(f32[96,960]{1,0:T(8,128)S(1)} %get-tuple-element.42.mine, bf16[96,960]{1,0:T(8,128)(2,1)S(1)} %collective-permute-done.14.other), custom_call_target="tpu_custom_call" | custom-call | tf_op jit(solution)/shard_map/pallas_call | solution.py:314
  (14 shorter events, 0.0 us)
Async XLA Ops:
  0.6 1.1 %copy-start.2 = (bf16[1,512,768]{2,1,0:T(8,128)(2,1)S(1)}, bf16[1,512,768]{2,1,0:T(8,128)(2,1)}, u32[]{:S(2)}) copy-start(bf16[1,512,768]{2,1,0:T(8,128)(2,1)} %param.10) | copy-start | bytes 2359300
  1.8 0.7 %copy-start.8 = (bf16[4,768]{1,0:T(4,128)(2,1)S(1)}, bf16[4,768]{1,0:T(4,128)(2,1)}, u32[]{:S(2)}) copy-start(bf16[4,768]{1,0:T(4,128)(2,1)} %table.3) | copy-start | bytes 18436
  2.5 0.7 %copy-start.9 = (s32[1,512]{1,0:T(1,128)S(1)}, s32[1,512]{1,0:T(1,128)}, u32[]{:S(2)}) copy-start(s32[1,512]{1,0:T(1,128)} %base.3) | copy-start | bytes 6148
  3.1 15.7 %copy-start.7 = (bf16[1,32,768]{2,1,0:T(8,128)(2,1)S(1)}, bf16[1,32,768]{2,1,0:T(8,128)(2,1)}, u32[]{:S(2)}) copy-start(bf16[1,32,768]{2,1,0:T(8,128)(2,1)} %param.19) | copy-start | bytes 147460
  3.4 5.4 %collective-permute-start = (f32[2,768]{1,0:T(2,128)S(1)}, f32[2,768]{1,0:T(2,128)S(1)}, u32[]{:S(2)}, u32[]{:S(2)}) collective-permute-start(f32[2,768]{1,0:T(2,128)S(1)} %get-tuple-element.24), channel_id=1, source_target_pairs={{0,1},{1,0},{2,3},{3,2},{4,5},{5,4},{6,7},{7,6},{8,9},{9,8},{10,11... | collective-permute-start | bytes 18440 | tf_op jit(solution)/shard_map/ppermute | solution.py:305
  3.9 4.9 %collective-permute-start.1 = (f32[2,768]{1,0:T(2,128)S(1)}, f32[2,768]{1,0:T(2,128)S(1)}, u32[]{:S(2)}, u32[]{:S(2)}) collective-permute-start(f32[2,768]{1,0:T(2,128)S(1)} %get-tuple-element.25), channel_id=1, source_target_pairs={{1,2},{2,1},{5,6},{6,5},{9,10},{10,9},{13,14},{14,13},{17,18},{18,... | collective-permute-start | bytes 18440 | tf_op jit(solution)/shard_map/ppermute | solution.py:367
  4.6 0.7 %copy-start.10 = (bf16[768]{0:T(1024)(128)(2,1)S(1)}, bf16[768]{0:T(1024)(128)(2,1)}, u32[]{:S(2)}) copy-start(bf16[768]{0:T(1024)(128)(2,1)} %gain.3) | copy-start | bytes 4612
  9.1 6.1 %collective-permute-start.5 = (bf16[32,960]{1,0:T(8,128)(2,1)S(1)}, bf16[32,960]{1,0:T(8,128)(2,1)S(1)}, u32[]{:S(2)}, u32[]{:S(2)}) collective-permute-start(bf16[32,960]{1,0:T(8,128)(2,1)S(1)} %get-tuple-element.35), channel_id=1, source_target_pairs={{0,2},{1,3},{2,0},{3,1},{4,6},{5,7},{6,4},{7,5},{8,10},{9,11},{10,... | collective-permute-start | bytes 184328 | tf_op jit(solution)/shard_map/ppermute | solution.py:305
  12.9 2.2 %collective-permute-start.6 = (bf16[32,960]{1,0:T(8,128)(2,1)S(1)}, bf16[32,960]{1,0:T(8,128)(2,1)S(1)}, u32[]{:S(2)}, u32[]{:S(2)}) collective-permute-start(bf16[32,960]{1,0:T(8,128)(2,1)S(1)} %get-tuple-element.36), channel_id=1, source_target_pairs={{0,1},{1,0},{2,3},{3,2},{4,5},{5,4},{6,7},{7,6},{8,9},{9,8},{10,11... | collective-permute-start | bytes 184328 | tf_op jit(solution)/shard_map/ppermute | solution.py:305
  13.1 4.3 %collective-permute-start.7 = (bf16[32,960]{1,0:T(8,128)(2,1)S(1)}, bf16[32,960]{1,0:T(8,128)(2,1)S(1)}, u32[]{:S(2)}, u32[]{:S(2)}) collective-permute-start(bf16[32,960]{1,0:T(8,128)(2,1)S(1)} %get-tuple-element.37), channel_id=1, source_target_pairs={{0,3},{1,2},{2,1},{3,0},{4,7},{5,6},{6,5},{7,4},{8,11},{9,10},{10,... | collective-permute-start | bytes 184328 | tf_op jit(solution)/shard_map/ppermute | solution.py:305
  17.5 8.6 %collective-permute-start.9 = (bf16[128,960]{1,0:T(8,128)(2,1)S(1)}, bf16[128,960]{1,0:T(8,128)(2,1)S(1)}, u32[]{:S(2)}, u32[]{:S(2)}) collective-permute-start(bf16[128,960]{1,0:T(8,128)(2,1)S(1)} %shard_map.120.refs_0_), channel_id=1, source_target_pairs={{0,8},{4,12},{8,0},{12,4},{16,24},{20,28},{24,16},{28,20},{1,9},{5... | collective-permute-start | bytes 737288 | tf_op jit(solution)/shard_map/ppermute | solution.py:305
  18.9 2.7 %copy-start = (bf16[5,768,768]{2,1,0:T(8,128)(2,1)S(1)}, bf16[5,768,768]{2,1,0:T(8,128)(2,1)}, u32[]{:S(2)}) copy-start(bf16[5,768,768]{2,1,0:T(8,128)(2,1)} %weights.3) | copy-start | bytes 17694724
  21.6 7.5 %copy-start.3 = (bf16[768,768]{1,0:T(8,128)(2,1)S(1)}, bf16[768,768]{1,0:T(8,128)(2,1)}, u32[]{:S(2)}) copy-start(bf16[768,768]{1,0:T(8,128)(2,1)} %refs_4_.1) | copy-start | bytes 3538948
  21.6 7.5 %copy-start.4 = (bf16[768,768]{1,0:T(8,128)(2,1)S(1)}, bf16[768,768]{1,0:T(8,128)(2,1)}, u32[]{:S(2)}) copy-start(bf16[768,768]{1,0:T(8,128)(2,1)} %refs_5_.1) | copy-start | bytes 3538948
  21.6 7.5 %copy-start.5 = (bf16[768,768]{1,0:T(8,128)(2,1)S(1)}, bf16[768,768]{1,0:T(8,128)(2,1)}, u32[]{:S(2)}) copy-start(bf16[768,768]{1,0:T(8,128)(2,1)} %refs_6_.1) | copy-start | bytes 3538948
  21.6 7.5 %copy-start.6 = (bf16[768,768]{1,0:T(8,128)(2,1)S(1)}, bf16[768,768]{1,0:T(8,128)(2,1)}, u32[]{:S(2)}) copy-start(bf16[768,768]{1,0:T(8,128)(2,1)} %refs_7_.1) | copy-start | bytes 3538948
  22.7 5.0 %collective-permute-start.2 = (bf16[2,32,768]{2,1,0:T(8,128)(2,1)S(1)}, bf16[2,32,768]{2,1,0:T(8,128)(2,1)S(1)}, u32[]{:S(2)}, u32[]{:S(2)}) collective-permute-start(bf16[2,32,768]{2,1,0:T(8,128)(2,1)S(1)} %shard_map.116.refs_0_), channel_id=1, source_target_pairs={{0,2},{1,3},{2,0},{3,1},{4,6},{5,7},{6,4},{7,5},{8,10},{9,11},{10,... | collective-permute-start | bytes 294920 | tf_op jit(solution)/shard_map/ppermute | solution.py:305
  24.6 17.5 %collective-permute-start.8 = (bf16[128,960]{1,0:T(8,128)(2,1)S(1)}, bf16[128,960]{1,0:T(8,128)(2,1)S(1)}, u32[]{:S(2)}, u32[]{:S(2)}) collective-permute-start(bf16[128,960]{1,0:T(8,128)(2,1)S(1)} %shard_map.120.refs_0_), channel_id=1, source_target_pairs={{0,4},{4,0},{8,12},{12,8},{16,20},{20,16},{24,28},{28,24},{1,5},{5... | collective-permute-start | bytes 737288 | tf_op jit(solution)/shard_map/ppermute | solution.py:305
  26.1 16.0 %collective-permute-start.10 = (bf16[128,960]{1,0:T(8,128)(2,1)S(1)}, bf16[128,960]{1,0:T(8,128)(2,1)S(1)}, u32[]{:S(2)}, u32[]{:S(2)}) collective-permute-start(bf16[128,960]{1,0:T(8,128)(2,1)S(1)} %collective-permute-done.9.refs_2_), channel_id=1, source_target_pairs={{0,4},{4,0},{8,12},{12,8},{16,20},{20,16},{24,28},{28,24},{1,5},{5... | collective-permute-start | bytes 737288 | tf_op jit(solution)/shard_map/ppermute | solution.py:305
  27.5 1.3 %collective-permute-start.3 = (bf16[2,32,768]{2,1,0:T(8,128)(2,1)S(1)}, bf16[2,32,768]{2,1,0:T(8,128)(2,1)S(1)}, u32[]{:S(2)}, u32[]{:S(2)}) collective-permute-start(bf16[2,32,768]{2,1,0:T(8,128)(2,1)S(1)} %shard_map.116.refs_0_), channel_id=1, source_target_pairs={{0,1},{1,0},{2,3},{3,2},{4,5},{5,4},{6,7},{7,6},{8,9},{9,8},{10,11... | collective-permute-start | bytes 294920 | tf_op jit(solution)/shard_map/ppermute | solution.py:305
  27.7 1.3 %collective-permute-start.4 = (bf16[2,32,768]{2,1,0:T(8,128)(2,1)S(1)}, bf16[2,32,768]{2,1,0:T(8,128)(2,1)S(1)}, u32[]{:S(2)}, u32[]{:S(2)}) collective-permute-start(bf16[2,32,768]{2,1,0:T(8,128)(2,1)S(1)} %collective-permute-done.2.refs_1_), channel_id=1, source_target_pairs={{0,1},{1,0},{2,3},{3,2},{4,5},{5,4},{6,7},{7,6},{8,9},{9,8},{10,11... | collective-permute-start | bytes 294920 | tf_op jit(solution)/shard_map/ppermute | solution.py:305
  29.0 16.2 %copy-start.1 = (bf16[5,768,768]{2,1,0:T(8,128)(2,1)S(1)}, bf16[5,768,768]{2,1,0:T(8,128)(2,1)}, u32[]{:S(2)}) copy-start(bf16[5,768,768]{2,1,0:T(8,128)(2,1)} %weights.3) | copy-start | bytes 17694724
  34.9 4.2 %collective-permute-start.11 = (bf16[192,128]{1,0:T(8,128)(2,1)S(1)}, bf16[192,128]{1,0:T(8,128)(2,1)S(1)}, u32[]{:S(2)}, u32[]{:S(2)}) collective-permute-start(bf16[192,128]{1,0:T(8,128)(2,1)S(1)} %get-tuple-element.39), channel_id=1, source_target_pairs={{0,4},{4,0},{8,12},{12,8},{16,20},{20,16},{24,28},{28,24},{1,5},{5... | collective-permute-start | bytes 147464 | tf_op jit(solution)/shard_map/ppermute | solution.py:305
  36.5 4.3 %collective-permute-start.12 = (bf16[192,128]{1,0:T(8,128)(2,1)S(1)}, bf16[192,128]{1,0:T(8,128)(2,1)S(1)}, u32[]{:S(2)}, u32[]{:S(2)}) collective-permute-start(bf16[192,128]{1,0:T(8,128)(2,1)S(1)} %get-tuple-element.40), channel_id=1, source_target_pairs={{0,8},{4,12},{8,0},{12,4},{16,24},{20,28},{24,16},{28,20},{1,9},{5... | collective-permute-start | bytes 147464 | tf_op jit(solution)/shard_map/ppermute | solution.py:305
  37.0 5.0 %collective-permute-start.13 = (bf16[192,128]{1,0:T(8,128)(2,1)S(1)}, bf16[192,128]{1,0:T(8,128)(2,1)S(1)}, u32[]{:S(2)}, u32[]{:S(2)}) collective-permute-start(bf16[192,128]{1,0:T(8,128)(2,1)S(1)} %get-tuple-element.41), channel_id=1, source_target_pairs={{0,12},{4,8},{8,4},{12,0},{16,28},{20,24},{24,20},{28,16},{1,13},{... | collective-permute-start | bytes 147464 | tf_op jit(solution)/shard_map/ppermute | solution.py:305
  42.6 10.8 %collective-permute-start.14 = (bf16[96,960]{1,0:T(8,128)(2,1)S(1)}, bf16[96,960]{1,0:T(8,128)(2,1)S(1)}, u32[]{:S(2)}, u32[]{:S(2)}) collective-permute-start(bf16[96,960]{1,0:T(8,128)(2,1)S(1)} %get-tuple-element.43), channel_id=1, source_target_pairs={{0,16},{4,20},{8,24},{12,28},{16,0},{20,4},{24,8},{28,12},{1,17},{... | collective-permute-start | bytes 552968 | tf_op jit(solution)/shard_map/ppermute | solution.py:305
where the time goes:
time: 54.7 us; the launch traced here: 54.4 us
  starting transfers between devices  19.2 us (35%)
  Pallas kernels  16.8 us (31%)
  waiting for transfers between devices  11.7 us (21%)
  local copies, waits for them, and re-layouts  5.87 us (11%)
  between operations  0.77 us (1%)
    ppermute x14, starting transfers between devices, swap(): return lax.ppermute(value, axis, [(i, i ^ bit) for i in range(count)])  18.6 us
    pallas_call x10, Pallas kernels, call(): pl.pallas_call(body, out_shape=list(outs), scratch_shapes=list(scratch),...  16.8 us
    ppermute x14, waiting for transfers between devices, swap(): return lax.ppermute(value, axis, [(i, i ^ bit) for i in range(count)])  11.7 us
    unnamed x22, local copies, waits for them, and re-layouts  5.87 us
  transfers between devices with their start and end apart: 15, of which 9 were waited for; matrix products, arithmetic and copies ran while one was open for 0% of the time, Pallas kernels for 27%

commit v1 on v0

--- a/solution.py
+++ b/solution.py
@@ -17,7 +17,7 @@
 F32 = jnp.float32
 BF16 = jnp.bfloat16
 VMEM_LIMIT = 20 << 20
-GATHER = 4
+X_BIT, Z_BIT = 1, 4
 
 
 def dot_nn(left, right):
@@ -58,7 +58,16 @@
     return out
 
 
-def edge_kernel(half, feat, base, table, near, far, rows_buf, base_buf, table_buf, sems):
+def start_copies(pairs, sems):
+    copies = [pltpu.make_async_copy(src, dst, sems.at[i]) for i, (src, dst) in enumerate(pairs)]
+    for copy in copies:
+        copy.start()
+    return copies
+
+
+def edge_kernel(
+    half, feat, base, table, gain, near, far, feat_buf, base_buf, table_buf, gain_buf, rows_buf, sems
+):
     length = feat.shape[0]
     edge = rows_buf.shape[1]
     copies = [
@@ -66,10 +75,12 @@
         pltpu.make_async_copy(feat.at[pl.ds(length - edge, edge)], rows_buf.at[1], sems.at[1]),
         pltpu.make_async_copy(base, base_buf, sems.at[2]),
         pltpu.make_async_copy(table, table_buf, sems.at[3]),
+        pltpu.make_async_copy(gain, gain_buf, sems.at[4]),
+        pltpu.make_async_copy(feat, feat_buf, sems.at[5]),
     ]
     for copy in copies:
         copy.start()
-    for copy in copies:
+    for copy in copies[:4]:
         copy.wait()
     odd = lax.axis_index("ctx") % 2 == 1
     table_f = table_buf[...].astype(F32)
@@ -88,12 +99,15 @@
         last = row(bottom, edge - half + i, length - half + i)
         near[i : i + 1, :] = jnp.where(odd, first, last)
         far[i : i + 1, :] = jnp.where(odd, last, first)
+    for copy in copies[4:]:
+        copy.wait()
 
 
 def act_kernel(
-    kernel, pool, tok_rows, feat, base, table, gain,
-    taps, sums, slope_out, normed_out, act_buf, high_buf, low_buf,
+    kernel, pool, tok_rows, feat, base, table, gain, w_a, w_b, w_c,
+    taps, sums, slope_out, normed_out, v_a, v_b, v_c, act_buf, high_buf, low_buf, sems,
 ):
+    copies = start_copies(((w_a, v_a), (w_b, v_b), (w_c, v_c)), sems)
     half = kernel // 2
     rows, channels = feat.shape
     block = act_buf.shape[0]
@@ -130,6 +144,9 @@
         taps[...] += dot_nn(spread, act_buf[...])
         plain = spread[half * tok_rows : (half + 1) * tok_rows, :]
         sums[...] += dot_nn(plain, high_buf[...]) + dot_nn(plain, low_buf[...])
+
+    for copy in copies:
+        copy.wait()
 
 
 def taps_kernel(kernel, tok_rows, blocks, taps, gain, near, far, pairs, *rest):
@@ -165,14 +182,16 @@
         outs[b][...] = turn[b]
 
 
-def pool_kernel(pool, pairs, sums, weights, cot, rows):
+def pool_kernel(pool, pairs, sums, weights, cot, w_a, w_b, rows, v_a, v_b, sems):
+    copies = start_copies(((w_a, v_a), (w_b, v_b), (cot, rows.at[1])), sems)
     tok_rows = sums.shape[0]
     total = dot_nn(pairs[0], weights[0])
     for j in range(1, pairs.shape[0]):
         total = total + dot_nn(pairs[j], weights[j])
     conv = total[:tok_rows] + total[tok_rows:]
     rows[0] = ((sums[...] + conv) * (1.0 / pool)).astype(BF16)
-    rows[1] = cot[...]
+    for copy in copies:
+        copy.wait()
 
 
 def pack_kernel(*refs):
@@ -183,11 +202,11 @@
         at += part.shape[0]
 
 
-def attention_kernel(pool, blocks, late, *refs):
+def attention_kernel(pool, blocks, near_rels, late, *refs):
     parts, refs = refs[:blocks], refs[blocks:]
     weights, refs = refs[:4], refs[4:]
     g_out, refs = refs[0], refs[1:]
-    gts, refs = refs[:GATHER], refs[GATHER:]
+    gts, refs = refs[: len(near_rels)], refs[len(near_rels) :]
     p_buf, c_buf, q_buf, k_buf, v_buf, ga_buf, gq_buf, gk_buf, gv_buf, turn = refs
     size = parts[0].shape[1]
     for at, part in enumerate(parts):
@@ -223,9 +242,9 @@
     me = lax.axis_index("dp")
     for o in range(count):
         turn[o ^ me] = turned[o * span : (o + 1) * span, :]
-    for r in range(GATHER):
+    for gt, base in zip(gts, near_rels):
         for at, rel in enumerate(late):
-            gts[r][at * span : (at + 1) * span, :] = turn[r ^ rel]
+            gt[at * span : (at + 1) * span, :] = turn[base ^ rel]
 
 
 def spread_kernel(kernel, tok_rows, befores, afters, g_ref, weights, highs, lows, near):
@@ -267,7 +286,8 @@
 
 
 def kernel_grad_kernel(factor, *refs):
-    acts, gts, (mine, theirs) = refs[:GATHER], refs[GATHER : 2 * GATHER], refs[2 * GATHER :]
+    count = len(refs) // 2 - 1
+    acts, gts, (mine, theirs) = refs[:count], refs[count : 2 * count], refs[2 * count :]
     total = None
     for act, gt in zip(acts, gts):
         term = dot_nn(gt[...], act[...])
@@ -320,8 +340,19 @@
     )(*args)
 
 
-def held(value):
-    return pltpu.with_memory_space_constraint(value, pltpu.VMEM)
+def outside(*values):
+    return [pltpu.with_memory_space_constraint(value, pltpu.HBM) for value in values]
+
+
+def bits_of(count):
+    return [1 << at for at in range(count.bit_length() - 1)]
+
+
+def sums_of(bits):
+    out = [0]
+    for bit in bits:
+        out = out + [bit + value for value in out]
+    return out
 
 
 def per_device(
@@ -337,62 +368,59 @@
     tokens = n_ctx * tok_rows
     width = channels // n_ctx
     narrow = channels // n_dp
-    late = list(range(0, n_dp, GATHER))
+    near_rels = [0, X_BIT, Z_BIT, X_BIT + Z_BIT]
+    late = sums_of([bit for bit in bits_of(n_dp) if bit not in (X_BIT, Z_BIT)])
 
     order = xor_order(n_ctx)
     place = {rel: at for at, rel in enumerate(order)}
     befores = [-1] + [place[c ^ (c - 1)] * tok_rows + tok_rows - 1 for c in range(1, n_ctx)]
     afters = [place[c ^ (c + 1)] * tok_rows for c in range(n_ctx - 1)] + [-1]
 
-    feat_v = held(feat)
-    w_conv_v = held(w_conv)
-    squares = [held(w) for w in (w_query, w_key, w_value, w_out)]
-
     edge = 16
     hbm = pl.BlockSpec(memory_space=pltpu.HBM)
-    near, far = call(
+    near, far, feat_v, base_v, table_v, gain_v = call(
         functools.partial(edge_kernel, half),
-        (feat, bases, dna_table),
-        [pltpu.VMEM((half, channels), F32)] * 2,
-        [
-            pltpu.VMEM((2, edge, channels), BF16),
-            pltpu.VMEM(bases.shape, jnp.int32),
-            pltpu.VMEM(dna_table.shape, BF16),
-            pltpu.SemaphoreType.DMA((4,)),
-        ],
-        in_specs=[hbm] * 3,
+        outside(feat, bases, dna_table, norm_gain),
+        [pltpu.VMEM((half, channels), F32)] * 2
+        + [pltpu.VMEM(value.shape, value.dtype) for value in (feat, bases, dna_table, norm_gain)],
+        [pltpu.VMEM((2, edge, channels), BF16), pltpu.SemaphoreType.DMA((6,))],
+        in_specs=[hbm] * 4,
     )
     near = swap(near, "ctx", 1)
     links = [(i, i + 1) for i in range(1, n_ctx - 1, 2)]
     far = lax.ppermute(far, "ctx", links + [(b, a) for a, b in links])
 
     block = 128
-    taps, sums, slope, normed = call(
+    taps, sums, slope, normed, w_conv_v, w_query_v, w_key_v = call(
         functools.partial(act_kernel, kernel, pool, tok_rows),
-        (feat_v, bases, dna_table, norm_gain),
+        [feat_v, base_v, table_v, gain_v] + outside(w_conv, w_query, w_key),
         [
             pltpu.VMEM((kernel * tok_rows, channels), F32),
             pltpu.VMEM((tok_rows, channels), F32),
             pltpu.VMEM((length, channels), F32),
             pltpu.VMEM((length, channels), F32),
-        ],
-        [pltpu.VMEM((block, channels), BF16)] * 3,
+        ]
+        + [pltpu.VMEM(value.shape, BF16) for value in (w_conv, w_query, w_key)],
+        [pltpu.VMEM((block, channels), BF16)] * 3 + [pltpu.SemaphoreType.DMA((3,))],
+        in_specs=[WHOLE] * 4 + [hbm] * 3,
     )
     pairs, *acts = call(
         functools.partial(taps_kernel, kernel, tok_rows, n_ctx),
-        (taps, norm_gain, near, far),
+        (taps, gain_v, near, far),
         [pltpu.VMEM((kernel, 2 * tok_rows, channels), BF16)]
         + [pltpu.VMEM((tok_rows, kernel * width), BF16)] * n_ctx,
         [pltpu.VMEM((n_ctx, tok_rows, kernel * width), BF16)],
     )
     acts = [acts[0]] + [swap(acts[rel], "ctx", rel) for rel in order[1:]]
-    rows = list(
-        call(
-            functools.partial(pool_kernel, pool),
-            (pairs, sums, w_conv_v, cot),
-            [pltpu.VMEM((2, tok_rows, channels), BF16)],
-        )
-    )
+    pooled, w_value_v, w_out_v = call(
+        functools.partial(pool_kernel, pool),
+        [pairs, sums, w_conv_v] + outside(cot, w_value, w_out),
+        [pltpu.VMEM((2, tok_rows, channels), BF16)]
+        + [pltpu.VMEM(value.shape, BF16) for value in (w_value, w_out)],
+        [pltpu.SemaphoreType.DMA((3,))],
+        in_specs=[WHOLE] * 3 + [hbm] * 3,
+    )
+    rows = [pooled]
     bit = n_ctx // 2
     while bit:
         rows = rows + [swap(value, "ctx", bit) for value in rows]
@@ -400,19 +428,21 @@
 
     act = call(pack_kernel, acts, [pltpu.VMEM((tokens, kernel * width), BF16)])[0]
 
-    act_z = swap(act, "dp", 2)
-    act_x = swap(act, "dp", 1)
+    act_z = swap(act, "dp", Z_BIT)
+    act_x = swap(act, "dp", X_BIT)
 
     g_all, *gts = call(
-        functools.partial(attention_kernel, pool, n_ctx, late),
-        (*rows, *squares),
+        functools.partial(attention_kernel, pool, n_ctx, near_rels, late),
+        (*rows, w_query_v, w_key_v, w_value_v, w_out_v),
         [pltpu.VMEM((tokens, channels), BF16)]
-        + [pltpu.VMEM((len(late) * narrow, tokens), BF16)] * GATHER,
+        + [pltpu.VMEM((len(late) * narrow, tokens), BF16)] * len(near_rels),
         [pltpu.VMEM((tokens, channels), BF16)] * 9 + [pltpu.VMEM((n_dp, narrow, tokens), BF16)],
     )
 
-    act_zx = swap(act_z, "dp", 1)
-    gts = [gts[0]] + [swap(gts[rel], "dp", rel) for rel in range(1, GATHER)]
+    act_zx = swap(act_z, "dp", X_BIT)
+    swapped = [gts[0]]
+    for at, rel in enumerate(near_rels[1:], 1):
+        swapped.append(swap(gts[at], "dp", rel))
 
     padded = -(-(tok_rows + 2) // 8) * 8
     highs, lows, near_g = call(
@@ -425,13 +455,13 @@
     kept = len(late) // 2
     mine, theirs = call(
         functools.partial(kernel_grad_kernel, factor),
-        (act, act_x, act_z, act_zx, *gts),
+        (act, act_x, act_z, act_zx, *swapped),
         [
             pltpu.VMEM((kept * narrow, kernel * width), F32),
             pltpu.VMEM((kept * narrow, kernel * width), BF16),
         ],
     )
-    other = swap(theirs, "dp", GATHER * kept)
+    other = swap(theirs, "dp", late[kept])
     while kept > 1:
         kept //= 2
         mine, theirs = call(
@@ -442,7 +472,7 @@
                 pltpu.VMEM((kept * narrow, kernel * width), BF16),
             ],
         )
-        other = swap(theirs, "dp", GATHER * kept)
+        other = swap(theirs, "dp", late[kept])
 
     by_rows = pl.BlockSpec((block, channels), lambda i: (i, 0))
     grad_in = call(

time: 54.7 us -> 55.9 us (1.022)
  local copies, waits for them, and re-layouts: 5.87 us -> 0 us
  waiting for transfers between devices: 11.7 us -> 15.4 us
  starting transfers between devices: 19.2 us -> 21.2 us
  Pallas kernels: 16.8 us -> 18.4 us
    unnamed x22 -> x0, local copies, waits for them, and re-layouts: 5.87 us -> none
    ppermute x14, waiting for transfers between devices: 11.7 us -> 15.4 us  [swap(): return lax.ppermute(value, axis, [(i, i ^ bit) for i in range(count)])]
    ppermute x14, starting transfers between devices: 18.6 us -> 20.5 us  [swap(): return lax.ppermute(value, axis, [(i, i ^ bit) for i in range(count)])]
    pallas_call x10, Pallas kernels: 16.8 us -> 18.4 us  [call(): pl.pallas_call(body, out_shape=list(outs), scratch_shapes=list(scratch),...]
  transfers between devices with their start and end apart: 15 -> 15, of which waited for: 9 -> 7; matrix products, arithmetic and copies ran while one was open for 0% -> 0% of each run, Pallas kernels for 27% -> 28%
where the time goes in v1:
time: 55.9 us; the launch traced here: 55.7 us
  starting transfers between devices  21.2 us (38%)
  Pallas kernels  18.4 us (33%)
  waiting for transfers between devices  15.4 us (28%)
  between operations  0.72 us (1%)
    ppermute x14, starting transfers between devices, swap(): return lax.ppermute(value, axis, [(i, i ^ bit) for i in range(count)])  20.5 us
    pallas_call x10, Pallas kernels, call(): pl.pallas_call(body, out_shape=list(outs), scratch_shapes=list(scratch),...  18.4 us
    ppermute x14, waiting for transfers between devices, swap(): return lax.ppermute(value, axis, [(i, i ^ bit) for i in range(count)])  15.4 us
  transfers between devices with their start and end apart: 15, of which 7 were waited for; matrix products, arithmetic and copies ran while one was open for 0% of the time, Pallas kernels for 28%

profile of v1, /device:TPU:0, one launch (start us, length us, event | category | flops | bytes accessed | tf_op | source)
XLA Modules:
  0.0 55.7 jit_solution(10585472459140434194)
XLA Ops:
  0.6 1.3 %shard_map.113 = (f32[2,768]{1,0:T(2,128)S(1)}, f32[2,768]{1,0:T(2,128)S(1)}, bf16[512,768]{1,0:T(8,128)(2,1)S(1)}, s32[1,512]{1,0:T(1,128)S(1)}, bf16[4,768]{1,...) custom-call(bf16[512,768]{1,0:T(8,128)(2,1)} %bitcast.4, s32[1,512]{1,0:T(1,128)} %base.1, bf16[4,768]{1,0:T(4,128)(2,1)} %table.1, ...), custom_call_target="tpu_custom_call" | custom-call | tf_op jit(solution)/shard_map/pallas_call | solution.py:334
  1.9 0.6 %collective-permute-start = (f32[2,768]{1,0:T(2,128)S(1)}, f32[2,768]{1,0:T(2,128)S(1)}, u32[]{:S(2)}, u32[]{:S(2)}) collective-permute-start(f32[2,768]{1,0:T(2,128)S(1)} %get-tuple-element.38), channel_id=1, source_target_pairs={{0,1},{1,0},{2,3},{3,2},{4,5},{5,4},{6,7},{7,6},{8,9},{9,8},{10,11... | collective-permute-start | bytes 18440 | tf_op jit(solution)/shard_map/ppermute | solution.py:325
  2.5 0.6 %collective-permute-start.1 = (f32[2,768]{1,0:T(2,128)S(1)}, f32[2,768]{1,0:T(2,128)S(1)}, u32[]{:S(2)}, u32[]{:S(2)}) collective-permute-start(f32[2,768]{1,0:T(2,128)S(1)} %get-tuple-element.39), channel_id=1, source_target_pairs={{1,2},{2,1},{5,6},{6,5},{9,10},{10,9},{13,14},{14,13},{17,18},{18,... | collective-permute-start | bytes 18440 | tf_op jit(solution)/shard_map/ppermute | solution.py:391
  3.1 3.6 %shard_map.114 = (f32[160,768]{1,0:T(8,128)S(1)}, f32[32,768]{1,0:T(8,128)S(1)}, f32[512,768]{1,0:T(8,128)S(1)}, f32[512,768]{1,0:T(8,128)S(1)}, bf16[5,768,768]...) custom-call(bf16[512,768]{1,0:T(8,128)(2,1)S(1)} %get-tuple-element.33.feat, ...), custom_call_target="tpu_custom_call" | custom-call | tf_op jit(solution)/shard_map/pallas_call | solution.py:334
  6.7 0.0 collective-permute-done.near
  6.7 0.0 collective-permute-done.1.far
  6.7 0.3 shard_map.115
  7.0 3.9 %collective-permute-start.5 = (bf16[32,960]{1,0:T(8,128)(2,1)S(1)}, bf16[32,960]{1,0:T(8,128)(2,1)S(1)}, u32[]{:S(2)}, u32[]{:S(2)}) collective-permute-start(bf16[32,960]{1,0:T(8,128)(2,1)S(1)} %get-tuple-element.55), channel_id=1, source_target_pairs={{0,2},{1,3},{2,0},{3,1},{4,6},{5,7},{6,4},{7,5},{8,10},{9,11},{10,... | collective-permute-start | bytes 184328 | tf_op jit(solution)/shard_map/ppermute | solution.py:325
  10.8 0.2 collective-permute-start.6
  11.0 1.3 %collective-permute-start.7 = (bf16[32,960]{1,0:T(8,128)(2,1)S(1)}, bf16[32,960]{1,0:T(8,128)(2,1)S(1)}, u32[]{:S(2)}, u32[]{:S(2)}) collective-permute-start(bf16[32,960]{1,0:T(8,128)(2,1)S(1)} %get-tuple-element.57), channel_id=1, source_target_pairs={{0,3},{1,2},{2,1},{3,0},{4,7},{5,6},{6,5},{7,4},{8,11},{9,10},{10,... | collective-permute-start | bytes 184328 | tf_op jit(solution)/shard_map/ppermute | solution.py:325
  12.3 0.8 %collective-permute-done.5.refs_1_ = bf16[32,960]{1,0:T(8,128)(2,1)S(1)} collective-permute-done((bf16[32,960]{1,0:T(8,128)(2,1)S(1)}, bf16[32,960]{1,0:T(8,128)(2,1)S(1)}, u32[]{:S(2)}, u32[]{:S(2)}) %collective-permute-start.5) | collective-permute-done | bytes 61472 | tf_op jit(solution)/shard_map/ppermute | solution.py:325
  13.1 0.0 collective-permute-done.6.refs_2_
  13.1 2.3 %collective-permute-done.7.refs_3_ = bf16[32,960]{1,0:T(8,128)(2,1)S(1)} collective-permute-done((bf16[32,960]{1,0:T(8,128)(2,1)S(1)}, bf16[32,960]{1,0:T(8,128)(2,1)S(1)}, u32[]{:S(2)}, u32[]{:S(2)}) %collective-permute-start.7) | collective-permute-done | bytes 61472 | tf_op jit(solution)/shard_map/ppermute | solution.py:325
  15.4 2.4 %collective-permute-start.9 = (bf16[128,960]{1,0:T(8,128)(2,1)S(1)}, bf16[128,960]{1,0:T(8,128)(2,1)S(1)}, u32[]{:S(2)}, u32[]{:S(2)}) collective-permute-start(bf16[128,960]{1,0:T(8,128)(2,1)S(1)} %shard_map.120.refs_0_), channel_id=1, source_target_pairs={{0,16},{4,20},{8,24},{12,28},{16,0},{20,4},{24,8},{28,12},{1,17},{... | collective-permute-start | bytes 737288 | tf_op jit(solution)/shard_map/ppermute | solution.py:325
  17.8 1.7 %shard_map.116 = (bf16[2,32,768]{2,1,0:T(8,128)(2,1)S(1)}, bf16[768,768]{1,0:T(8,128)(2,1)S(1)}, bf16[768,768]{1,0:T(8,128)(2,1)S(1)}) custom-call(bf16[5,64,768]{2,1,0:T(8,128)(2,1)S(1)} %get-tuple-element.40.pairs, f32[32,768]{1,0:T(8,128)S(1)} %get-tuple-element.41.sums, bf16[5,768,768]{2,1,0:T(8,128)(2,1)S(1)} %get-tuple-element.42.weights, ...), custom_call_target="tpu_custom_call" | custom-call | tf_op jit(solution)/shard_map/pallas_call | solution.py:334
  19.5 1.9 %collective-permute-start.2 = (bf16[2,32,768]{2,1,0:T(8,128)(2,1)S(1)}, bf16[2,32,768]{2,1,0:T(8,128)(2,1)S(1)}, u32[]{:S(2)}, u32[]{:S(2)}) collective-permute-start(bf16[2,32,768]{2,1,0:T(8,128)(2,1)S(1)} %get-tuple-element.43.refs_0_), channel_id=1, source_target_pairs={{0,2},{1,3},{2,0},{3,1},{4,6},{5,7},{6,4},{7,5},{8,10},{9,11},{10,... | collective-permute-start | bytes 294920 | tf_op jit(solution)/shard_map/ppermute | solution.py:325
  21.3 1.5 %collective-permute-start.8 = (bf16[128,960]{1,0:T(8,128)(2,1)S(1)}, bf16[128,960]{1,0:T(8,128)(2,1)S(1)}, u32[]{:S(2)}, u32[]{:S(2)}) collective-permute-start(bf16[128,960]{1,0:T(8,128)(2,1)S(1)} %shard_map.120.refs_0_), channel_id=1, source_target_pairs={{0,4},{4,0},{8,12},{12,8},{16,20},{20,16},{24,28},{28,24},{1,5},{5... | collective-permute-start | bytes 737288 | tf_op jit(solution)/shard_map/ppermute | solution.py:325
  22.8 7.6 %collective-permute-done.9.refs_2_ = bf16[128,960]{1,0:T(8,128)(2,1)S(1)} collective-permute-done((bf16[128,960]{1,0:T(8,128)(2,1)S(1)}, bf16[128,960]{1,0:T(8,128)(2,1)S(1)}, u32[]{:S(2)}, u32[]{:S(2)}) %collective-permute-start.9) | collective-permute-done | bytes 245792 | tf_op jit(solution)/shard_map/ppermute | solution.py:325
  30.4 1.5 %collective-permute-start.10 = (bf16[128,960]{1,0:T(8,128)(2,1)S(1)}, bf16[128,960]{1,0:T(8,128)(2,1)S(1)}, u32[]{:S(2)}, u32[]{:S(2)}) collective-permute-start(bf16[128,960]{1,0:T(8,128)(2,1)S(1)} %collective-permute-done.9.refs_2_), channel_id=1, source_target_pairs={{0,4},{4,0},{8,12},{12,8},{16,20},{20,16},{24,28},{28,24},{1,5},{5... | collective-permute-start | bytes 737288 | tf_op jit(solution)/shard_map/ppermute | solution.py:325
  31.9 0.0 collective-permute-start.3
  31.9 0.0 collective-permute-done.2.refs_1_
  32.0 0.5 collective-permute-start.4
  32.5 0.8 %collective-permute-done.3.refs_2_ = bf16[2,32,768]{2,1,0:T(8,128)(2,1)S(1)} collective-permute-done((bf16[2,32,768]{2,1,0:T(8,128)(2,1)S(1)}, bf16[2,32,768]{2,1,0:T(8,128)(2,1)S(1)}, u32[]{:S(2)}, u32[]{:S(2)}) %collective-permute-start.3) | collective-permute-done | bytes 98336 | tf_op jit(solution)/shard_map/ppermute | solution.py:325
  33.2 0.2 collective-permute-done.4.refs_3_
  33.4 5.8 %shard_map.117 = (bf16[128,768]{1,0:T(8,128)(2,1)S(1)}, bf16[192,128]{1,0:T(8,128)(2,1)S(1)}, bf16[192,128]{1,0:T(8,128)(2,1)S(1)}, bf16[192,128]{1,0:T(8,128)(2,1)S(1)}, bf16[192,128]{1,0:T(8,128)(2,1)S(1)}) custom-call(bf16[2,32,768]{2,1,0:T(8,128)(2,1)S(1)} %get-tuple-element.43.refs_0_, bf16[2,32,768]{2,1,0:T(8,128)(2,1)S(1)} %collective-permute-done.2.refs_1_, ...), custom_call_target="tpu_custom_call" | custom-call | tf_op jit(solution)/shard_map/pallas_call | solution.py:334
  39.2 0.6 collective-permute-start.11
  39.8 0.0 collective-permute-start.12
  39.8 3.9 %collective-permute-start.13 = (bf16[192,128]{1,0:T(8,128)(2,1)S(1)}, bf16[192,128]{1,0:T(8,128)(2,1)S(1)}, u32[]{:S(2)}, u32[]{:S(2)}) collective-permute-start(bf16[192,128]{1,0:T(8,128)(2,1)S(1)} %get-tuple-element.61), channel_id=1, source_target_pairs={{0,20},{4,16},{8,28},{12,24},{16,4},{20,0},{24,12},{28,8},{1,21},{... | collective-permute-start | bytes 147464 | tf_op jit(solution)/shard_map/ppermute | solution.py:325
  43.7 0.0 collective-permute-done.11.refs_5_
  43.7 2.6 %collective-permute-done.12.refs_6_ = bf16[192,128]{1,0:T(8,128)(2,1)S(1)} collective-permute-done((bf16[192,128]{1,0:T(8,128)(2,1)S(1)}, bf16[192,128]{1,0:T(8,128)(2,1)S(1)}, u32[]{:S(2)}, u32[]{:S(2)}) %collective-permute-start.12) | collective-permute-done | bytes 49184 | tf_op jit(solution)/shard_map/ppermute | solution.py:325
  46.3 1.2 %collective-permute-done.13.refs_7_ = bf16[192,128]{1,0:T(8,128)(2,1)S(1)} collective-permute-done((bf16[192,128]{1,0:T(8,128)(2,1)S(1)}, bf16[192,128]{1,0:T(8,128)(2,1)S(1)}, u32[]{:S(2)}, u32[]{:S(2)}) %collective-permute-start.13) | collective-permute-done | bytes 49184 | tf_op jit(solution)/shard_map/ppermute | solution.py:325
  47.5 0.0 collective-permute-done.8.refs_1_
  47.5 0.0 collective-permute-done.10.refs_3_
  47.5 0.5 shard_map.121
  48.1 2.4 %collective-permute-start.14 = (bf16[96,960]{1,0:T(8,128)(2,1)S(1)}, bf16[96,960]{1,0:T(8,128)(2,1)S(1)}, u32[]{:S(2)}, u32[]{:S(2)}) collective-permute-start(bf16[96,960]{1,0:T(8,128)(2,1)S(1)} %get-tuple-element.63), channel_id=1, source_target_pairs={{0,8},{4,12},{8,0},{12,4},{16,24},{20,28},{24,16},{28,20},{1,9},{5... | collective-permute-start | bytes 552968 | tf_op jit(solution)/shard_map/ppermute | solution.py:325
  50.4 1.8 %shard_map.118 = (bf16[200,768]{1,0:T(8,128)(2,1)S(1)}, bf16[200,768]{1,0:T(8,128)(2,1)S(1)}, bf16[40,768]{1,0:T(8,128)(2,1)S(1)}) custom-call(bf16[128,768]{1,0:T(8,128)(2,1)S(1)} %get-tuple-element.48.g_ref, bf16[5,768,768]{2,1,0:T(8,128)(2,1)S(1)} %get-tuple-element.42.weights), custom_call_target="tpu_custom_call" | custom-call | tf_op jit(solution)/shard_map/pallas_call | solution.py:334
  52.2 2.5 %shard_map.119 = bf16[512,768]{1,0:T(8,128)(2,1)} custom-call(bf16[200,768]{1,0:T(8,128)(2,1)S(1)} %get-tuple-element.49.highs, bf16[200,768]{1,0:T(8,128)(2,1)S(1)} %get-tuple-element.50.lows, bf16[40,768]{1,0:T(8,128)(2,1)S(1)} %get-tuple-element.51.near, f32[512,768]{1,0:T(8,128)S(1)} %get-tuple-element.52.slope, f32[512,768]{1,0:T(8,128)S(1)} %get-tuple-element.53.normed), custom_call_target="tpu_custom_call" | custom-call | tf_op jit(solution)/shard_map/pallas_call | solution.py:334
  54.7 0.0 collective-permute-done.14.other
  54.7 1.0 %shard_map.122 = f32[5,192,96]{2,1,0:T(8,128)} custom-call(f32[96,960]{1,0:T(8,128)S(1)} %get-tuple-element.62.mine, bf16[96,960]{1,0:T(8,128)(2,1)S(1)} %collective-permute-done.14.other), custom_call_target="tpu_custom_call" | custom-call | tf_op jit(solution)/shard_map/pallas_call | solution.py:334
  (1 shorter events, 0.0 us)
Async XLA Ops:
  1.9 4.8 %collective-permute-start = (f32[2,768]{1,0:T(2,128)S(1)}, f32[2,768]{1,0:T(2,128)S(1)}, u32[]{:S(2)}, u32[]{:S(2)}) collective-permute-start(f32[2,768]{1,0:T(2,128)S(1)} %get-tuple-element.38), channel_id=1, source_target_pairs={{0,1},{1,0},{2,3},{3,2},{4,5},{5,4},{6,7},{7,6},{8,9},{9,8},{10,11... | collective-permute-start | bytes 18440 | tf_op jit(solution)/shard_map/ppermute | solution.py:325
  2.5 4.2 %collective-permute-start.1 = (f32[2,768]{1,0:T(2,128)S(1)}, f32[2,768]{1,0:T(2,128)S(1)}, u32[]{:S(2)}, u32[]{:S(2)}) collective-permute-start(f32[2,768]{1,0:T(2,128)S(1)} %get-tuple-element.39), channel_id=1, source_target_pairs={{1,2},{2,1},{5,6},{6,5},{9,10},{10,9},{13,14},{14,13},{17,18},{18,... | collective-permute-start | bytes 18440 | tf_op jit(solution)/shard_map/ppermute | solution.py:391
  7.0 6.1 %collective-permute-start.5 = (bf16[32,960]{1,0:T(8,128)(2,1)S(1)}, bf16[32,960]{1,0:T(8,128)(2,1)S(1)}, u32[]{:S(2)}, u32[]{:S(2)}) collective-permute-start(bf16[32,960]{1,0:T(8,128)(2,1)S(1)} %get-tuple-element.55), channel_id=1, source_target_pairs={{0,2},{1,3},{2,0},{3,1},{4,6},{5,7},{6,4},{7,5},{8,10},{9,11},{10,... | collective-permute-start | bytes 184328 | tf_op jit(solution)/shard_map/ppermute | solution.py:325
  10.8 2.2 %collective-permute-start.6 = (bf16[32,960]{1,0:T(8,128)(2,1)S(1)}, bf16[32,960]{1,0:T(8,128)(2,1)S(1)}, u32[]{:S(2)}, u32[]{:S(2)}) collective-permute-start(bf16[32,960]{1,0:T(8,128)(2,1)S(1)} %get-tuple-element.56), channel_id=1, source_target_pairs={{0,1},{1,0},{2,3},{3,2},{4,5},{5,4},{6,7},{7,6},{8,9},{9,8},{10,11... | collective-permute-start | bytes 184328 | tf_op jit(solution)/shard_map/ppermute | solution.py:325
  11.0 4.3 %collective-permute-start.7 = (bf16[32,960]{1,0:T(8,128)(2,1)S(1)}, bf16[32,960]{1,0:T(8,128)(2,1)S(1)}, u32[]{:S(2)}, u32[]{:S(2)}) collective-permute-start(bf16[32,960]{1,0:T(8,128)(2,1)S(1)} %get-tuple-element.57), channel_id=1, source_target_pairs={{0,3},{1,2},{2,1},{3,0},{4,7},{5,6},{6,5},{7,4},{8,11},{9,10},{10,... | collective-permute-start | bytes 184328 | tf_op jit(solution)/shard_map/ppermute | solution.py:325
  15.4 15.0 %collective-permute-start.9 = (bf16[128,960]{1,0:T(8,128)(2,1)S(1)}, bf16[128,960]{1,0:T(8,128)(2,1)S(1)}, u32[]{:S(2)}, u32[]{:S(2)}) collective-permute-start(bf16[128,960]{1,0:T(8,128)(2,1)S(1)} %shard_map.120.refs_0_), channel_id=1, source_target_pairs={{0,16},{4,20},{8,24},{12,28},{16,0},{20,4},{24,8},{28,12},{1,17},{... | collective-permute-start | bytes 737288 | tf_op jit(solution)/shard_map/ppermute | solution.py:325
  19.5 12.5 %collective-permute-start.2 = (bf16[2,32,768]{2,1,0:T(8,128)(2,1)S(1)}, bf16[2,32,768]{2,1,0:T(8,128)(2,1)S(1)}, u32[]{:S(2)}, u32[]{:S(2)}) collective-permute-start(bf16[2,32,768]{2,1,0:T(8,128)(2,1)S(1)} %get-tuple-element.43.refs_0_), channel_id=1, source_target_pairs={{0,2},{1,3},{2,0},{3,1},{4,6},{5,7},{6,4},{7,5},{8,10},{9,11},{10,... | collective-permute-start | bytes 294920 | tf_op jit(solution)/shard_map/ppermute | solution.py:325
  21.3 26.2 %collective-permute-start.8 = (bf16[128,960]{1,0:T(8,128)(2,1)S(1)}, bf16[128,960]{1,0:T(8,128)(2,1)S(1)}, u32[]{:S(2)}, u32[]{:S(2)}) collective-permute-start(bf16[128,960]{1,0:T(8,128)(2,1)S(1)} %shard_map.120.refs_0_), channel_id=1, source_target_pairs={{0,4},{4,0},{8,12},{12,8},{16,20},{20,16},{24,28},{28,24},{1,5},{5... | collective-permute-start | bytes 737288 | tf_op jit(solution)/shard_map/ppermute | solution.py:325
  30.4 17.1 %collective-permute-start.10 = (bf16[128,960]{1,0:T(8,128)(2,1)S(1)}, bf16[128,960]{1,0:T(8,128)(2,1)S(1)}, u32[]{:S(2)}, u32[]{:S(2)}) collective-permute-start(bf16[128,960]{1,0:T(8,128)(2,1)S(1)} %collective-permute-done.9.refs_2_), channel_id=1, source_target_pairs={{0,4},{4,0},{8,12},{12,8},{16,20},{20,16},{24,28},{28,24},{1,5},{5... | collective-permute-start | bytes 737288 | tf_op jit(solution)/shard_map/ppermute | solution.py:325
  31.9 1.3 %collective-permute-start.3 = (bf16[2,32,768]{2,1,0:T(8,128)(2,1)S(1)}, bf16[2,32,768]{2,1,0:T(8,128)(2,1)S(1)}, u32[]{:S(2)}, u32[]{:S(2)}) collective-permute-start(bf16[2,32,768]{2,1,0:T(8,128)(2,1)S(1)} %get-tuple-element.43.refs_0_), channel_id=1, source_target_pairs={{0,1},{1,0},{2,3},{3,2},{4,5},{5,4},{6,7},{7,6},{8,9},{9,8},{10,11... | collective-permute-start | bytes 294920 | tf_op jit(solution)/shard_map/ppermute | solution.py:325
  32.0 1.5 %collective-permute-start.4 = (bf16[2,32,768]{2,1,0:T(8,128)(2,1)S(1)}, bf16[2,32,768]{2,1,0:T(8,128)(2,1)S(1)}, u32[]{:S(2)}, u32[]{:S(2)}) collective-permute-start(bf16[2,32,768]{2,1,0:T(8,128)(2,1)S(1)} %collective-permute-done.2.refs_1_), channel_id=1, source_target_pairs={{0,1},{1,0},{2,3},{3,2},{4,5},{5,4},{6,7},{7,6},{8,9},{9,8},{10,11... | collective-permute-start | bytes 294920 | tf_op jit(solution)/shard_map/ppermute | solution.py:325
  39.2 4.5 %collective-permute-start.11 = (bf16[192,128]{1,0:T(8,128)(2,1)S(1)}, bf16[192,128]{1,0:T(8,128)(2,1)S(1)}, u32[]{:S(2)}, u32[]{:S(2)}) collective-permute-start(bf16[192,128]{1,0:T(8,128)(2,1)S(1)} %get-tuple-element.59), channel_id=1, source_target_pairs={{0,4},{4,0},{8,12},{12,8},{16,20},{20,16},{24,28},{28,24},{1,5},{5... | collective-permute-start | bytes 147464 | tf_op jit(solution)/shard_map/ppermute | solution.py:325
  39.8 6.5 %collective-permute-start.12 = (bf16[192,128]{1,0:T(8,128)(2,1)S(1)}, bf16[192,128]{1,0:T(8,128)(2,1)S(1)}, u32[]{:S(2)}, u32[]{:S(2)}) collective-permute-start(bf16[192,128]{1,0:T(8,128)(2,1)S(1)} %get-tuple-element.60), channel_id=1, source_target_pairs={{0,16},{4,20},{8,24},{12,28},{16,0},{20,4},{24,8},{28,12},{1,17},{... | collective-permute-start | bytes 147464 | tf_op jit(solution)/shard_map/ppermute | solution.py:325
  39.8 7.7 %collective-permute-start.13 = (bf16[192,128]{1,0:T(8,128)(2,1)S(1)}, bf16[192,128]{1,0:T(8,128)(2,1)S(1)}, u32[]{:S(2)}, u32[]{:S(2)}) collective-permute-start(bf16[192,128]{1,0:T(8,128)(2,1)S(1)} %get-tuple-element.61), channel_id=1, source_target_pairs={{0,20},{4,16},{8,28},{12,24},{16,4},{20,0},{24,12},{28,8},{1,21},{... | collective-permute-start | bytes 147464 | tf_op jit(solution)/shard_map/ppermute | solution.py:325
  48.1 6.6 %collective-permute-start.14 = (bf16[96,960]{1,0:T(8,128)(2,1)S(1)}, bf16[96,960]{1,0:T(8,128)(2,1)S(1)}, u32[]{:S(2)}, u32[]{:S(2)}) collective-permute-start(bf16[96,960]{1,0:T(8,128)(2,1)S(1)} %get-tuple-element.63), channel_id=1, source_target_pairs={{0,8},{4,12},{8,0},{12,4},{16,24},{20,28},{24,16},{28,20},{1,9},{5... | collective-permute-start | bytes 552968 | tf_op jit(solution)/shard_map/ppermute | solution.py:325

commit v2 on v1

--- a/solution.py
+++ b/solution.py
@@ -104,10 +104,10 @@
 
 
 def act_kernel(
-    kernel, pool, tok_rows, feat, base, table, gain, w_a, w_b, w_c,
-    taps, sums, slope_out, normed_out, v_a, v_b, v_c, act_buf, high_buf, low_buf, sems,
+    kernel, pool, tok_rows, feat, base, table, gain, w_hbm,
+    taps, sums, tanh_out, normed_out, inv_out, weights, act_buf, high_buf, low_buf, sems,
 ):
-    copies = start_copies(((w_a, v_a), (w_b, v_b), (w_c, v_c)), sems)
+    copies = start_copies(((w_hbm, weights),), sems)
     half = kernel // 2
     rows, channels = feat.shape
     block = act_buf.shape[0]
@@ -128,13 +128,11 @@
             inv_rms, normed = normed_of(summed)
             u = normed * gain_f
             tanh_val, value = gelu_of(u)
-            slopes = 0.5 * (1.0 + tanh_val) + 0.5 * u * (1.0 - tanh_val * tanh_val) * GELU_SCALE * (
-                1.0 + 3.0 * CUBIC * (u * u)
-            )
             act_buf[part, :] = value.astype(BF16)
             high_buf[part, :], low_buf[part, :] = split2(summed)
-            slope_out[here, :] = inv_rms * (slopes * gain_f)
+            tanh_out[here, :] = tanh_val
             normed_out[here, :] = normed
+            inv_out[here, :] = jnp.broadcast_to(inv_rms, (chunk, inv_out.shape[1]))
         shape = (kernel * tok_rows, block)
         row = iota(shape, 0)
         tap = sum((row >= tok_rows * j).astype(jnp.int32) for j in range(1, kernel))
@@ -144,6 +142,28 @@
         taps[...] += dot_nn(spread, act_buf[...])
         plain = spread[half * tok_rows : (half + 1) * tok_rows, :]
         sums[...] += dot_nn(plain, high_buf[...]) + dot_nn(plain, low_buf[...])
+
+    for copy in copies:
+        copy.wait()
+
+
+def slope_kernel(tanh_ref, normed_ref, inv_ref, gain, *refs):
+    count = len(refs) // 2 - 1
+    sources, slope_out, copied, sems = refs[:count], refs[count], refs[count + 1 : -1], refs[-1]
+    copies = start_copies(tuple(zip(sources, copied)), sems)
+    rows, channels = normed_ref.shape
+    gain_f = gain[...].reshape(1, channels).astype(F32)
+    chunk = 32
+
+    @pl.loop(0, rows // chunk)
+    def _(step):
+        here = pl.ds(pl.multiple_of(step * chunk, chunk), chunk)
+        tanh_val = tanh_ref[here, :]
+        u = normed_ref[here, :] * gain_f
+        slopes = 0.5 * (1.0 + tanh_val) + 0.5 * u * (1.0 - tanh_val * tanh_val) * GELU_SCALE * (
+            1.0 + 3.0 * CUBIC * (u * u)
+        )
+        slope_out[here, :] = inv_ref[here, :1] * (slopes * gain_f)
 
     for copy in copies:
         copy.wait()
@@ -182,8 +202,8 @@
         outs[b][...] = turn[b]
 
 
-def pool_kernel(pool, pairs, sums, weights, cot, w_a, w_b, rows, v_a, v_b, sems):
-    copies = start_copies(((w_a, v_a), (w_b, v_b), (cot, rows.at[1])), sems)
+def pool_kernel(pool, pairs, sums, weights, cot, rows, sems):
+    copies = start_copies(((cot, rows.at[1]),), sems)
     tok_rows = sums.shape[0]
     total = dot_nn(pairs[0], weights[0])
     for j in range(1, pairs.shape[0]):
@@ -195,11 +215,13 @@
 
 
 def pack_kernel(*refs):
-    *parts, out = refs
+    *parts, out, buf = refs
     at = 0
     for part in parts:
-        out[at : at + part.shape[0], :] = part[...]
+        buf[at : at + part.shape[0], :] = part[...]
         at += part.shape[0]
+    eye = (iota((at, at), 0) == iota((at, at), 1)).astype(BF16)
+    out[...] = dot_tn(buf[...], eye).astype(BF16)
 
 
 def attention_kernel(pool, blocks, near_rels, late, *refs):
@@ -290,7 +312,7 @@
     acts, gts, (mine, theirs) = refs[:count], refs[count : 2 * count], refs[2 * count :]
     total = None
     for act, gt in zip(acts, gts):
-        term = dot_nn(gt[...], act[...])
+        term = dot_nt(gt[...], act[...])
         total = term if total is None else total + term
     total = total * factor
     span = mine.shape[0]
@@ -391,18 +413,19 @@
     far = lax.ppermute(far, "ctx", links + [(b, a) for a, b in links])
 
     block = 128
-    taps, sums, slope, normed, w_conv_v, w_query_v, w_key_v = call(
+    taps, sums, tanh_val, normed, inv_rms, w_conv_v = call(
         functools.partial(act_kernel, kernel, pool, tok_rows),
-        [feat_v, base_v, table_v, gain_v] + outside(w_conv, w_query, w_key),
+        [feat_v, base_v, table_v, gain_v] + outside(w_conv),
         [
             pltpu.VMEM((kernel * tok_rows, channels), F32),
             pltpu.VMEM((tok_rows, channels), F32),
             pltpu.VMEM((length, channels), F32),
             pltpu.VMEM((length, channels), F32),
-        ]
-        + [pltpu.VMEM(value.shape, BF16) for value in (w_conv, w_query, w_key)],
-        [pltpu.VMEM((block, channels), BF16)] * 3 + [pltpu.SemaphoreType.DMA((3,))],
-        in_specs=[WHOLE] * 4 + [hbm] * 3,
+            pltpu.VMEM((length, 128), F32),
+            pltpu.VMEM(w_conv.shape, BF16),
+        ],
+        [pltpu.VMEM((block, channels), BF16)] * 3 + [pltpu.SemaphoreType.DMA((1,))],
+        in_specs=[WHOLE] * 4 + [hbm],
     )
     pairs, *acts = call(
         functools.partial(taps_kernel, kernel, tok_rows, n_ctx),
@@ -412,13 +435,20 @@
         [pltpu.VMEM((n_ctx, tok_rows, kernel * width), BF16)],
     )
     acts = [acts[0]] + [swap(acts[rel], "ctx", rel) for rel in order[1:]]
-    pooled, w_value_v, w_out_v = call(
+    pooled = call(
         functools.partial(pool_kernel, pool),
-        [pairs, sums, w_conv_v] + outside(cot, w_value, w_out),
-        [pltpu.VMEM((2, tok_rows, channels), BF16)]
-        + [pltpu.VMEM(value.shape, BF16) for value in (w_value, w_out)],
-        [pltpu.SemaphoreType.DMA((3,))],
-        in_specs=[WHOLE] * 3 + [hbm] * 3,
+        [pairs, sums, w_conv_v] + outside(cot),
+        [pltpu.VMEM((2, tok_rows, channels), BF16)],
+        [pltpu.SemaphoreType.DMA((1,))],
+        in_specs=[WHOLE] * 3 + [hbm],
+    )[0]
+    squares = (w_query, w_key, w_value, w_out)
+    slope, *squares_v = call(
+        slope_kernel,
+        [tanh_val, normed, inv_rms, gain_v] + outside(*squares),
+        [pltpu.VMEM((length, channels), F32)] + [pltpu.VMEM(w.shape, BF16) for w in squares],
+        [pltpu.SemaphoreType.DMA((4,))],
+        in_specs=[WHOLE] * 4 + [hbm] * 4,
     )
     rows = [pooled]
     bit = n_ctx // 2
@@ -426,14 +456,19 @@
         rows = rows + [swap(value, "ctx", bit) for value in rows]
         bit //= 2
 
-    act = call(pack_kernel, acts, [pltpu.VMEM((tokens, kernel * width), BF16)])[0]
+    act = call(
+        pack_kernel,
+        acts,
+        [pltpu.VMEM((kernel * width, tokens), BF16)],
+        [pltpu.VMEM((tokens, kernel * width), BF16)],
+    )[0]
 
     act_z = swap(act, "dp", Z_BIT)
     act_x = swap(act, "dp", X_BIT)
 
     g_all, *gts = call(
         functools.partial(attention_kernel, pool, n_ctx, near_rels, late),
-        (*rows, w_query_v, w_key_v, w_value_v, w_out_v),
+        (*rows, *squares_v),
         [pltpu.VMEM((tokens, channels), BF16)]
         + [pltpu.VMEM((len(late) * narrow, tokens), BF16)] * len(near_rels),
         [pltpu.VMEM((tokens, channels), BF16)] * 9 + [pltpu.VMEM((n_dp, narrow, tokens), BF16)],

time: 55.9 us -> 56.3 us (level)
  Pallas kernels: 18.4 us -> 20.5 us
  waiting for transfers between devices: 15.4 us -> 13.3 us
    ppermute x14, waiting for transfers between devices: 15.4 us -> 13.3 us  [swap(): return lax.ppermute(value, axis, [(i, i ^ bit) for i in range(count)])]
    pallas_call x10 -> x11, Pallas kernels: 18.4 us -> 20.5 us  [call(): pl.pallas_call(body, out_shape=list(outs), scratch_shapes=list(scratch),...]
  transfers between devices with their start and end apart: 15 -> 15, of which waited for: 7 -> 5; matrix products, arithmetic and copies ran while one was open for 0% -> 0% of each run, Pallas kernels for 28% -> 31%
where the time goes in v2:
time: 56.3 us; the launch traced here: 56.1 us
  starting transfers between devices  21.6 us (38%)
  Pallas kernels  20.5 us (36%)
  waiting for transfers between devices  13.3 us (24%)
  between operations  0.75 us (1%)
    ppermute x14, starting transfers between devices, swap(): return lax.ppermute(value, axis, [(i, i ^ bit) for i in range(count)])  20.9 us
    pallas_call x11, Pallas kernels, call(): pl.pallas_call(body, out_shape=list(outs), scratch_shapes=list(scratch),...  20.5 us
    ppermute x14, waiting for transfers between devices, swap(): return lax.ppermute(value, axis, [(i, i ^ bit) for i in range(count)])  13.3 us
  transfers between devices with their start and end apart: 15, of which 5 were waited for; matrix products, arithmetic and copies ran while one was open for 0% of the time, Pallas kernels for 31%

profile of v2, /device:TPU:0, one launch (start us, length us, event | category | flops | bytes accessed | tf_op | source)
XLA Modules:
  0.0 56.1 jit_solution(95461914297533591)
XLA Ops:
  0.6 1.3 %shard_map.113 = (f32[2,768]{1,0:T(2,128)S(1)}, f32[2,768]{1,0:T(2,128)S(1)}, bf16[512,768]{1,0:T(8,128)(2,1)S(1)}, s32[1,512]{1,0:T(1,128)S(1)}, bf16[4,768]{1,...) custom-call(bf16[512,768]{1,0:T(8,128)(2,1)} %bitcast.4, s32[1,512]{1,0:T(1,128)} %base.1, bf16[4,768]{1,0:T(4,128)(2,1)} %table.1, ...), custom_call_target="tpu_custom_call" | custom-call | tf_op jit(solution)/shard_map/pallas_call | solution.py:356
  1.9 0.6 collective-permute-start
  2.5 0.6 %collective-permute-start.1 = (f32[2,768]{1,0:T(2,128)S(1)}, f32[2,768]{1,0:T(2,128)S(1)}, u32[]{:S(2)}, u32[]{:S(2)}) collective-permute-start(f32[2,768]{1,0:T(2,128)S(1)} %get-tuple-element.40), channel_id=1, source_target_pairs={{1,2},{2,1},{5,6},{6,5},{9,10},{10,9},{13,14},{14,13},{17,18},{18,... | collective-permute-start | bytes 18440 | tf_op jit(solution)/shard_map/ppermute | solution.py:413
  3.1 2.9 %shard_map.114 = (f32[160,768]{1,0:T(8,128)S(1)}, f32[32,768]{1,0:T(8,128)S(1)}, f32[512,768]{1,0:T(8,128)S(1)}, f32[512,768]{1,0:T(8,128)S(1)}, f32[512,128]{1,...) custom-call(bf16[512,768]{1,0:T(8,128)(2,1)S(1)} %get-tuple-element.34.feat, s32[1,512]{1,0:T(1,128)S(1)} %get-tuple-element.35.base, ...), custom_call_target="tpu_custom_call" | custom-call | tf_op jit(solution)/shard_map/pallas_call | solution.py:356
  6.1 0.0 collective-permute-done.near
  6.1 0.0 collective-permute-done.1.far
  6.1 0.3 shard_map.115
  6.3 3.9 %collective-permute-start.5 = (bf16[32,960]{1,0:T(8,128)(2,1)S(1)}, bf16[32,960]{1,0:T(8,128)(2,1)S(1)}, u32[]{:S(2)}, u32[]{:S(2)}) collective-permute-start(bf16[32,960]{1,0:T(8,128)(2,1)S(1)} %get-tuple-element.57), channel_id=1, source_target_pairs={{0,2},{1,3},{2,0},{3,1},{4,6},{5,7},{6,4},{7,5},{8,10},{9,11},{10,... | collective-permute-start | bytes 184328 | tf_op jit(solution)/shard_map/ppermute | solution.py:347
  10.3 0.1 collective-permute-start.6
  10.4 1.3 %collective-permute-start.7 = (bf16[32,960]{1,0:T(8,128)(2,1)S(1)}, bf16[32,960]{1,0:T(8,128)(2,1)S(1)}, u32[]{:S(2)}, u32[]{:S(2)}) collective-permute-start(bf16[32,960]{1,0:T(8,128)(2,1)S(1)} %get-tuple-element.59), channel_id=1, source_target_pairs={{0,3},{1,2},{2,1},{3,0},{4,7},{5,6},{6,5},{7,4},{8,11},{9,10},{10,... | collective-permute-start | bytes 184328 | tf_op jit(solution)/shard_map/ppermute | solution.py:347
  11.6 0.9 %collective-permute-done.5.refs_1_ = bf16[32,960]{1,0:T(8,128)(2,1)S(1)} collective-permute-done((bf16[32,960]{1,0:T(8,128)(2,1)S(1)}, bf16[32,960]{1,0:T(8,128)(2,1)S(1)}, u32[]{:S(2)}, u32[]{:S(2)}) %collective-permute-start.5) | collective-permute-done | bytes 61472 | tf_op jit(solution)/shard_map/ppermute | solution.py:347
  12.5 0.0 collective-permute-done.6.refs_2_
  12.5 2.1 %collective-permute-done.7.refs_3_ = bf16[32,960]{1,0:T(8,128)(2,1)S(1)} collective-permute-done((bf16[32,960]{1,0:T(8,128)(2,1)S(1)}, bf16[32,960]{1,0:T(8,128)(2,1)S(1)}, u32[]{:S(2)}, u32[]{:S(2)}) %collective-permute-start.7) | collective-permute-done | bytes 61472 | tf_op jit(solution)/shard_map/ppermute | solution.py:347
  14.6 0.3 shard_map.121.refs_0_
  14.9 2.5 %collective-permute-start.9 = (bf16[960,128]{1,0:T(8,128)(2,1)S(1)}, bf16[960,128]{1,0:T(8,128)(2,1)S(1)}, u32[]{:S(2)}, u32[]{:S(2)}) collective-permute-start(bf16[960,128]{1,0:T(8,128)(2,1)S(1)} %shard_map.121.refs_0_), channel_id=1, source_target_pairs={{0,16},{4,20},{8,24},{12,28},{16,0},{20,4},{24,8},{28,12},{1,17},{... | collective-permute-start | bytes 737288 | tf_op jit(solution)/shard_map/ppermute | solution.py:347
  17.4 1.7 %shard_map.116.refs_0_ = bf16[2,32,768]{2,1,0:T(8,128)(2,1)S(1)} custom-call(bf16[5,64,768]{2,1,0:T(8,128)(2,1)S(1)} %get-tuple-element.41.pairs, f32[32,768]{1,0:T(8,128)S(1)} %get-tuple-element.42.sums, bf16[5,768,768]{2,1,0:T(8,128)(2,1)S(1)} %get-tuple-element.43.weights, bf16[32,768]{1,0:T(8,128)(2,1)} %bitcast.7), custom_call_target="tpu_custom_call" | custom-call | tf_op jit(solution)/shard_map/pallas_call | solution.py:356
  19.1 1.9 %collective-permute-start.2 = (bf16[2,32,768]{2,1,0:T(8,128)(2,1)S(1)}, bf16[2,32,768]{2,1,0:T(8,128)(2,1)S(1)}, u32[]{:S(2)}, u32[]{:S(2)}) collective-permute-start(bf16[2,32,768]{2,1,0:T(8,128)(2,1)S(1)} %shard_map.116.refs_0_), channel_id=1, source_target_pairs={{0,2},{1,3},{2,0},{3,1},{4,6},{5,7},{6,4},{7,5},{8,10},{9,11},{10,... | collective-permute-start | bytes 294920 | tf_op jit(solution)/shard_map/ppermute | solution.py:347
  21.0 1.5 %collective-permute-start.8 = (bf16[960,128]{1,0:T(8,128)(2,1)S(1)}, bf16[960,128]{1,0:T(8,128)(2,1)S(1)}, u32[]{:S(2)}, u32[]{:S(2)}) collective-permute-start(bf16[960,128]{1,0:T(8,128)(2,1)S(1)} %shard_map.121.refs_0_), channel_id=1, source_target_pairs={{0,4},{4,0},{8,12},{12,8},{16,20},{20,16},{24,28},{28,24},{1,5},{5... | collective-permute-start | bytes 737288 | tf_op jit(solution)/shard_map/ppermute | solution.py:347
  22.4 6.8 %collective-permute-done.9.refs_2_ = bf16[960,128]{1,0:T(8,128)(2,1)S(1)} collective-permute-done((bf16[960,128]{1,0:T(8,128)(2,1)S(1)}, bf16[960,128]{1,0:T(8,128)(2,1)S(1)}, u32[]{:S(2)}, u32[]{:S(2)}) %collective-permute-start.9) | collective-permute-done | bytes 245792 | tf_op jit(solution)/shard_map/ppermute | solution.py:347
  29.3 1.5 %collective-permute-start.10 = (bf16[960,128]{1,0:T(8,128)(2,1)S(1)}, bf16[960,128]{1,0:T(8,128)(2,1)S(1)}, u32[]{:S(2)}, u32[]{:S(2)}) collective-permute-start(bf16[960,128]{1,0:T(8,128)(2,1)S(1)} %collective-permute-done.9.refs_2_), channel_id=1, source_target_pairs={{0,4},{4,0},{8,12},{12,8},{16,20},{20,16},{24,28},{28,24},{1,5},{5... | collective-permute-start | bytes 737288 | tf_op jit(solution)/shard_map/ppermute | solution.py:347
  30.8 0.0 collective-permute-start.3
  30.8 0.0 collective-permute-done.2.refs_1_
  30.8 0.5 collective-permute-start.4
  31.3 2.4 %shard_map.117 = (f32[512,768]{1,0:T(8,128)S(1)}, bf16[768,768]{1,0:T(8,128)(2,1)S(1)}, bf16[768,768]{1,0:T(8,128)(2,1)S(1)}, bf16[768,768]{1,0:T(8,128)(2,1)S(1)}, bf16[768,768]{1,0:T(8,128)(2,1)S(1)}) custom-call(f32[512,768]{1,0:T(8,128)S(1)} %get-tuple-element.44.tanh_ref, f32[512,768]{1,0:T(8,128)S(1)} %get-tuple-element.45.normed_ref.normed, ...), custom_call_target="tpu_custom_call" | custom-call | tf_op jit(solution)/shard_map/pallas_call | solution.py:356
  33.7 0.0 collective-permute-done.3.refs_2_
  33.7 0.0 collective-permute-done.4.refs_3_
  33.7 5.8 %shard_map.118 = (bf16[128,768]{1,0:T(8,128)(2,1)S(1)}, bf16[192,128]{1,0:T(8,128)(2,1)S(1)}, bf16[192,128]{1,0:T(8,128)(2,1)S(1)}, bf16[192,128]{1,0:T(8,128)(2,1)S(1)}, bf16[192,128]{1,0:T(8,128)(2,1)S(1)}) custom-call(bf16[2,32,768]{2,1,0:T(8,128)(2,1)S(1)} %shard_map.116.refs_0_, bf16[2,32,768]{2,1,0:T(8,128)(2,1)S(1)} %collective-permute-done.2.refs_1_, ...), custom_call_target="tpu_custom_call" | custom-call | tf_op jit(solution)/shard_map/pallas_call | solution.py:356
  39.6 0.5 collective-permute-start.11
  40.1 0.0 collective-permute-start.12
  40.1 3.9 %collective-permute-start.13 = (bf16[192,128]{1,0:T(8,128)(2,1)S(1)}, bf16[192,128]{1,0:T(8,128)(2,1)S(1)}, u32[]{:S(2)}, u32[]{:S(2)}) collective-permute-start(bf16[192,128]{1,0:T(8,128)(2,1)S(1)} %get-tuple-element.63), channel_id=1, source_target_pairs={{0,20},{4,16},{8,28},{12,24},{16,4},{20,0},{24,12},{28,8},{1,21},{... | collective-permute-start | bytes 147464 | tf_op jit(solution)/shard_map/ppermute | solution.py:347
  44.1 0.0 collective-permute-done.11.refs_5_
  44.1 2.3 %collective-permute-done.12.refs_6_ = bf16[192,128]{1,0:T(8,128)(2,1)S(1)} collective-permute-done((bf16[192,128]{1,0:T(8,128)(2,1)S(1)}, bf16[192,128]{1,0:T(8,128)(2,1)S(1)}, u32[]{:S(2)}, u32[]{:S(2)}) %collective-permute-start.12) | collective-permute-done | bytes 49184 | tf_op jit(solution)/shard_map/ppermute | solution.py:347
  46.4 1.1 %collective-permute-done.13.refs_7_ = bf16[192,128]{1,0:T(8,128)(2,1)S(1)} collective-permute-done((bf16[192,128]{1,0:T(8,128)(2,1)S(1)}, bf16[192,128]{1,0:T(8,128)(2,1)S(1)}, u32[]{:S(2)}, u32[]{:S(2)}) %collective-permute-start.13) | collective-permute-done | bytes 49184 | tf_op jit(solution)/shard_map/ppermute | solution.py:347
  47.5 0.0 collective-permute-done.8.refs_1_
  47.5 0.0 collective-permute-done.10.refs_3_
  47.5 0.6 %shard_map.122 = (f32[96,960]{1,0:T(8,128)S(1)}, bf16[96,960]{1,0:T(8,128)(2,1)S(1)}) custom-call(bf16[960,128]{1,0:T(8,128)(2,1)S(1)} %shard_map.121.refs_0_, bf16[960,128]{1,0:T(8,128)(2,1)S(1)} %collective-permute-done.8.refs_1_, bf16[960,128]{1,0:T(8,128)(2,1)S(1)} %collective-permute-done.9.refs_2_, ...), custom_call_target="tpu_custom_call" | custom-call | tf_op jit(solution)/shard_map/pallas_call | solution.py:356
  48.1 2.7 %collective-permute-start.14 = (bf16[96,960]{1,0:T(8,128)(2,1)S(1)}, bf16[96,960]{1,0:T(8,128)(2,1)S(1)}, u32[]{:S(2)}, u32[]{:S(2)}) collective-permute-start(bf16[96,960]{1,0:T(8,128)(2,1)S(1)} %get-tuple-element.65), channel_id=1, source_target_pairs={{0,8},{4,12},{8,0},{12,4},{16,24},{20,28},{24,16},{28,20},{1,9},{5... | collective-permute-start | bytes 552968 | tf_op jit(solution)/shard_map/ppermute | solution.py:347
  50.8 1.8 %shard_map.119 = (bf16[200,768]{1,0:T(8,128)(2,1)S(1)}, bf16[200,768]{1,0:T(8,128)(2,1)S(1)}, bf16[40,768]{1,0:T(8,128)(2,1)S(1)}) custom-call(bf16[128,768]{1,0:T(8,128)(2,1)S(1)} %get-tuple-element.51.g_ref, bf16[5,768,768]{2,1,0:T(8,128)(2,1)S(1)} %get-tuple-element.43.weights), custom_call_target="tpu_custom_call" | custom-call | tf_op jit(solution)/shard_map/pallas_call | solution.py:356
  52.6 2.5 %shard_map.120 = bf16[512,768]{1,0:T(8,128)(2,1)} custom-call(bf16[200,768]{1,0:T(8,128)(2,1)S(1)} %get-tuple-element.52.highs, bf16[200,768]{1,0:T(8,128)(2,1)S(1)} %get-tuple-element.53.lows, bf16[40,768]{1,0:T(8,128)(2,1)S(1)} %get-tuple-element.54.near, f32[512,768]{1,0:T(8,128)S(1)} %get-tuple-element.55.slope, ...), custom_call_target="tpu_custom_call" | custom-call | tf_op jit(solution)/shard_map/pallas_call | solution.py:356
  55.1 0.0 collective-permute-done.14.other
  55.1 1.0 %shard_map.123 = f32[5,192,96]{2,1,0:T(8,128)} custom-call(f32[96,960]{1,0:T(8,128)S(1)} %get-tuple-element.64.mine, bf16[96,960]{1,0:T(8,128)(2,1)S(1)} %collective-permute-done.14.other), custom_call_target="tpu_custom_call" | custom-call | tf_op jit(solution)/shard_map/pallas_call | solution.py:356
Async XLA Ops:
  1.9 4.1 %collective-permute-start = (f32[2,768]{1,0:T(2,128)S(1)}, f32[2,768]{1,0:T(2,128)S(1)}, u32[]{:S(2)}, u32[]{:S(2)}) collective-permute-start(f32[2,768]{1,0:T(2,128)S(1)} %get-tuple-element.39), channel_id=1, source_target_pairs={{0,1},{1,0},{2,3},{3,2},{4,5},{5,4},{6,7},{7,6},{8,9},{9,8},{10,11... | collective-permute-start | bytes 18440 | tf_op jit(solution)/shard_map/ppermute | solution.py:347
  2.5 3.6 %collective-permute-start.1 = (f32[2,768]{1,0:T(2,128)S(1)}, f32[2,768]{1,0:T(2,128)S(1)}, u32[]{:S(2)}, u32[]{:S(2)}) collective-permute-start(f32[2,768]{1,0:T(2,128)S(1)} %get-tuple-element.40), channel_id=1, source_target_pairs={{1,2},{2,1},{5,6},{6,5},{9,10},{10,9},{13,14},{14,13},{17,18},{18,... | collective-permute-start | bytes 18440 | tf_op jit(solution)/shard_map/ppermute | solution.py:413
  6.3 6.2 %collective-permute-start.5 = (bf16[32,960]{1,0:T(8,128)(2,1)S(1)}, bf16[32,960]{1,0:T(8,128)(2,1)S(1)}, u32[]{:S(2)}, u32[]{:S(2)}) collective-permute-start(bf16[32,960]{1,0:T(8,128)(2,1)S(1)} %get-tuple-element.57), channel_id=1, source_target_pairs={{0,2},{1,3},{2,0},{3,1},{4,6},{5,7},{6,4},{7,5},{8,10},{9,11},{10,... | collective-permute-start | bytes 184328 | tf_op jit(solution)/shard_map/ppermute | solution.py:347
  10.3 2.2 %collective-permute-start.6 = (bf16[32,960]{1,0:T(8,128)(2,1)S(1)}, bf16[32,960]{1,0:T(8,128)(2,1)S(1)}, u32[]{:S(2)}, u32[]{:S(2)}) collective-permute-start(bf16[32,960]{1,0:T(8,128)(2,1)S(1)} %get-tuple-element.58), channel_id=1, source_target_pairs={{0,1},{1,0},{2,3},{3,2},{4,5},{5,4},{6,7},{7,6},{8,9},{9,8},{10,11... | collective-permute-start | bytes 184328 | tf_op jit(solution)/shard_map/ppermute | solution.py:347
  10.4 4.3 %collective-permute-start.7 = (bf16[32,960]{1,0:T(8,128)(2,1)S(1)}, bf16[32,960]{1,0:T(8,128)(2,1)S(1)}, u32[]{:S(2)}, u32[]{:S(2)}) collective-permute-start(bf16[32,960]{1,0:T(8,128)(2,1)S(1)} %get-tuple-element.59), channel_id=1, source_target_pairs={{0,3},{1,2},{2,1},{3,0},{4,7},{5,6},{6,5},{7,4},{8,11},{9,10},{10,... | collective-permute-start | bytes 184328 | tf_op jit(solution)/shard_map/ppermute | solution.py:347
  14.9 14.4 %collective-permute-start.9 = (bf16[960,128]{1,0:T(8,128)(2,1)S(1)}, bf16[960,128]{1,0:T(8,128)(2,1)S(1)}, u32[]{:S(2)}, u32[]{:S(2)}) collective-permute-start(bf16[960,128]{1,0:T(8,128)(2,1)S(1)} %shard_map.121.refs_0_), channel_id=1, source_target_pairs={{0,16},{4,20},{8,24},{12,28},{16,0},{20,4},{24,8},{28,12},{1,17},{... | collective-permute-start | bytes 737288 | tf_op jit(solution)/shard_map/ppermute | solution.py:347
  19.1 11.7 %collective-permute-start.2 = (bf16[2,32,768]{2,1,0:T(8,128)(2,1)S(1)}, bf16[2,32,768]{2,1,0:T(8,128)(2,1)S(1)}, u32[]{:S(2)}, u32[]{:S(2)}) collective-permute-start(bf16[2,32,768]{2,1,0:T(8,128)(2,1)S(1)} %shard_map.116.refs_0_), channel_id=1, source_target_pairs={{0,2},{1,3},{2,0},{3,1},{4,6},{5,7},{6,4},{7,5},{8,10},{9,11},{10,... | collective-permute-start | bytes 294920 | tf_op jit(solution)/shard_map/ppermute | solution.py:347
  21.0 26.6 %collective-permute-start.8 = (bf16[960,128]{1,0:T(8,128)(2,1)S(1)}, bf16[960,128]{1,0:T(8,128)(2,1)S(1)}, u32[]{:S(2)}, u32[]{:S(2)}) collective-permute-start(bf16[960,128]{1,0:T(8,128)(2,1)S(1)} %shard_map.121.refs_0_), channel_id=1, source_target_pairs={{0,4},{4,0},{8,12},{12,8},{16,20},{20,16},{24,28},{28,24},{1,5},{5... | collective-permute-start | bytes 737288 | tf_op jit(solution)/shard_map/ppermute | solution.py:347
  29.3 18.2 %collective-permute-start.10 = (bf16[960,128]{1,0:T(8,128)(2,1)S(1)}, bf16[960,128]{1,0:T(8,128)(2,1)S(1)}, u32[]{:S(2)}, u32[]{:S(2)}) collective-permute-start(bf16[960,128]{1,0:T(8,128)(2,1)S(1)} %collective-permute-done.9.refs_2_), channel_id=1, source_target_pairs={{0,4},{4,0},{8,12},{12,8},{16,20},{20,16},{24,28},{28,24},{1,5},{5... | collective-permute-start | bytes 737288 | tf_op jit(solution)/shard_map/ppermute | solution.py:347
  30.8 2.9 %collective-permute-start.3 = (bf16[2,32,768]{2,1,0:T(8,128)(2,1)S(1)}, bf16[2,32,768]{2,1,0:T(8,128)(2,1)S(1)}, u32[]{:S(2)}, u32[]{:S(2)}) collective-permute-start(bf16[2,32,768]{2,1,0:T(8,128)(2,1)S(1)} %shard_map.116.refs_0_), channel_id=1, source_target_pairs={{0,1},{1,0},{2,3},{3,2},{4,5},{5,4},{6,7},{7,6},{8,9},{9,8},{10,11... | collective-permute-start | bytes 294920 | tf_op jit(solution)/shard_map/ppermute | solution.py:347
  30.8 2.9 %collective-permute-start.4 = (bf16[2,32,768]{2,1,0:T(8,128)(2,1)S(1)}, bf16[2,32,768]{2,1,0:T(8,128)(2,1)S(1)}, u32[]{:S(2)}, u32[]{:S(2)}) collective-permute-start(bf16[2,32,768]{2,1,0:T(8,128)(2,1)S(1)} %collective-permute-done.2.refs_1_), channel_id=1, source_target_pairs={{0,1},{1,0},{2,3},{3,2},{4,5},{5,4},{6,7},{7,6},{8,9},{9,8},{10,11... | collective-permute-start | bytes 294920 | tf_op jit(solution)/shard_map/ppermute | solution.py:347
  39.6 4.5 %collective-permute-start.11 = (bf16[192,128]{1,0:T(8,128)(2,1)S(1)}, bf16[192,128]{1,0:T(8,128)(2,1)S(1)}, u32[]{:S(2)}, u32[]{:S(2)}) collective-permute-start(bf16[192,128]{1,0:T(8,128)(2,1)S(1)} %get-tuple-element.61), channel_id=1, source_target_pairs={{0,4},{4,0},{8,12},{12,8},{16,20},{20,16},{24,28},{28,24},{1,5},{5... | collective-permute-start | bytes 147464 | tf_op jit(solution)/shard_map/ppermute | solution.py:347
  40.1 6.2 %collective-permute-start.12 = (bf16[192,128]{1,0:T(8,128)(2,1)S(1)}, bf16[192,128]{1,0:T(8,128)(2,1)S(1)}, u32[]{:S(2)}, u32[]{:S(2)}) collective-permute-start(bf16[192,128]{1,0:T(8,128)(2,1)S(1)} %get-tuple-element.62), channel_id=1, source_target_pairs={{0,16},{4,20},{8,24},{12,28},{16,0},{20,4},{24,8},{28,12},{1,17},{... | collective-permute-start | bytes 147464 | tf_op jit(solution)/shard_map/ppermute | solution.py:347
  40.1 7.4 %collective-permute-start.13 = (bf16[192,128]{1,0:T(8,128)(2,1)S(1)}, bf16[192,128]{1,0:T(8,128)(2,1)S(1)}, u32[]{:S(2)}, u32[]{:S(2)}) collective-permute-start(bf16[192,128]{1,0:T(8,128)(2,1)S(1)} %get-tuple-element.63), channel_id=1, source_target_pairs={{0,20},{4,16},{8,28},{12,24},{16,4},{20,0},{24,12},{28,8},{1,21},{... | collective-permute-start | bytes 147464 | tf_op jit(solution)/shard_map/ppermute | solution.py:347
  48.1 7.0 %collective-permute-start.14 = (bf16[96,960]{1,0:T(8,128)(2,1)S(1)}, bf16[96,960]{1,0:T(8,128)(2,1)S(1)}, u32[]{:S(2)}, u32[]{:S(2)}) collective-permute-start(bf16[96,960]{1,0:T(8,128)(2,1)S(1)} %get-tuple-element.65), channel_id=1, source_target_pairs={{0,8},{4,12},{8,0},{12,4},{16,24},{20,28},{24,16},{28,20},{1,9},{5... | collective-permute-start | bytes 552968 | tf_op jit(solution)/shard_map/ppermute | solution.py:347

commit v3 on v1

v3 whole, which is shorter than its diff:
```python
import functools

import jax
import jax.numpy as jnp
from jax import lax
from jax.experimental import pallas as pl
from jax.experimental.pallas import tpu as pltpu
from jax.sharding import PartitionSpec as P


HEADS = 6
DH = 128

EPSILON = 1e-06
GELU_SCALE = 0.7978845608028654
CUBIC = 0.044715
F32 = jnp.float32
BF16 = jnp.bfloat16
VMEM_LIMIT = 28 << 20
X_BIT, Z_BIT = 1, 4


def dot_nn(left, right):
    return lax.dot_general(left, right, (((1,), (0,)), ((), ())), preferred_element_type=F32)


def dot_nt(left, right):
    return lax.dot_general(left, right, (((1,), (1,)), ((), ())), preferred_element_type=F32)


def dot_tn(left, right):
    return lax.dot_general(left, right, (((0,), (0,)), ((), ())), preferred_element_type=F32)


def split2(value):
    high = value.astype(BF16)
    return high, (value - high.astype(F32)).astype(BF16)


def iota(shape, dim):
    return lax.broadcasted_iota(jnp.int32, shape, dim)


def normed_of(summed):
    inv_rms = lax.rsqrt(jnp.mean(summed * summed, axis=-1, keepdims=True) + EPSILON)
    return inv_rms, summed * inv_rms


def gelu_of(u):
    tanh_val = jnp.tanh(GELU_SCALE * (u + CUBIC * (u * u * u)))
    return tanh_val, 0.5 * u * (1.0 + tanh_val)


def pick(index, values):
    out = jnp.int32(values[0])
    for at, value in enumerate(values[1:], 1):
        out = jnp.where(index == at, jnp.int32(value), out)
    return out


def start_copies(pairs, sems):
    copies = [pltpu.make_async_copy(src, dst, sems.at[i]) for i, (src, dst) in enumerate(pairs)]
    for copy in copies:
        copy.start()
    return copies


def act_kernel(
    kernel, pool, tok_rows, feat_hbm, base_hbm, table_hbm, gain_hbm, cot_hbm, w_hbm,
    taps, sums, tanh_out, normed_out, inv_out, gain, cot, weights,
    feat, base, table, act_buf, high_buf, low_buf, sems,
):
    half = kernel // 2
    rows, channels = feat.shape
    block = act_buf.shape[0]
    count = rows // block
    small = ((base_hbm, base), (table_hbm, table), (gain_hbm, gain))
    parts = tuple(
        (feat_hbm.at[pl.ds(i * block, block)], feat.at[pl.ds(i * block, block)]) for i in range(count)
    )
    copies = start_copies(small + parts + ((cot_hbm, cot), (w_hbm, weights)), sems)
    padded = taps.shape[0] // kernel
    taps[...] = jnp.zeros_like(taps)
    sums[...] = jnp.zeros_like(sums)
    for copy in copies[: len(small)]:
        copy.wait()
    gain_f = gain[...].reshape(1, channels).astype(F32)
    chunk = 32

    @pl.loop(0, count)
    def _(step):
        start = pl.multiple_of(step * block, block)
        here = pl.ds(start, block)
        pltpu.make_async_copy(feat_hbm.at[here], feat.at[here], sems.at[len(small) + step]).wait()
        onehot = (iota((table.shape[0], block), 0) == base[:, here]).astype(BF16)
        embed = dot_tn(onehot, table[...])
        for begin in range(0, block, chunk):
            part = slice(begin, begin + chunk)
            here = pl.ds(start + begin, chunk)
            summed = feat[here, :].astype(F32) + embed[part, :]
            inv_rms, normed = normed_of(summed)
            u = normed * gain_f
            tanh_val, value = gelu_of(u)
            act_buf[part, :] = value.astype(BF16)
            high_buf[part, :], low_buf[part, :] = split2(summed)
            tanh_out[here, :] = tanh_val
            normed_out[here, :] = normed
            inv_out[here, :] = jnp.broadcast_to(inv_rms, (chunk, inv_out.shape[1]))
        shape = (kernel * padded, block)
        row = iota(shape, 0)
        tap = sum((row >= padded * j).astype(jnp.int32) for j in range(1, kernel))
        token = row - tap * padded
        token = jnp.where(token == tok_rows, -1, jnp.where(token == tok_rows + 1, tok_rows, token))
        known = row - tap * padded < tok_rows + 2
        offset = iota(shape, 1) + start - tap + half - token * pool
        spread = ((offset >= 0) & (offset < pool) & known).astype(BF16)
        taps[...] += dot_nn(spread, act_buf[...])
        plain = spread[half * padded : (half + 1) * padded, :]
        sums[...] += dot_nn(plain, high_buf[...]) + dot_nn(plain, low_buf[...])

    for copy in copies[len(small) + count :]:
        copy.wait()


def taps_kernel(kernel, blocks, taps, pairs, *rest):
    outs, turn = rest[:blocks], rest[blocks]
    me = lax.axis_index("ctx")
    padded = taps.shape[0] // kernel
    highs = []
    for j in range(kernel):
        high, low = split2(taps[j * padded : (j + 1) * padded, :])
        highs.append(high)
        pairs[j] = jnp.concatenate([high, low], axis=0)
    width = taps.shape[1] // blocks
    for b in range(blocks):
        turn[b ^ me] = jnp.concatenate([h[:, b * width : (b + 1) * width] for h in highs], axis=1)
    for b in range(blocks):
        outs[b][...] = turn[b]


def pool_kernel(pool, tok_rows, pairs, sums, weights, cot, rows):
    padded = sums.shape[0]
    total = dot_nn(pairs[0], weights[0])
    for j in range(1, pairs.shape[0]):
        total = total + dot_nn(pairs[j], weights[j])
    conv = total[:padded] + total[padded:]
    value = (sums[...] + conv) * (1.0 / pool)
    high, low = split2(value)
    rows[:padded, :] = high
    rows[padded : padded + tok_rows, :] = cot[...]
    low_f = low.astype(F32)
    ends = [low_f[:1], low_f[tok_rows - 1 : tok_rows + 2]]
    ends = jnp.concatenate(ends + [jnp.zeros((4, low.shape[1]), F32)], axis=0)
    rows[padded + tok_rows :, :] = ends.astype(BF16)


def neighbours(me, order, count, befores, afters, ends):
    zero = jnp.zeros(ends.shape[1:], F32)
    ends[0] = zero
    ends[count + 1] = zero
    for rel, before, after in zip(order, befores, afters):
        owner = me ^ rel
        ends[owner + 1, 0:1, :] = before
        ends[owner + 1, 1:2, :] = after
    return [(ends[me ^ rel, 1:2, :], ends[(me ^ rel) + 2, 0:1, :]) for rel in order]


def pack_kernel(order, tok_rows, *refs):
    *parts, out, buf, ends = refs
    me = lax.axis_index("ctx")
    tails = [part[tok_rows : tok_rows + 8, :].astype(F32) for part in parts]
    extra = neighbours(
        me, order, len(parts), [tail[0:1] for tail in tails], [tail[1:2] for tail in tails], ends
    )
    for at, (part, (first, last)) in enumerate(zip(parts, extra)):
        value = part[:tok_rows, :].astype(F32)
        row = iota(value.shape, 0)
        value = value + jnp.where(row == 0, first, 0.0) + jnp.where(row == tok_rows - 1, last, 0.0)
        buf[at * tok_rows : (at + 1) * tok_rows, :] = value.astype(BF16)
    total = buf.shape[0]
    eye = (iota((total, total), 0) == iota((total, total), 1)).astype(BF16)
    out[...] = dot_tn(buf[...], eye).astype(BF16)


def attention_kernel(pool, order, tok_rows, near_rels, late, *refs):
    blocks = len(order)
    parts, refs = refs[:blocks], refs[blocks:]
    (wq, wk, wv_hbm, wo_hbm), refs = refs[:4], refs[4:]
    g_out, refs = refs[0], refs[1:]
    gts, refs = refs[: len(near_rels)], refs[len(near_rels) :]
    p_buf, c_buf, q_buf, k_buf, v_buf, ga_buf, gq_buf, gk_buf, gv_buf = refs[:9]
    probs_buf, turn, ends, wv, wo, sems = refs[9:]
    copies = start_copies(((wv_hbm, wv), (wo_hbm, wo)), sems)
    padded = parts[0].shape[0] - tok_rows - 8
    befores, afters, firsts, lasts = [], [], [], []
    for part in parts:
        tail = part[tok_rows : tok_rows + 8, :].astype(F32)
        lows = part[padded + tok_rows :, :].astype(F32)
        firsts.append(part[:8, :].astype(F32)[0:1] + lows[0:1])
        lasts.append(part[tok_rows - 8 : tok_rows, :].astype(F32)[7:8] + lows[1:2])
        befores.append(tail[0:1] + lows[2:3])
        afters.append(tail[1:2] + lows[3:4])
    extra = neighbours(lax.axis_index("ctx"), order, blocks, befores, afters, ends)
    for at, (part, first, last, (to_first, to_last)) in enumerate(zip(parts, firsts, lasts, extra)):
        value = part[:tok_rows, :].astype(F32)
        row = iota(value.shape, 0)
        value = jnp.where(row == 0, first + to_first, value)
        value = jnp.where(row == tok_rows - 1, last + to_last, value)
        here = slice(at * tok_rows, (at + 1) * tok_rows)
        p_buf[here, :] = value.astype(BF16)
        c_buf[here, :] = part[padded : padded + tok_rows, :]
    q_buf[...] = dot_nn(p_buf[...], wq[...]).astype(BF16)
    k_buf[...] = dot_nn(p_buf[...], wk[...]).astype(BF16)
    scale = 1.0 / DH**0.5
    for h in range(HEADS):
        cols = slice(h * DH, (h + 1) * DH)
        scores = dot_nt(q_buf[:, cols], k_buf[:, cols]) * scale
        expo = jnp.exp(scores - jnp.max(scores, axis=-1, keepdims=True))
        probs_buf[h] = expo / jnp.sum(expo, axis=-1, keepdims=True)
    copies[0].wait()
    v_buf[...] = dot_nn(p_buf[...], wv[...]).astype(BF16)
    copies[1].wait()
    ga_buf[...] = dot_nt(c_buf[...], wo[...]).astype(BF16)
    for h in range(HEADS):
        cols = slice(h * DH, (h + 1) * DH)
        q, k, v, ga = q_buf[:, cols], k_buf[:, cols], v_buf[:, cols], ga_buf[:, cols]
        probs = probs_buf[h]
        probs_b = probs.astype(BF16)
        out = dot_nn(probs_b, v).astype(BF16)
        delta = jnp.sum(ga.astype(F32) * out.astype(F32), axis=-1, keepdims=True)
        grad_score = (probs * (dot_nt(ga, v) - delta) * scale).astype(BF16)
        gq_buf[:, cols] = dot_nn(grad_score, k).astype(BF16)
        gk_buf[:, cols] = dot_tn(grad_score, q).astype(BF16)
        gv_buf[:, cols] = dot_tn(probs_b, ga).astype(BF16)
    grad = c_buf[...].astype(F32)
    for src, weight in ((gq_buf, wq), (gk_buf, wk), (gv_buf, wv)):
        grad = grad + dot_nt(src[...], weight[...])
    g = (grad * (1.0 / pool)).astype(BF16)
    g_out[...] = g
    tokens = g.shape[0]
    eye = (iota((tokens, tokens), 0) == iota((tokens, tokens), 1)).astype(BF16)
    turned = dot_tn(g, eye).astype(BF16)
    count = turn.shape[0]
    span = turned.shape[0] // count
    me = lax.axis_index("dp")
    for o in range(count):
        turn[o ^ me] = turned[o * span : (o + 1) * span, :]
    for gt, base in zip(gts, near_rels):
        for at, rel in enumerate(late):
            gt[at * span : (at + 1) * span, :] = turn[base ^ rel]


def spread_kernel(kernel, tok_rows, befores, afters, g_ref, weights, highs, lows, near):
    tokens = g_ref.shape[0]
    padded = near.shape[0]
    me = lax.axis_index("ctx")
    row = iota((padded, tokens), 0)
    source = jnp.where(
        row == 0, pick(me, befores), jnp.where(row == tok_rows + 1, pick(me, afters), row - 1)
    )
    source = jnp.where(row > tok_rows + 1, -1, source)
    chosen = (source == iota((padded, tokens), 1)).astype(BF16)
    rows = dot_nn(chosen, g_ref[...]).astype(BF16)
    near[...] = rows
    for j in range(kernel):
        part = slice(j * padded, (j + 1) * padded)
        highs[part, :], lows[part, :] = split2(dot_nt(rows, weights[j]))


def input_grad_kernel(
    kernel, pool, highs, lows, near, tanh_ref, normed_ref, inv_ref, gain, out
):
    half = kernel // 2
    rows, channels = out.shape
    padded = near.shape[0]
    start = pl.program_id(0) * rows
    here = pl.ds(pl.multiple_of(start, rows), rows)
    shape = (rows, kernel * padded)
    col = iota(shape, 1)
    tap = sum((col >= padded * j).astype(jnp.int32) for j in range(1, kernel))
    token = col - tap * padded - 1
    offset = iota(shape, 0) + start - tap + half - token * pool
    spread = ((offset >= 0) & (offset < pool)).astype(BF16)
    grad_act = dot_nn(spread, highs[...]) + dot_nn(spread, lows[...])
    plain = spread[:, half * padded : (half + 1) * padded]
    grad_rows = dot_nn(plain, near[...])
    gain_f = gain[...].reshape(1, channels).astype(F32)
    tanh_val, unit = tanh_ref[here, :], normed_ref[here, :]
    u = unit * gain_f
    slopes = 0.5 * (1.0 + tanh_val) + 0.5 * u * (1.0 - tanh_val * tanh_val) * GELU_SCALE * (
        1.0 + 3.0 * CUBIC * (u * u)
    )
    grad_norm = grad_act * slopes * gain_f
    mean = jnp.mean(grad_norm * unit, axis=-1, keepdims=True)
    out[...] = (grad_rows + inv_ref[here, :1] * (grad_norm - unit * mean)).astype(BF16)


def kernel_grad_kernel(factor, *refs):
    count = len(refs) // 2 - 1
    acts, gts, (mine, theirs) = refs[:count], refs[count : 2 * count], refs[2 * count :]
    total = None
    for act, gt in zip(acts, gts):
        term = dot_nt(gt[...], act[...])
        total = term if total is None else total + term
    total = total * factor
    span = mine.shape[0]
    mine[...] = total[:span, :]
    theirs[...] = total[span:, :].astype(BF16)


def fold_kernel(mine, other, kept, sent):
    span = kept.shape[0]
    kept[...] = mine[:span, :] + other[:span, :].astype(F32)
    sent[...] = (mine[span:, :] + other[span:, :].astype(F32)).astype(BF16)


def join_kernel(kernel, mine, other, out):
    width = out.shape[1]
    total = jnp.transpose(mine[...] + other[...].astype(F32))
    for j in range(kernel):
        out[j] = total[j * width : (j + 1) * width, :]


def xor_order(count):
    order = [0]
    bit = count // 2
    while bit:
        order = order + [v ^ bit for v in order]
        bit //= 2
    return order


def swap(value, axis, bit):
    count = lax.axis_size(axis)
    return lax.ppermute(value, axis, [(i, i ^ bit) for i in range(count)])


WHOLE = pl.BlockSpec(memory_space=pltpu.VMEM)


def call(body, args, outs, scratch=(), **options):
    options.setdefault("in_specs", [WHOLE] * len(args))
    options.setdefault("out_specs", [WHOLE] * len(outs))
    return pl.pallas_call(
        body,
        out_shape=list(outs),
        scratch_shapes=list(scratch),
        compiler_params=pltpu.CompilerParams(vmem_limit_bytes=VMEM_LIMIT),
        **options,
    )(*args)


def outside(*values):
    return [pltpu.with_memory_space_constraint(value, pltpu.HBM) for value in values]


def bits_of(count):
    return [1 << at for at in range(count.bit_length() - 1)]


def sums_of(bits):
    out = [0]
    for bit in bits:
        out = out + [bit + value for value in out]
    return out


def per_device(
    features, bases, dna_table, norm_gain, w_conv, w_query, w_key, w_value, w_out, cotangent
):
    feat, cot = features[0], cotangent[0]
    kernel = w_conv.shape[0]
    length, channels = feat.shape
    tok_rows = cot.shape[0]
    pool = length // tok_rows
    n_ctx, n_dp = lax.axis_size("ctx"), lax.axis_size("dp")
    tokens = n_ctx * tok_rows
    width = channels // n_ctx
    narrow = channels // n_dp
    near_rels = [0, X_BIT, Z_BIT, X_BIT + Z_BIT]
    late = sums_of([bit for bit in bits_of(n_dp) if bit not in (X_BIT, Z_BIT)])

    order = xor_order(n_ctx)
    place = {rel: at for at, rel in enumerate(order)}
    befores = [-1] + [place[c ^ (c - 1)] * tok_rows + tok_rows - 1 for c in range(1, n_ctx)]
    afters = [place[c ^ (c + 1)] * tok_rows for c in range(n_ctx - 1)] + [-1]

    hbm = pl.BlockSpec(memory_space=pltpu.HBM)
    block = 128
    wide = -(-(tok_rows + 2) // 8) * 8
    taps, sums, tanh_val, normed, inv_rms, gain_v, cot_v, w_conv_v = call(
        functools.partial(act_kernel, kernel, pool, tok_rows),
        outside(feat, bases, dna_table, norm_gain, cot, w_conv),
        [
            pltpu.VMEM((kernel * wide, channels), F32),
            pltpu.VMEM((wide, channels), F32),
            pltpu.VMEM((length, channels), F32),
            pltpu.VMEM((length, channels), F32),
            pltpu.VMEM((length, 128), F32),
            pltpu.VMEM(norm_gain.shape, BF16),
            pltpu.VMEM(cot.shape, BF16),
            pltpu.VMEM(w_conv.shape, BF16),
        ],
        [
            pltpu.VMEM(feat.shape, BF16),
            pltpu.VMEM(bases.shape, jnp.int32),
            pltpu.VMEM(dna_table.shape, BF16),
        ]
        + [pltpu.VMEM((block, channels), BF16)] * 3
        + [pltpu.SemaphoreType.DMA((5 + length // block,))],
        in_specs=[hbm] * 6,
    )
    pairs, *acts = call(
        functools.partial(taps_kernel, kernel, n_ctx),
        (taps,),
        [pltpu.VMEM((kernel, 2 * wide, channels), BF16)]
        + [pltpu.VMEM((wide, kernel * width), BF16)] * n_ctx,
        [pltpu.VMEM((n_ctx, wide, kernel * width), BF16)],
    )
    acts = [acts[0]] + [swap(acts[rel], "ctx", rel) for rel in order[1:]]
    pooled = call(
        functools.partial(pool_kernel, pool, tok_rows),
        (pairs, sums, w_conv_v, cot_v),
        [pltpu.VMEM((wide + tok_rows + 8, channels), BF16)],
    )[0]
    rows = [pooled]
    bit = n_ctx // 2
    while bit:
        rows = rows + [swap(value, "ctx", bit) for value in rows]
        bit //= 2

    act = call(
        functools.partial(pack_kernel, order, tok_rows),
        acts,
        [pltpu.VMEM((kernel * width, tokens), BF16)],
        [
            pltpu.VMEM((tokens, kernel * width), BF16),
            pltpu.VMEM((n_ctx + 2, 8, kernel * width), F32),
        ],
    )[0]

    act_z = swap(act, "dp", Z_BIT)
    act_x = swap(act, "dp", X_BIT)

    g_all, *gts = call(
        functools.partial(attention_kernel, pool, order, tok_rows, near_rels, late),
        [*rows, w_query, w_key] + outside(w_value, w_out),
        [pltpu.VMEM((tokens, channels), BF16)]
        + [pltpu.VMEM((len(late) * narrow, tokens), BF16)] * len(near_rels),
        [pltpu.VMEM((tokens, channels), BF16)] * 9
        + [
            pltpu.VMEM((HEADS, tokens, tokens), F32),
            pltpu.VMEM((n_dp, narrow, tokens), BF16),
            pltpu.VMEM((n_ctx + 2, 8, channels), F32),
            pltpu.VMEM(w_value.shape, BF16),
            pltpu.VMEM(w_out.shape, BF16),
            pltpu.SemaphoreType.DMA((2,)),
        ],
        in_specs=[WHOLE] * (n_ctx + 2) + [hbm] * 2,
    )

    act_zx = swap(act_z, "dp", X_BIT)
    swapped = [gts[0]]
    for at, rel in enumerate(near_rels[1:], 1):
        swapped.append(swap(gts[at], "dp", rel))

    padded = -(-(tok_rows + 2) // 8) * 8
    highs, lows, near_g = call(
        functools.partial(spread_kernel, kernel, tok_rows, befores, afters),
        (g_all, w_conv_v),
        [pltpu.VMEM((kernel * padded, channels), BF16)] * 2
        + [pltpu.VMEM((padded, channels), BF16)],
    )
    factor = 1.0 / (n_dp * length * n_ctx) ** 0.5
    kept = len(late) // 2
    mine, theirs = call(
        functools.partial(kernel_grad_kernel, factor),
        (act, act_x, act_z, act_zx, *swapped),
        [
            pltpu.VMEM((kept * narrow, kernel * width), F32),
            pltpu.VMEM((kept * narrow, kernel * width), BF16),
        ],
    )
    other = swap(theirs, "dp", late[kept])
    while kept > 1:
        kept //= 2
        mine, theirs = call(
            fold_kernel,
            (mine, other),
            [
                pltpu.VMEM((kept * narrow, kernel * width), F32),
                pltpu.VMEM((kept * narrow, kernel * width), BF16),
            ],
        )
        other = swap(theirs, "dp", late[kept])

    by_rows = pl.BlockSpec((block, channels), lambda i: (i, 0))
    grad_in = call(
        functools.partial(input_grad_kernel, kernel, pool),
        (highs, lows, near_g, tanh_val, normed, inv_rms, gain_v),
        [jax.ShapeDtypeStruct((length, channels), BF16)],
        grid=(length // block,),
        out_specs=[by_rows],
    )[0]
    grad_conv = call(
        functools.partial(join_kernel, kernel),
        (mine, other),
        [jax.ShapeDtypeStruct((kernel, width, narrow), F32)],
    )[0]
    return grad_in[None], jnp.transpose(grad_conv, (1, 0, 2))


def solution(mesh):
    in_specs = (
        P("dp", "ctx", None),
        P("dp", "ctx"),
        P(),
        P(),
        P(),
        P(),
        P(),
        P(),
        P(),
        P("dp", "ctx", None),
    )
    out_specs = (P("dp", "ctx", None), P("ctx", None, "dp"))
    return jax.shard_map(
        per_device, mesh=mesh, in_specs=in_specs, out_specs=out_specs, check_vma=False
    )
```

time: 55.9 us -> 52.3 us (0.936)
  starting transfers between devices: 21.2 us -> 17.5 us
  waiting for transfers between devices: 15.4 us -> 16.6 us
  Pallas kernels: 18.4 us -> 17.3 us
    ppermute x14 -> x13, starting transfers between devices: 20.5 us -> 17.5 us  [swap(): return lax.ppermute(value, axis, [(i, i ^ bit) for i in range(count)])]
    ppermute x14 -> x13, waiting for transfers between devices: 15.4 us -> 16.6 us  [swap(): return lax.ppermute(value, axis, [(i, i ^ bit) for i in range(count)])]
    pallas_call x10 -> x9, Pallas kernels: 18.4 us -> 17.3 us  [call(): pl.pallas_call(body, out_shape=list(outs), scratch_shapes=list(scratch),...]
    ppermute x1 -> x0, starting transfers between devices: 0.65 us -> none  [per_device(): far = lax.ppermute(far, 'ctx', links + [(b, a) for a, b in links])]
  transfers between devices with their start and end apart: 15 -> 13, of which waited for: 7 -> 7; matrix products, arithmetic and copies ran while one was open for 0% -> 0% of each run, Pallas kernels for 28% -> 22%
where the time goes in v3:
time: 52.3 us; the launch traced here: 52.2 us
  starting transfers between devices  17.5 us (33%)
  Pallas kernels  17.3 us (33%)
  waiting for transfers between devices  16.6 us (32%)
  between operations  0.7 us (1%)
    ppermute x13, starting transfers between devices, swap(): return lax.ppermute(value, axis, [(i, i ^ bit) for i in range(count)])  17.5 us
    pallas_call x9, Pallas kernels, call(): pl.pallas_call(body, out_shape=list(outs), scratch_shapes=list(scratch),...  17.3 us
    ppermute x13, waiting for transfers between devices, swap(): return lax.ppermute(value, axis, [(i, i ^ bit) for i in range(count)])  16.6 us
  transfers between devices with their start and end apart: 13, of which 7 were waited for; matrix products, arithmetic and copies ran while one was open for 0% of the time, Pallas kernels for 22%

profile of v3, /device:TPU:0, one launch (start us, length us, event | category | flops | bytes accessed | tf_op | source)
XLA Modules:
  0.0 52.2 jit_solution(6912146851786037277)
XLA Ops:
  0.6 4.0 %shard_map.113 = (f32[200,768]{1,0:T(8,128)S(1)}, f32[40,768]{1,0:T(8,128)S(1)}, f32[512,768]{1,0:T(8,128)S(1)}, f32[512,768]{1,0:T(8,128)S(1)}, f32[512,128]{1,...) custom-call(bf16[512,768]{1,0:T(8,128)(2,1)} %bitcast.4, ...), custom_call_target="tpu_custom_call" | custom-call | tf_op jit(solution)/shard_map/pallas_call | solution.py:344
  4.7 0.2 shard_map.114
  4.9 3.1 %collective-permute-start.3 = (bf16[40,960]{1,0:T(8,128)(2,1)S(1)}, bf16[40,960]{1,0:T(8,128)(2,1)S(1)}, u32[]{:S(2)}, u32[]{:S(2)}) collective-permute-start(bf16[40,960]{1,0:T(8,128)(2,1)S(1)} %get-tuple-element.39), channel_id=1, source_target_pairs={{0,2},{1,3},{2,0},{3,1},{4,6},{5,7},{6,4},{7,5},{8,10},{9,11},{10,... | collective-permute-start | bytes 230408 | tf_op jit(solution)/shard_map/ppermute | solution.py:335
  7.9 0.0 collective-permute-start.4
  7.9 0.2 collective-permute-start.5
  8.1 2.5 %collective-permute-done.3.refs_1_ = bf16[40,960]{1,0:T(8,128)(2,1)S(1)} collective-permute-done((bf16[40,960]{1,0:T(8,128)(2,1)S(1)}, bf16[40,960]{1,0:T(8,128)(2,1)S(1)}, u32[]{:S(2)}, u32[]{:S(2)}) %collective-permute-start.3) | collective-permute-done | bytes 76832 | tf_op jit(solution)/shard_map/ppermute | solution.py:335
  10.6 0.0 collective-permute-done.4.refs_2_
  10.6 1.4 %collective-permute-done.5.refs_3_ = bf16[40,960]{1,0:T(8,128)(2,1)S(1)} collective-permute-done((bf16[40,960]{1,0:T(8,128)(2,1)S(1)}, bf16[40,960]{1,0:T(8,128)(2,1)S(1)}, u32[]{:S(2)}, u32[]{:S(2)}) %collective-permute-start.5) | collective-permute-done | bytes 76832 | tf_op jit(solution)/shard_map/ppermute | solution.py:335
  12.0 0.3 shard_map.119.refs_0_
  12.3 2.7 %collective-permute-start.7 = (bf16[960,128]{1,0:T(8,128)(2,1)S(1)}, bf16[960,128]{1,0:T(8,128)(2,1)S(1)}, u32[]{:S(2)}, u32[]{:S(2)}) collective-permute-start(bf16[960,128]{1,0:T(8,128)(2,1)S(1)} %shard_map.119.refs_0_), channel_id=1, source_target_pairs={{0,16},{4,20},{8,24},{12,28},{16,0},{20,4},{24,8},{28,12},{1,17},{... | collective-permute-start | bytes 737288 | tf_op jit(solution)/shard_map/ppermute | solution.py:335
  14.9 0.0 copy-start
  14.9 0.0 copy-start.1
  14.9 1.2 %shard_map.115.refs_0_ = bf16[80,768]{1,0:T(8,128)(2,1)S(1)} custom-call(bf16[5,80,768]{2,1,0:T(8,128)(2,1)S(1)} %get-tuple-element.26.pairs, f32[40,768]{1,0:T(8,128)S(1)} %get-tuple-element.27.sums, bf16[5,768,768]{2,1,0:T(8,128)(2,1)S(1)} %get-tuple-element.28.weights, bf16[32,768]{1,0:T(8,128)(2,1)S(1)} %get-tuple-element.29.cot), custom_call_target="tpu_custom_call" | custom-call | tf_op jit(solution)/shard_map/pallas_call | solution.py:344
  16.1 1.3 %collective-permute-start = (bf16[80,768]{1,0:T(8,128)(2,1)S(1)}, bf16[80,768]{1,0:T(8,128)(2,1)S(1)}, u32[]{:S(2)}, u32[]{:S(2)}) collective-permute-start(bf16[80,768]{1,0:T(8,128)(2,1)S(1)} %shard_map.115.refs_0_), channel_id=1, source_target_pairs={{0,2},{1,3},{2,0},{3,1},{4,6},{5,7},{6,4},{7,5},{8,10},{9,11},{10,... | collective-permute-start | bytes 368648 | tf_op jit(solution)/shard_map/ppermute | solution.py:335
  17.4 1.5 %collective-permute-start.6 = (bf16[960,128]{1,0:T(8,128)(2,1)S(1)}, bf16[960,128]{1,0:T(8,128)(2,1)S(1)}, u32[]{:S(2)}, u32[]{:S(2)}) collective-permute-start(bf16[960,128]{1,0:T(8,128)(2,1)S(1)} %shard_map.119.refs_0_), channel_id=1, source_target_pairs={{0,4},{4,0},{8,12},{12,8},{16,20},{20,16},{24,28},{28,24},{1,5},{5... | collective-permute-start | bytes 737288 | tf_op jit(solution)/shard_map/ppermute | solution.py:335
  18.9 8.0 %collective-permute-done.7.refs_2_ = bf16[960,128]{1,0:T(8,128)(2,1)S(1)} collective-permute-done((bf16[960,128]{1,0:T(8,128)(2,1)S(1)}, bf16[960,128]{1,0:T(8,128)(2,1)S(1)}, u32[]{:S(2)}, u32[]{:S(2)}) %collective-permute-start.7) | collective-permute-done | bytes 245792 | tf_op jit(solution)/shard_map/ppermute | solution.py:335
  26.9 1.5 %collective-permute-start.8 = (bf16[960,128]{1,0:T(8,128)(2,1)S(1)}, bf16[960,128]{1,0:T(8,128)(2,1)S(1)}, u32[]{:S(2)}, u32[]{:S(2)}) collective-permute-start(bf16[960,128]{1,0:T(8,128)(2,1)S(1)} %collective-permute-done.7.refs_2_), channel_id=1, source_target_pairs={{0,4},{4,0},{8,12},{12,8},{16,20},{20,16},{24,28},{28,24},{1,5},{5... | collective-permute-start | bytes 737288 | tf_op jit(solution)/shard_map/ppermute | solution.py:335
  28.4 0.0 collective-permute-start.1
  28.4 0.0 collective-permute-done.refs_1_
  28.4 0.5 collective-permute-start.2
  28.9 0.8 %collective-permute-done.1.refs_2_ = bf16[80,768]{1,0:T(8,128)(2,1)S(1)} collective-permute-done((bf16[80,768]{1,0:T(8,128)(2,1)S(1)}, bf16[80,768]{1,0:T(8,128)(2,1)S(1)}, u32[]{:S(2)}, u32[]{:S(2)}) %collective-permute-start.1) | collective-permute-done | bytes 122912 | tf_op jit(solution)/shard_map/ppermute | solution.py:335
  29.7 0.2 collective-permute-done.2.refs_3_
  29.9 0.0 copy-done
  29.9 0.0 copy-done.1
  29.9 5.5 %shard_map.116 = (bf16[128,768]{1,0:T(8,128)(2,1)S(1)}, bf16[192,128]{1,0:T(8,128)(2,1)S(1)}, bf16[192,128]{1,0:T(8,128)(2,1)S(1)}, bf16[192,128]{1,0:T(8,128)(2,1)S(1)}, bf16[192,128]{1,0:T(8,128)(2,1)S(1)}) custom-call(bf16[80,768]{1,0:T(8,128)(2,1)S(1)} %shard_map.115.refs_0_, bf16[80,768]{1,0:T(8,128)(2,1)S(1)} %collective-permute-done.refs_1_, ...), custom_call_target="tpu_custom_call" | custom-call | tf_op jit(solution)/shard_map/pallas_call | solution.py:344
  35.4 0.6 %collective-permute-start.9 = (bf16[192,128]{1,0:T(8,128)(2,1)S(1)}, bf16[192,128]{1,0:T(8,128)(2,1)S(1)}, u32[]{:S(2)}, u32[]{:S(2)}) collective-permute-start(bf16[192,128]{1,0:T(8,128)(2,1)S(1)} %get-tuple-element.43), channel_id=1, source_target_pairs={{0,4},{4,0},{8,12},{12,8},{16,20},{20,16},{24,28},{28,24},{1,5},{5... | collective-permute-start | bytes 147464 | tf_op jit(solution)/shard_map/ppermute | solution.py:335
  36.0 0.0 collective-permute-start.10
  36.0 3.9 %collective-permute-start.11 = (bf16[192,128]{1,0:T(8,128)(2,1)S(1)}, bf16[192,128]{1,0:T(8,128)(2,1)S(1)}, u32[]{:S(2)}, u32[]{:S(2)}) collective-permute-start(bf16[192,128]{1,0:T(8,128)(2,1)S(1)} %get-tuple-element.45), channel_id=1, source_target_pairs={{0,20},{4,16},{8,28},{12,24},{16,4},{20,0},{24,12},{28,8},{1,21},{... | collective-permute-start | bytes 147464 | tf_op jit(solution)/shard_map/ppermute | solution.py:335
  39.9 0.0 collective-permute-done.9.refs_5_
  39.9 2.6 %collective-permute-done.10.refs_6_ = bf16[192,128]{1,0:T(8,128)(2,1)S(1)} collective-permute-done((bf16[192,128]{1,0:T(8,128)(2,1)S(1)}, bf16[192,128]{1,0:T(8,128)(2,1)S(1)}, u32[]{:S(2)}, u32[]{:S(2)}) %collective-permute-start.10) | collective-permute-done | bytes 49184 | tf_op jit(solution)/shard_map/ppermute | solution.py:335
  42.5 1.1 %collective-permute-done.11.refs_7_ = bf16[192,128]{1,0:T(8,128)(2,1)S(1)} collective-permute-done((bf16[192,128]{1,0:T(8,128)(2,1)S(1)}, bf16[192,128]{1,0:T(8,128)(2,1)S(1)}, u32[]{:S(2)}, u32[]{:S(2)}) %collective-permute-start.11) | collective-permute-done | bytes 49184 | tf_op jit(solution)/shard_map/ppermute | solution.py:335
  43.7 0.0 collective-permute-done.6.refs_1_
  43.7 0.0 collective-permute-done.8.refs_3_
  43.7 0.6 %shard_map.120 = (f32[96,960]{1,0:T(8,128)S(1)}, bf16[96,960]{1,0:T(8,128)(2,1)S(1)}) custom-call(bf16[960,128]{1,0:T(8,128)(2,1)S(1)} %shard_map.119.refs_0_, bf16[960,128]{1,0:T(8,128)(2,1)S(1)} %collective-permute-done.6.refs_1_, bf16[960,128]{1,0:T(8,128)(2,1)S(1)} %collective-permute-done.7.refs_2_, ...), custom_call_target="tpu_custom_call" | custom-call | tf_op jit(solution)/shard_map/pallas_call | solution.py:344
  44.2 2.4 %collective-permute-start.12 = (bf16[96,960]{1,0:T(8,128)(2,1)S(1)}, bf16[96,960]{1,0:T(8,128)(2,1)S(1)}, u32[]{:S(2)}, u32[]{:S(2)}) collective-permute-start(bf16[96,960]{1,0:T(8,128)(2,1)S(1)} %get-tuple-element.47), channel_id=1, source_target_pairs={{0,8},{4,12},{8,0},{12,4},{16,24},{20,28},{24,16},{28,20},{1,9},{5... | collective-permute-start | bytes 552968 | tf_op jit(solution)/shard_map/ppermute | solution.py:335
  46.6 1.8 %shard_map.117 = (bf16[200,768]{1,0:T(8,128)(2,1)S(1)}, bf16[200,768]{1,0:T(8,128)(2,1)S(1)}, bf16[40,768]{1,0:T(8,128)(2,1)S(1)}) custom-call(bf16[128,768]{1,0:T(8,128)(2,1)S(1)} %get-tuple-element.30.g_ref, bf16[5,768,768]{2,1,0:T(8,128)(2,1)S(1)} %get-tuple-element.28.weights), custom_call_target="tpu_custom_call" | custom-call | tf_op jit(solution)/shard_map/pallas_call | solution.py:344
  48.4 2.8 %shard_map.118 = bf16[512,768]{1,0:T(8,128)(2,1)} custom-call(bf16[200,768]{1,0:T(8,128)(2,1)S(1)} %get-tuple-element.31.highs, bf16[200,768]{1,0:T(8,128)(2,1)S(1)} %get-tuple-element.32.lows, bf16[40,768]{1,0:T(8,128)(2,1)S(1)} %get-tuple-element.33.near, f32[512,768]{1,0:T(8,128)S(1)} %get-tuple-element.34.tanh_ref, ...), custom_call_target="tpu_custom_call" | custom-call | tf_op jit(solution)/shard_map/pallas_call | solution.py:344
  51.2 0.0 collective-permute-done.12.other
  51.2 1.0 %shard_map.121 = f32[5,192,96]{2,1,0:T(8,128)} custom-call(f32[96,960]{1,0:T(8,128)S(1)} %get-tuple-element.46.mine, bf16[96,960]{1,0:T(8,128)(2,1)S(1)} %collective-permute-done.12.other), custom_call_target="tpu_custom_call" | custom-call | tf_op jit(solution)/shard_map/pallas_call | solution.py:344
Async XLA Ops:
  4.9 5.7 %collective-permute-start.3 = (bf16[40,960]{1,0:T(8,128)(2,1)S(1)}, bf16[40,960]{1,0:T(8,128)(2,1)S(1)}, u32[]{:S(2)}, u32[]{:S(2)}) collective-permute-start(bf16[40,960]{1,0:T(8,128)(2,1)S(1)} %get-tuple-element.39), channel_id=1, source_target_pairs={{0,2},{1,3},{2,0},{3,1},{4,6},{5,7},{6,4},{7,5},{8,10},{9,11},{10,... | collective-permute-start | bytes 230408 | tf_op jit(solution)/shard_map/ppermute | solution.py:335
  7.9 2.7 %collective-permute-start.4 = (bf16[40,960]{1,0:T(8,128)(2,1)S(1)}, bf16[40,960]{1,0:T(8,128)(2,1)S(1)}, u32[]{:S(2)}, u32[]{:S(2)}) collective-permute-start(bf16[40,960]{1,0:T(8,128)(2,1)S(1)} %get-tuple-element.40), channel_id=1, source_target_pairs={{0,1},{1,0},{2,3},{3,2},{4,5},{5,4},{6,7},{7,6},{8,9},{9,8},{10,11... | collective-permute-start | bytes 230408 | tf_op jit(solution)/shard_map/ppermute | solution.py:335
  7.9 4.1 %collective-permute-start.5 = (bf16[40,960]{1,0:T(8,128)(2,1)S(1)}, bf16[40,960]{1,0:T(8,128)(2,1)S(1)}, u32[]{:S(2)}, u32[]{:S(2)}) collective-permute-start(bf16[40,960]{1,0:T(8,128)(2,1)S(1)} %get-tuple-element.41), channel_id=1, source_target_pairs={{0,3},{1,2},{2,1},{3,0},{4,7},{5,6},{6,5},{7,4},{8,11},{9,10},{10,... | collective-permute-start | bytes 230408 | tf_op jit(solution)/shard_map/ppermute | solution.py:335
  12.3 14.6 %collective-permute-start.7 = (bf16[960,128]{1,0:T(8,128)(2,1)S(1)}, bf16[960,128]{1,0:T(8,128)(2,1)S(1)}, u32[]{:S(2)}, u32[]{:S(2)}) collective-permute-start(bf16[960,128]{1,0:T(8,128)(2,1)S(1)} %shard_map.119.refs_0_), channel_id=1, source_target_pairs={{0,16},{4,20},{8,24},{12,28},{16,0},{20,4},{24,8},{28,12},{1,17},{... | collective-permute-start | bytes 737288 | tf_op jit(solution)/shard_map/ppermute | solution.py:335
  14.9 15.0 %copy-start = (bf16[768,768]{1,0:T(8,128)(2,1)S(1)}, bf16[768,768]{1,0:T(8,128)(2,1)}, u32[]{:S(2)}) copy-start(bf16[768,768]{1,0:T(8,128)(2,1)} %refs_4_.1) | copy-start | bytes 3538948
  14.9 15.0 %copy-start.1 = (bf16[768,768]{1,0:T(8,128)(2,1)S(1)}, bf16[768,768]{1,0:T(8,128)(2,1)}, u32[]{:S(2)}) copy-start(bf16[768,768]{1,0:T(8,128)(2,1)} %refs_5_.1) | copy-start | bytes 3538948
  16.1 12.3 %collective-permute-start = (bf16[80,768]{1,0:T(8,128)(2,1)S(1)}, bf16[80,768]{1,0:T(8,128)(2,1)S(1)}, u32[]{:S(2)}, u32[]{:S(2)}) collective-permute-start(bf16[80,768]{1,0:T(8,128)(2,1)S(1)} %shard_map.115.refs_0_), channel_id=1, source_target_pairs={{0,2},{1,3},{2,0},{3,1},{4,6},{5,7},{6,4},{7,5},{8,10},{9,11},{10,... | collective-permute-start | bytes 368648 | tf_op jit(solution)/shard_map/ppermute | solution.py:335
  17.4 26.3 %collective-permute-start.6 = (bf16[960,128]{1,0:T(8,128)(2,1)S(1)}, bf16[960,128]{1,0:T(8,128)(2,1)S(1)}, u32[]{:S(2)}, u32[]{:S(2)}) collective-permute-start(bf16[960,128]{1,0:T(8,128)(2,1)S(1)} %shard_map.119.refs_0_), channel_id=1, source_target_pairs={{0,4},{4,0},{8,12},{12,8},{16,20},{20,16},{24,28},{28,24},{1,5},{5... | collective-permute-start | bytes 737288 | tf_op jit(solution)/shard_map/ppermute | solution.py:335
  26.9 16.8 %collective-permute-start.8 = (bf16[960,128]{1,0:T(8,128)(2,1)S(1)}, bf16[960,128]{1,0:T(8,128)(2,1)S(1)}, u32[]{:S(2)}, u32[]{:S(2)}) collective-permute-start(bf16[960,128]{1,0:T(8,128)(2,1)S(1)} %collective-permute-done.7.refs_2_), channel_id=1, source_target_pairs={{0,4},{4,0},{8,12},{12,8},{16,20},{20,16},{24,28},{28,24},{1,5},{5... | collective-permute-start | bytes 737288 | tf_op jit(solution)/shard_map/ppermute | solution.py:335
  28.4 1.3 %collective-permute-start.1 = (bf16[80,768]{1,0:T(8,128)(2,1)S(1)}, bf16[80,768]{1,0:T(8,128)(2,1)S(1)}, u32[]{:S(2)}, u32[]{:S(2)}) collective-permute-start(bf16[80,768]{1,0:T(8,128)(2,1)S(1)} %shard_map.115.refs_0_), channel_id=1, source_target_pairs={{0,1},{1,0},{2,3},{3,2},{4,5},{5,4},{6,7},{7,6},{8,9},{9,8},{10,11... | collective-permute-start | bytes 368648 | tf_op jit(solution)/shard_map/ppermute | solution.py:335
  28.4 1.5 %collective-permute-start.2 = (bf16[80,768]{1,0:T(8,128)(2,1)S(1)}, bf16[80,768]{1,0:T(8,128)(2,1)S(1)}, u32[]{:S(2)}, u32[]{:S(2)}) collective-permute-start(bf16[80,768]{1,0:T(8,128)(2,1)S(1)} %collective-permute-done.refs_1_), channel_id=1, source_target_pairs={{0,1},{1,0},{2,3},{3,2},{4,5},{5,4},{6,7},{7,6},{8,9},{9,8},{10,11... | collective-permute-start | bytes 368648 | tf_op jit(solution)/shard_map/ppermute | solution.py:335
  35.4 4.5 %collective-permute-start.9 = (bf16[192,128]{1,0:T(8,128)(2,1)S(1)}, bf16[192,128]{1,0:T(8,128)(2,1)S(1)}, u32[]{:S(2)}, u32[]{:S(2)}) collective-permute-start(bf16[192,128]{1,0:T(8,128)(2,1)S(1)} %get-tuple-element.43), channel_id=1, source_target_pairs={{0,4},{4,0},{8,12},{12,8},{16,20},{20,16},{24,28},{28,24},{1,5},{5... | collective-permute-start | bytes 147464 | tf_op jit(solution)/shard_map/ppermute | solution.py:335
  36.0 6.5 %collective-permute-start.10 = (bf16[192,128]{1,0:T(8,128)(2,1)S(1)}, bf16[192,128]{1,0:T(8,128)(2,1)S(1)}, u32[]{:S(2)}, u32[]{:S(2)}) collective-permute-start(bf16[192,128]{1,0:T(8,128)(2,1)S(1)} %get-tuple-element.44), channel_id=1, source_target_pairs={{0,16},{4,20},{8,24},{12,28},{16,0},{20,4},{24,8},{28,12},{1,17},{... | collective-permute-start | bytes 147464 | tf_op jit(solution)/shard_map/ppermute | solution.py:335
  36.0 7.6 %collective-permute-start.11 = (bf16[192,128]{1,0:T(8,128)(2,1)S(1)}, bf16[192,128]{1,0:T(8,128)(2,1)S(1)}, u32[]{:S(2)}, u32[]{:S(2)}) collective-permute-start(bf16[192,128]{1,0:T(8,128)(2,1)S(1)} %get-tuple-element.45), channel_id=1, source_target_pairs={{0,20},{4,16},{8,28},{12,24},{16,4},{20,0},{24,12},{28,8},{1,21},{... | collective-permute-start | bytes 147464 | tf_op jit(solution)/shard_map/ppermute | solution.py:335
  44.2 6.9 %collective-permute-start.12 = (bf16[96,960]{1,0:T(8,128)(2,1)S(1)}, bf16[96,960]{1,0:T(8,128)(2,1)S(1)}, u32[]{:S(2)}, u32[]{:S(2)}) collective-permute-start(bf16[96,960]{1,0:T(8,128)(2,1)S(1)} %get-tuple-element.47), channel_id=1, source_target_pairs={{0,8},{4,12},{8,0},{12,4},{16,24},{20,28},{24,16},{28,20},{1,9},{5... | collective-permute-start | bytes 552968 | tf_op jit(solution)/shard_map/ppermute | solution.py:335

commit v4 on v3

--- a/solution.py
+++ b/solution.py
@@ -67,45 +67,35 @@
 
 def act_kernel(
     kernel, pool, tok_rows, feat_hbm, base_hbm, table_hbm, gain_hbm, cot_hbm, w_hbm,
-    taps, sums, tanh_out, normed_out, inv_out, gain, cot, weights,
-    feat, base, table, act_buf, high_buf, low_buf, sems,
+    taps, sums, normed_out, inv_out, gain, cot, weights, feat, base, table, act_buf, sems,
 ):
     half = kernel // 2
-    rows, channels = feat.shape
-    block = act_buf.shape[0]
-    count = rows // block
+    _, channels = feat.shape
+    count, block = act_buf.shape[:2]
     small = ((base_hbm, base), (table_hbm, table), (gain_hbm, gain))
     parts = tuple(
         (feat_hbm.at[pl.ds(i * block, block)], feat.at[pl.ds(i * block, block)]) for i in range(count)
     )
     copies = start_copies(small + parts + ((cot_hbm, cot), (w_hbm, weights)), sems)
     padded = taps.shape[0] // kernel
-    taps[...] = jnp.zeros_like(taps)
-    sums[...] = jnp.zeros_like(sums)
     for copy in copies[: len(small)]:
         copy.wait()
     gain_f = gain[...].reshape(1, channels).astype(F32)
     chunk = 32
-
-    @pl.loop(0, count)
-    def _(step):
-        start = pl.multiple_of(step * block, block)
-        here = pl.ds(start, block)
-        pltpu.make_async_copy(feat_hbm.at[here], feat.at[here], sems.at[len(small) + step]).wait()
+    for step in range(count):
+        start = step * block
+        here = slice(start, start + block)
+        copies[len(small) + step].wait()
         onehot = (iota((table.shape[0], block), 0) == base[:, here]).astype(BF16)
         embed = dot_tn(onehot, table[...])
         for begin in range(0, block, chunk):
             part = slice(begin, begin + chunk)
-            here = pl.ds(start + begin, chunk)
-            summed = feat[here, :].astype(F32) + embed[part, :]
+            some = slice(start + begin, start + begin + chunk)
+            summed = feat[some, :].astype(F32) + embed[part, :]
             inv_rms, normed = normed_of(summed)
-            u = normed * gain_f
-            tanh_val, value = gelu_of(u)
-            act_buf[part, :] = value.astype(BF16)
-            high_buf[part, :], low_buf[part, :] = split2(summed)
-            tanh_out[here, :] = tanh_val
-            normed_out[here, :] = normed
-            inv_out[here, :] = jnp.broadcast_to(inv_rms, (chunk, inv_out.shape[1]))
+            act_buf[step, part, :] = gelu_of(normed * gain_f)[1].astype(BF16)
+            normed_out[some, :] = normed
+            inv_out[some, :] = jnp.broadcast_to(inv_rms, (chunk, inv_out.shape[1]))
         shape = (kernel * padded, block)
         row = iota(shape, 0)
         tap = sum((row >= padded * j).astype(jnp.int32) for j in range(1, kernel))
@@ -114,9 +104,12 @@
         known = row - tap * padded < tok_rows + 2
         offset = iota(shape, 1) + start - tap + half - token * pool
         spread = ((offset >= 0) & (offset < pool) & known).astype(BF16)
-        taps[...] += dot_nn(spread, act_buf[...])
+        term = dot_nn(spread, act_buf[step])
+        taps[...] = term if step == 0 else taps[...] + term
         plain = spread[half * padded : (half + 1) * padded, :]
-        sums[...] += dot_nn(plain, high_buf[...]) + dot_nn(plain, low_buf[...])
+        counts = dot_nt(plain, onehot).astype(BF16)
+        term = dot_nn(plain, feat[here, :]) + dot_nn(counts, table[...])
+        sums[...] = term if step == 0 else sums[...] + term
 
     for copy in copies[len(small) + count :]:
         copy.wait()
@@ -268,7 +261,7 @@
 
 
 def input_grad_kernel(
-    kernel, pool, highs, lows, near, tanh_ref, normed_ref, inv_ref, gain, out
+    kernel, pool, highs, lows, near, normed_ref, inv_ref, gain, out
 ):
     half = kernel // 2
     rows, channels = out.shape
@@ -285,8 +278,9 @@
     plain = spread[:, half * padded : (half + 1) * padded]
     grad_rows = dot_nn(plain, near[...])
     gain_f = gain[...].reshape(1, channels).astype(F32)
-    tanh_val, unit = tanh_ref[here, :], normed_ref[here, :]
+    unit = normed_ref[here, :]
     u = unit * gain_f
+    tanh_val = gelu_of(u)[0]
     slopes = 0.5 * (1.0 + tanh_val) + 0.5 * u * (1.0 - tanh_val * tanh_val) * GELU_SCALE * (
         1.0 + 3.0 * CUBIC * (u * u)
     )
@@ -295,15 +289,23 @@
     out[...] = (grad_rows + inv_ref[here, :1] * (grad_norm - unit * mean)).astype(BF16)
 
 
-def kernel_grad_kernel(factor, *refs):
+def cut_kernel(value, *outs):
+    at = 0
+    for out in outs:
+        out[...] = value[at : at + out.shape[0], :]
+        at += out.shape[0]
+
+
+def kernel_grad_kernel(factor, begin, *refs):
     count = len(refs) // 2 - 1
     acts, gts, (mine, theirs) = refs[:count], refs[count : 2 * count], refs[2 * count :]
+    span, size = mine.shape
     total = None
     for act, gt in zip(acts, gts):
-        term = dot_nt(gt[...], act[...])
+        at = begin if act.shape[0] > size else 0
+        term = dot_nt(gt[...], act[at : at + size, :])
         total = term if total is None else total + term
     total = total * factor
-    span = mine.shape[0]
     mine[...] = total[:span, :]
     theirs[...] = total[span:, :].astype(BF16)
 
@@ -314,9 +316,12 @@
     sent[...] = (mine[span:, :] + other[span:, :].astype(F32)).astype(BF16)
 
 
-def join_kernel(kernel, mine, other, out):
+def join_kernel(kernel, *refs):
+    *parts, out = refs
     width = out.shape[1]
-    total = jnp.transpose(mine[...] + other[...].astype(F32))
+    half = len(parts) // 2
+    sums = [a[...] + b[...].astype(F32) for a, b in zip(parts[:half], parts[half:])]
+    total = jnp.transpose(jnp.concatenate(sums, axis=1))
     for j in range(kernel):
         out[j] = total[j * width : (j + 1) * width, :]
 
@@ -388,13 +393,12 @@
     hbm = pl.BlockSpec(memory_space=pltpu.HBM)
     block = 128
     wide = -(-(tok_rows + 2) // 8) * 8
-    taps, sums, tanh_val, normed, inv_rms, gain_v, cot_v, w_conv_v = call(
+    taps, sums, normed, inv_rms, gain_v, cot_v, w_conv_v = call(
         functools.partial(act_kernel, kernel, pool, tok_rows),
         outside(feat, bases, dna_table, norm_gain, cot, w_conv),
         [
             pltpu.VMEM((kernel * wide, channels), F32),
             pltpu.VMEM((wide, channels), F32),
-            pltpu.VMEM((length, channels), F32),
             pltpu.VMEM((length, channels), F32),
             pltpu.VMEM((length, 128), F32),
             pltpu.VMEM(norm_gain.shape, BF16),
@@ -405,8 +409,8 @@
             pltpu.VMEM(feat.shape, BF16),
             pltpu.VMEM(bases.shape, jnp.int32),
             pltpu.VMEM(dna_table.shape, BF16),
+            pltpu.VMEM((length // block, block, channels), BF16),
         ]
-        + [pltpu.VMEM((block, channels), BF16)] * 3
         + [pltpu.SemaphoreType.DMA((5 + length // block,))],
         in_specs=[hbm] * 6,
     )
@@ -459,7 +463,13 @@
         in_specs=[WHOLE] * (n_ctx + 2) + [hbm] * 2,
     )
 
-    act_zx = swap(act_z, "dp", X_BIT)
+    depth = kernel * width
+    cuts = [0, -(-depth // 32) * 16, depth]
+    sizes = [end - begin for begin, end in zip(cuts, cuts[1:])]
+    act_zx = call(cut_kernel, (act_z,), [pltpu.VMEM((size, tokens), BF16) for size in sizes])
+    act_zx = list(act_zx)
+    for at, value in enumerate(act_zx):
+        act_zx[at] = swap(value, "dp", X_BIT)
     swapped = [gts[0]]
     for at, rel in enumerate(near_rels[1:], 1):
         swapped.append(swap(gts[at], "dp", rel))
@@ -472,39 +482,37 @@
         + [pltpu.VMEM((padded, channels), BF16)],
     )
     factor = 1.0 / (n_dp * length * n_ctx) ** 0.5
-    kept = len(late) // 2
-    mine, theirs = call(
-        functools.partial(kernel_grad_kernel, factor),
-        (act, act_x, act_z, act_zx, *swapped),
-        [
-            pltpu.VMEM((kept * narrow, kernel * width), F32),
-            pltpu.VMEM((kept * narrow, kernel * width), BF16),
-        ],
-    )
-    other = swap(theirs, "dp", late[kept])
-    while kept > 1:
-        kept //= 2
+    mines, others = [], []
+    for at, size in enumerate(sizes):
+        kept = len(late) // 2
         mine, theirs = call(
-            fold_kernel,
-            (mine, other),
-            [
-                pltpu.VMEM((kept * narrow, kernel * width), F32),
-                pltpu.VMEM((kept * narrow, kernel * width), BF16),
-            ],
+            functools.partial(kernel_grad_kernel, factor, cuts[at]),
+            (act, act_x, act_z, act_zx[at], *swapped),
+            [pltpu.VMEM((kept * narrow, size), F32), pltpu.VMEM((kept * narrow, size), BF16)],
         )
         other = swap(theirs, "dp", late[kept])
+        while kept > 1:
+            kept //= 2
+            mine, theirs = call(
+                fold_kernel,
+                (mine, other),
+                [pltpu.VMEM((kept * narrow, size), F32), pltpu.VMEM((kept * narrow, size), BF16)],
+            )
+            other = swap(theirs, "dp", late[kept])
+        mines.append(mine)
+        others.append(other)
 
     by_rows = pl.BlockSpec((block, channels), lambda i: (i, 0))
     grad_in = call(
         functools.partial(input_grad_kernel, kernel, pool),
-        (highs, lows, near_g, tanh_val, normed, inv_rms, gain_v),
+        (highs, lows, near_g, normed, inv_rms, gain_v),
         [jax.ShapeDtypeStruct((length, channels), BF16)],
         grid=(length // block,),
         out_specs=[by_rows],
     )[0]
     grad_conv = call(
         functools.partial(join_kernel, kernel),
-        (mine, other),
+        (*mines, *others),
         [jax.ShapeDtypeStruct((kernel, width, narrow), F32)],
     )[0]
     return grad_in[None], jnp.transpose(grad_conv, (1, 0, 2))

time: 52.3 us -> 53.4 us (1.021)
  waiting for transfers between devices: 16.6 us -> 19.9 us
  starting transfers between devices: 17.5 us -> 15 us
    ppermute x13 -> x15, waiting for transfers between devices: 16.6 us -> 19.9 us  [swap(): return lax.ppermute(value, axis, [(i, i ^ bit) for i in range(count)])]
    ppermute x13 -> x15, starting transfers between devices: 17.5 us -> 15 us  [swap(): return lax.ppermute(value, axis, [(i, i ^ bit) for i in range(count)])]
    pallas_call x9 -> x11, Pallas kernels: 17.3 us -> 17.6 us  [call(): pl.pallas_call(body, out_shape=list(outs), scratch_shapes=list(scratch),...]
  transfers between devices with their start and end apart: 13 -> 15, of which waited for: 7 -> 7; matrix products, arithmetic and copies ran while one was open for 0% -> 0% of each run, Pallas kernels for 22% -> 23%
where the time goes in v4:
time: 53.4 us; the launch traced here: 53.2 us
  waiting for transfers between devices  19.9 us (37%)
  Pallas kernels  17.6 us (33%)
  starting transfers between devices  15 us (28%)
  between operations  0.72 us (1%)
    ppermute x15, waiting for transfers between devices, swap(): return lax.ppermute(value, axis, [(i, i ^ bit) for i in range(count)])  19.9 us
    pallas_call x11, Pallas kernels, call(): pl.pallas_call(body, out_shape=list(outs), scratch_shapes=list(scratch),...  17.6 us
    ppermute x15, starting transfers between devices, swap(): return lax.ppermute(value, axis, [(i, i ^ bit) for i in range(count)])  15 us
  transfers between devices with their start and end apart: 15, of which 7 were waited for; matrix products, arithmetic and copies ran while one was open for 0% of the time, Pallas kernels for 23%

profile of v4, /device:TPU:0, one launch (start us, length us, event | category | flops | bytes accessed | tf_op | source)
XLA Modules:
  0.0 53.2 jit_solution(4139635706623969595)
XLA Ops:
  0.6 4.0 %shard_map.113 = (f32[200,768]{1,0:T(8,128)S(1)}, f32[40,768]{1,0:T(8,128)S(1)}, f32[512,768]{1,0:T(8,128)S(1)}, f32[512,128]{1,0:T(8,128)S(1)}, bf16[768]{0:T(1...) custom-call(bf16[512,768]{1,0:T(8,128)(2,1)} %bitcast.4, s32[1,512]{1,0:T(1,128)} %base_hbm.1, ...), custom_call_target="tpu_custom_call" | custom-call | tf_op jit(solution)/shard_map/pallas_call | solution.py:349
  4.6 0.2 shard_map.114
  4.8 3.1 %collective-permute-start.3 = (bf16[40,960]{1,0:T(8,128)(2,1)S(1)}, bf16[40,960]{1,0:T(8,128)(2,1)S(1)}, u32[]{:S(2)}, u32[]{:S(2)}) collective-permute-start(bf16[40,960]{1,0:T(8,128)(2,1)S(1)} %get-tuple-element.41), channel_id=1, source_target_pairs={{0,2},{1,3},{2,0},{3,1},{4,6},{5,7},{6,4},{7,5},{8,10},{9,11},{10,... | collective-permute-start | bytes 230408 | tf_op jit(solution)/shard_map/ppermute | solution.py:340
  7.9 0.0 collective-permute-start.4
  7.9 0.2 collective-permute-start.5
  8.1 2.5 %collective-permute-done.3.refs_1_ = bf16[40,960]{1,0:T(8,128)(2,1)S(1)} collective-permute-done((bf16[40,960]{1,0:T(8,128)(2,1)S(1)}, bf16[40,960]{1,0:T(8,128)(2,1)S(1)}, u32[]{:S(2)}, u32[]{:S(2)}) %collective-permute-start.3) | collective-permute-done | bytes 76832 | tf_op jit(solution)/shard_map/ppermute | solution.py:340
  10.5 0.0 collective-permute-done.4.refs_2_
  10.5 1.4 %collective-permute-done.5.refs_3_ = bf16[40,960]{1,0:T(8,128)(2,1)S(1)} collective-permute-done((bf16[40,960]{1,0:T(8,128)(2,1)S(1)}, bf16[40,960]{1,0:T(8,128)(2,1)S(1)}, u32[]{:S(2)}, u32[]{:S(2)}) %collective-permute-start.5) | collective-permute-done | bytes 76832 | tf_op jit(solution)/shard_map/ppermute | solution.py:340
  11.9 0.3 shard_map.119.refs_0_
  12.2 2.7 %collective-permute-start.7 = (bf16[960,128]{1,0:T(8,128)(2,1)S(1)}, bf16[960,128]{1,0:T(8,128)(2,1)S(1)}, u32[]{:S(2)}, u32[]{:S(2)}) collective-permute-start(bf16[960,128]{1,0:T(8,128)(2,1)S(1)} %shard_map.119.refs_0_), channel_id=1, source_target_pairs={{0,16},{4,20},{8,24},{12,28},{16,0},{20,4},{24,8},{28,12},{1,17},{... | collective-permute-start | bytes 737288 | tf_op jit(solution)/shard_map/ppermute | solution.py:340
  14.9 0.0 copy-start
  14.9 0.0 copy-start.1
  14.9 1.2 %shard_map.115.refs_0_ = bf16[80,768]{1,0:T(8,128)(2,1)S(1)} custom-call(bf16[5,80,768]{2,1,0:T(8,128)(2,1)S(1)} %get-tuple-element.29.pairs, f32[40,768]{1,0:T(8,128)S(1)} %get-tuple-element.30.sums, bf16[5,768,768]{2,1,0:T(8,128)(2,1)S(1)} %get-tuple-element.31.weights, bf16[32,768]{1,0:T(8,128)(2,1)S(1)} %get-tuple-element.32.cot), custom_call_target="tpu_custom_call" | custom-call | tf_op jit(solution)/shard_map/pallas_call | solution.py:349
  16.1 1.3 %collective-permute-start = (bf16[80,768]{1,0:T(8,128)(2,1)S(1)}, bf16[80,768]{1,0:T(8,128)(2,1)S(1)}, u32[]{:S(2)}, u32[]{:S(2)}) collective-permute-start(bf16[80,768]{1,0:T(8,128)(2,1)S(1)} %shard_map.115.refs_0_), channel_id=1, source_target_pairs={{0,2},{1,3},{2,0},{3,1},{4,6},{5,7},{6,4},{7,5},{8,10},{9,11},{10,... | collective-permute-start | bytes 368648 | tf_op jit(solution)/shard_map/ppermute | solution.py:340
  17.4 1.5 %collective-permute-start.6 = (bf16[960,128]{1,0:T(8,128)(2,1)S(1)}, bf16[960,128]{1,0:T(8,128)(2,1)S(1)}, u32[]{:S(2)}, u32[]{:S(2)}) collective-permute-start(bf16[960,128]{1,0:T(8,128)(2,1)S(1)} %shard_map.119.refs_0_), channel_id=1, source_target_pairs={{0,4},{4,0},{8,12},{12,8},{16,20},{20,16},{24,28},{28,24},{1,5},{5... | collective-permute-start | bytes 737288 | tf_op jit(solution)/shard_map/ppermute | solution.py:340
  18.8 0.0 collective-permute-start.1
  18.8 2.8 %collective-permute-done.refs_1_ = bf16[80,768]{1,0:T(8,128)(2,1)S(1)} collective-permute-done((bf16[80,768]{1,0:T(8,128)(2,1)S(1)}, bf16[80,768]{1,0:T(8,128)(2,1)S(1)}, u32[]{:S(2)}, u32[]{:S(2)}) %collective-permute-start) | collective-permute-done | bytes 122912 | tf_op jit(solution)/shard_map/ppermute | solution.py:340
  21.6 0.0 collective-permute-start.2
  21.6 5.2 %collective-permute-done.7.value.refs_2_ = bf16[960,128]{1,0:T(8,128)(2,1)S(1)} collective-permute-done((bf16[960,128]{1,0:T(8,128)(2,1)S(1)}, bf16[960,128]{1,0:T(8,128)(2,1)S(1)}, u32[]{:S(2)}, u32[]{:S(2)}) %collective-permute-start.7) | collective-permute-done | bytes 245792 | tf_op jit(solution)/shard_map/ppermute | solution.py:340
  26.9 1.6 %collective-permute-start.12 = (bf16[480,128]{1,0:T(8,128)(2,1)S(1)}, bf16[480,128]{1,0:T(8,128)(2,1)S(1)}, u32[]{:S(2)}, u32[]{:S(2)}) collective-permute-start(bf16[480,128]{1,0:T(8,128)(2,1)S(1)} %get-tuple-element.50), channel_id=1, source_target_pairs={{0,4},{4,0},{8,12},{12,8},{16,20},{20,16},{24,28},{28,24},{1,5},{5... | collective-permute-start | bytes 368648 | tf_op jit(solution)/shard_map/ppermute | solution.py:340
  28.4 0.5 %collective-permute-start.8 = (bf16[480,128]{1,0:T(8,128)(2,1)S(1)}, bf16[480,128]{1,0:T(8,128)(2,1)S(1)}, u32[]{:S(2)}, u32[]{:S(2)}) collective-permute-start(bf16[480,128]{1,0:T(8,128)(2,1)S(1)} %get-tuple-element.44), channel_id=1, source_target_pairs={{0,4},{4,0},{8,12},{12,8},{16,20},{20,16},{24,28},{28,24},{1,5},{5... | collective-permute-start | bytes 368648 | tf_op jit(solution)/shard_map/ppermute | solution.py:340
  29.0 0.0 collective-permute-done.1.refs_2_
  29.0 0.0 collective-permute-done.2.refs_3_
  29.0 0.0 copy-done
  29.0 0.0 copy-done.1
  29.0 5.5 %shard_map.116 = (bf16[128,768]{1,0:T(8,128)(2,1)S(1)}, bf16[192,128]{1,0:T(8,128)(2,1)S(1)}, bf16[192,128]{1,0:T(8,128)(2,1)S(1)}, bf16[192,128]{1,0:T(8,128)(2,1)S(1)}, bf16[192,128]{1,0:T(8,128)(2,1)S(1)}) custom-call(bf16[80,768]{1,0:T(8,128)(2,1)S(1)} %shard_map.115.refs_0_, bf16[80,768]{1,0:T(8,128)(2,1)S(1)} %collective-permute-done.refs_1_, ...), custom_call_target="tpu_custom_call" | custom-call | tf_op jit(solution)/shard_map/pallas_call | solution.py:349
  34.5 1.6 %collective-permute-start.9 = (bf16[192,128]{1,0:T(8,128)(2,1)S(1)}, bf16[192,128]{1,0:T(8,128)(2,1)S(1)}, u32[]{:S(2)}, u32[]{:S(2)}) collective-permute-start(bf16[192,128]{1,0:T(8,128)(2,1)S(1)} %get-tuple-element.46), channel_id=1, source_target_pairs={{0,4},{4,0},{8,12},{12,8},{16,20},{20,16},{24,28},{28,24},{1,5},{5... | collective-permute-start | bytes 147464 | tf_op jit(solution)/shard_map/ppermute | solution.py:340
  36.1 0.0 collective-permute-start.10
  36.1 2.6 %collective-permute-done.9.refs_5_ = bf16[192,128]{1,0:T(8,128)(2,1)S(1)} collective-permute-done((bf16[192,128]{1,0:T(8,128)(2,1)S(1)}, bf16[192,128]{1,0:T(8,128)(2,1)S(1)}, u32[]{:S(2)}, u32[]{:S(2)}) %collective-permute-start.9) | collective-permute-done | bytes 49184 | tf_op jit(solution)/shard_map/ppermute | solution.py:340
  38.7 0.5 collective-permute-start.11
  39.1 1.9 %collective-permute-done.10.refs_6_ = bf16[192,128]{1,0:T(8,128)(2,1)S(1)} collective-permute-done((bf16[192,128]{1,0:T(8,128)(2,1)S(1)}, bf16[192,128]{1,0:T(8,128)(2,1)S(1)}, u32[]{:S(2)}, u32[]{:S(2)}) %collective-permute-start.10) | collective-permute-done | bytes 49184 | tf_op jit(solution)/shard_map/ppermute | solution.py:340
  41.1 3.5 %collective-permute-done.11.refs_7_ = bf16[192,128]{1,0:T(8,128)(2,1)S(1)} collective-permute-done((bf16[192,128]{1,0:T(8,128)(2,1)S(1)}, bf16[192,128]{1,0:T(8,128)(2,1)S(1)}, u32[]{:S(2)}, u32[]{:S(2)}) %collective-permute-start.11) | collective-permute-done | bytes 49184 | tf_op jit(solution)/shard_map/ppermute | solution.py:340
  44.6 0.0 collective-permute-done.6.refs_1_
  44.6 0.0 collective-permute-done.12.refs_3_
  44.6 0.4 shard_map.122
  45.0 1.5 %collective-permute-start.14 = (bf16[96,480]{1,0:T(8,128)(2,1)S(1)}, bf16[96,480]{1,0:T(8,128)(2,1)S(1)}, u32[]{:S(2)}, u32[]{:S(2)}) collective-permute-start(bf16[96,480]{1,0:T(8,128)(2,1)S(1)} %get-tuple-element.53), channel_id=1, source_target_pairs={{0,8},{4,12},{8,0},{12,4},{16,24},{20,28},{24,16},{28,20},{1,9},{5... | collective-permute-start | bytes 276488 | tf_op jit(solution)/shard_map/ppermute | solution.py:340
  46.5 0.0 collective-permute-done.8.refs_3_
  46.5 0.4 shard_map.121
  46.9 0.6 %collective-permute-start.13 = (bf16[96,480]{1,0:T(8,128)(2,1)S(1)}, bf16[96,480]{1,0:T(8,128)(2,1)S(1)}, u32[]{:S(2)}, u32[]{:S(2)}) collective-permute-start(bf16[96,480]{1,0:T(8,128)(2,1)S(1)} %get-tuple-element.52), channel_id=1, source_target_pairs={{0,8},{4,12},{8,0},{12,4},{16,24},{20,28},{24,16},{28,20},{1,9},{5... | collective-permute-start | bytes 276488 | tf_op jit(solution)/shard_map/ppermute | solution.py:340
  47.5 1.8 %shard_map.117 = (bf16[200,768]{1,0:T(8,128)(2,1)S(1)}, bf16[200,768]{1,0:T(8,128)(2,1)S(1)}, bf16[40,768]{1,0:T(8,128)(2,1)S(1)}) custom-call(bf16[128,768]{1,0:T(8,128)(2,1)S(1)} %get-tuple-element.33.g_ref, bf16[5,768,768]{2,1,0:T(8,128)(2,1)S(1)} %get-tuple-element.31.weights), custom_call_target="tpu_custom_call" | custom-call | tf_op jit(solution)/shard_map/pallas_call | solution.py:349
  49.3 2.8 %shard_map.118 = bf16[512,768]{1,0:T(8,128)(2,1)} custom-call(bf16[200,768]{1,0:T(8,128)(2,1)S(1)} %get-tuple-element.34.highs, bf16[200,768]{1,0:T(8,128)(2,1)S(1)} %get-tuple-element.35.lows, bf16[40,768]{1,0:T(8,128)(2,1)S(1)} %get-tuple-element.36.near, f32[512,768]{1,0:T(8,128)S(1)} %get-tuple-element.37.normed_ref, ...), custom_call_target="tpu_custom_call" | custom-call | tf_op jit(solution)/shard_map/pallas_call | solution.py:349
  52.1 0.0 collective-permute-done.14.refs_3_
  52.1 0.0 collective-permute-done.13.refs_2_
  52.1 1.1 %shard_map.123 = f32[5,192,96]{2,1,0:T(8,128)} custom-call(f32[96,480]{1,0:T(8,128)S(1)} %get-tuple-element.49.refs_0_, f32[96,480]{1,0:T(8,128)S(1)} %get-tuple-element.51.refs_1_, bf16[96,480]{1,0:T(8,128)(2,1)S(1)} %collective-permute-done.13.refs_2_, bf16[96,480]{1,0:T(8,128)(2,1)S(1)} %collective-permute-done.14.refs_3_), custom_call_target="tpu_custom_call" | custom-call | tf_op jit(solution)/shard_map/pallas_call | solution.py:349
  (1 shorter events, 0.0 us)
Async XLA Ops:
  4.8 5.7 %collective-permute-start.3 = (bf16[40,960]{1,0:T(8,128)(2,1)S(1)}, bf16[40,960]{1,0:T(8,128)(2,1)S(1)}, u32[]{:S(2)}, u32[]{:S(2)}) collective-permute-start(bf16[40,960]{1,0:T(8,128)(2,1)S(1)} %get-tuple-element.41), channel_id=1, source_target_pairs={{0,2},{1,3},{2,0},{3,1},{4,6},{5,7},{6,4},{7,5},{8,10},{9,11},{10,... | collective-permute-start | bytes 230408 | tf_op jit(solution)/shard_map/ppermute | solution.py:340
  7.9 2.7 %collective-permute-start.4 = (bf16[40,960]{1,0:T(8,128)(2,1)S(1)}, bf16[40,960]{1,0:T(8,128)(2,1)S(1)}, u32[]{:S(2)}, u32[]{:S(2)}) collective-permute-start(bf16[40,960]{1,0:T(8,128)(2,1)S(1)} %get-tuple-element.42), channel_id=1, source_target_pairs={{0,1},{1,0},{2,3},{3,2},{4,5},{5,4},{6,7},{7,6},{8,9},{9,8},{10,11... | collective-permute-start | bytes 230408 | tf_op jit(solution)/shard_map/ppermute | solution.py:340
  7.9 4.1 %collective-permute-start.5 = (bf16[40,960]{1,0:T(8,128)(2,1)S(1)}, bf16[40,960]{1,0:T(8,128)(2,1)S(1)}, u32[]{:S(2)}, u32[]{:S(2)}) collective-permute-start(bf16[40,960]{1,0:T(8,128)(2,1)S(1)} %get-tuple-element.43), channel_id=1, source_target_pairs={{0,3},{1,2},{2,1},{3,0},{4,7},{5,6},{6,5},{7,4},{8,11},{9,10},{10,... | collective-permute-start | bytes 230408 | tf_op jit(solution)/shard_map/ppermute | solution.py:340
  12.2 14.6 %collective-permute-start.7 = (bf16[960,128]{1,0:T(8,128)(2,1)S(1)}, bf16[960,128]{1,0:T(8,128)(2,1)S(1)}, u32[]{:S(2)}, u32[]{:S(2)}) collective-permute-start(bf16[960,128]{1,0:T(8,128)(2,1)S(1)} %shard_map.119.refs_0_), channel_id=1, source_target_pairs={{0,16},{4,20},{8,24},{12,28},{16,0},{20,4},{24,8},{28,12},{1,17},{... | collective-permute-start | bytes 737288 | tf_op jit(solution)/shard_map/ppermute | solution.py:340
  14.9 14.1 %copy-start = (bf16[768,768]{1,0:T(8,128)(2,1)S(1)}, bf16[768,768]{1,0:T(8,128)(2,1)}, u32[]{:S(2)}) copy-start(bf16[768,768]{1,0:T(8,128)(2,1)} %refs_4_.1) | copy-start | bytes 3538948
  14.9 14.1 %copy-start.1 = (bf16[768,768]{1,0:T(8,128)(2,1)S(1)}, bf16[768,768]{1,0:T(8,128)(2,1)}, u32[]{:S(2)}) copy-start(bf16[768,768]{1,0:T(8,128)(2,1)} %refs_5_.1) | copy-start | bytes 3538948
  16.1 5.5 %collective-permute-start = (bf16[80,768]{1,0:T(8,128)(2,1)S(1)}, bf16[80,768]{1,0:T(8,128)(2,1)S(1)}, u32[]{:S(2)}, u32[]{:S(2)}) collective-permute-start(bf16[80,768]{1,0:T(8,128)(2,1)S(1)} %shard_map.115.refs_0_), channel_id=1, source_target_pairs={{0,2},{1,3},{2,0},{3,1},{4,6},{5,7},{6,4},{7,5},{8,10},{9,11},{10,... | collective-permute-start | bytes 368648 | tf_op jit(solution)/shard_map/ppermute | solution.py:340
  17.4 27.2 %collective-permute-start.6 = (bf16[960,128]{1,0:T(8,128)(2,1)S(1)}, bf16[960,128]{1,0:T(8,128)(2,1)S(1)}, u32[]{:S(2)}, u32[]{:S(2)}) collective-permute-start(bf16[960,128]{1,0:T(8,128)(2,1)S(1)} %shard_map.119.refs_0_), channel_id=1, source_target_pairs={{0,4},{4,0},{8,12},{12,8},{16,20},{20,16},{24,28},{28,24},{1,5},{5... | collective-permute-start | bytes 737288 | tf_op jit(solution)/shard_map/ppermute | solution.py:340
  18.8 10.1 %collective-permute-start.1 = (bf16[80,768]{1,0:T(8,128)(2,1)S(1)}, bf16[80,768]{1,0:T(8,128)(2,1)S(1)}, u32[]{:S(2)}, u32[]{:S(2)}) collective-permute-start(bf16[80,768]{1,0:T(8,128)(2,1)S(1)} %shard_map.115.refs_0_), channel_id=1, source_target_pairs={{0,1},{1,0},{2,3},{3,2},{4,5},{5,4},{6,7},{7,6},{8,9},{9,8},{10,11... | collective-permute-start | bytes 368648 | tf_op jit(solution)/shard_map/ppermute | solution.py:340
  21.6 7.4 %collective-permute-start.2 = (bf16[80,768]{1,0:T(8,128)(2,1)S(1)}, bf16[80,768]{1,0:T(8,128)(2,1)S(1)}, u32[]{:S(2)}, u32[]{:S(2)}) collective-permute-start(bf16[80,768]{1,0:T(8,128)(2,1)S(1)} %collective-permute-done.refs_1_), channel_id=1, source_target_pairs={{0,1},{1,0},{2,3},{3,2},{4,5},{5,4},{6,7},{7,6},{8,9},{9,8},{10,11... | collective-permute-start | bytes 368648 | tf_op jit(solution)/shard_map/ppermute | solution.py:340
  26.9 17.7 %collective-permute-start.12 = (bf16[480,128]{1,0:T(8,128)(2,1)S(1)}, bf16[480,128]{1,0:T(8,128)(2,1)S(1)}, u32[]{:S(2)}, u32[]{:S(2)}) collective-permute-start(bf16[480,128]{1,0:T(8,128)(2,1)S(1)} %get-tuple-element.50), channel_id=1, source_target_pairs={{0,4},{4,0},{8,12},{12,8},{16,20},{20,16},{24,28},{28,24},{1,5},{5... | collective-permute-start | bytes 368648 | tf_op jit(solution)/shard_map/ppermute | solution.py:340
  28.4 18.1 %collective-permute-start.8 = (bf16[480,128]{1,0:T(8,128)(2,1)S(1)}, bf16[480,128]{1,0:T(8,128)(2,1)S(1)}, u32[]{:S(2)}, u32[]{:S(2)}) collective-permute-start(bf16[480,128]{1,0:T(8,128)(2,1)S(1)} %get-tuple-element.44), channel_id=1, source_target_pairs={{0,4},{4,0},{8,12},{12,8},{16,20},{20,16},{24,28},{28,24},{1,5},{5... | collective-permute-start | bytes 368648 | tf_op jit(solution)/shard_map/ppermute | solution.py:340
  34.5 4.2 %collective-permute-start.9 = (bf16[192,128]{1,0:T(8,128)(2,1)S(1)}, bf16[192,128]{1,0:T(8,128)(2,1)S(1)}, u32[]{:S(2)}, u32[]{:S(2)}) collective-permute-start(bf16[192,128]{1,0:T(8,128)(2,1)S(1)} %get-tuple-element.46), channel_id=1, source_target_pairs={{0,4},{4,0},{8,12},{12,8},{16,20},{20,16},{24,28},{28,24},{1,5},{5... | collective-permute-start | bytes 147464 | tf_op jit(solution)/shard_map/ppermute | solution.py:340
  36.1 5.0 %collective-permute-start.10 = (bf16[192,128]{1,0:T(8,128)(2,1)S(1)}, bf16[192,128]{1,0:T(8,128)(2,1)S(1)}, u32[]{:S(2)}, u32[]{:S(2)}) collective-permute-start(bf16[192,128]{1,0:T(8,128)(2,1)S(1)} %get-tuple-element.47), channel_id=1, source_target_pairs={{0,16},{4,20},{8,24},{12,28},{16,0},{20,4},{24,8},{28,12},{1,17},{... | collective-permute-start | bytes 147464 | tf_op jit(solution)/shard_map/ppermute | solution.py:340
  38.7 5.9 %collective-permute-start.11 = (bf16[192,128]{1,0:T(8,128)(2,1)S(1)}, bf16[192,128]{1,0:T(8,128)(2,1)S(1)}, u32[]{:S(2)}, u32[]{:S(2)}) collective-permute-start(bf16[192,128]{1,0:T(8,128)(2,1)S(1)} %get-tuple-element.48), channel_id=1, source_target_pairs={{0,20},{4,16},{8,28},{12,24},{16,4},{20,0},{24,12},{28,8},{1,21},{... | collective-permute-start | bytes 147464 | tf_op jit(solution)/shard_map/ppermute | solution.py:340
  45.0 7.2 %collective-permute-start.14 = (bf16[96,480]{1,0:T(8,128)(2,1)S(1)}, bf16[96,480]{1,0:T(8,128)(2,1)S(1)}, u32[]{:S(2)}, u32[]{:S(2)}) collective-permute-start(bf16[96,480]{1,0:T(8,128)(2,1)S(1)} %get-tuple-element.53), channel_id=1, source_target_pairs={{0,8},{4,12},{8,0},{12,4},{16,24},{20,28},{24,16},{28,20},{1,9},{5... | collective-permute-start | bytes 276488 | tf_op jit(solution)/shard_map/ppermute | solution.py:340
  46.9 5.3 %collective-permute-start.13 = (bf16[96,480]{1,0:T(8,128)(2,1)S(1)}, bf16[96,480]{1,0:T(8,128)(2,1)S(1)}, u32[]{:S(2)}, u32[]{:S(2)}) collective-permute-start(bf16[96,480]{1,0:T(8,128)(2,1)S(1)} %get-tuple-element.52), channel_id=1, source_target_pairs={{0,8},{4,12},{8,0},{12,4},{16,24},{20,28},{24,16},{28,20},{1,9},{5... | collective-permute-start | bytes 276488 | tf_op jit(solution)/shard_map/ppermute | solution.py:340

commit v5 on v4

--- a/solution.py
+++ b/solution.py
@@ -17,6 +17,7 @@
 F32 = jnp.float32
 BF16 = jnp.bfloat16
 VMEM_LIMIT = 28 << 20
+FLOPS_PER_MICRO = 1.15e9
 X_BIT, Z_BIT = 1, 4
 
 
@@ -66,8 +67,8 @@
 
 
 def act_kernel(
-    kernel, pool, tok_rows, feat_hbm, base_hbm, table_hbm, gain_hbm, cot_hbm, w_hbm,
-    taps, sums, normed_out, inv_out, gain, cot, weights, feat, base, table, act_buf, sems,
+    kernel, pool, tok_rows, feat_hbm, base_hbm, table_hbm, gain_hbm, cot_hbm,
+    taps, sums, normed_out, inv_out, gain, cot, feat, base, table, act_buf, sems,
 ):
     half = kernel // 2
     _, channels = feat.shape
@@ -76,7 +77,7 @@
     parts = tuple(
         (feat_hbm.at[pl.ds(i * block, block)], feat.at[pl.ds(i * block, block)]) for i in range(count)
     )
-    copies = start_copies(small + parts + ((cot_hbm, cot), (w_hbm, weights)), sems)
+    copies = start_copies(small + parts + ((cot_hbm, cot),), sems)
     padded = taps.shape[0] // kernel
     for copy in copies[: len(small)]:
         copy.wait()
@@ -343,7 +344,7 @@
 WHOLE = pl.BlockSpec(memory_space=pltpu.VMEM)
 
 
-def call(body, args, outs, scratch=(), **options):
+def call(body, args, outs, scratch=(), micros=1, **options):
     options.setdefault("in_specs", [WHOLE] * len(args))
     options.setdefault("out_specs", [WHOLE] * len(outs))
     return pl.pallas_call(
@@ -351,6 +352,9 @@
         out_shape=list(outs),
         scratch_shapes=list(scratch),
         compiler_params=pltpu.CompilerParams(vmem_limit_bytes=VMEM_LIMIT),
+        cost_estimate=pl.CostEstimate(
+            flops=int(micros * FLOPS_PER_MICRO), bytes_accessed=0, transcendentals=0
+        ),
         **options,
     )(*args)
 
@@ -393,9 +397,9 @@
     hbm = pl.BlockSpec(memory_space=pltpu.HBM)
     block = 128
     wide = -(-(tok_rows + 2) // 8) * 8
-    taps, sums, normed, inv_rms, gain_v, cot_v, w_conv_v = call(
+    taps, sums, normed, inv_rms, gain_v, cot_v = call(
         functools.partial(act_kernel, kernel, pool, tok_rows),
-        outside(feat, bases, dna_table, norm_gain, cot, w_conv),
+        outside(feat, bases, dna_table, norm_gain, cot),
         [
             pltpu.VMEM((kernel * wide, channels), F32),
             pltpu.VMEM((wide, channels), F32),
@@ -403,7 +407,6 @@
             pltpu.VMEM((length, 128), F32),
             pltpu.VMEM(norm_gain.shape, BF16),
             pltpu.VMEM(cot.shape, BF16),
-            pltpu.VMEM(w_conv.shape, BF16),
         ],
         [
             pltpu.VMEM(feat.shape, BF16),
@@ -411,8 +414,9 @@
             pltpu.VMEM(dna_table.shape, BF16),
             pltpu.VMEM((length // block, block, channels), BF16),
         ]
-        + [pltpu.SemaphoreType.DMA((5 + length // block,))],
-        in_specs=[hbm] * 6,
+        + [pltpu.SemaphoreType.DMA((4 + length // block,))],
+        in_specs=[hbm] * 5,
+        micros=3,
     )
     pairs, *acts = call(
         functools.partial(taps_kernel, kernel, n_ctx),
@@ -421,10 +425,13 @@
         + [pltpu.VMEM((wide, kernel * width), BF16)] * n_ctx,
         [pltpu.VMEM((n_ctx, wide, kernel * width), BF16)],
     )
-    acts = [acts[0]] + [swap(acts[rel], "ctx", rel) for rel in order[1:]]
+    swapped = [acts[0]]
+    for rel in order[1:]:
+        swapped.append(swap(acts[rel], "ctx", rel))
+    acts = swapped
     pooled = call(
         functools.partial(pool_kernel, pool, tok_rows),
-        (pairs, sums, w_conv_v, cot_v),
+        (pairs, sums, w_conv, cot_v),
         [pltpu.VMEM((wide + tok_rows + 8, channels), BF16)],
     )[0]
     rows = [pooled]
@@ -461,6 +468,7 @@
             pltpu.SemaphoreType.DMA((2,)),
         ],
         in_specs=[WHOLE] * (n_ctx + 2) + [hbm] * 2,
+        micros=5,
     )
 
     depth = kernel * width
@@ -477,7 +485,7 @@
     padded = -(-(tok_rows + 2) // 8) * 8
     highs, lows, near_g = call(
         functools.partial(spread_kernel, kernel, tok_rows, befores, afters),
-        (g_all, w_conv_v),
+        (g_all, w_conv),
         [pltpu.VMEM((kernel * padded, channels), BF16)] * 2
         + [pltpu.VMEM((padded, channels), BF16)],
     )

time: 53.4 us -> 48.8 us (0.914)
  waiting for transfers between devices: 19.9 us -> 10.5 us
  starting transfers between devices: 15 us -> 19.6 us
    ppermute x15, waiting for transfers between devices: 19.9 us -> 10.5 us  [swap(): return lax.ppermute(value, axis, [(i, i ^ bit) for i in range(count)])]
    ppermute x15, starting transfers between devices: 15 us -> 19.6 us  [swap(): return lax.ppermute(value, axis, [(i, i ^ bit) for i in range(count)])]
  transfers between devices with their start and end apart: 15 -> 15, of which waited for: 7 -> 6; matrix products, arithmetic and copies ran while one was open for 0% -> 0% of each run, Pallas kernels for 23% -> 23%
where the time goes in v5:
time: 48.8 us; the launch traced here: 48.7 us
  starting transfers between devices  19.6 us (40%)
  Pallas kernels  17.8 us (36%)
  waiting for transfers between devices  10.5 us (22%)
  between operations  0.77 us (2%)
    ppermute x15, starting transfers between devices, swap(): return lax.ppermute(value, axis, [(i, i ^ bit) for i in range(count)])  19.6 us
    pallas_call x11, Pallas kernels, call(): pl.pallas_call(body, out_shape=list(outs), scratch_shapes=list(scratch),...  17.8 us
    ppermute x15, waiting for transfers between devices, swap(): return lax.ppermute(value, axis, [(i, i ^ bit) for i in range(count)])  10.5 us
  transfers between devices with their start and end apart: 15, of which 6 were waited for; matrix products, arithmetic and copies ran while one was open for 0% of the time, Pallas kernels for 23%

profile of v5, /device:TPU:0, one launch (start us, length us, event | category | flops | bytes accessed | tf_op | source)
XLA Modules:
  0.0 48.7 jit_solution(5426025923815313754)
XLA Ops:
  0.6 0.0 slice-start
  0.6 0.0 slice-start.1
  0.7 4.1 %shard_map.113 = (f32[200,768]{1,0:T(8,128)S(1)}, f32[40,768]{1,0:T(8,128)S(1)}, f32[512,768]{1,0:T(8,128)S(1)}, f32[512,128]{1,0:T(8,128)S(1)}, bf16[768]{0:T(1...) custom-call(bf16[512,768]{1,0:T(8,128)(2,1)} %bitcast.6, s32[1,512]{1,0:T(1,128)} %base_hbm.1, bf16[4,768]{1,0:T(4,128)(2,1)} %table_hbm.1, ...), custom_call_target="tpu_custom_call" | custom-call | flops 3449999872 | tf_op jit(solution)/shard_map/pallas_call | solution.py:350
  4.8 0.2 shard_map.114
  5.0 0.0 slice-done
  5.0 0.0 slice-done.1
  5.0 1.2 %shard_map.115.refs_0_ = bf16[80,768]{1,0:T(8,128)(2,1)S(1)} custom-call(bf16[5,80,768]{2,1,0:T(8,128)(2,1)S(1)} %get-tuple-element.28.pairs, f32[40,768]{1,0:T(8,128)S(1)} %get-tuple-element.29.sums, bf16[5,768,768]{2,1,0:T(8,128)(2,1)S(1)} %bitcast.5, bf16[32,768]{1,0:T(8,128)(2,1)S(1)} %get-tuple-element.30.cot), custom_call_target="tpu_custom_call" | custom-call | flops 1150000000 | tf_op jit(solution)/shard_map/pallas_call | solution.py:350
  6.2 3.1 %collective-permute-start = (bf16[80,768]{1,0:T(8,128)(2,1)S(1)}, bf16[80,768]{1,0:T(8,128)(2,1)S(1)}, u32[]{:S(2)}, u32[]{:S(2)}) collective-permute-start(bf16[80,768]{1,0:T(8,128)(2,1)S(1)} %shard_map.115.refs_0_), channel_id=1, source_target_pairs={{0,2},{1,3},{2,0},{3,1},{4,6},{5,7},{6,4},{7,5},{8,10},{9,11},{10,... | collective-permute-start | bytes 368648 | tf_op jit(solution)/shard_map/ppermute | solution.py:341
  9.2 0.1 collective-permute-start.3
  9.3 0.0 collective-permute-start.4
  9.3 2.1 %collective-permute-start.5 = (bf16[40,960]{1,0:T(8,128)(2,1)S(1)}, bf16[40,960]{1,0:T(8,128)(2,1)S(1)}, u32[]{:S(2)}, u32[]{:S(2)}) collective-permute-start(bf16[40,960]{1,0:T(8,128)(2,1)S(1)} %get-tuple-element.41), channel_id=1, source_target_pairs={{0,3},{1,2},{2,1},{3,0},{4,7},{5,6},{6,5},{7,4},{8,11},{9,10},{10,... | collective-permute-start | bytes 230408 | tf_op jit(solution)/shard_map/ppermute | solution.py:341
  11.4 0.0 collective-permute-start.1
  11.4 2.0 %collective-permute-done.refs_1_ = bf16[80,768]{1,0:T(8,128)(2,1)S(1)} collective-permute-done((bf16[80,768]{1,0:T(8,128)(2,1)S(1)}, bf16[80,768]{1,0:T(8,128)(2,1)S(1)}, u32[]{:S(2)}, u32[]{:S(2)}) %collective-permute-start) | collective-permute-done | bytes 122912 | tf_op jit(solution)/shard_map/ppermute | solution.py:341
  13.4 0.0 collective-permute-start.2
  13.4 1.8 %collective-permute-done.3.refs_1_ = bf16[40,960]{1,0:T(8,128)(2,1)S(1)} collective-permute-done((bf16[40,960]{1,0:T(8,128)(2,1)S(1)}, bf16[40,960]{1,0:T(8,128)(2,1)S(1)}, u32[]{:S(2)}, u32[]{:S(2)}) %collective-permute-start.3) | collective-permute-done | bytes 76832 | tf_op jit(solution)/shard_map/ppermute | solution.py:341
  15.2 0.0 collective-permute-done.4.refs_2_
  15.2 0.2 collective-permute-done.5.refs_3_
  15.3 0.0 copy-start
  15.3 0.0 copy-start.1
  15.3 0.3 shard_map.119.refs_0_
  15.6 2.8 %collective-permute-start.7 = (bf16[960,128]{1,0:T(8,128)(2,1)S(1)}, bf16[960,128]{1,0:T(8,128)(2,1)S(1)}, u32[]{:S(2)}, u32[]{:S(2)}) collective-permute-start(bf16[960,128]{1,0:T(8,128)(2,1)S(1)} %shard_map.119.refs_0_), channel_id=1, source_target_pairs={{0,16},{4,20},{8,24},{12,28},{16,0},{20,4},{24,8},{28,12},{1,17},{... | collective-permute-start | bytes 737288 | tf_op jit(solution)/shard_map/ppermute | solution.py:341
  18.4 1.5 %collective-permute-start.6 = (bf16[960,128]{1,0:T(8,128)(2,1)S(1)}, bf16[960,128]{1,0:T(8,128)(2,1)S(1)}, u32[]{:S(2)}, u32[]{:S(2)}) collective-permute-start(bf16[960,128]{1,0:T(8,128)(2,1)S(1)} %shard_map.119.refs_0_), channel_id=1, source_target_pairs={{0,4},{4,0},{8,12},{12,8},{16,20},{20,16},{24,28},{28,24},{1,5},{5... | collective-permute-start | bytes 737288 | tf_op jit(solution)/shard_map/ppermute | solution.py:341
  19.9 0.0 collective-permute-done.1.refs_2_
  19.9 0.0 collective-permute-done.2.refs_3_
  19.9 0.0 copy-done
  19.9 0.0 copy-done.1
  19.9 5.5 %shard_map.116 = (bf16[128,768]{1,0:T(8,128)(2,1)S(1)}, bf16[192,128]{1,0:T(8,128)(2,1)S(1)}, bf16[192,128]{1,0:T(8,128)(2,1)S(1)}, bf16[192,128]{1,0:T(8,128)(2,1)S(1)}, bf16[192,128]{1,0:T(8,128)(2,1)S(1)}) custom-call(bf16[80,768]{1,0:T(8,128)(2,1)S(1)} %shard_map.115.refs_0_, bf16[80,768]{1,0:T(8,128)(2,1)S(1)} %collective-permute-done.refs_1_, ...), custom_call_target="tpu_custom_call" | custom-call | flops 5750000128 | tf_op jit(solution)/shard_map/pallas_call | solution.py:350
  25.4 0.6 %collective-permute-start.9 = (bf16[192,128]{1,0:T(8,128)(2,1)S(1)}, bf16[192,128]{1,0:T(8,128)(2,1)S(1)}, u32[]{:S(2)}, u32[]{:S(2)}) collective-permute-start(bf16[192,128]{1,0:T(8,128)(2,1)S(1)} %get-tuple-element.44), channel_id=1, source_target_pairs={{0,4},{4,0},{8,12},{12,8},{16,20},{20,16},{24,28},{28,24},{1,5},{5... | collective-permute-start | bytes 147464 | tf_op jit(solution)/shard_map/ppermute | solution.py:341
  26.0 4.4 %collective-permute-done.7.value.refs_2_ = bf16[960,128]{1,0:T(8,128)(2,1)S(1)} collective-permute-done((bf16[960,128]{1,0:T(8,128)(2,1)S(1)}, bf16[960,128]{1,0:T(8,128)(2,1)S(1)}, u32[]{:S(2)}, u32[]{:S(2)}) %collective-permute-start.7) | collective-permute-done | bytes 245792 | tf_op jit(solution)/shard_map/ppermute | solution.py:341
  30.5 1.6 %collective-permute-start.12 = (bf16[480,128]{1,0:T(8,128)(2,1)S(1)}, bf16[480,128]{1,0:T(8,128)(2,1)S(1)}, u32[]{:S(2)}, u32[]{:S(2)}) collective-permute-start(bf16[480,128]{1,0:T(8,128)(2,1)S(1)} %get-tuple-element.48), channel_id=1, source_target_pairs={{0,4},{4,0},{8,12},{12,8},{16,20},{20,16},{24,28},{28,24},{1,5},{5... | collective-permute-start | bytes 368648 | tf_op jit(solution)/shard_map/ppermute | solution.py:341
  32.1 0.0 collective-permute-start.10
  32.1 2.8 %collective-permute-start.11 = (bf16[192,128]{1,0:T(8,128)(2,1)S(1)}, bf16[192,128]{1,0:T(8,128)(2,1)S(1)}, u32[]{:S(2)}, u32[]{:S(2)}) collective-permute-start(bf16[192,128]{1,0:T(8,128)(2,1)S(1)} %get-tuple-element.46), channel_id=1, source_target_pairs={{0,20},{4,16},{8,28},{12,24},{16,4},{20,0},{24,12},{28,8},{1,21},{... | collective-permute-start | bytes 147464 | tf_op jit(solution)/shard_map/ppermute | solution.py:341
  34.9 0.0 collective-permute-done.9.refs_5_
  34.9 1.5 %collective-permute-start.8 = (bf16[480,128]{1,0:T(8,128)(2,1)S(1)}, bf16[480,128]{1,0:T(8,128)(2,1)S(1)}, u32[]{:S(2)}, u32[]{:S(2)}) collective-permute-start(bf16[480,128]{1,0:T(8,128)(2,1)S(1)} %get-tuple-element.42), channel_id=1, source_target_pairs={{0,4},{4,0},{8,12},{12,8},{16,20},{20,16},{24,28},{28,24},{1,5},{5... | collective-permute-start | bytes 368648 | tf_op jit(solution)/shard_map/ppermute | solution.py:341
  36.5 1.8 %shard_map.117 = (bf16[200,768]{1,0:T(8,128)(2,1)S(1)}, bf16[200,768]{1,0:T(8,128)(2,1)S(1)}, bf16[40,768]{1,0:T(8,128)(2,1)S(1)}) custom-call(bf16[128,768]{1,0:T(8,128)(2,1)S(1)} %get-tuple-element.31.g_ref, bf16[5,768,768]{2,1,0:T(8,128)(2,1)S(1)} %bitcast.5), custom_call_target="tpu_custom_call" | custom-call | flops 1150000000 | tf_op jit(solution)/shard_map/pallas_call | solution.py:350
  38.2 0.0 collective-permute-done.10.refs_6_
  38.3 0.4 collective-permute-done.11.refs_7_
  38.7 0.0 collective-permute-done.6.refs_1_
  38.7 0.0 collective-permute-done.12.refs_3_
  38.7 0.4 shard_map.122
  39.1 3.5 %collective-permute-start.14 = (bf16[96,480]{1,0:T(8,128)(2,1)S(1)}, bf16[96,480]{1,0:T(8,128)(2,1)S(1)}, u32[]{:S(2)}, u32[]{:S(2)}) collective-permute-start(bf16[96,480]{1,0:T(8,128)(2,1)S(1)} %get-tuple-element.51), channel_id=1, source_target_pairs={{0,8},{4,12},{8,0},{12,4},{16,24},{20,28},{24,16},{28,20},{1,9},{5... | collective-permute-start | bytes 276488 | tf_op jit(solution)/shard_map/ppermute | solution.py:341
  42.5 0.0 collective-permute-done.8.refs_3_
  42.5 0.4 shard_map.121
  42.9 0.1 collective-permute-start.13
  43.0 2.9 %shard_map.118 = bf16[512,768]{1,0:T(8,128)(2,1)} custom-call(bf16[200,768]{1,0:T(8,128)(2,1)S(1)} %get-tuple-element.32.highs, bf16[200,768]{1,0:T(8,128)(2,1)S(1)} %get-tuple-element.33.lows, bf16[40,768]{1,0:T(8,128)(2,1)S(1)} %get-tuple-element.34.near, f32[512,768]{1,0:T(8,128)S(1)} %get-tuple-element.35.normed_ref, ...), custom_call_target="tpu_custom_call" | custom-call | flops 1150000000 | tf_op jit(solution)/shard_map/pallas_call | solution.py:350
  45.9 0.0 collective-permute-done.14.refs_3_
  45.9 1.7 %collective-permute-done.13.refs_2_ = bf16[96,480]{1,0:T(8,128)(2,1)S(1)} collective-permute-done((bf16[96,480]{1,0:T(8,128)(2,1)S(1)}, bf16[96,480]{1,0:T(8,128)(2,1)S(1)}, u32[]{:S(2)}, u32[]{:S(2)}) %collective-permute-start.13) | collective-permute-done | bytes 92192 | tf_op jit(solution)/shard_map/ppermute | solution.py:341
  47.6 1.1 %shard_map.123 = f32[5,192,96]{2,1,0:T(8,128)} custom-call(f32[96,480]{1,0:T(8,128)S(1)} %get-tuple-element.47.refs_0_, f32[96,480]{1,0:T(8,128)S(1)} %get-tuple-element.49.refs_1_, bf16[96,480]{1,0:T(8,128)(2,1)S(1)} %collective-permute-done.13.refs_2_, bf16[96,480]{1,0:T(8,128)(2,1)S(1)} %collective-permute-done.14.refs_3_), custom_call_target="tpu_custom_call" | custom-call | flops 1150000000 | tf_op jit(solution)/shard_map/pallas_call | solution.py:350
  (2 shorter events, 0.0 us)
Async XLA Ops:
  0.6 4.3 %slice-start = ((s8[5898240]{0:T(1024)(128)(4,1)}), s8[4194304]{0:T(1024)(128)(4,1)S(1)}, s32[]{:S(2)}) async-start(s8[5898240]{0:T(1024)(128)(4,1)} %bitcast.4), calls=%async_computation | async-start | bytes 8388608
  0.6 4.3 %slice-start.1 = ((s8[5898240]{0:T(1024)(128)(4,1)}), s8[1703936]{0:T(1024)(128)(4,1)S(1)}, s32[]{:S(2)}) async-start(s8[5898240]{0:T(1024)(128)(4,1)} %bitcast.4), calls=%async_computation.1 | async-start | bytes 3407872
  6.2 7.2 %collective-permute-start = (bf16[80,768]{1,0:T(8,128)(2,1)S(1)}, bf16[80,768]{1,0:T(8,128)(2,1)S(1)}, u32[]{:S(2)}, u32[]{:S(2)}) collective-permute-start(bf16[80,768]{1,0:T(8,128)(2,1)S(1)} %shard_map.115.refs_0_), channel_id=1, source_target_pairs={{0,2},{1,3},{2,0},{3,1},{4,6},{5,7},{6,4},{7,5},{8,10},{9,11},{10,... | collective-permute-start | bytes 368648 | tf_op jit(solution)/shard_map/ppermute | solution.py:341
  9.2 5.9 %collective-permute-start.3 = (bf16[40,960]{1,0:T(8,128)(2,1)S(1)}, bf16[40,960]{1,0:T(8,128)(2,1)S(1)}, u32[]{:S(2)}, u32[]{:S(2)}) collective-permute-start(bf16[40,960]{1,0:T(8,128)(2,1)S(1)} %get-tuple-element.39), channel_id=1, source_target_pairs={{0,2},{1,3},{2,0},{3,1},{4,6},{5,7},{6,4},{7,5},{8,10},{9,11},{10,... | collective-permute-start | bytes 230408 | tf_op jit(solution)/shard_map/ppermute | solution.py:341
  9.3 5.9 %collective-permute-start.4 = (bf16[40,960]{1,0:T(8,128)(2,1)S(1)}, bf16[40,960]{1,0:T(8,128)(2,1)S(1)}, u32[]{:S(2)}, u32[]{:S(2)}) collective-permute-start(bf16[40,960]{1,0:T(8,128)(2,1)S(1)} %get-tuple-element.40), channel_id=1, source_target_pairs={{0,1},{1,0},{2,3},{3,2},{4,5},{5,4},{6,7},{7,6},{8,9},{9,8},{10,11... | collective-permute-start | bytes 230408 | tf_op jit(solution)/shard_map/ppermute | solution.py:341
  9.3 6.0 %collective-permute-start.5 = (bf16[40,960]{1,0:T(8,128)(2,1)S(1)}, bf16[40,960]{1,0:T(8,128)(2,1)S(1)}, u32[]{:S(2)}, u32[]{:S(2)}) collective-permute-start(bf16[40,960]{1,0:T(8,128)(2,1)S(1)} %get-tuple-element.41), channel_id=1, source_target_pairs={{0,3},{1,2},{2,1},{3,0},{4,7},{5,6},{6,5},{7,4},{8,11},{9,10},{10,... | collective-permute-start | bytes 230408 | tf_op jit(solution)/shard_map/ppermute | solution.py:341
  11.4 8.5 %collective-permute-start.1 = (bf16[80,768]{1,0:T(8,128)(2,1)S(1)}, bf16[80,768]{1,0:T(8,128)(2,1)S(1)}, u32[]{:S(2)}, u32[]{:S(2)}) collective-permute-start(bf16[80,768]{1,0:T(8,128)(2,1)S(1)} %shard_map.115.refs_0_), channel_id=1, source_target_pairs={{0,1},{1,0},{2,3},{3,2},{4,5},{5,4},{6,7},{7,6},{8,9},{9,8},{10,11... | collective-permute-start | bytes 368648 | tf_op jit(solution)/shard_map/ppermute | solution.py:341
  13.4 6.5 %collective-permute-start.2 = (bf16[80,768]{1,0:T(8,128)(2,1)S(1)}, bf16[80,768]{1,0:T(8,128)(2,1)S(1)}, u32[]{:S(2)}, u32[]{:S(2)}) collective-permute-start(bf16[80,768]{1,0:T(8,128)(2,1)S(1)} %collective-permute-done.refs_1_), channel_id=1, source_target_pairs={{0,1},{1,0},{2,3},{3,2},{4,5},{5,4},{6,7},{7,6},{8,9},{9,8},{10,11... | collective-permute-start | bytes 368648 | tf_op jit(solution)/shard_map/ppermute | solution.py:341
  15.3 4.6 %copy-start = (bf16[768,768]{1,0:T(8,128)(2,1)S(1)}, bf16[768,768]{1,0:T(8,128)(2,1)}, u32[]{:S(2)}) copy-start(bf16[768,768]{1,0:T(8,128)(2,1)} %refs_4_.1) | copy-start | bytes 3538948
  15.3 4.6 %copy-start.1 = (bf16[768,768]{1,0:T(8,128)(2,1)S(1)}, bf16[768,768]{1,0:T(8,128)(2,1)}, u32[]{:S(2)}) copy-start(bf16[768,768]{1,0:T(8,128)(2,1)} %refs_5_.1) | copy-start | bytes 3538948
  15.6 14.8 %collective-permute-start.7 = (bf16[960,128]{1,0:T(8,128)(2,1)S(1)}, bf16[960,128]{1,0:T(8,128)(2,1)S(1)}, u32[]{:S(2)}, u32[]{:S(2)}) collective-permute-start(bf16[960,128]{1,0:T(8,128)(2,1)S(1)} %shard_map.119.refs_0_), channel_id=1, source_target_pairs={{0,16},{4,20},{8,24},{12,28},{16,0},{20,4},{24,8},{28,12},{1,17},{... | collective-permute-start | bytes 737288 | tf_op jit(solution)/shard_map/ppermute | solution.py:341
  18.4 20.3 %collective-permute-start.6 = (bf16[960,128]{1,0:T(8,128)(2,1)S(1)}, bf16[960,128]{1,0:T(8,128)(2,1)S(1)}, u32[]{:S(2)}, u32[]{:S(2)}) collective-permute-start(bf16[960,128]{1,0:T(8,128)(2,1)S(1)} %shard_map.119.refs_0_), channel_id=1, source_target_pairs={{0,4},{4,0},{8,12},{12,8},{16,20},{20,16},{24,28},{28,24},{1,5},{5... | collective-permute-start | bytes 737288 | tf_op jit(solution)/shard_map/ppermute | solution.py:341
  25.4 9.5 %collective-permute-start.9 = (bf16[192,128]{1,0:T(8,128)(2,1)S(1)}, bf16[192,128]{1,0:T(8,128)(2,1)S(1)}, u32[]{:S(2)}, u32[]{:S(2)}) collective-permute-start(bf16[192,128]{1,0:T(8,128)(2,1)S(1)} %get-tuple-element.44), channel_id=1, source_target_pairs={{0,4},{4,0},{8,12},{12,8},{16,20},{20,16},{24,28},{28,24},{1,5},{5... | collective-permute-start | bytes 147464 | tf_op jit(solution)/shard_map/ppermute | solution.py:341
  30.5 8.2 %collective-permute-start.12 = (bf16[480,128]{1,0:T(8,128)(2,1)S(1)}, bf16[480,128]{1,0:T(8,128)(2,1)S(1)}, u32[]{:S(2)}, u32[]{:S(2)}) collective-permute-start(bf16[480,128]{1,0:T(8,128)(2,1)S(1)} %get-tuple-element.48), channel_id=1, source_target_pairs={{0,4},{4,0},{8,12},{12,8},{16,20},{20,16},{24,28},{28,24},{1,5},{5... | collective-permute-start | bytes 368648 | tf_op jit(solution)/shard_map/ppermute | solution.py:341
  32.1 6.2 %collective-permute-start.10 = (bf16[192,128]{1,0:T(8,128)(2,1)S(1)}, bf16[192,128]{1,0:T(8,128)(2,1)S(1)}, u32[]{:S(2)}, u32[]{:S(2)}) collective-permute-start(bf16[192,128]{1,0:T(8,128)(2,1)S(1)} %get-tuple-element.45), channel_id=1, source_target_pairs={{0,16},{4,20},{8,24},{12,28},{16,0},{20,4},{24,8},{28,12},{1,17},{... | collective-permute-start | bytes 147464 | tf_op jit(solution)/shard_map/ppermute | solution.py:341
  32.1 6.6 %collective-permute-start.11 = (bf16[192,128]{1,0:T(8,128)(2,1)S(1)}, bf16[192,128]{1,0:T(8,128)(2,1)S(1)}, u32[]{:S(2)}, u32[]{:S(2)}) collective-permute-start(bf16[192,128]{1,0:T(8,128)(2,1)S(1)} %get-tuple-element.46), channel_id=1, source_target_pairs={{0,20},{4,16},{8,28},{12,24},{16,4},{20,0},{24,12},{28,8},{1,21},{... | collective-permute-start | bytes 147464 | tf_op jit(solution)/shard_map/ppermute | solution.py:341
  34.9 7.6 %collective-permute-start.8 = (bf16[480,128]{1,0:T(8,128)(2,1)S(1)}, bf16[480,128]{1,0:T(8,128)(2,1)S(1)}, u32[]{:S(2)}, u32[]{:S(2)}) collective-permute-start(bf16[480,128]{1,0:T(8,128)(2,1)S(1)} %get-tuple-element.42), channel_id=1, source_target_pairs={{0,4},{4,0},{8,12},{12,8},{16,20},{20,16},{24,28},{28,24},{1,5},{5... | collective-permute-start | bytes 368648 | tf_op jit(solution)/shard_map/ppermute | solution.py:341
  39.1 6.8 %collective-permute-start.14 = (bf16[96,480]{1,0:T(8,128)(2,1)S(1)}, bf16[96,480]{1,0:T(8,128)(2,1)S(1)}, u32[]{:S(2)}, u32[]{:S(2)}) collective-permute-start(bf16[96,480]{1,0:T(8,128)(2,1)S(1)} %get-tuple-element.51), channel_id=1, source_target_pairs={{0,8},{4,12},{8,0},{12,4},{16,24},{20,28},{24,16},{28,20},{1,9},{5... | collective-permute-start | bytes 276488 | tf_op jit(solution)/shard_map/ppermute | solution.py:341
  42.9 4.7 %collective-permute-start.13 = (bf16[96,480]{1,0:T(8,128)(2,1)S(1)}, bf16[96,480]{1,0:T(8,128)(2,1)S(1)}, u32[]{:S(2)}, u32[]{:S(2)}) collective-permute-start(bf16[96,480]{1,0:T(8,128)(2,1)S(1)} %get-tuple-element.50), channel_id=1, source_target_pairs={{0,8},{4,12},{8,0},{12,4},{16,24},{20,28},{24,16},{28,20},{1,9},{5... | collective-permute-start | bytes 276488 | tf_op jit(solution)/shard_map/ppermute | solution.py:341

commit v6 on v5

--- a/solution.py
+++ b/solution.py
@@ -19,6 +19,7 @@
 VMEM_LIMIT = 28 << 20
 FLOPS_PER_MICRO = 1.15e9
 X_BIT, Z_BIT = 1, 4
+BLOCK = 128
 
 
 def dot_nn(left, right):
@@ -68,49 +69,43 @@
 
 def act_kernel(
     kernel, pool, tok_rows, feat_hbm, base_hbm, table_hbm, gain_hbm, cot_hbm,
-    taps, sums, normed_out, inv_out, gain, cot, feat, base, table, act_buf, sems,
+    taps, sums, normed_out, inv_out, gain, cot, feat, base, table, act_buf, spread, embed, sems,
 ):
     half = kernel // 2
-    _, channels = feat.shape
-    count, block = act_buf.shape[:2]
+    rows, channels = feat.shape
+    block = BLOCK
+    count = rows // block
     small = ((base_hbm, base), (table_hbm, table), (gain_hbm, gain))
     parts = tuple(
         (feat_hbm.at[pl.ds(i * block, block)], feat.at[pl.ds(i * block, block)]) for i in range(count)
     )
     copies = start_copies(small + parts + ((cot_hbm, cot),), sems)
     padded = taps.shape[0] // kernel
+    shape = (kernel * padded, rows)
+    row = iota(shape, 0)
+    tap = sum((row >= padded * j).astype(jnp.int32) for j in range(1, kernel))
+    token = row - tap * padded
+    known = token < tok_rows + 2
+    token = jnp.where(token == tok_rows, -1, jnp.where(token == tok_rows + 1, tok_rows, token))
+    offset = iota(shape, 1) - tap + half - token * pool
+    spread[...] = ((offset >= 0) & (offset < pool) & known).astype(BF16)
     for copy in copies[: len(small)]:
         copy.wait()
     gain_f = gain[...].reshape(1, channels).astype(F32)
-    chunk = 32
-    for step in range(count):
-        start = step * block
-        here = slice(start, start + block)
-        copies[len(small) + step].wait()
-        onehot = (iota((table.shape[0], block), 0) == base[:, here]).astype(BF16)
-        embed = dot_tn(onehot, table[...])
-        for begin in range(0, block, chunk):
-            part = slice(begin, begin + chunk)
-            some = slice(start + begin, start + begin + chunk)
-            summed = feat[some, :].astype(F32) + embed[part, :]
-            inv_rms, normed = normed_of(summed)
-            act_buf[step, part, :] = gelu_of(normed * gain_f)[1].astype(BF16)
-            normed_out[some, :] = normed
-            inv_out[some, :] = jnp.broadcast_to(inv_rms, (chunk, inv_out.shape[1]))
-        shape = (kernel * padded, block)
-        row = iota(shape, 0)
-        tap = sum((row >= padded * j).astype(jnp.int32) for j in range(1, kernel))
-        token = row - tap * padded
-        token = jnp.where(token == tok_rows, -1, jnp.where(token == tok_rows + 1, tok_rows, token))
-        known = row - tap * padded < tok_rows + 2
-        offset = iota(shape, 1) + start - tap + half - token * pool
-        spread = ((offset >= 0) & (offset < pool) & known).astype(BF16)
-        term = dot_nn(spread, act_buf[step])
-        taps[...] = term if step == 0 else taps[...] + term
-        plain = spread[half * padded : (half + 1) * padded, :]
-        counts = dot_nt(plain, onehot).astype(BF16)
-        term = dot_nn(plain, feat[here, :]) + dot_nn(counts, table[...])
-        sums[...] = term if step == 0 else sums[...] + term
+    onehot = (iota((table.shape[0], rows), 0) == base[...]).astype(BF16)
+    embed[...] = dot_tn(onehot, table[...])
+    for copy in copies[len(small) : len(small) + count]:
+        copy.wait()
+
+    summed = feat[...].astype(F32) + embed[...]
+    inv_rms, normed = normed_of(summed)
+    act_buf[...] = gelu_of(normed * gain_f)[1].astype(BF16)
+    normed_out[...] = normed
+    inv_out[...] = jnp.broadcast_to(inv_rms, inv_out.shape)
+    taps[...] = dot_nn(spread[...], act_buf[...])
+    plain = spread[half * padded : (half + 1) * padded, :]
+    counts = dot_nt(plain, onehot).astype(BF16)
+    sums[...] = dot_nn(plain, feat[...]) + dot_nn(counts, table[...])
 
     for copy in copies[len(small) + count :]:
         copy.wait()
@@ -208,32 +203,29 @@
     scale = 1.0 / DH**0.5
     for h in range(HEADS):
         cols = slice(h * DH, (h + 1) * DH)
-        scores = dot_nt(q_buf[:, cols], k_buf[:, cols]) * scale
-        expo = jnp.exp(scores - jnp.max(scores, axis=-1, keepdims=True))
-        probs_buf[h] = expo / jnp.sum(expo, axis=-1, keepdims=True)
+        scores = dot_nt(k_buf[:, cols], q_buf[:, cols]) * scale
+        expo = jnp.exp(scores - jnp.max(scores, axis=0, keepdims=True))
+        probs_buf[h] = expo / jnp.sum(expo, axis=0, keepdims=True)
     copies[0].wait()
     v_buf[...] = dot_nn(p_buf[...], wv[...]).astype(BF16)
     copies[1].wait()
-    ga_buf[...] = dot_nt(c_buf[...], wo[...]).astype(BF16)
+    ga_buf[...] = dot_nt(wo[...], c_buf[...]).astype(BF16)
     for h in range(HEADS):
         cols = slice(h * DH, (h + 1) * DH)
-        q, k, v, ga = q_buf[:, cols], k_buf[:, cols], v_buf[:, cols], ga_buf[:, cols]
+        q, k, v, ga = q_buf[:, cols], k_buf[:, cols], v_buf[:, cols], ga_buf[cols, :]
         probs = probs_buf[h]
         probs_b = probs.astype(BF16)
-        out = dot_nn(probs_b, v).astype(BF16)
-        delta = jnp.sum(ga.astype(F32) * out.astype(F32), axis=-1, keepdims=True)
-        grad_score = (probs * (dot_nt(ga, v) - delta) * scale).astype(BF16)
-        gq_buf[:, cols] = dot_nn(grad_score, k).astype(BF16)
-        gk_buf[:, cols] = dot_tn(grad_score, q).astype(BF16)
-        gv_buf[:, cols] = dot_tn(probs_b, ga).astype(BF16)
-    grad = c_buf[...].astype(F32)
+        out = dot_tn(v, probs_b).astype(BF16)
+        delta = jnp.sum(ga.astype(F32) * out.astype(F32), axis=0, keepdims=True)
+        grad_score = (probs * (dot_nn(v, ga) - delta) * scale).astype(BF16)
+        gq_buf[:, cols] = dot_tn(grad_score, k).astype(BF16)
+        gk_buf[:, cols] = dot_nn(grad_score, q).astype(BF16)
+        gv_buf[:, cols] = dot_nt(probs_b, ga).astype(BF16)
+    grad = jnp.transpose(c_buf[...].astype(F32))
     for src, weight in ((gq_buf, wq), (gk_buf, wk), (gv_buf, wv)):
-        grad = grad + dot_nt(src[...], weight[...])
-    g = (grad * (1.0 / pool)).astype(BF16)
-    g_out[...] = g
-    tokens = g.shape[0]
-    eye = (iota((tokens, tokens), 0) == iota((tokens, tokens), 1)).astype(BF16)
-    turned = dot_tn(g, eye).astype(BF16)
+        grad = grad + dot_nt(weight[...], src[...])
+    turned = (grad * (1.0 / pool)).astype(BF16)
+    g_out[...] = turned
     count = turn.shape[0]
     span = turned.shape[0] // count
     me = lax.axis_index("dp")
@@ -245,7 +237,7 @@
 
 
 def spread_kernel(kernel, tok_rows, befores, afters, g_ref, weights, highs, lows, near):
-    tokens = g_ref.shape[0]
+    tokens = g_ref.shape[1]
     padded = near.shape[0]
     me = lax.axis_index("ctx")
     row = iota((padded, tokens), 0)
@@ -254,7 +246,7 @@
     )
     source = jnp.where(row > tok_rows + 1, -1, source)
     chosen = (source == iota((padded, tokens), 1)).astype(BF16)
-    rows = dot_nn(chosen, g_ref[...]).astype(BF16)
+    rows = dot_nt(chosen, g_ref[...]).astype(BF16)
     near[...] = rows
     for j in range(kernel):
         part = slice(j * padded, (j + 1) * padded)
@@ -395,7 +387,7 @@
     afters = [place[c ^ (c + 1)] * tok_rows for c in range(n_ctx - 1)] + [-1]
 
     hbm = pl.BlockSpec(memory_space=pltpu.HBM)
-    block = 128
+    block = BLOCK
     wide = -(-(tok_rows + 2) // 8) * 8
     taps, sums, normed, inv_rms, gain_v, cot_v = call(
         functools.partial(act_kernel, kernel, pool, tok_rows),
@@ -412,7 +404,9 @@
             pltpu.VMEM(feat.shape, BF16),
             pltpu.VMEM(bases.shape, jnp.int32),
             pltpu.VMEM(dna_table.shape, BF16),
-            pltpu.VMEM((length // block, block, channels), BF16),
+            pltpu.VMEM(feat.shape, BF16),
+            pltpu.VMEM((kernel * wide, length), BF16),
+            pltpu.VMEM((length, channels), F32),
         ]
         + [pltpu.SemaphoreType.DMA((4 + length // block,))],
         in_specs=[hbm] * 5,
@@ -456,9 +450,11 @@
     g_all, *gts = call(
         functools.partial(attention_kernel, pool, order, tok_rows, near_rels, late),
         [*rows, w_query, w_key] + outside(w_value, w_out),
-        [pltpu.VMEM((tokens, channels), BF16)]
+        [pltpu.VMEM((channels, tokens), BF16)]
         + [pltpu.VMEM((len(late) * narrow, tokens), BF16)] * len(near_rels),
-        [pltpu.VMEM((tokens, channels), BF16)] * 9
+        [pltpu.VMEM((tokens, channels), BF16)] * 5
+        + [pltpu.VMEM((channels, tokens), BF16)]
+        + [pltpu.VMEM((tokens, channels), BF16)] * 3
         + [
             pltpu.VMEM((HEADS, tokens, tokens), F32),
             pltpu.VMEM((n_dp, narrow, tokens), BF16),

time: 48.8 us -> 47.6 us (0.975)
  Pallas kernels: 17.8 us -> 17 us
  waiting for transfers between devices: 10.5 us -> 10 us
    pallas_call x11, Pallas kernels: 17.8 us -> 17 us  [call(): pl.pallas_call(body, out_shape=list(outs), scratch_shapes=list(scratch),...]
    ppermute x15, waiting for transfers between devices: 10.5 us -> 10 us  [swap(): return lax.ppermute(value, axis, [(i, i ^ bit) for i in range(count)])]
  transfers between devices with their start and end apart: 15 -> 15, of which waited for: 6 -> 6; matrix products, arithmetic and copies ran while one was open for 0% -> 0% of each run, Pallas kernels for 23% -> 25%
where the time goes in v6:
time: 47.6 us; the launch traced here: 47.4 us
  starting transfers between devices  19.6 us (41%)
  Pallas kernels  17 us (36%)
  waiting for transfers between devices  10 us (21%)
  between operations  0.75 us (2%)
    ppermute x15, starting transfers between devices, swap(): return lax.ppermute(value, axis, [(i, i ^ bit) for i in range(count)])  19.6 us
    pallas_call x11, Pallas kernels, call(): pl.pallas_call(body, out_shape=list(outs), scratch_shapes=list(scratch),...  17 us
    ppermute x15, waiting for transfers between devices, swap(): return lax.ppermute(value, axis, [(i, i ^ bit) for i in range(count)])  10 us
  transfers between devices with their start and end apart: 15, of which 6 were waited for; matrix products, arithmetic and copies ran while one was open for 0% of the time, Pallas kernels for 25%

profile of v6, /device:TPU:0, one launch (start us, length us, event | category | flops | bytes accessed | tf_op | source)
XLA Modules:
  0.0 47.4 jit_solution(9715707146467208938)
XLA Ops:
  0.6 0.0 slice-start
  0.6 0.0 slice-start.1
  0.7 2.8 %shard_map.113 = (f32[200,768]{1,0:T(8,128)S(1)}, f32[40,768]{1,0:T(8,128)S(1)}, f32[512,768]{1,0:T(8,128)S(1)}, f32[512,128]{1,0:T(8,128)S(1)}, bf16[768]{0:T(1...) custom-call(bf16[512,768]{1,0:T(8,128)(2,1)} %bitcast.6, s32[1,512]{1,0:T(1,128)} %base_hbm.1, bf16[4,768]{1,0:T(4,128)(2,1)} %table_hbm.1, ...), custom_call_target="tpu_custom_call" | custom-call | flops 3449999872 | tf_op jit(solution)/shard_map/pallas_call | solution.py:342
  3.5 0.2 shard_map.114
  3.7 0.0 slice-done
  3.7 0.1 slice-done.1
  3.8 1.2 %shard_map.115.refs_0_ = bf16[80,768]{1,0:T(8,128)(2,1)S(1)} custom-call(bf16[5,80,768]{2,1,0:T(8,128)(2,1)S(1)} %get-tuple-element.28.pairs, f32[40,768]{1,0:T(8,128)S(1)} %get-tuple-element.29.sums, bf16[5,768,768]{2,1,0:T(8,128)(2,1)S(1)} %bitcast.5, bf16[32,768]{1,0:T(8,128)(2,1)S(1)} %get-tuple-element.30.cot), custom_call_target="tpu_custom_call" | custom-call | flops 1150000000 | tf_op jit(solution)/shard_map/pallas_call | solution.py:342
  4.9 3.1 %collective-permute-start = (bf16[80,768]{1,0:T(8,128)(2,1)S(1)}, bf16[80,768]{1,0:T(8,128)(2,1)S(1)}, u32[]{:S(2)}, u32[]{:S(2)}) collective-permute-start(bf16[80,768]{1,0:T(8,128)(2,1)S(1)} %shard_map.115.refs_0_), channel_id=1, source_target_pairs={{0,2},{1,3},{2,0},{3,1},{4,6},{5,7},{6,4},{7,5},{8,10},{9,11},{10,... | collective-permute-start | bytes 368648 | tf_op jit(solution)/shard_map/ppermute | solution.py:333
  8.0 0.1 collective-permute-start.3
  8.1 0.0 collective-permute-start.4
  8.1 2.1 %collective-permute-start.5 = (bf16[40,960]{1,0:T(8,128)(2,1)S(1)}, bf16[40,960]{1,0:T(8,128)(2,1)S(1)}, u32[]{:S(2)}, u32[]{:S(2)}) collective-permute-start(bf16[40,960]{1,0:T(8,128)(2,1)S(1)} %get-tuple-element.41), channel_id=1, source_target_pairs={{0,3},{1,2},{2,1},{3,0},{4,7},{5,6},{6,5},{7,4},{8,11},{9,10},{10,... | collective-permute-start | bytes 230408 | tf_op jit(solution)/shard_map/ppermute | solution.py:333
  10.1 0.0 collective-permute-start.1
  10.1 2.0 %collective-permute-done.refs_1_ = bf16[80,768]{1,0:T(8,128)(2,1)S(1)} collective-permute-done((bf16[80,768]{1,0:T(8,128)(2,1)S(1)}, bf16[80,768]{1,0:T(8,128)(2,1)S(1)}, u32[]{:S(2)}, u32[]{:S(2)}) %collective-permute-start) | collective-permute-done | bytes 122912 | tf_op jit(solution)/shard_map/ppermute | solution.py:333
  12.2 0.0 collective-permute-start.2
  12.2 1.8 %collective-permute-done.3.refs_1_ = bf16[40,960]{1,0:T(8,128)(2,1)S(1)} collective-permute-done((bf16[40,960]{1,0:T(8,128)(2,1)S(1)}, bf16[40,960]{1,0:T(8,128)(2,1)S(1)}, u32[]{:S(2)}, u32[]{:S(2)}) %collective-permute-start.3) | collective-permute-done | bytes 76832 | tf_op jit(solution)/shard_map/ppermute | solution.py:333
  13.9 0.0 collective-permute-done.4.refs_2_
  13.9 0.2 collective-permute-done.5.refs_3_
  14.1 0.0 copy-start
  14.1 0.0 copy-start.1
  14.1 0.3 shard_map.119.refs_0_
  14.4 2.8 %collective-permute-start.7 = (bf16[960,128]{1,0:T(8,128)(2,1)S(1)}, bf16[960,128]{1,0:T(8,128)(2,1)S(1)}, u32[]{:S(2)}, u32[]{:S(2)}) collective-permute-start(bf16[960,128]{1,0:T(8,128)(2,1)S(1)} %shard_map.119.refs_0_), channel_id=1, source_target_pairs={{0,16},{4,20},{8,24},{12,28},{16,0},{20,4},{24,8},{28,12},{1,17},{... | collective-permute-start | bytes 737288 | tf_op jit(solution)/shard_map/ppermute | solution.py:333
  17.1 1.5 %collective-permute-start.6 = (bf16[960,128]{1,0:T(8,128)(2,1)S(1)}, bf16[960,128]{1,0:T(8,128)(2,1)S(1)}, u32[]{:S(2)}, u32[]{:S(2)}) collective-permute-start(bf16[960,128]{1,0:T(8,128)(2,1)S(1)} %shard_map.119.refs_0_), channel_id=1, source_target_pairs={{0,4},{4,0},{8,12},{12,8},{16,20},{20,16},{24,28},{28,24},{1,5},{5... | collective-permute-start | bytes 737288 | tf_op jit(solution)/shard_map/ppermute | solution.py:333
  18.6 0.0 collective-permute-done.1.refs_2_
  18.6 0.0 collective-permute-done.2.refs_3_
  18.6 0.0 copy-done
  18.6 0.0 copy-done.1
  18.7 5.8 %shard_map.116 = (bf16[768,128]{1,0:T(8,128)(2,1)S(1)}, bf16[192,128]{1,0:T(8,128)(2,1)S(1)}, bf16[192,128]{1,0:T(8,128)(2,1)S(1)}, bf16[192,128]{1,0:T(8,128)(2,1)S(1)}, bf16[192,128]{1,0:T(8,128)(2,1)S(1)}) custom-call(bf16[80,768]{1,0:T(8,128)(2,1)S(1)} %shard_map.115.refs_0_, bf16[80,768]{1,0:T(8,128)(2,1)S(1)} %collective-permute-done.refs_1_, ...), custom_call_target="tpu_custom_call" | custom-call | flops 5750000128 | tf_op jit(solution)/shard_map/pallas_call | solution.py:342
  24.5 0.6 %collective-permute-start.9 = (bf16[192,128]{1,0:T(8,128)(2,1)S(1)}, bf16[192,128]{1,0:T(8,128)(2,1)S(1)}, u32[]{:S(2)}, u32[]{:S(2)}) collective-permute-start(bf16[192,128]{1,0:T(8,128)(2,1)S(1)} %get-tuple-element.44), channel_id=1, source_target_pairs={{0,4},{4,0},{8,12},{12,8},{16,20},{20,16},{24,28},{28,24},{1,5},{5... | collective-permute-start | bytes 147464 | tf_op jit(solution)/shard_map/ppermute | solution.py:333
  25.1 4.1 %collective-permute-done.7.value.refs_2_ = bf16[960,128]{1,0:T(8,128)(2,1)S(1)} collective-permute-done((bf16[960,128]{1,0:T(8,128)(2,1)S(1)}, bf16[960,128]{1,0:T(8,128)(2,1)S(1)}, u32[]{:S(2)}, u32[]{:S(2)}) %collective-permute-start.7) | collective-permute-done | bytes 245792 | tf_op jit(solution)/shard_map/ppermute | solution.py:333
  29.2 1.6 %collective-permute-start.12 = (bf16[480,128]{1,0:T(8,128)(2,1)S(1)}, bf16[480,128]{1,0:T(8,128)(2,1)S(1)}, u32[]{:S(2)}, u32[]{:S(2)}) collective-permute-start(bf16[480,128]{1,0:T(8,128)(2,1)S(1)} %get-tuple-element.48), channel_id=1, source_target_pairs={{0,4},{4,0},{8,12},{12,8},{16,20},{20,16},{24,28},{28,24},{1,5},{5... | collective-permute-start | bytes 368648 | tf_op jit(solution)/shard_map/ppermute | solution.py:333
  30.8 0.0 collective-permute-start.10
  30.8 2.8 %collective-permute-start.11 = (bf16[192,128]{1,0:T(8,128)(2,1)S(1)}, bf16[192,128]{1,0:T(8,128)(2,1)S(1)}, u32[]{:S(2)}, u32[]{:S(2)}) collective-permute-start(bf16[192,128]{1,0:T(8,128)(2,1)S(1)} %get-tuple-element.46), channel_id=1, source_target_pairs={{0,20},{4,16},{8,28},{12,24},{16,4},{20,0},{24,12},{28,8},{1,21},{... | collective-permute-start | bytes 147464 | tf_op jit(solution)/shard_map/ppermute | solution.py:333
  33.7 0.0 collective-permute-done.9.refs_5_
  33.7 1.5 %collective-permute-start.8 = (bf16[480,128]{1,0:T(8,128)(2,1)S(1)}, bf16[480,128]{1,0:T(8,128)(2,1)S(1)}, u32[]{:S(2)}, u32[]{:S(2)}) collective-permute-start(bf16[480,128]{1,0:T(8,128)(2,1)S(1)} %get-tuple-element.42), channel_id=1, source_target_pairs={{0,4},{4,0},{8,12},{12,8},{16,20},{20,16},{24,28},{28,24},{1,5},{5... | collective-permute-start | bytes 368648 | tf_op jit(solution)/shard_map/ppermute | solution.py:333
  35.2 1.9 %shard_map.117 = (bf16[200,768]{1,0:T(8,128)(2,1)S(1)}, bf16[200,768]{1,0:T(8,128)(2,1)S(1)}, bf16[40,768]{1,0:T(8,128)(2,1)S(1)}) custom-call(bf16[768,128]{1,0:T(8,128)(2,1)S(1)} %get-tuple-element.31.g_ref, bf16[5,768,768]{2,1,0:T(8,128)(2,1)S(1)} %bitcast.5), custom_call_target="tpu_custom_call" | custom-call | flops 1150000000 | tf_op jit(solution)/shard_map/pallas_call | solution.py:342
  37.2 0.0 collective-permute-done.10.refs_6_
  37.2 0.2 collective-permute-done.11.refs_7_
  37.4 0.0 collective-permute-done.6.refs_1_
  37.4 0.0 collective-permute-done.12.refs_3_
  37.4 0.4 shard_map.122
  37.8 3.5 %collective-permute-start.14 = (bf16[96,480]{1,0:T(8,128)(2,1)S(1)}, bf16[96,480]{1,0:T(8,128)(2,1)S(1)}, u32[]{:S(2)}, u32[]{:S(2)}) collective-permute-start(bf16[96,480]{1,0:T(8,128)(2,1)S(1)} %get-tuple-element.51), channel_id=1, source_target_pairs={{0,8},{4,12},{8,0},{12,4},{16,24},{20,28},{24,16},{28,20},{1,9},{5... | collective-permute-start | bytes 276488 | tf_op jit(solution)/shard_map/ppermute | solution.py:333
  41.3 0.0 collective-permute-done.8.refs_3_
  41.3 0.4 shard_map.121
  41.7 0.1 collective-permute-start.13
  41.8 2.9 %shard_map.118 = bf16[512,768]{1,0:T(8,128)(2,1)} custom-call(bf16[200,768]{1,0:T(8,128)(2,1)S(1)} %get-tuple-element.32.highs, bf16[200,768]{1,0:T(8,128)(2,1)S(1)} %get-tuple-element.33.lows, bf16[40,768]{1,0:T(8,128)(2,1)S(1)} %get-tuple-element.34.near, f32[512,768]{1,0:T(8,128)S(1)} %get-tuple-element.35.normed_ref, ...), custom_call_target="tpu_custom_call" | custom-call | flops 1150000000 | tf_op jit(solution)/shard_map/pallas_call | solution.py:342
  44.7 0.0 collective-permute-done.14.refs_3_
  44.7 1.7 %collective-permute-done.13.refs_2_ = bf16[96,480]{1,0:T(8,128)(2,1)S(1)} collective-permute-done((bf16[96,480]{1,0:T(8,128)(2,1)S(1)}, bf16[96,480]{1,0:T(8,128)(2,1)S(1)}, u32[]{:S(2)}, u32[]{:S(2)}) %collective-permute-start.13) | collective-permute-done | bytes 92192 | tf_op jit(solution)/shard_map/ppermute | solution.py:333
  46.4 1.1 %shard_map.123 = f32[5,192,96]{2,1,0:T(8,128)} custom-call(f32[96,480]{1,0:T(8,128)S(1)} %get-tuple-element.47.refs_0_, f32[96,480]{1,0:T(8,128)S(1)} %get-tuple-element.49.refs_1_, bf16[96,480]{1,0:T(8,128)(2,1)S(1)} %collective-permute-done.13.refs_2_, bf16[96,480]{1,0:T(8,128)(2,1)S(1)} %collective-permute-done.14.refs_3_), custom_call_target="tpu_custom_call" | custom-call | flops 1150000000 | tf_op jit(solution)/shard_map/pallas_call | solution.py:342
  (2 shorter events, 0.0 us)
Async XLA Ops:
  0.6 3.0 %slice-start = ((s8[5898240]{0:T(1024)(128)(4,1)}), s8[4194304]{0:T(1024)(128)(4,1)S(1)}, s32[]{:S(2)}) async-start(s8[5898240]{0:T(1024)(128)(4,1)} %bitcast.4), calls=%async_computation | async-start | bytes 8388608
  0.6 3.1 %slice-start.1 = ((s8[5898240]{0:T(1024)(128)(4,1)}), s8[1703936]{0:T(1024)(128)(4,1)S(1)}, s32[]{:S(2)}) async-start(s8[5898240]{0:T(1024)(128)(4,1)} %bitcast.4), calls=%async_computation.1 | async-start | bytes 3407872
  4.9 7.2 %collective-permute-start = (bf16[80,768]{1,0:T(8,128)(2,1)S(1)}, bf16[80,768]{1,0:T(8,128)(2,1)S(1)}, u32[]{:S(2)}, u32[]{:S(2)}) collective-permute-start(bf16[80,768]{1,0:T(8,128)(2,1)S(1)} %shard_map.115.refs_0_), channel_id=1, source_target_pairs={{0,2},{1,3},{2,0},{3,1},{4,6},{5,7},{6,4},{7,5},{8,10},{9,11},{10,... | collective-permute-start | bytes 368648 | tf_op jit(solution)/shard_map/ppermute | solution.py:333
  8.0 5.9 %collective-permute-start.3 = (bf16[40,960]{1,0:T(8,128)(2,1)S(1)}, bf16[40,960]{1,0:T(8,128)(2,1)S(1)}, u32[]{:S(2)}, u32[]{:S(2)}) collective-permute-start(bf16[40,960]{1,0:T(8,128)(2,1)S(1)} %get-tuple-element.39), channel_id=1, source_target_pairs={{0,2},{1,3},{2,0},{3,1},{4,6},{5,7},{6,4},{7,5},{8,10},{9,11},{10,... | collective-permute-start | bytes 230408 | tf_op jit(solution)/shard_map/ppermute | solution.py:333
  8.1 5.9 %collective-permute-start.4 = (bf16[40,960]{1,0:T(8,128)(2,1)S(1)}, bf16[40,960]{1,0:T(8,128)(2,1)S(1)}, u32[]{:S(2)}, u32[]{:S(2)}) collective-permute-start(bf16[40,960]{1,0:T(8,128)(2,1)S(1)} %get-tuple-element.40), channel_id=1, source_target_pairs={{0,1},{1,0},{2,3},{3,2},{4,5},{5,4},{6,7},{7,6},{8,9},{9,8},{10,11... | collective-permute-start | bytes 230408 | tf_op jit(solution)/shard_map/ppermute | solution.py:333
  8.1 6.0 %collective-permute-start.5 = (bf16[40,960]{1,0:T(8,128)(2,1)S(1)}, bf16[40,960]{1,0:T(8,128)(2,1)S(1)}, u32[]{:S(2)}, u32[]{:S(2)}) collective-permute-start(bf16[40,960]{1,0:T(8,128)(2,1)S(1)} %get-tuple-element.41), channel_id=1, source_target_pairs={{0,3},{1,2},{2,1},{3,0},{4,7},{5,6},{6,5},{7,4},{8,11},{9,10},{10,... | collective-permute-start | bytes 230408 | tf_op jit(solution)/shard_map/ppermute | solution.py:333
  10.1 8.5 %collective-permute-start.1 = (bf16[80,768]{1,0:T(8,128)(2,1)S(1)}, bf16[80,768]{1,0:T(8,128)(2,1)S(1)}, u32[]{:S(2)}, u32[]{:S(2)}) collective-permute-start(bf16[80,768]{1,0:T(8,128)(2,1)S(1)} %shard_map.115.refs_0_), channel_id=1, source_target_pairs={{0,1},{1,0},{2,3},{3,2},{4,5},{5,4},{6,7},{7,6},{8,9},{9,8},{10,11... | collective-permute-start | bytes 368648 | tf_op jit(solution)/shard_map/ppermute | solution.py:333
  12.2 6.5 %collective-permute-start.2 = (bf16[80,768]{1,0:T(8,128)(2,1)S(1)}, bf16[80,768]{1,0:T(8,128)(2,1)S(1)}, u32[]{:S(2)}, u32[]{:S(2)}) collective-permute-start(bf16[80,768]{1,0:T(8,128)(2,1)S(1)} %collective-permute-done.refs_1_), channel_id=1, source_target_pairs={{0,1},{1,0},{2,3},{3,2},{4,5},{5,4},{6,7},{7,6},{8,9},{9,8},{10,11... | collective-permute-start | bytes 368648 | tf_op jit(solution)/shard_map/ppermute | solution.py:333
  14.1 4.6 %copy-start = (bf16[768,768]{1,0:T(8,128)(2,1)S(1)}, bf16[768,768]{1,0:T(8,128)(2,1)}, u32[]{:S(2)}) copy-start(bf16[768,768]{1,0:T(8,128)(2,1)} %refs_4_.1) | copy-start | bytes 3538948
  14.1 4.6 %copy-start.1 = (bf16[768,768]{1,0:T(8,128)(2,1)S(1)}, bf16[768,768]{1,0:T(8,128)(2,1)}, u32[]{:S(2)}) copy-start(bf16[768,768]{1,0:T(8,128)(2,1)} %refs_5_.1) | copy-start | bytes 3538948
  14.4 14.8 %collective-permute-start.7 = (bf16[960,128]{1,0:T(8,128)(2,1)S(1)}, bf16[960,128]{1,0:T(8,128)(2,1)S(1)}, u32[]{:S(2)}, u32[]{:S(2)}) collective-permute-start(bf16[960,128]{1,0:T(8,128)(2,1)S(1)} %shard_map.119.refs_0_), channel_id=1, source_target_pairs={{0,16},{4,20},{8,24},{12,28},{16,0},{20,4},{24,8},{28,12},{1,17},{... | collective-permute-start | bytes 737288 | tf_op jit(solution)/shard_map/ppermute | solution.py:333
  17.1 20.3 %collective-permute-start.6 = (bf16[960,128]{1,0:T(8,128)(2,1)S(1)}, bf16[960,128]{1,0:T(8,128)(2,1)S(1)}, u32[]{:S(2)}, u32[]{:S(2)}) collective-permute-start(bf16[960,128]{1,0:T(8,128)(2,1)S(1)} %shard_map.119.refs_0_), channel_id=1, source_target_pairs={{0,4},{4,0},{8,12},{12,8},{16,20},{20,16},{24,28},{28,24},{1,5},{5... | collective-permute-start | bytes 737288 | tf_op jit(solution)/shard_map/ppermute | solution.py:333
  24.5 9.2 %collective-permute-start.9 = (bf16[192,128]{1,0:T(8,128)(2,1)S(1)}, bf16[192,128]{1,0:T(8,128)(2,1)S(1)}, u32[]{:S(2)}, u32[]{:S(2)}) collective-permute-start(bf16[192,128]{1,0:T(8,128)(2,1)S(1)} %get-tuple-element.44), channel_id=1, source_target_pairs={{0,4},{4,0},{8,12},{12,8},{16,20},{20,16},{24,28},{28,24},{1,5},{5... | collective-permute-start | bytes 147464 | tf_op jit(solution)/shard_map/ppermute | solution.py:333
  29.2 8.2 %collective-permute-start.12 = (bf16[480,128]{1,0:T(8,128)(2,1)S(1)}, bf16[480,128]{1,0:T(8,128)(2,1)S(1)}, u32[]{:S(2)}, u32[]{:S(2)}) collective-permute-start(bf16[480,128]{1,0:T(8,128)(2,1)S(1)} %get-tuple-element.48), channel_id=1, source_target_pairs={{0,4},{4,0},{8,12},{12,8},{16,20},{20,16},{24,28},{28,24},{1,5},{5... | collective-permute-start | bytes 368648 | tf_op jit(solution)/shard_map/ppermute | solution.py:333
  30.8 6.3 %collective-permute-start.10 = (bf16[192,128]{1,0:T(8,128)(2,1)S(1)}, bf16[192,128]{1,0:T(8,128)(2,1)S(1)}, u32[]{:S(2)}, u32[]{:S(2)}) collective-permute-start(bf16[192,128]{1,0:T(8,128)(2,1)S(1)} %get-tuple-element.45), channel_id=1, source_target_pairs={{0,16},{4,20},{8,24},{12,28},{16,0},{20,4},{24,8},{28,12},{1,17},{... | collective-permute-start | bytes 147464 | tf_op jit(solution)/shard_map/ppermute | solution.py:333
  30.8 6.6 %collective-permute-start.11 = (bf16[192,128]{1,0:T(8,128)(2,1)S(1)}, bf16[192,128]{1,0:T(8,128)(2,1)S(1)}, u32[]{:S(2)}, u32[]{:S(2)}) collective-permute-start(bf16[192,128]{1,0:T(8,128)(2,1)S(1)} %get-tuple-element.46), channel_id=1, source_target_pairs={{0,20},{4,16},{8,28},{12,24},{16,4},{20,0},{24,12},{28,8},{1,21},{... | collective-permute-start | bytes 147464 | tf_op jit(solution)/shard_map/ppermute | solution.py:333
  33.7 7.6 %collective-permute-start.8 = (bf16[480,128]{1,0:T(8,128)(2,1)S(1)}, bf16[480,128]{1,0:T(8,128)(2,1)S(1)}, u32[]{:S(2)}, u32[]{:S(2)}) collective-permute-start(bf16[480,128]{1,0:T(8,128)(2,1)S(1)} %get-tuple-element.42), channel_id=1, source_target_pairs={{0,4},{4,0},{8,12},{12,8},{16,20},{20,16},{24,28},{28,24},{1,5},{5... | collective-permute-start | bytes 368648 | tf_op jit(solution)/shard_map/ppermute | solution.py:333
  37.8 6.8 %collective-permute-start.14 = (bf16[96,480]{1,0:T(8,128)(2,1)S(1)}, bf16[96,480]{1,0:T(8,128)(2,1)S(1)}, u32[]{:S(2)}, u32[]{:S(2)}) collective-permute-start(bf16[96,480]{1,0:T(8,128)(2,1)S(1)} %get-tuple-element.51), channel_id=1, source_target_pairs={{0,8},{4,12},{8,0},{12,4},{16,24},{20,28},{24,16},{28,20},{1,9},{5... | collective-permute-start | bytes 276488 | tf_op jit(solution)/shard_map/ppermute | solution.py:333
  41.7 4.7 %collective-permute-start.13 = (bf16[96,480]{1,0:T(8,128)(2,1)S(1)}, bf16[96,480]{1,0:T(8,128)(2,1)S(1)}, u32[]{:S(2)}, u32[]{:S(2)}) collective-permute-start(bf16[96,480]{1,0:T(8,128)(2,1)S(1)} %get-tuple-element.50), channel_id=1, source_target_pairs={{0,8},{4,12},{8,0},{12,4},{16,24},{20,28},{24,16},{28,20},{1,9},{5... | collective-permute-start | bytes 276488 | tf_op jit(solution)/shard_map/ppermute | solution.py:333

commit v7 on v6

--- a/solution.py
+++ b/solution.py
@@ -201,26 +201,27 @@
     q_buf[...] = dot_nn(p_buf[...], wq[...]).astype(BF16)
     k_buf[...] = dot_nn(p_buf[...], wk[...]).astype(BF16)
     scale = 1.0 / DH**0.5
-    for h in range(HEADS):
-        cols = slice(h * DH, (h + 1) * DH)
-        scores = dot_nt(k_buf[:, cols], q_buf[:, cols]) * scale
-        expo = jnp.exp(scores - jnp.max(scores, axis=0, keepdims=True))
+    heads = [slice(h * DH, (h + 1) * DH) for h in range(HEADS)]
+    scores = [dot_nt(k_buf[:, cols], q_buf[:, cols]) * scale for cols in heads]
+    for h, score in enumerate(scores):
+        expo = jnp.exp(score - jnp.max(score, axis=0, keepdims=True))
         probs_buf[h] = expo / jnp.sum(expo, axis=0, keepdims=True)
     copies[0].wait()
     v_buf[...] = dot_nn(p_buf[...], wv[...]).astype(BF16)
     copies[1].wait()
     ga_buf[...] = dot_nt(wo[...], c_buf[...]).astype(BF16)
-    for h in range(HEADS):
-        cols = slice(h * DH, (h + 1) * DH)
-        q, k, v, ga = q_buf[:, cols], k_buf[:, cols], v_buf[:, cols], ga_buf[cols, :]
-        probs = probs_buf[h]
-        probs_b = probs.astype(BF16)
-        out = dot_tn(v, probs_b).astype(BF16)
-        delta = jnp.sum(ga.astype(F32) * out.astype(F32), axis=0, keepdims=True)
-        grad_score = (probs * (dot_nn(v, ga) - delta) * scale).astype(BF16)
-        gq_buf[:, cols] = dot_tn(grad_score, k).astype(BF16)
-        gk_buf[:, cols] = dot_nn(grad_score, q).astype(BF16)
-        gv_buf[:, cols] = dot_nt(probs_b, ga).astype(BF16)
+    probs_b = [probs_buf[h].astype(BF16) for h in range(HEADS)]
+    outs = [dot_tn(v_buf[:, cols], p).astype(BF16) for cols, p in zip(heads, probs_b)]
+    terms = [dot_nn(v_buf[:, cols], ga_buf[cols, :]) for cols in heads]
+    for cols, p in zip(heads, probs_b):
+        gv_buf[:, cols] = dot_nt(p, ga_buf[cols, :]).astype(BF16)
+    slopes = []
+    for h, cols in enumerate(heads):
+        delta = jnp.sum(ga_buf[cols, :].astype(F32) * outs[h].astype(F32), axis=0, keepdims=True)
+        slopes.append((probs_buf[h] * (terms[h] - delta) * scale).astype(BF16))
+    for cols, slope in zip(heads, slopes):
+        gk_buf[:, cols] = dot_nn(slope, q_buf[:, cols]).astype(BF16)
+        gq_buf[:, cols] = dot_tn(slope, k_buf[:, cols]).astype(BF16)
     grad = jnp.transpose(c_buf[...].astype(F32))
     for src, weight in ((gq_buf, wq), (gk_buf, wk), (gv_buf, wv)):
         grad = grad + dot_nt(weight[...], src[...])

time: 47.6 us -> 47.6 us (level)
  Pallas kernels: 17 us -> 15.4 us
  waiting for transfers between devices: 10 us -> 11.6 us
    ppermute x15, waiting for transfers between devices: 10 us -> 11.6 us  [swap(): return lax.ppermute(value, axis, [(i, i ^ bit) for i in range(count)])]
    pallas_call x11, Pallas kernels: 17 us -> 15.4 us  [call(): pl.pallas_call(body, out_shape=list(outs), scratch_shapes=list(scratch),...]
  transfers between devices with their start and end apart: 15 -> 15, of which waited for: 6 -> 6; matrix products, arithmetic and copies ran while one was open for 0% -> 0% of each run, Pallas kernels for 25% -> 22%
where the time goes in v7:
time: 47.6 us; the launch traced here: 47.4 us
  starting transfers between devices  19.6 us (41%)
  Pallas kernels  15.4 us (32%)
  waiting for transfers between devices  11.6 us (24%)
  between operations  0.75 us (2%)
    ppermute x15, starting transfers between devices, swap(): return lax.ppermute(value, axis, [(i, i ^ bit) for i in range(count)])  19.6 us
    pallas_call x11, Pallas kernels, call(): pl.pallas_call(body, out_shape=list(outs), scratch_shapes=list(scratch),...  15.4 us
    ppermute x15, waiting for transfers between devices, swap(): return lax.ppermute(value, axis, [(i, i ^ bit) for i in range(count)])  11.6 us
  transfers between devices with their start and end apart: 15, of which 6 were waited for; matrix products, arithmetic and copies ran while one was open for 0% of the time, Pallas kernels for 22%

profile of v7, /device:TPU:0, one launch (start us, length us, event | category | flops | bytes accessed | tf_op | source)
XLA Modules:
  0.0 47.4 jit_solution(8046132990173519392)
XLA Ops:
  0.6 0.0 slice-start
  0.6 0.0 slice-start.1
  0.7 2.8 %shard_map.113 = (f32[200,768]{1,0:T(8,128)S(1)}, f32[40,768]{1,0:T(8,128)S(1)}, f32[512,768]{1,0:T(8,128)S(1)}, f32[512,128]{1,0:T(8,128)S(1)}, bf16[768]{0:T(1...) custom-call(bf16[512,768]{1,0:T(8,128)(2,1)} %bitcast.6, s32[1,512]{1,0:T(1,128)} %base_hbm.1, bf16[4,768]{1,0:T(4,128)(2,1)} %table_hbm.1, ...), custom_call_target="tpu_custom_call" | custom-call | flops 3449999872 | tf_op jit(solution)/shard_map/pallas_call | solution.py:343
  3.5 0.2 shard_map.114
  3.7 0.0 slice-done
  3.7 0.1 slice-done.1
  3.8 1.2 %shard_map.115.refs_0_ = bf16[80,768]{1,0:T(8,128)(2,1)S(1)} custom-call(bf16[5,80,768]{2,1,0:T(8,128)(2,1)S(1)} %get-tuple-element.28.pairs, f32[40,768]{1,0:T(8,128)S(1)} %get-tuple-element.29.sums, bf16[5,768,768]{2,1,0:T(8,128)(2,1)S(1)} %bitcast.5, bf16[32,768]{1,0:T(8,128)(2,1)S(1)} %get-tuple-element.30.cot), custom_call_target="tpu_custom_call" | custom-call | flops 1150000000 | tf_op jit(solution)/shard_map/pallas_call | solution.py:343
  4.9 3.1 %collective-permute-start = (bf16[80,768]{1,0:T(8,128)(2,1)S(1)}, bf16[80,768]{1,0:T(8,128)(2,1)S(1)}, u32[]{:S(2)}, u32[]{:S(2)}) collective-permute-start(bf16[80,768]{1,0:T(8,128)(2,1)S(1)} %shard_map.115.refs_0_), channel_id=1, source_target_pairs={{0,2},{1,3},{2,0},{3,1},{4,6},{5,7},{6,4},{7,5},{8,10},{9,11},{10,... | collective-permute-start | bytes 368648 | tf_op jit(solution)/shard_map/ppermute | solution.py:334
  8.0 0.1 collective-permute-start.3
  8.1 0.0 collective-permute-start.4
  8.1 2.1 %collective-permute-start.5 = (bf16[40,960]{1,0:T(8,128)(2,1)S(1)}, bf16[40,960]{1,0:T(8,128)(2,1)S(1)}, u32[]{:S(2)}, u32[]{:S(2)}) collective-permute-start(bf16[40,960]{1,0:T(8,128)(2,1)S(1)} %get-tuple-element.41), channel_id=1, source_target_pairs={{0,3},{1,2},{2,1},{3,0},{4,7},{5,6},{6,5},{7,4},{8,11},{9,10},{10,... | collective-permute-start | bytes 230408 | tf_op jit(solution)/shard_map/ppermute | solution.py:334
  10.1 0.0 collective-permute-start.1
  10.1 2.0 %collective-permute-done.refs_1_ = bf16[80,768]{1,0:T(8,128)(2,1)S(1)} collective-permute-done((bf16[80,768]{1,0:T(8,128)(2,1)S(1)}, bf16[80,768]{1,0:T(8,128)(2,1)S(1)}, u32[]{:S(2)}, u32[]{:S(2)}) %collective-permute-start) | collective-permute-done | bytes 122912 | tf_op jit(solution)/shard_map/ppermute | solution.py:334
  12.2 0.0 collective-permute-start.2
  12.2 1.8 %collective-permute-done.3.refs_1_ = bf16[40,960]{1,0:T(8,128)(2,1)S(1)} collective-permute-done((bf16[40,960]{1,0:T(8,128)(2,1)S(1)}, bf16[40,960]{1,0:T(8,128)(2,1)S(1)}, u32[]{:S(2)}, u32[]{:S(2)}) %collective-permute-start.3) | collective-permute-done | bytes 76832 | tf_op jit(solution)/shard_map/ppermute | solution.py:334
  13.9 0.0 collective-permute-done.4.refs_2_
  13.9 0.2 collective-permute-done.5.refs_3_
  14.1 0.0 copy-start
  14.1 0.0 copy-start.1
  14.1 0.3 shard_map.119.refs_0_
  14.4 2.8 %collective-permute-start.7 = (bf16[960,128]{1,0:T(8,128)(2,1)S(1)}, bf16[960,128]{1,0:T(8,128)(2,1)S(1)}, u32[]{:S(2)}, u32[]{:S(2)}) collective-permute-start(bf16[960,128]{1,0:T(8,128)(2,1)S(1)} %shard_map.119.refs_0_), channel_id=1, source_target_pairs={{0,16},{4,20},{8,24},{12,28},{16,0},{20,4},{24,8},{28,12},{1,17},{... | collective-permute-start | bytes 737288 | tf_op jit(solution)/shard_map/ppermute | solution.py:334
  17.1 1.5 %collective-permute-start.6 = (bf16[960,128]{1,0:T(8,128)(2,1)S(1)}, bf16[960,128]{1,0:T(8,128)(2,1)S(1)}, u32[]{:S(2)}, u32[]{:S(2)}) collective-permute-start(bf16[960,128]{1,0:T(8,128)(2,1)S(1)} %shard_map.119.refs_0_), channel_id=1, source_target_pairs={{0,4},{4,0},{8,12},{12,8},{16,20},{20,16},{24,28},{28,24},{1,5},{5... | collective-permute-start | bytes 737288 | tf_op jit(solution)/shard_map/ppermute | solution.py:334
  18.6 0.0 collective-permute-done.1.refs_2_
  18.6 0.0 collective-permute-done.2.refs_3_
  18.6 0.0 copy-done
  18.6 0.0 copy-done.1
  18.7 4.3 %shard_map.116 = (bf16[768,128]{1,0:T(8,128)(2,1)S(1)}, bf16[192,128]{1,0:T(8,128)(2,1)S(1)}, bf16[192,128]{1,0:T(8,128)(2,1)S(1)}, bf16[192,128]{1,0:T(8,128)(2,1)S(1)}, bf16[192,128]{1,0:T(8,128)(2,1)S(1)}) custom-call(bf16[80,768]{1,0:T(8,128)(2,1)S(1)} %shard_map.115.refs_0_, bf16[80,768]{1,0:T(8,128)(2,1)S(1)} %collective-permute-done.refs_1_, ...), custom_call_target="tpu_custom_call" | custom-call | flops 5750000128 | tf_op jit(solution)/shard_map/pallas_call | solution.py:343
  23.0 0.6 %collective-permute-start.9 = (bf16[192,128]{1,0:T(8,128)(2,1)S(1)}, bf16[192,128]{1,0:T(8,128)(2,1)S(1)}, u32[]{:S(2)}, u32[]{:S(2)}) collective-permute-start(bf16[192,128]{1,0:T(8,128)(2,1)S(1)} %get-tuple-element.44), channel_id=1, source_target_pairs={{0,4},{4,0},{8,12},{12,8},{16,20},{20,16},{24,28},{28,24},{1,5},{5... | collective-permute-start | bytes 147464 | tf_op jit(solution)/shard_map/ppermute | solution.py:334
  23.6 5.7 %collective-permute-done.7.value.refs_2_ = bf16[960,128]{1,0:T(8,128)(2,1)S(1)} collective-permute-done((bf16[960,128]{1,0:T(8,128)(2,1)S(1)}, bf16[960,128]{1,0:T(8,128)(2,1)S(1)}, u32[]{:S(2)}, u32[]{:S(2)}) %collective-permute-start.7) | collective-permute-done | bytes 245792 | tf_op jit(solution)/shard_map/ppermute | solution.py:334
  29.2 1.6 %collective-permute-start.12 = (bf16[480,128]{1,0:T(8,128)(2,1)S(1)}, bf16[480,128]{1,0:T(8,128)(2,1)S(1)}, u32[]{:S(2)}, u32[]{:S(2)}) collective-permute-start(bf16[480,128]{1,0:T(8,128)(2,1)S(1)} %get-tuple-element.48), channel_id=1, source_target_pairs={{0,4},{4,0},{8,12},{12,8},{16,20},{20,16},{24,28},{28,24},{1,5},{5... | collective-permute-start | bytes 368648 | tf_op jit(solution)/shard_map/ppermute | solution.py:334
  30.8 0.0 collective-permute-start.10
  30.8 2.8 %collective-permute-start.11 = (bf16[192,128]{1,0:T(8,128)(2,1)S(1)}, bf16[192,128]{1,0:T(8,128)(2,1)S(1)}, u32[]{:S(2)}, u32[]{:S(2)}) collective-permute-start(bf16[192,128]{1,0:T(8,128)(2,1)S(1)} %get-tuple-element.46), channel_id=1, source_target_pairs={{0,20},{4,16},{8,28},{12,24},{16,4},{20,0},{24,12},{28,8},{1,21},{... | collective-permute-start | bytes 147464 | tf_op jit(solution)/shard_map/ppermute | solution.py:334
  33.7 0.0 collective-permute-done.9.refs_5_
  33.7 1.5 %collective-permute-start.8 = (bf16[480,128]{1,0:T(8,128)(2,1)S(1)}, bf16[480,128]{1,0:T(8,128)(2,1)S(1)}, u32[]{:S(2)}, u32[]{:S(2)}) collective-permute-start(bf16[480,128]{1,0:T(8,128)(2,1)S(1)} %get-tuple-element.42), channel_id=1, source_target_pairs={{0,4},{4,0},{8,12},{12,8},{16,20},{20,16},{24,28},{28,24},{1,5},{5... | collective-permute-start | bytes 368648 | tf_op jit(solution)/shard_map/ppermute | solution.py:334
  35.2 1.9 %shard_map.117 = (bf16[200,768]{1,0:T(8,128)(2,1)S(1)}, bf16[200,768]{1,0:T(8,128)(2,1)S(1)}, bf16[40,768]{1,0:T(8,128)(2,1)S(1)}) custom-call(bf16[768,128]{1,0:T(8,128)(2,1)S(1)} %get-tuple-element.31.g_ref, bf16[5,768,768]{2,1,0:T(8,128)(2,1)S(1)} %bitcast.5), custom_call_target="tpu_custom_call" | custom-call | flops 1150000000 | tf_op jit(solution)/shard_map/pallas_call | solution.py:343
  37.2 0.0 collective-permute-done.10.refs_6_
  37.2 0.2 collective-permute-done.11.refs_7_
  37.4 0.0 collective-permute-done.6.refs_1_
  37.4 0.0 collective-permute-done.12.refs_3_
  37.4 0.4 shard_map.122
  37.8 3.5 %collective-permute-start.14 = (bf16[96,480]{1,0:T(8,128)(2,1)S(1)}, bf16[96,480]{1,0:T(8,128)(2,1)S(1)}, u32[]{:S(2)}, u32[]{:S(2)}) collective-permute-start(bf16[96,480]{1,0:T(8,128)(2,1)S(1)} %get-tuple-element.51), channel_id=1, source_target_pairs={{0,8},{4,12},{8,0},{12,4},{16,24},{20,28},{24,16},{28,20},{1,9},{5... | collective-permute-start | bytes 276488 | tf_op jit(solution)/shard_map/ppermute | solution.py:334
  41.3 0.0 collective-permute-done.8.refs_3_
  41.3 0.4 shard_map.121
  41.7 0.1 collective-permute-start.13
  41.8 2.9 %shard_map.118 = bf16[512,768]{1,0:T(8,128)(2,1)} custom-call(bf16[200,768]{1,0:T(8,128)(2,1)S(1)} %get-tuple-element.32.highs, bf16[200,768]{1,0:T(8,128)(2,1)S(1)} %get-tuple-element.33.lows, bf16[40,768]{1,0:T(8,128)(2,1)S(1)} %get-tuple-element.34.near, f32[512,768]{1,0:T(8,128)S(1)} %get-tuple-element.35.normed_ref, ...), custom_call_target="tpu_custom_call" | custom-call | flops 1150000000 | tf_op jit(solution)/shard_map/pallas_call | solution.py:343
  44.7 0.0 collective-permute-done.14.refs_3_
  44.7 1.7 %collective-permute-done.13.refs_2_ = bf16[96,480]{1,0:T(8,128)(2,1)S(1)} collective-permute-done((bf16[96,480]{1,0:T(8,128)(2,1)S(1)}, bf16[96,480]{1,0:T(8,128)(2,1)S(1)}, u32[]{:S(2)}, u32[]{:S(2)}) %collective-permute-start.13) | collective-permute-done | bytes 92192 | tf_op jit(solution)/shard_map/ppermute | solution.py:334
  46.4 1.1 %shard_map.123 = f32[5,192,96]{2,1,0:T(8,128)} custom-call(f32[96,480]{1,0:T(8,128)S(1)} %get-tuple-element.47.refs_0_, f32[96,480]{1,0:T(8,128)S(1)} %get-tuple-element.49.refs_1_, bf16[96,480]{1,0:T(8,128)(2,1)S(1)} %collective-permute-done.13.refs_2_, bf16[96,480]{1,0:T(8,128)(2,1)S(1)} %collective-permute-done.14.refs_3_), custom_call_target="tpu_custom_call" | custom-call | flops 1150000000 | tf_op jit(solution)/shard_map/pallas_call | solution.py:343
  (2 shorter events, 0.0 us)
Async XLA Ops:
  0.6 3.0 %slice-start = ((s8[5898240]{0:T(1024)(128)(4,1)}), s8[4194304]{0:T(1024)(128)(4,1)S(1)}, s32[]{:S(2)}) async-start(s8[5898240]{0:T(1024)(128)(4,1)} %bitcast.4), calls=%async_computation | async-start | bytes 8388608
  0.6 3.1 %slice-start.1 = ((s8[5898240]{0:T(1024)(128)(4,1)}), s8[1703936]{0:T(1024)(128)(4,1)S(1)}, s32[]{:S(2)}) async-start(s8[5898240]{0:T(1024)(128)(4,1)} %bitcast.4), calls=%async_computation.1 | async-start | bytes 3407872
  4.9 7.2 %collective-permute-start = (bf16[80,768]{1,0:T(8,128)(2,1)S(1)}, bf16[80,768]{1,0:T(8,128)(2,1)S(1)}, u32[]{:S(2)}, u32[]{:S(2)}) collective-permute-start(bf16[80,768]{1,0:T(8,128)(2,1)S(1)} %shard_map.115.refs_0_), channel_id=1, source_target_pairs={{0,2},{1,3},{2,0},{3,1},{4,6},{5,7},{6,4},{7,5},{8,10},{9,11},{10,... | collective-permute-start | bytes 368648 | tf_op jit(solution)/shard_map/ppermute | solution.py:334
  8.0 5.9 %collective-permute-start.3 = (bf16[40,960]{1,0:T(8,128)(2,1)S(1)}, bf16[40,960]{1,0:T(8,128)(2,1)S(1)}, u32[]{:S(2)}, u32[]{:S(2)}) collective-permute-start(bf16[40,960]{1,0:T(8,128)(2,1)S(1)} %get-tuple-element.39), channel_id=1, source_target_pairs={{0,2},{1,3},{2,0},{3,1},{4,6},{5,7},{6,4},{7,5},{8,10},{9,11},{10,... | collective-permute-start | bytes 230408 | tf_op jit(solution)/shard_map/ppermute | solution.py:334
  8.1 5.9 %collective-permute-start.4 = (bf16[40,960]{1,0:T(8,128)(2,1)S(1)}, bf16[40,960]{1,0:T(8,128)(2,1)S(1)}, u32[]{:S(2)}, u32[]{:S(2)}) collective-permute-start(bf16[40,960]{1,0:T(8,128)(2,1)S(1)} %get-tuple-element.40), channel_id=1, source_target_pairs={{0,1},{1,0},{2,3},{3,2},{4,5},{5,4},{6,7},{7,6},{8,9},{9,8},{10,11... | collective-permute-start | bytes 230408 | tf_op jit(solution)/shard_map/ppermute | solution.py:334
  8.1 6.0 %collective-permute-start.5 = (bf16[40,960]{1,0:T(8,128)(2,1)S(1)}, bf16[40,960]{1,0:T(8,128)(2,1)S(1)}, u32[]{:S(2)}, u32[]{:S(2)}) collective-permute-start(bf16[40,960]{1,0:T(8,128)(2,1)S(1)} %get-tuple-element.41), channel_id=1, source_target_pairs={{0,3},{1,2},{2,1},{3,0},{4,7},{5,6},{6,5},{7,4},{8,11},{9,10},{10,... | collective-permute-start | bytes 230408 | tf_op jit(solution)/shard_map/ppermute | solution.py:334
  10.1 8.5 %collective-permute-start.1 = (bf16[80,768]{1,0:T(8,128)(2,1)S(1)}, bf16[80,768]{1,0:T(8,128)(2,1)S(1)}, u32[]{:S(2)}, u32[]{:S(2)}) collective-permute-start(bf16[80,768]{1,0:T(8,128)(2,1)S(1)} %shard_map.115.refs_0_), channel_id=1, source_target_pairs={{0,1},{1,0},{2,3},{3,2},{4,5},{5,4},{6,7},{7,6},{8,9},{9,8},{10,11... | collective-permute-start | bytes 368648 | tf_op jit(solution)/shard_map/ppermute | solution.py:334
  12.2 6.5 %collective-permute-start.2 = (bf16[80,768]{1,0:T(8,128)(2,1)S(1)}, bf16[80,768]{1,0:T(8,128)(2,1)S(1)}, u32[]{:S(2)}, u32[]{:S(2)}) collective-permute-start(bf16[80,768]{1,0:T(8,128)(2,1)S(1)} %collective-permute-done.refs_1_), channel_id=1, source_target_pairs={{0,1},{1,0},{2,3},{3,2},{4,5},{5,4},{6,7},{7,6},{8,9},{9,8},{10,11... | collective-permute-start | bytes 368648 | tf_op jit(solution)/shard_map/ppermute | solution.py:334
  14.1 4.6 %copy-start = (bf16[768,768]{1,0:T(8,128)(2,1)S(1)}, bf16[768,768]{1,0:T(8,128)(2,1)}, u32[]{:S(2)}) copy-start(bf16[768,768]{1,0:T(8,128)(2,1)} %refs_4_.1) | copy-start | bytes 3538948
  14.1 4.6 %copy-start.1 = (bf16[768,768]{1,0:T(8,128)(2,1)S(1)}, bf16[768,768]{1,0:T(8,128)(2,1)}, u32[]{:S(2)}) copy-start(bf16[768,768]{1,0:T(8,128)(2,1)} %refs_5_.1) | copy-start | bytes 3538948
  14.4 14.8 %collective-permute-start.7 = (bf16[960,128]{1,0:T(8,128)(2,1)S(1)}, bf16[960,128]{1,0:T(8,128)(2,1)S(1)}, u32[]{:S(2)}, u32[]{:S(2)}) collective-permute-start(bf16[960,128]{1,0:T(8,128)(2,1)S(1)} %shard_map.119.refs_0_), channel_id=1, source_target_pairs={{0,16},{4,20},{8,24},{12,28},{16,0},{20,4},{24,8},{28,12},{1,17},{... | collective-permute-start | bytes 737288 | tf_op jit(solution)/shard_map/ppermute | solution.py:334
  17.1 20.3 %collective-permute-start.6 = (bf16[960,128]{1,0:T(8,128)(2,1)S(1)}, bf16[960,128]{1,0:T(8,128)(2,1)S(1)}, u32[]{:S(2)}, u32[]{:S(2)}) collective-permute-start(bf16[960,128]{1,0:T(8,128)(2,1)S(1)} %shard_map.119.refs_0_), channel_id=1, source_target_pairs={{0,4},{4,0},{8,12},{12,8},{16,20},{20,16},{24,28},{28,24},{1,5},{5... | collective-permute-start | bytes 737288 | tf_op jit(solution)/shard_map/ppermute | solution.py:334
  23.0 10.7 %collective-permute-start.9 = (bf16[192,128]{1,0:T(8,128)(2,1)S(1)}, bf16[192,128]{1,0:T(8,128)(2,1)S(1)}, u32[]{:S(2)}, u32[]{:S(2)}) collective-permute-start(bf16[192,128]{1,0:T(8,128)(2,1)S(1)} %get-tuple-element.44), channel_id=1, source_target_pairs={{0,4},{4,0},{8,12},{12,8},{16,20},{20,16},{24,28},{28,24},{1,5},{5... | collective-permute-start | bytes 147464 | tf_op jit(solution)/shard_map/ppermute | solution.py:334
  29.2 8.2 %collective-permute-start.12 = (bf16[480,128]{1,0:T(8,128)(2,1)S(1)}, bf16[480,128]{1,0:T(8,128)(2,1)S(1)}, u32[]{:S(2)}, u32[]{:S(2)}) collective-permute-start(bf16[480,128]{1,0:T(8,128)(2,1)S(1)} %get-tuple-element.48), channel_id=1, source_target_pairs={{0,4},{4,0},{8,12},{12,8},{16,20},{20,16},{24,28},{28,24},{1,5},{5... | collective-permute-start | bytes 368648 | tf_op jit(solution)/shard_map/ppermute | solution.py:334
  30.8 6.3 %collective-permute-start.10 = (bf16[192,128]{1,0:T(8,128)(2,1)S(1)}, bf16[192,128]{1,0:T(8,128)(2,1)S(1)}, u32[]{:S(2)}, u32[]{:S(2)}) collective-permute-start(bf16[192,128]{1,0:T(8,128)(2,1)S(1)} %get-tuple-element.45), channel_id=1, source_target_pairs={{0,16},{4,20},{8,24},{12,28},{16,0},{20,4},{24,8},{28,12},{1,17},{... | collective-permute-start | bytes 147464 | tf_op jit(solution)/shard_map/ppermute | solution.py:334
  30.8 6.6 %collective-permute-start.11 = (bf16[192,128]{1,0:T(8,128)(2,1)S(1)}, bf16[192,128]{1,0:T(8,128)(2,1)S(1)}, u32[]{:S(2)}, u32[]{:S(2)}) collective-permute-start(bf16[192,128]{1,0:T(8,128)(2,1)S(1)} %get-tuple-element.46), channel_id=1, source_target_pairs={{0,20},{4,16},{8,28},{12,24},{16,4},{20,0},{24,12},{28,8},{1,21},{... | collective-permute-start | bytes 147464 | tf_op jit(solution)/shard_map/ppermute | solution.py:334
  33.7 7.6 %collective-permute-start.8 = (bf16[480,128]{1,0:T(8,128)(2,1)S(1)}, bf16[480,128]{1,0:T(8,128)(2,1)S(1)}, u32[]{:S(2)}, u32[]{:S(2)}) collective-permute-start(bf16[480,128]{1,0:T(8,128)(2,1)S(1)} %get-tuple-element.42), channel_id=1, source_target_pairs={{0,4},{4,0},{8,12},{12,8},{16,20},{20,16},{24,28},{28,24},{1,5},{5... | collective-permute-start | bytes 368648 | tf_op jit(solution)/shard_map/ppermute | solution.py:334
  37.8 6.8 %collective-permute-start.14 = (bf16[96,480]{1,0:T(8,128)(2,1)S(1)}, bf16[96,480]{1,0:T(8,128)(2,1)S(1)}, u32[]{:S(2)}, u32[]{:S(2)}) collective-permute-start(bf16[96,480]{1,0:T(8,128)(2,1)S(1)} %get-tuple-element.51), channel_id=1, source_target_pairs={{0,8},{4,12},{8,0},{12,4},{16,24},{20,28},{24,16},{28,20},{1,9},{5... | collective-permute-start | bytes 276488 | tf_op jit(solution)/shard_map/ppermute | solution.py:334
  41.7 4.7 %collective-permute-start.13 = (bf16[96,480]{1,0:T(8,128)(2,1)S(1)}, bf16[96,480]{1,0:T(8,128)(2,1)S(1)}, u32[]{:S(2)}, u32[]{:S(2)}) collective-permute-start(bf16[96,480]{1,0:T(8,128)(2,1)S(1)} %get-tuple-element.50), channel_id=1, source_target_pairs={{0,8},{4,12},{8,0},{12,4},{16,24},{20,28},{24,16},{28,20},{1,9},{5... | collective-permute-start | bytes 276488 | tf_op jit(solution)/shard_map/ppermute | solution.py:334

commit v8 on v7

--- a/solution.py
+++ b/solution.py
@@ -232,8 +232,13 @@
     me = lax.axis_index("dp")
     for o in range(count):
         turn[o ^ me] = turned[o * span : (o + 1) * span, :]
-    for gt, base in zip(gts, near_rels):
-        for at, rel in enumerate(late):
+    for at, rel in enumerate(late):
+        gts[0][at * span : (at + 1) * span, :] = turn[rel]
+    half = len(late) // 2
+    core = lax.axis_index("ctx") % 2
+    for gt, base in zip(gts[1:], near_rels[1:]):
+        for at in range(half):
+            rel = pick(core, [late[at], late[half + at]])
             gt[at * span : (at + 1) * span, :] = turn[base ^ rel]
 
 
@@ -291,13 +296,20 @@
 
 
 def kernel_grad_kernel(factor, begin, *refs):
-    count = len(refs) // 2 - 1
-    acts, gts, (mine, theirs) = refs[:count], refs[count : 2 * count], refs[2 * count :]
+    *refs, mine, theirs = refs
+    count = (len(refs) + 1) // 3
+    acts, own, refs = refs[:count], refs[count], refs[count + 1 :]
+    first = lax.axis_index("ctx") % 2 == 0
+    gts = [own[...]]
+    for here, other in zip(refs[: count - 1], refs[count - 1 :]):
+        turned = pltpu.roll(other[...].astype(F32), other.shape[1] // 2, axis=1)
+        a, b = here[...], turned.astype(BF16)
+        gts.append(jnp.concatenate([jnp.where(first, a, b), jnp.where(first, b, a)], axis=0))
     span, size = mine.shape
     total = None
     for act, gt in zip(acts, gts):
         at = begin if act.shape[0] > size else 0
-        term = dot_nt(gt[...], act[at : at + size, :])
+        term = dot_nt(gt, act[at : at + size, :])
         total = term if total is None else total + term
     total = total * factor
     mine[...] = total[:span, :]
@@ -451,8 +463,8 @@
     g_all, *gts = call(
         functools.partial(attention_kernel, pool, order, tok_rows, near_rels, late),
         [*rows, w_query, w_key] + outside(w_value, w_out),
-        [pltpu.VMEM((channels, tokens), BF16)]
-        + [pltpu.VMEM((len(late) * narrow, tokens), BF16)] * len(near_rels),
+        [pltpu.VMEM((channels, tokens), BF16), pltpu.VMEM((len(late) * narrow, tokens), BF16)]
+        + [pltpu.VMEM((len(late) // 2 * narrow, tokens), BF16)] * (len(near_rels) - 1),
         [pltpu.VMEM((tokens, channels), BF16)] * 5
         + [pltpu.VMEM((channels, tokens), BF16)]
         + [pltpu.VMEM((tokens, channels), BF16)] * 3
@@ -475,9 +487,10 @@
     act_zx = list(act_zx)
     for at, value in enumerate(act_zx):
         act_zx[at] = swap(value, "dp", X_BIT)
-    swapped = [gts[0]]
+    swapped, shared = [], []
     for at, rel in enumerate(near_rels[1:], 1):
         swapped.append(swap(gts[at], "dp", rel))
+        shared.append(swap(swapped[-1], "ctx", 1))
 
     padded = -(-(tok_rows + 2) // 8) * 8
     highs, lows, near_g = call(
@@ -492,7 +505,7 @@
         kept = len(late) // 2
         mine, theirs = call(
             functools.partial(kernel_grad_kernel, factor, cuts[at]),
-            (act, act_x, act_z, act_zx[at], *swapped),
+            (act, act_x, act_z, act_zx[at], gts[0], *swapped, *shared),
             [pltpu.VMEM((kept * narrow, size), F32), pltpu.VMEM((kept * narrow, size), BF16)],
         )
         other = swap(theirs, "dp", late[kept])

time: 47.6 us -> 44.4 us (0.933)
  waiting for transfers between devices: 11.6 us -> 8.89 us
    ppermute x15 -> x18, waiting for transfers between devices: 11.6 us -> 8.89 us  [swap(): return lax.ppermute(value, axis, [(i, i ^ bit) for i in range(count)])]
    ppermute x15 -> x18, starting transfers between devices: 19.6 us -> 19.2 us  [swap(): return lax.ppermute(value, axis, [(i, i ^ bit) for i in range(count)])]
  transfers between devices with their start and end apart: 15 -> 18, of which waited for: 6 -> 8; matrix products, arithmetic and copies ran while one was open for 0% -> 0% of each run, Pallas kernels for 22% -> 23%
where the time goes in v8:
time: 44.4 us; the launch traced here: 44.2 us
  starting transfers between devices  19.2 us (43%)
  Pallas kernels  15.3 us (34%)
  waiting for transfers between devices  8.89 us (20%)
  between operations  0.77 us (2%)
    ppermute x18, starting transfers between devices, swap(): return lax.ppermute(value, axis, [(i, i ^ bit) for i in range(count)])  19.2 us
    pallas_call x11, Pallas kernels, call(): pl.pallas_call(body, out_shape=list(outs), scratch_shapes=list(scratch),...  15.3 us
    ppermute x18, waiting for transfers between devices, swap(): return lax.ppermute(value, axis, [(i, i ^ bit) for i in range(count)])  8.89 us
  transfers between devices with their start and end apart: 18, of which 8 were waited for; matrix products, arithmetic and copies ran while one was open for 0% of the time, Pallas kernels for 23%

profile of v8, /device:TPU:0, one launch (start us, length us, event | category | flops | bytes accessed | tf_op | source)
XLA Modules:
  0.0 44.2 jit_solution(17109779859601710619)
XLA Ops:
  0.6 0.0 slice-start
  0.6 0.0 slice-start.1
  0.7 2.8 %shard_map.113 = (f32[200,768]{1,0:T(8,128)S(1)}, f32[40,768]{1,0:T(8,128)S(1)}, f32[512,768]{1,0:T(8,128)S(1)}, f32[512,128]{1,0:T(8,128)S(1)}, bf16[768]{0:T(1...) custom-call(bf16[512,768]{1,0:T(8,128)(2,1)} %bitcast.6, s32[1,512]{1,0:T(1,128)} %base_hbm.1, bf16[4,768]{1,0:T(4,128)(2,1)} %table_hbm.1, ...), custom_call_target="tpu_custom_call" | custom-call | flops 3449999872 | tf_op jit(solution)/shard_map/pallas_call | solution.py:355
  3.5 0.2 shard_map.114
  3.7 0.1 slice-done.1
  3.8 1.2 %shard_map.115.refs_0_ = bf16[80,768]{1,0:T(8,128)(2,1)S(1)} custom-call(bf16[5,80,768]{2,1,0:T(8,128)(2,1)S(1)} %get-tuple-element.28.pairs, f32[40,768]{1,0:T(8,128)S(1)} %get-tuple-element.29.sums, bf16[5,768,768]{2,1,0:T(8,128)(2,1)S(1)} %bitcast.5, bf16[32,768]{1,0:T(8,128)(2,1)S(1)} %get-tuple-element.30.cot), custom_call_target="tpu_custom_call" | custom-call | flops 1150000000 | tf_op jit(solution)/shard_map/pallas_call | solution.py:355
  4.9 3.1 %collective-permute-start = (bf16[80,768]{1,0:T(8,128)(2,1)S(1)}, bf16[80,768]{1,0:T(8,128)(2,1)S(1)}, u32[]{:S(2)}, u32[]{:S(2)}) collective-permute-start(bf16[80,768]{1,0:T(8,128)(2,1)S(1)} %shard_map.115.refs_0_), channel_id=1, source_target_pairs={{0,2},{1,3},{2,0},{3,1},{4,6},{5,7},{6,4},{7,5},{8,10},{9,11},{10,... | collective-permute-start | bytes 368648 | tf_op jit(solution)/shard_map/ppermute | solution.py:346
  8.0 0.1 collective-permute-start.3
  8.1 0.0 collective-permute-start.4
  8.1 2.1 %collective-permute-start.5 = (bf16[40,960]{1,0:T(8,128)(2,1)S(1)}, bf16[40,960]{1,0:T(8,128)(2,1)S(1)}, u32[]{:S(2)}, u32[]{:S(2)}) collective-permute-start(bf16[40,960]{1,0:T(8,128)(2,1)S(1)} %get-tuple-element.41), channel_id=1, source_target_pairs={{0,3},{1,2},{2,1},{3,0},{4,7},{5,6},{6,5},{7,4},{8,11},{9,10},{10,... | collective-permute-start | bytes 230408 | tf_op jit(solution)/shard_map/ppermute | solution.py:346
  10.1 0.0 collective-permute-start.1
  10.1 2.0 %collective-permute-done.refs_1_ = bf16[80,768]{1,0:T(8,128)(2,1)S(1)} collective-permute-done((bf16[80,768]{1,0:T(8,128)(2,1)S(1)}, bf16[80,768]{1,0:T(8,128)(2,1)S(1)}, u32[]{:S(2)}, u32[]{:S(2)}) %collective-permute-start) | collective-permute-done | bytes 122912 | tf_op jit(solution)/shard_map/ppermute | solution.py:346
  12.2 0.0 collective-permute-start.2
  12.2 1.8 %collective-permute-done.3.refs_1_ = bf16[40,960]{1,0:T(8,128)(2,1)S(1)} collective-permute-done((bf16[40,960]{1,0:T(8,128)(2,1)S(1)}, bf16[40,960]{1,0:T(8,128)(2,1)S(1)}, u32[]{:S(2)}, u32[]{:S(2)}) %collective-permute-start.3) | collective-permute-done | bytes 76832 | tf_op jit(solution)/shard_map/ppermute | solution.py:346
  13.9 0.0 collective-permute-done.4.refs_2_
  13.9 0.2 collective-permute-done.5.refs_3_
  14.1 0.3 shard_map.119.refs_0_
  14.4 2.8 %collective-permute-start.7 = (bf16[960,128]{1,0:T(8,128)(2,1)S(1)}, bf16[960,128]{1,0:T(8,128)(2,1)S(1)}, u32[]{:S(2)}, u32[]{:S(2)}) collective-permute-start(bf16[960,128]{1,0:T(8,128)(2,1)S(1)} %shard_map.119.refs_0_), channel_id=1, source_target_pairs={{0,16},{4,20},{8,24},{12,28},{16,0},{20,4},{24,8},{28,12},{1,17},{... | collective-permute-start | bytes 737288 | tf_op jit(solution)/shard_map/ppermute | solution.py:346
  17.1 0.0 collective-permute-done.1.refs_2_
  17.1 0.0 collective-permute-done.2.refs_3_
  17.2 4.1 %shard_map.116 = (bf16[768,128]{1,0:T(8,128)(2,1)S(1)}, bf16[192,128]{1,0:T(8,128)(2,1)S(1)}, bf16[96,128]{1,0:T(8,128)(2,1)S(1)}, bf16[96,128]{1,0:T(8,128)(2,1)S(1)}, bf16[96,128]{1,0:T(8,128)(2,1)S(1)}) custom-call(bf16[80,768]{1,0:T(8,128)(2,1)S(1)} %shard_map.115.refs_0_, bf16[80,768]{1,0:T(8,128)(2,1)S(1)} %collective-permute-done.refs_1_, ...), custom_call_target="tpu_custom_call" | custom-call | flops 5750000128 | tf_op jit(solution)/shard_map/pallas_call | solution.py:355
  21.3 1.6 %collective-permute-start.9 = (bf16[96,128]{1,0:T(8,128)(2,1)S(1)}, bf16[96,128]{1,0:T(8,128)(2,1)S(1)}, u32[]{:S(2)}, u32[]{:S(2)}) collective-permute-start(bf16[96,128]{1,0:T(8,128)(2,1)S(1)} %get-tuple-element.44), channel_id=1, source_target_pairs={{0,4},{4,0},{8,12},{12,8},{16,20},{20,16},{24,28},{28,24},{1,5},{5... | collective-permute-start | bytes 73736 | tf_op jit(solution)/shard_map/ppermute | solution.py:346
  22.9 0.5 %collective-permute-start.6 = (bf16[960,128]{1,0:T(8,128)(2,1)S(1)}, bf16[960,128]{1,0:T(8,128)(2,1)S(1)}, u32[]{:S(2)}, u32[]{:S(2)}) collective-permute-start(bf16[960,128]{1,0:T(8,128)(2,1)S(1)} %shard_map.119.refs_0_), channel_id=1, source_target_pairs={{0,4},{4,0},{8,12},{12,8},{16,20},{20,16},{24,28},{28,24},{1,5},{5... | collective-permute-start | bytes 737288 | tf_op jit(solution)/shard_map/ppermute | solution.py:346
  23.4 1.2 %collective-permute-start.10 = (bf16[96,128]{1,0:T(8,128)(2,1)S(1)}, bf16[96,128]{1,0:T(8,128)(2,1)S(1)}, u32[]{:S(2)}, u32[]{:S(2)}) collective-permute-start(bf16[96,128]{1,0:T(8,128)(2,1)S(1)} %get-tuple-element.45), channel_id=1, source_target_pairs={{0,16},{4,20},{8,24},{12,28},{16,0},{20,4},{24,8},{28,12},{1,17},{... | collective-permute-start | bytes 73736 | tf_op jit(solution)/shard_map/ppermute | solution.py:346
  24.6 2.6 %collective-permute-start.11 = (bf16[96,128]{1,0:T(8,128)(2,1)S(1)}, bf16[96,128]{1,0:T(8,128)(2,1)S(1)}, u32[]{:S(2)}, u32[]{:S(2)}) collective-permute-start(bf16[96,128]{1,0:T(8,128)(2,1)S(1)} %get-tuple-element.46), channel_id=1, source_target_pairs={{0,20},{4,16},{8,28},{12,24},{16,4},{20,0},{24,12},{28,8},{1,21},{... | collective-permute-start | bytes 73736 | tf_op jit(solution)/shard_map/ppermute | solution.py:346
  27.2 0.0 collective-permute-done.9.refs_5_
  27.2 0.0 collective-permute-start.12
  27.2 2.7 %collective-permute-done.7.value.refs_2_ = bf16[960,128]{1,0:T(8,128)(2,1)S(1)} collective-permute-done((bf16[960,128]{1,0:T(8,128)(2,1)S(1)}, bf16[960,128]{1,0:T(8,128)(2,1)S(1)}, u32[]{:S(2)}, u32[]{:S(2)}) %collective-permute-start.7) | collective-permute-done | bytes 245792 | tf_op jit(solution)/shard_map/ppermute | solution.py:346
  30.0 2.2 %collective-permute-start.8 = (bf16[480,128]{1,0:T(8,128)(2,1)S(1)}, bf16[480,128]{1,0:T(8,128)(2,1)S(1)}, u32[]{:S(2)}, u32[]{:S(2)}) collective-permute-start(bf16[480,128]{1,0:T(8,128)(2,1)S(1)} %get-tuple-element.42), channel_id=1, source_target_pairs={{0,4},{4,0},{8,12},{12,8},{16,20},{20,16},{24,28},{28,24},{1,5},{5... | collective-permute-start | bytes 368648 | tf_op jit(solution)/shard_map/ppermute | solution.py:346
  32.2 0.0 collective-permute-done.10.refs_6_
  32.2 0.0 collective-permute-start.13
  32.2 0.1 collective-permute-done.11.refs_7_
  32.3 0.4 collective-permute-start.14
  32.7 0.0 collective-permute-done.12.refs_8_
  32.7 0.4 collective-permute-start.15
  33.1 2.0 %shard_map.117 = (bf16[200,768]{1,0:T(8,128)(2,1)S(1)}, bf16[200,768]{1,0:T(8,128)(2,1)S(1)}, bf16[40,768]{1,0:T(8,128)(2,1)S(1)}) custom-call(bf16[768,128]{1,0:T(8,128)(2,1)S(1)} %get-tuple-element.31.g_ref, bf16[5,768,768]{2,1,0:T(8,128)(2,1)S(1)} %bitcast.5), custom_call_target="tpu_custom_call" | custom-call | flops 1150000000 | tf_op jit(solution)/shard_map/pallas_call | solution.py:355
  35.1 0.0 collective-permute-done.13.refs_9_
  35.1 0.0 collective-permute-done.14.refs_10_
  35.1 0.0 collective-permute-done.6.refs_1_
  35.1 0.8 %collective-permute-done.8.refs_3_ = bf16[480,128]{1,0:T(8,128)(2,1)S(1)} collective-permute-done((bf16[480,128]{1,0:T(8,128)(2,1)S(1)}, bf16[480,128]{1,0:T(8,128)(2,1)S(1)}, u32[]{:S(2)}, u32[]{:S(2)}) %collective-permute-start.8) | collective-permute-done | bytes 122912 | tf_op jit(solution)/shard_map/ppermute | solution.py:346
  35.9 0.4 %shard_map.121 = (f32[96,480]{1,0:T(8,128)S(1)}, bf16[96,480]{1,0:T(8,128)(2,1)S(1)}) custom-call(bf16[960,128]{1,0:T(8,128)(2,1)S(1)} %shard_map.119.refs_0_, bf16[960,128]{1,0:T(8,128)(2,1)S(1)} %collective-permute-done.6.refs_1_, bf16[960,128]{1,0:T(8,128)(2,1)S(1)} %collective-permute-done.7.value.refs_2_, ...), custom_call_target="tpu_custom_call" | custom-call | flops 1150000000 | tf_op jit(solution)/shard_map/pallas_call | solution.py:355
  36.3 1.2 %collective-permute-start.16 = (bf16[96,480]{1,0:T(8,128)(2,1)S(1)}, bf16[96,480]{1,0:T(8,128)(2,1)S(1)}, u32[]{:S(2)}, u32[]{:S(2)}) collective-permute-start(bf16[96,480]{1,0:T(8,128)(2,1)S(1)} %get-tuple-element.50), channel_id=1, source_target_pairs={{0,8},{4,12},{8,0},{12,4},{16,24},{20,28},{24,16},{28,20},{1,9},{5... | collective-permute-start | bytes 276488 | tf_op jit(solution)/shard_map/ppermute | solution.py:346
  37.5 0.5 %collective-permute-done.15.refs_3_ = bf16[480,128]{1,0:T(8,128)(2,1)S(1)} collective-permute-done((bf16[480,128]{1,0:T(8,128)(2,1)S(1)}, bf16[480,128]{1,0:T(8,128)(2,1)S(1)}, u32[]{:S(2)}, u32[]{:S(2)}) %collective-permute-start.15) | collective-permute-done | bytes 122912 | tf_op jit(solution)/shard_map/ppermute | solution.py:346
  38.0 0.4 shard_map.122
  38.5 1.1 %collective-permute-start.17 = (bf16[96,480]{1,0:T(8,128)(2,1)S(1)}, bf16[96,480]{1,0:T(8,128)(2,1)S(1)}, u32[]{:S(2)}, u32[]{:S(2)}) collective-permute-start(bf16[96,480]{1,0:T(8,128)(2,1)S(1)} %get-tuple-element.51), channel_id=1, source_target_pairs={{0,8},{4,12},{8,0},{12,4},{16,24},{20,28},{24,16},{28,20},{1,9},{5... | collective-permute-start | bytes 276488 | tf_op jit(solution)/shard_map/ppermute | solution.py:346
  39.5 2.8 %shard_map.118 = bf16[512,768]{1,0:T(8,128)(2,1)} custom-call(bf16[200,768]{1,0:T(8,128)(2,1)S(1)} %get-tuple-element.32.highs, bf16[200,768]{1,0:T(8,128)(2,1)S(1)} %get-tuple-element.33.lows, bf16[40,768]{1,0:T(8,128)(2,1)S(1)} %get-tuple-element.34.near, f32[512,768]{1,0:T(8,128)S(1)} %get-tuple-element.35.normed_ref, ...), custom_call_target="tpu_custom_call" | custom-call | flops 1150000000 | tf_op jit(solution)/shard_map/pallas_call | solution.py:355
  42.4 0.8 %collective-permute-done.17.refs_3_ = bf16[96,480]{1,0:T(8,128)(2,1)S(1)} collective-permute-done((bf16[96,480]{1,0:T(8,128)(2,1)S(1)}, bf16[96,480]{1,0:T(8,128)(2,1)S(1)}, u32[]{:S(2)}, u32[]{:S(2)}) %collective-permute-start.17) | collective-permute-done | bytes 92192 | tf_op jit(solution)/shard_map/ppermute | solution.py:346
  43.2 1.1 %shard_map.123 = f32[5,192,96]{2,1,0:T(8,128)} custom-call(f32[96,480]{1,0:T(8,128)S(1)} %get-tuple-element.47.refs_0_, f32[96,480]{1,0:T(8,128)S(1)} %get-tuple-element.49.refs_1_, bf16[96,480]{1,0:T(8,128)(2,1)S(1)} %collective-permute-done.16.refs_2_, bf16[96,480]{1,0:T(8,128)(2,1)S(1)} %collective-permute-done.17.refs_3_), custom_call_target="tpu_custom_call" | custom-call | flops 1150000000 | tf_op jit(solution)/shard_map/pallas_call | solution.py:355
  (8 shorter events, 0.0 us)
Async XLA Ops:
  0.6 3.0 %slice-start = ((s8[5898240]{0:T(1024)(128)(4,1)}), s8[4194304]{0:T(1024)(128)(4,1)S(1)}, s32[]{:S(2)}) async-start(s8[5898240]{0:T(1024)(128)(4,1)} %bitcast.4), calls=%async_computation | async-start | bytes 8388608
  0.6 3.1 %slice-start.1 = ((s8[5898240]{0:T(1024)(128)(4,1)}), s8[1703936]{0:T(1024)(128)(4,1)S(1)}, s32[]{:S(2)}) async-start(s8[5898240]{0:T(1024)(128)(4,1)} %bitcast.4), calls=%async_computation.1 | async-start | bytes 3407872
  4.9 7.2 %collective-permute-start = (bf16[80,768]{1,0:T(8,128)(2,1)S(1)}, bf16[80,768]{1,0:T(8,128)(2,1)S(1)}, u32[]{:S(2)}, u32[]{:S(2)}) collective-permute-start(bf16[80,768]{1,0:T(8,128)(2,1)S(1)} %shard_map.115.refs_0_), channel_id=1, source_target_pairs={{0,2},{1,3},{2,0},{3,1},{4,6},{5,7},{6,4},{7,5},{8,10},{9,11},{10,... | collective-permute-start | bytes 368648 | tf_op jit(solution)/shard_map/ppermute | solution.py:346
  8.0 5.9 %collective-permute-start.3 = (bf16[40,960]{1,0:T(8,128)(2,1)S(1)}, bf16[40,960]{1,0:T(8,128)(2,1)S(1)}, u32[]{:S(2)}, u32[]{:S(2)}) collective-permute-start(bf16[40,960]{1,0:T(8,128)(2,1)S(1)} %get-tuple-element.39), channel_id=1, source_target_pairs={{0,2},{1,3},{2,0},{3,1},{4,6},{5,7},{6,4},{7,5},{8,10},{9,11},{10,... | collective-permute-start | bytes 230408 | tf_op jit(solution)/shard_map/ppermute | solution.py:346
  8.1 5.9 %collective-permute-start.4 = (bf16[40,960]{1,0:T(8,128)(2,1)S(1)}, bf16[40,960]{1,0:T(8,128)(2,1)S(1)}, u32[]{:S(2)}, u32[]{:S(2)}) collective-permute-start(bf16[40,960]{1,0:T(8,128)(2,1)S(1)} %get-tuple-element.40), channel_id=1, source_target_pairs={{0,1},{1,0},{2,3},{3,2},{4,5},{5,4},{6,7},{7,6},{8,9},{9,8},{10,11... | collective-permute-start | bytes 230408 | tf_op jit(solution)/shard_map/ppermute | solution.py:346
  8.1 6.0 %collective-permute-start.5 = (bf16[40,960]{1,0:T(8,128)(2,1)S(1)}, bf16[40,960]{1,0:T(8,128)(2,1)S(1)}, u32[]{:S(2)}, u32[]{:S(2)}) collective-permute-start(bf16[40,960]{1,0:T(8,128)(2,1)S(1)} %get-tuple-element.41), channel_id=1, source_target_pairs={{0,3},{1,2},{2,1},{3,0},{4,7},{5,6},{6,5},{7,4},{8,11},{9,10},{10,... | collective-permute-start | bytes 230408 | tf_op jit(solution)/shard_map/ppermute | solution.py:346
  10.1 7.0 %collective-permute-start.1 = (bf16[80,768]{1,0:T(8,128)(2,1)S(1)}, bf16[80,768]{1,0:T(8,128)(2,1)S(1)}, u32[]{:S(2)}, u32[]{:S(2)}) collective-permute-start(bf16[80,768]{1,0:T(8,128)(2,1)S(1)} %shard_map.115.refs_0_), channel_id=1, source_target_pairs={{0,1},{1,0},{2,3},{3,2},{4,5},{5,4},{6,7},{7,6},{8,9},{9,8},{10,11... | collective-permute-start | bytes 368648 | tf_op jit(solution)/shard_map/ppermute | solution.py:346
  12.2 5.0 %collective-permute-start.2 = (bf16[80,768]{1,0:T(8,128)(2,1)S(1)}, bf16[80,768]{1,0:T(8,128)(2,1)S(1)}, u32[]{:S(2)}, u32[]{:S(2)}) collective-permute-start(bf16[80,768]{1,0:T(8,128)(2,1)S(1)} %collective-permute-done.refs_1_), channel_id=1, source_target_pairs={{0,1},{1,0},{2,3},{3,2},{4,5},{5,4},{6,7},{7,6},{8,9},{9,8},{10,11... | collective-permute-start | bytes 368648 | tf_op jit(solution)/shard_map/ppermute | solution.py:346
  14.1 3.1 %copy-start = (bf16[768,768]{1,0:T(8,128)(2,1)S(1)}, bf16[768,768]{1,0:T(8,128)(2,1)}, u32[]{:S(2)}) copy-start(bf16[768,768]{1,0:T(8,128)(2,1)} %refs_4_.1) | copy-start | bytes 3538948
  14.1 3.1 %copy-start.1 = (bf16[768,768]{1,0:T(8,128)(2,1)S(1)}, bf16[768,768]{1,0:T(8,128)(2,1)}, u32[]{:S(2)}) copy-start(bf16[768,768]{1,0:T(8,128)(2,1)} %refs_5_.1) | copy-start | bytes 3538948
  14.4 15.6 %collective-permute-start.7 = (bf16[960,128]{1,0:T(8,128)(2,1)S(1)}, bf16[960,128]{1,0:T(8,128)(2,1)S(1)}, u32[]{:S(2)}, u32[]{:S(2)}) collective-permute-start(bf16[960,128]{1,0:T(8,128)(2,1)S(1)} %shard_map.119.refs_0_), channel_id=1, source_target_pairs={{0,16},{4,20},{8,24},{12,28},{16,0},{20,4},{24,8},{28,12},{1,17},{... | collective-permute-start | bytes 737288 | tf_op jit(solution)/shard_map/ppermute | solution.py:346
  21.3 5.9 %collective-permute-start.9 = (bf16[96,128]{1,0:T(8,128)(2,1)S(1)}, bf16[96,128]{1,0:T(8,128)(2,1)S(1)}, u32[]{:S(2)}, u32[]{:S(2)}) collective-permute-start(bf16[96,128]{1,0:T(8,128)(2,1)S(1)} %get-tuple-element.44), channel_id=1, source_target_pairs={{0,4},{4,0},{8,12},{12,8},{16,20},{20,16},{24,28},{28,24},{1,5},{5... | collective-permute-start | bytes 73736 | tf_op jit(solution)/shard_map/ppermute | solution.py:346
  22.9 12.2 %collective-permute-start.6 = (bf16[960,128]{1,0:T(8,128)(2,1)S(1)}, bf16[960,128]{1,0:T(8,128)(2,1)S(1)}, u32[]{:S(2)}, u32[]{:S(2)}) collective-permute-start(bf16[960,128]{1,0:T(8,128)(2,1)S(1)} %shard_map.119.refs_0_), channel_id=1, source_target_pairs={{0,4},{4,0},{8,12},{12,8},{16,20},{20,16},{24,28},{28,24},{1,5},{5... | collective-permute-start | bytes 737288 | tf_op jit(solution)/shard_map/ppermute | solution.py:346
  23.4 8.8 %collective-permute-start.10 = (bf16[96,128]{1,0:T(8,128)(2,1)S(1)}, bf16[96,128]{1,0:T(8,128)(2,1)S(1)}, u32[]{:S(2)}, u32[]{:S(2)}) collective-permute-start(bf16[96,128]{1,0:T(8,128)(2,1)S(1)} %get-tuple-element.45), channel_id=1, source_target_pairs={{0,16},{4,20},{8,24},{12,28},{16,0},{20,4},{24,8},{28,12},{1,17},{... | collective-permute-start | bytes 73736 | tf_op jit(solution)/shard_map/ppermute | solution.py:346
  24.6 7.7 %collective-permute-start.11 = (bf16[96,128]{1,0:T(8,128)(2,1)S(1)}, bf16[96,128]{1,0:T(8,128)(2,1)S(1)}, u32[]{:S(2)}, u32[]{:S(2)}) collective-permute-start(bf16[96,128]{1,0:T(8,128)(2,1)S(1)} %get-tuple-element.46), channel_id=1, source_target_pairs={{0,20},{4,16},{8,28},{12,24},{16,4},{20,0},{24,12},{28,8},{1,21},{... | collective-permute-start | bytes 73736 | tf_op jit(solution)/shard_map/ppermute | solution.py:346
  27.2 5.5 %collective-permute-start.12 = (bf16[96,128]{1,0:T(8,128)(2,1)S(1)}, bf16[96,128]{1,0:T(8,128)(2,1)S(1)}, u32[]{:S(2)}, u32[]{:S(2)}) collective-permute-start(bf16[96,128]{1,0:T(8,128)(2,1)S(1)} %collective-permute-done.9.refs_5_), channel_id=1, source_target_pairs={{0,1},{1,0},{2,3},{3,2},{4,5},{5,4},{6,7},{7,6},{8,9},{9,8},{10,11... | collective-permute-start | bytes 73736 | tf_op jit(solution)/shard_map/ppermute | solution.py:346
  30.0 5.9 %collective-permute-start.8 = (bf16[480,128]{1,0:T(8,128)(2,1)S(1)}, bf16[480,128]{1,0:T(8,128)(2,1)S(1)}, u32[]{:S(2)}, u32[]{:S(2)}) collective-permute-start(bf16[480,128]{1,0:T(8,128)(2,1)S(1)} %get-tuple-element.42), channel_id=1, source_target_pairs={{0,4},{4,0},{8,12},{12,8},{16,20},{20,16},{24,28},{28,24},{1,5},{5... | collective-permute-start | bytes 368648 | tf_op jit(solution)/shard_map/ppermute | solution.py:346
  32.2 2.9 %collective-permute-start.13 = (bf16[96,128]{1,0:T(8,128)(2,1)S(1)}, bf16[96,128]{1,0:T(8,128)(2,1)S(1)}, u32[]{:S(2)}, u32[]{:S(2)}) collective-permute-start(bf16[96,128]{1,0:T(8,128)(2,1)S(1)} %collective-permute-done.10.refs_6_), channel_id=1, source_target_pairs={{0,1},{1,0},{2,3},{3,2},{4,5},{5,4},{6,7},{7,6},{8,9},{9,8},{10,11... | collective-permute-start | bytes 73736 | tf_op jit(solution)/shard_map/ppermute | solution.py:346
  32.3 2.8 %collective-permute-start.14 = (bf16[96,128]{1,0:T(8,128)(2,1)S(1)}, bf16[96,128]{1,0:T(8,128)(2,1)S(1)}, u32[]{:S(2)}, u32[]{:S(2)}) collective-permute-start(bf16[96,128]{1,0:T(8,128)(2,1)S(1)} %collective-permute-done.11.refs_7_), channel_id=1, source_target_pairs={{0,1},{1,0},{2,3},{3,2},{4,5},{5,4},{6,7},{7,6},{8,9},{9,8},{10,11... | collective-permute-start | bytes 73736 | tf_op jit(solution)/shard_map/ppermute | solution.py:346
  32.7 5.3 %collective-permute-start.15 = (bf16[480,128]{1,0:T(8,128)(2,1)S(1)}, bf16[480,128]{1,0:T(8,128)(2,1)S(1)}, u32[]{:S(2)}, u32[]{:S(2)}) collective-permute-start(bf16[480,128]{1,0:T(8,128)(2,1)S(1)} %get-tuple-element.48), channel_id=1, source_target_pairs={{0,4},{4,0},{8,12},{12,8},{16,20},{20,16},{24,28},{28,24},{1,5},{5... | collective-permute-start | bytes 368648 | tf_op jit(solution)/shard_map/ppermute | solution.py:346
  36.3 6.0 %collective-permute-start.16 = (bf16[96,480]{1,0:T(8,128)(2,1)S(1)}, bf16[96,480]{1,0:T(8,128)(2,1)S(1)}, u32[]{:S(2)}, u32[]{:S(2)}) collective-permute-start(bf16[96,480]{1,0:T(8,128)(2,1)S(1)} %get-tuple-element.50), channel_id=1, source_target_pairs={{0,8},{4,12},{8,0},{12,4},{16,24},{20,28},{24,16},{28,20},{1,9},{5... | collective-permute-start | bytes 276488 | tf_op jit(solution)/shard_map/ppermute | solution.py:346
  38.5 4.7 %collective-permute-start.17 = (bf16[96,480]{1,0:T(8,128)(2,1)S(1)}, bf16[96,480]{1,0:T(8,128)(2,1)S(1)}, u32[]{:S(2)}, u32[]{:S(2)}) collective-permute-start(bf16[96,480]{1,0:T(8,128)(2,1)S(1)} %get-tuple-element.51), channel_id=1, source_target_pairs={{0,8},{4,12},{8,0},{12,4},{16,24},{20,28},{24,16},{28,20},{1,9},{5... | collective-permute-start | bytes 276488 | tf_op jit(solution)/shard_map/ppermute | solution.py:346

commit v9 on v8

--- a/solution.py
+++ b/solution.py
@@ -295,15 +295,24 @@
         at += out.shape[0]
 
 
+def merge_kernel(*refs):
+    *parts, out, turned = refs
+    at = 0
+    for part in parts:
+        here = slice(at, at + part.shape[0])
+        value = part[...]
+        out[here, :] = value
+        turned[here, :] = pltpu.roll(value.astype(F32), value.shape[1] // 2, axis=1).astype(BF16)
+        at += part.shape[0]
+
+
 def kernel_grad_kernel(factor, begin, *refs):
-    *refs, mine, theirs = refs
-    count = (len(refs) + 1) // 3
-    acts, own, refs = refs[:count], refs[count], refs[count + 1 :]
+    *acts, own, here, other, mine, theirs = refs
     first = lax.axis_index("ctx") % 2 == 0
     gts = [own[...]]
-    for here, other in zip(refs[: count - 1], refs[count - 1 :]):
-        turned = pltpu.roll(other[...].astype(F32), other.shape[1] // 2, axis=1)
-        a, b = here[...], turned.astype(BF16)
+    step = mine.shape[0]
+    for at in range(0, here.shape[0], step):
+        a, b = here[at : at + step, :], other[at : at + step, :]
         gts.append(jnp.concatenate([jnp.where(first, a, b), jnp.where(first, b, a)], axis=0))
     span, size = mine.shape
     total = None
@@ -323,13 +332,17 @@
 
 
 def join_kernel(kernel, *refs):
-    *parts, out = refs
+    *parts, out, buf, sems = refs
     width = out.shape[1]
     half = len(parts) // 2
     sums = [a[...] + b[...].astype(F32) for a, b in zip(parts[:half], parts[half:])]
     total = jnp.transpose(jnp.concatenate(sums, axis=1))
+    copies = [pltpu.make_async_copy(buf.at[j], out.at[j], sems.at[j]) for j in range(kernel)]
     for j in range(kernel):
-        out[j] = total[j * width : (j + 1) * width, :]
+        buf[j] = total[j * width : (j + 1) * width, :]
+        copies[j].start()
+    for copy in copies:
+        copy.wait()
 
 
 def xor_order(count):
@@ -487,10 +500,15 @@
     act_zx = list(act_zx)
     for at, value in enumerate(act_zx):
         act_zx[at] = swap(value, "dp", X_BIT)
-    swapped, shared = [], []
+    swapped = []
     for at, rel in enumerate(near_rels[1:], 1):
         swapped.append(swap(gts[at], "dp", rel))
-        shared.append(swap(swapped[-1], "ctx", 1))
+    merged, turned = call(
+        merge_kernel,
+        swapped,
+        [pltpu.VMEM((sum(value.shape[0] for value in swapped), tokens), BF16)] * 2,
+    )
+    shared = swap(turned, "ctx", 1)
 
     padded = -(-(tok_rows + 2) // 8) * 8
     highs, lows, near_g = call(
@@ -505,7 +523,7 @@
         kept = len(late) // 2
         mine, theirs = call(
             functools.partial(kernel_grad_kernel, factor, cuts[at]),
-            (act, act_x, act_z, act_zx[at], gts[0], *swapped, *shared),
+            (act, act_x, act_z, act_zx[at], gts[0], merged, shared),
             [pltpu.VMEM((kept * narrow, size), F32), pltpu.VMEM((kept * narrow, size), BF16)],
         )
         other = swap(theirs, "dp", late[kept])
@@ -532,6 +550,8 @@
         functools.partial(join_kernel, kernel),
         (*mines, *others),
         [jax.ShapeDtypeStruct((kernel, width, narrow), F32)],
+        [pltpu.VMEM((kernel, width, narrow), F32), pltpu.SemaphoreType.DMA((kernel,))],
+        out_specs=[hbm],
     )[0]
     return grad_in[None], jnp.transpose(grad_conv, (1, 0, 2))
 

time: 44.4 us -> 46 us (1.036)
  waiting for transfers between devices: 8.89 us -> 12.1 us
  starting transfers between devices: 19.2 us -> 17.6 us
    ppermute x18 -> x16, waiting for transfers between devices: 8.89 us -> 12.1 us  [swap(): return lax.ppermute(value, axis, [(i, i ^ bit) for i in range(count)])]
    ppermute x18 -> x16, starting transfers between devices: 19.2 us -> 17.6 us  [swap(): return lax.ppermute(value, axis, [(i, i ^ bit) for i in range(count)])]
    pallas_call x11 -> x12, Pallas kernels: 15.3 us -> 15.2 us  [call(): pl.pallas_call(body, out_shape=list(outs), scratch_shapes=list(scratch),...]
  transfers between devices with their start and end apart: 18 -> 16, of which waited for: 8 -> 7; matrix products, arithmetic and copies ran while one was open for 0% -> 0% of each run, Pallas kernels for 23% -> 22%
where the time goes in v9:
time: 46 us; the launch traced here: 45.8 us
  starting transfers between devices  17.6 us (38%)
  Pallas kernels  15.2 us (33%)
  waiting for transfers between devices  12.1 us (26%)
  between operations  0.78 us (2%)
    ppermute x16, starting transfers between devices, swap(): return lax.ppermute(value, axis, [(i, i ^ bit) for i in range(count)])  17.6 us
    pallas_call x12, Pallas kernels, call(): pl.pallas_call(body, out_shape=list(outs), scratch_shapes=list(scratch),...  15.2 us
    ppermute x16, waiting for transfers between devices, swap(): return lax.ppermute(value, axis, [(i, i ^ bit) for i in range(count)])  12.1 us
  transfers between devices with their start and end apart: 16, of which 7 were waited for; matrix products, arithmetic and copies ran while one was open for 0% of the time, Pallas kernels for 22%

profile of v9, /device:TPU:0, one launch (start us, length us, event | category | flops | bytes accessed | tf_op | source)
XLA Modules:
  0.0 45.8 jit_solution(6023524527287239682)
XLA Ops:
  0.6 0.0 slice-start
  0.6 0.0 slice-start.1
  0.7 2.8 %shard_map.113 = (f32[200,768]{1,0:T(8,128)S(1)}, f32[40,768]{1,0:T(8,128)S(1)}, f32[512,768]{1,0:T(8,128)S(1)}, f32[512,128]{1,0:T(8,128)S(1)}, bf16[768]{0:T(1...) custom-call(bf16[512,768]{1,0:T(8,128)(2,1)} %bitcast.6, s32[1,512]{1,0:T(1,128)} %base_hbm.1, bf16[4,768]{1,0:T(4,128)(2,1)} %table_hbm.1, ...), custom_call_target="tpu_custom_call" | custom-call | flops 3449999872 | tf_op jit(solution)/shard_map/pallas_call | solution.py:368
  3.5 0.2 shard_map.114
  3.7 0.0 slice-done
  3.7 0.1 slice-done.1
  3.8 1.2 %shard_map.115.refs_0_ = bf16[80,768]{1,0:T(8,128)(2,1)S(1)} custom-call(bf16[5,80,768]{2,1,0:T(8,128)(2,1)S(1)} %get-tuple-element.30.pairs, f32[40,768]{1,0:T(8,128)S(1)} %get-tuple-element.31.sums, bf16[5,768,768]{2,1,0:T(8,128)(2,1)S(1)} %bitcast.5, bf16[32,768]{1,0:T(8,128)(2,1)S(1)} %get-tuple-element.32.cot), custom_call_target="tpu_custom_call" | custom-call | flops 1150000000 | tf_op jit(solution)/shard_map/pallas_call | solution.py:368
  4.9 3.1 %collective-permute-start = (bf16[80,768]{1,0:T(8,128)(2,1)S(1)}, bf16[80,768]{1,0:T(8,128)(2,1)S(1)}, u32[]{:S(2)}, u32[]{:S(2)}) collective-permute-start(bf16[80,768]{1,0:T(8,128)(2,1)S(1)} %shard_map.115.refs_0_), channel_id=1, source_target_pairs={{0,2},{1,3},{2,0},{3,1},{4,6},{5,7},{6,4},{7,5},{8,10},{9,11},{10,... | collective-permute-start | bytes 368648 | tf_op jit(solution)/shard_map/ppermute | solution.py:359
  8.0 0.1 collective-permute-start.3
  8.1 0.0 collective-permute-start.4
  8.1 2.1 %collective-permute-start.5 = (bf16[40,960]{1,0:T(8,128)(2,1)S(1)}, bf16[40,960]{1,0:T(8,128)(2,1)S(1)}, u32[]{:S(2)}, u32[]{:S(2)}) collective-permute-start(bf16[40,960]{1,0:T(8,128)(2,1)S(1)} %get-tuple-element.43), channel_id=1, source_target_pairs={{0,3},{1,2},{2,1},{3,0},{4,7},{5,6},{6,5},{7,4},{8,11},{9,10},{10,... | collective-permute-start | bytes 230408 | tf_op jit(solution)/shard_map/ppermute | solution.py:359
  10.1 0.0 collective-permute-start.1
  10.1 2.0 %collective-permute-done.refs_1_ = bf16[80,768]{1,0:T(8,128)(2,1)S(1)} collective-permute-done((bf16[80,768]{1,0:T(8,128)(2,1)S(1)}, bf16[80,768]{1,0:T(8,128)(2,1)S(1)}, u32[]{:S(2)}, u32[]{:S(2)}) %collective-permute-start) | collective-permute-done | bytes 122912 | tf_op jit(solution)/shard_map/ppermute | solution.py:359
  12.2 0.0 collective-permute-start.2
  12.2 1.8 %collective-permute-done.3.refs_1_ = bf16[40,960]{1,0:T(8,128)(2,1)S(1)} collective-permute-done((bf16[40,960]{1,0:T(8,128)(2,1)S(1)}, bf16[40,960]{1,0:T(8,128)(2,1)S(1)}, u32[]{:S(2)}, u32[]{:S(2)}) %collective-permute-start.3) | collective-permute-done | bytes 76832 | tf_op jit(solution)/shard_map/ppermute | solution.py:359
  13.9 0.0 collective-permute-done.4.refs_2_
  13.9 0.2 collective-permute-done.5.refs_3_
  14.1 0.3 shard_map.119.refs_0_
  14.4 1.7 %collective-permute-start.6 = (bf16[960,128]{1,0:T(8,128)(2,1)S(1)}, bf16[960,128]{1,0:T(8,128)(2,1)S(1)}, u32[]{:S(2)}, u32[]{:S(2)}) collective-permute-start(bf16[960,128]{1,0:T(8,128)(2,1)S(1)} %shard_map.119.refs_0_), channel_id=1, source_target_pairs={{0,4},{4,0},{8,12},{12,8},{16,20},{20,16},{24,28},{28,24},{1,5},{5... | collective-permute-start | bytes 737288 | tf_op jit(solution)/shard_map/ppermute | solution.py:359
  16.0 2.6 %collective-permute-start.7 = (bf16[960,128]{1,0:T(8,128)(2,1)S(1)}, bf16[960,128]{1,0:T(8,128)(2,1)S(1)}, u32[]{:S(2)}, u32[]{:S(2)}) collective-permute-start(bf16[960,128]{1,0:T(8,128)(2,1)S(1)} %shard_map.119.refs_0_), channel_id=1, source_target_pairs={{0,16},{4,20},{8,24},{12,28},{16,0},{20,4},{24,8},{28,12},{1,17},{... | collective-permute-start | bytes 737288 | tf_op jit(solution)/shard_map/ppermute | solution.py:359
  18.6 0.0 collective-permute-done.1.refs_2_
  18.6 0.0 collective-permute-done.2.refs_3_
  18.6 0.0 copy-done
  18.7 4.1 %shard_map.116 = (bf16[768,128]{1,0:T(8,128)(2,1)S(1)}, bf16[192,128]{1,0:T(8,128)(2,1)S(1)}, bf16[96,128]{1,0:T(8,128)(2,1)S(1)}, bf16[96,128]{1,0:T(8,128)(2,1)S(1)}, bf16[96,128]{1,0:T(8,128)(2,1)S(1)}) custom-call(bf16[80,768]{1,0:T(8,128)(2,1)S(1)} %shard_map.115.refs_0_, bf16[80,768]{1,0:T(8,128)(2,1)S(1)} %collective-permute-done.refs_1_, ...), custom_call_target="tpu_custom_call" | custom-call | flops 5750000128 | tf_op jit(solution)/shard_map/pallas_call | solution.py:368
  22.8 0.6 %collective-permute-start.9 = (bf16[96,128]{1,0:T(8,128)(2,1)S(1)}, bf16[96,128]{1,0:T(8,128)(2,1)S(1)}, u32[]{:S(2)}, u32[]{:S(2)}) collective-permute-start(bf16[96,128]{1,0:T(8,128)(2,1)S(1)} %get-tuple-element.46), channel_id=1, source_target_pairs={{0,4},{4,0},{8,12},{12,8},{16,20},{20,16},{24,28},{28,24},{1,5},{5... | collective-permute-start | bytes 73736 | tf_op jit(solution)/shard_map/ppermute | solution.py:359
  23.4 0.7 %collective-permute-start.10 = (bf16[96,128]{1,0:T(8,128)(2,1)S(1)}, bf16[96,128]{1,0:T(8,128)(2,1)S(1)}, u32[]{:S(2)}, u32[]{:S(2)}) collective-permute-start(bf16[96,128]{1,0:T(8,128)(2,1)S(1)} %get-tuple-element.47), channel_id=1, source_target_pairs={{0,16},{4,20},{8,24},{12,28},{16,0},{20,4},{24,8},{28,12},{1,17},{... | collective-permute-start | bytes 73736 | tf_op jit(solution)/shard_map/ppermute | solution.py:359
  24.1 3.2 %collective-permute-start.11 = (bf16[96,128]{1,0:T(8,128)(2,1)S(1)}, bf16[96,128]{1,0:T(8,128)(2,1)S(1)}, u32[]{:S(2)}, u32[]{:S(2)}) collective-permute-start(bf16[96,128]{1,0:T(8,128)(2,1)S(1)} %get-tuple-element.48), channel_id=1, source_target_pairs={{0,20},{4,16},{8,28},{12,24},{16,4},{20,0},{24,12},{28,8},{1,21},{... | collective-permute-start | bytes 73736 | tf_op jit(solution)/shard_map/ppermute | solution.py:359
  27.2 4.8 %collective-permute-done.7.value.refs_2_ = bf16[960,128]{1,0:T(8,128)(2,1)S(1)} collective-permute-done((bf16[960,128]{1,0:T(8,128)(2,1)S(1)}, bf16[960,128]{1,0:T(8,128)(2,1)S(1)}, u32[]{:S(2)}, u32[]{:S(2)}) %collective-permute-start.7) | collective-permute-done | bytes 245792 | tf_op jit(solution)/shard_map/ppermute | solution.py:359
  32.1 0.5 %collective-permute-start.8 = (bf16[480,128]{1,0:T(8,128)(2,1)S(1)}, bf16[480,128]{1,0:T(8,128)(2,1)S(1)}, u32[]{:S(2)}, u32[]{:S(2)}) collective-permute-start(bf16[480,128]{1,0:T(8,128)(2,1)S(1)} %get-tuple-element.44), channel_id=1, source_target_pairs={{0,4},{4,0},{8,12},{12,8},{16,20},{20,16},{24,28},{28,24},{1,5},{5... | collective-permute-start | bytes 368648 | tf_op jit(solution)/shard_map/ppermute | solution.py:359
  32.6 0.0 collective-permute-done.9.refs_0_
  32.6 0.0 collective-permute-done.10.refs_1_
  32.6 0.0 collective-permute-done.11.refs_2_
  32.6 0.1 shard_map.121
  32.7 0.1 collective-permute-start.12
  32.8 1.6 %collective-permute-start.13 = (bf16[480,128]{1,0:T(8,128)(2,1)S(1)}, bf16[480,128]{1,0:T(8,128)(2,1)S(1)}, u32[]{:S(2)}, u32[]{:S(2)}) collective-permute-start(bf16[480,128]{1,0:T(8,128)(2,1)S(1)} %get-tuple-element.52), channel_id=1, source_target_pairs={{0,4},{4,0},{8,12},{12,8},{16,20},{20,16},{24,28},{28,24},{1,5},{5... | collective-permute-start | bytes 368648 | tf_op jit(solution)/shard_map/ppermute | solution.py:359
  34.4 2.0 %shard_map.117 = (bf16[200,768]{1,0:T(8,128)(2,1)S(1)}, bf16[200,768]{1,0:T(8,128)(2,1)S(1)}, bf16[40,768]{1,0:T(8,128)(2,1)S(1)}) custom-call(bf16[768,128]{1,0:T(8,128)(2,1)S(1)} %get-tuple-element.33.g_ref, bf16[5,768,768]{2,1,0:T(8,128)(2,1)S(1)} %bitcast.5), custom_call_target="tpu_custom_call" | custom-call | flops 1150000000 | tf_op jit(solution)/shard_map/pallas_call | solution.py:368
  36.4 0.0 collective-permute-done.6.refs_1_
  36.4 0.0 collective-permute-done.12.refs_6_
  36.4 1.7 %collective-permute-done.8.refs_3_ = bf16[480,128]{1,0:T(8,128)(2,1)S(1)} collective-permute-done((bf16[480,128]{1,0:T(8,128)(2,1)S(1)}, bf16[480,128]{1,0:T(8,128)(2,1)S(1)}, u32[]{:S(2)}, u32[]{:S(2)}) %collective-permute-start.8) | collective-permute-done | bytes 122912 | tf_op jit(solution)/shard_map/ppermute | solution.py:359
  38.1 0.4 shard_map.122
  38.5 0.4 collective-permute-start.14
  39.0 0.7 %collective-permute-done.13.refs_3_ = bf16[480,128]{1,0:T(8,128)(2,1)S(1)} collective-permute-done((bf16[480,128]{1,0:T(8,128)(2,1)S(1)}, bf16[480,128]{1,0:T(8,128)(2,1)S(1)}, u32[]{:S(2)}, u32[]{:S(2)}) %collective-permute-start.13) | collective-permute-done | bytes 122912 | tf_op jit(solution)/shard_map/ppermute | solution.py:359
  39.6 0.4 shard_map.123
  40.0 1.0 %collective-permute-start.15 = (bf16[96,480]{1,0:T(8,128)(2,1)S(1)}, bf16[96,480]{1,0:T(8,128)(2,1)S(1)}, u32[]{:S(2)}, u32[]{:S(2)}) collective-permute-start(bf16[96,480]{1,0:T(8,128)(2,1)S(1)} %get-tuple-element.55), channel_id=1, source_target_pairs={{0,8},{4,12},{8,0},{12,4},{16,24},{20,28},{24,16},{28,20},{1,9},{5... | collective-permute-start | bytes 276488 | tf_op jit(solution)/shard_map/ppermute | solution.py:359
  41.1 2.8 %shard_map.118 = bf16[512,768]{1,0:T(8,128)(2,1)} custom-call(bf16[200,768]{1,0:T(8,128)(2,1)S(1)} %get-tuple-element.34.highs, bf16[200,768]{1,0:T(8,128)(2,1)S(1)} %get-tuple-element.35.lows, bf16[40,768]{1,0:T(8,128)(2,1)S(1)} %get-tuple-element.36.near, f32[512,768]{1,0:T(8,128)S(1)} %get-tuple-element.37.normed_ref, ...), custom_call_target="tpu_custom_call" | custom-call | flops 1150000000 | tf_op jit(solution)/shard_map/pallas_call | solution.py:368
  43.9 0.0 collective-permute-done.14.refs_2_
  43.9 0.9 %collective-permute-done.15.refs_3_ = bf16[96,480]{1,0:T(8,128)(2,1)S(1)} collective-permute-done((bf16[96,480]{1,0:T(8,128)(2,1)S(1)}, bf16[96,480]{1,0:T(8,128)(2,1)S(1)}, u32[]{:S(2)}, u32[]{:S(2)}) %collective-permute-start.15) | collective-permute-done | bytes 92192 | tf_op jit(solution)/shard_map/ppermute | solution.py:359
  44.8 1.0 %shard_map.124 = f32[5,192,96]{2,1,0:T(8,128)} custom-call(f32[96,480]{1,0:T(8,128)S(1)} %get-tuple-element.51.refs_0_, f32[96,480]{1,0:T(8,128)S(1)} %get-tuple-element.53.refs_1_, bf16[96,480]{1,0:T(8,128)(2,1)S(1)} %collective-permute-done.14.refs_2_, bf16[96,480]{1,0:T(8,128)(2,1)S(1)} %collective-permute-done.15.refs_3_), custom_call_target="tpu_custom_call" | custom-call | flops 1150000000 | tf_op jit(solution)/shard_map/pallas_call | solution.py:368
  (5 shorter events, 0.0 us)
Async XLA Ops:
  0.6 3.0 %slice-start = ((s8[5898240]{0:T(1024)(128)(4,1)}), s8[4194304]{0:T(1024)(128)(4,1)S(1)}, s32[]{:S(2)}) async-start(s8[5898240]{0:T(1024)(128)(4,1)} %bitcast.4), calls=%async_computation | async-start | bytes 8388608
  0.6 3.1 %slice-start.1 = ((s8[5898240]{0:T(1024)(128)(4,1)}), s8[1703936]{0:T(1024)(128)(4,1)S(1)}, s32[]{:S(2)}) async-start(s8[5898240]{0:T(1024)(128)(4,1)} %bitcast.4), calls=%async_computation.1 | async-start | bytes 3407872
  4.9 7.2 %collective-permute-start = (bf16[80,768]{1,0:T(8,128)(2,1)S(1)}, bf16[80,768]{1,0:T(8,128)(2,1)S(1)}, u32[]{:S(2)}, u32[]{:S(2)}) collective-permute-start(bf16[80,768]{1,0:T(8,128)(2,1)S(1)} %shard_map.115.refs_0_), channel_id=1, source_target_pairs={{0,2},{1,3},{2,0},{3,1},{4,6},{5,7},{6,4},{7,5},{8,10},{9,11},{10,... | collective-permute-start | bytes 368648 | tf_op jit(solution)/shard_map/ppermute | solution.py:359
  8.0 5.9 %collective-permute-start.3 = (bf16[40,960]{1,0:T(8,128)(2,1)S(1)}, bf16[40,960]{1,0:T(8,128)(2,1)S(1)}, u32[]{:S(2)}, u32[]{:S(2)}) collective-permute-start(bf16[40,960]{1,0:T(8,128)(2,1)S(1)} %get-tuple-element.41), channel_id=1, source_target_pairs={{0,2},{1,3},{2,0},{3,1},{4,6},{5,7},{6,4},{7,5},{8,10},{9,11},{10,... | collective-permute-start | bytes 230408 | tf_op jit(solution)/shard_map/ppermute | solution.py:359
  8.1 5.9 %collective-permute-start.4 = (bf16[40,960]{1,0:T(8,128)(2,1)S(1)}, bf16[40,960]{1,0:T(8,128)(2,1)S(1)}, u32[]{:S(2)}, u32[]{:S(2)}) collective-permute-start(bf16[40,960]{1,0:T(8,128)(2,1)S(1)} %get-tuple-element.42), channel_id=1, source_target_pairs={{0,1},{1,0},{2,3},{3,2},{4,5},{5,4},{6,7},{7,6},{8,9},{9,8},{10,11... | collective-permute-start | bytes 230408 | tf_op jit(solution)/shard_map/ppermute | solution.py:359
  8.1 6.0 %collective-permute-start.5 = (bf16[40,960]{1,0:T(8,128)(2,1)S(1)}, bf16[40,960]{1,0:T(8,128)(2,1)S(1)}, u32[]{:S(2)}, u32[]{:S(2)}) collective-permute-start(bf16[40,960]{1,0:T(8,128)(2,1)S(1)} %get-tuple-element.43), channel_id=1, source_target_pairs={{0,3},{1,2},{2,1},{3,0},{4,7},{5,6},{6,5},{7,4},{8,11},{9,10},{10,... | collective-permute-start | bytes 230408 | tf_op jit(solution)/shard_map/ppermute | solution.py:359
  10.1 8.5 %collective-permute-start.1 = (bf16[80,768]{1,0:T(8,128)(2,1)S(1)}, bf16[80,768]{1,0:T(8,128)(2,1)S(1)}, u32[]{:S(2)}, u32[]{:S(2)}) collective-permute-start(bf16[80,768]{1,0:T(8,128)(2,1)S(1)} %shard_map.115.refs_0_), channel_id=1, source_target_pairs={{0,1},{1,0},{2,3},{3,2},{4,5},{5,4},{6,7},{7,6},{8,9},{9,8},{10,11... | collective-permute-start | bytes 368648 | tf_op jit(solution)/shard_map/ppermute | solution.py:359
  12.2 6.5 %collective-permute-start.2 = (bf16[80,768]{1,0:T(8,128)(2,1)S(1)}, bf16[80,768]{1,0:T(8,128)(2,1)S(1)}, u32[]{:S(2)}, u32[]{:S(2)}) collective-permute-start(bf16[80,768]{1,0:T(8,128)(2,1)S(1)} %collective-permute-done.refs_1_), channel_id=1, source_target_pairs={{0,1},{1,0},{2,3},{3,2},{4,5},{5,4},{6,7},{7,6},{8,9},{9,8},{10,11... | collective-permute-start | bytes 368648 | tf_op jit(solution)/shard_map/ppermute | solution.py:359
  14.1 4.6 %copy-start = (bf16[768,768]{1,0:T(8,128)(2,1)S(1)}, bf16[768,768]{1,0:T(8,128)(2,1)}, u32[]{:S(2)}) copy-start(bf16[768,768]{1,0:T(8,128)(2,1)} %refs_4_.1) | copy-start | bytes 3538948
  14.1 4.6 %copy-start.1 = (bf16[768,768]{1,0:T(8,128)(2,1)S(1)}, bf16[768,768]{1,0:T(8,128)(2,1)}, u32[]{:S(2)}) copy-start(bf16[768,768]{1,0:T(8,128)(2,1)} %refs_5_.1) | copy-start | bytes 3538948
  14.4 22.0 %collective-permute-start.6 = (bf16[960,128]{1,0:T(8,128)(2,1)S(1)}, bf16[960,128]{1,0:T(8,128)(2,1)S(1)}, u32[]{:S(2)}, u32[]{:S(2)}) collective-permute-start(bf16[960,128]{1,0:T(8,128)(2,1)S(1)} %shard_map.119.refs_0_), channel_id=1, source_target_pairs={{0,4},{4,0},{8,12},{12,8},{16,20},{20,16},{24,28},{28,24},{1,5},{5... | collective-permute-start | bytes 737288 | tf_op jit(solution)/shard_map/ppermute | solution.py:359
  16.0 16.0 %collective-permute-start.7 = (bf16[960,128]{1,0:T(8,128)(2,1)S(1)}, bf16[960,128]{1,0:T(8,128)(2,1)S(1)}, u32[]{:S(2)}, u32[]{:S(2)}) collective-permute-start(bf16[960,128]{1,0:T(8,128)(2,1)S(1)} %shard_map.119.refs_0_), channel_id=1, source_target_pairs={{0,16},{4,20},{8,24},{12,28},{16,0},{20,4},{24,8},{28,12},{1,17},{... | collective-permute-start | bytes 737288 | tf_op jit(solution)/shard_map/ppermute | solution.py:359
  22.8 9.8 %collective-permute-start.9 = (bf16[96,128]{1,0:T(8,128)(2,1)S(1)}, bf16[96,128]{1,0:T(8,128)(2,1)S(1)}, u32[]{:S(2)}, u32[]{:S(2)}) collective-permute-start(bf16[96,128]{1,0:T(8,128)(2,1)S(1)} %get-tuple-element.46), channel_id=1, source_target_pairs={{0,4},{4,0},{8,12},{12,8},{16,20},{20,16},{24,28},{28,24},{1,5},{5... | collective-permute-start | bytes 73736 | tf_op jit(solution)/shard_map/ppermute | solution.py:359
  23.4 9.2 %collective-permute-start.10 = (bf16[96,128]{1,0:T(8,128)(2,1)S(1)}, bf16[96,128]{1,0:T(8,128)(2,1)S(1)}, u32[]{:S(2)}, u32[]{:S(2)}) collective-permute-start(bf16[96,128]{1,0:T(8,128)(2,1)S(1)} %get-tuple-element.47), channel_id=1, source_target_pairs={{0,16},{4,20},{8,24},{12,28},{16,0},{20,4},{24,8},{28,12},{1,17},{... | collective-permute-start | bytes 73736 | tf_op jit(solution)/shard_map/ppermute | solution.py:359
  24.1 8.5 %collective-permute-start.11 = (bf16[96,128]{1,0:T(8,128)(2,1)S(1)}, bf16[96,128]{1,0:T(8,128)(2,1)S(1)}, u32[]{:S(2)}, u32[]{:S(2)}) collective-permute-start(bf16[96,128]{1,0:T(8,128)(2,1)S(1)} %get-tuple-element.48), channel_id=1, source_target_pairs={{0,20},{4,16},{8,28},{12,24},{16,4},{20,0},{24,12},{28,8},{1,21},{... | collective-permute-start | bytes 73736 | tf_op jit(solution)/shard_map/ppermute | solution.py:359
  32.1 6.1 %collective-permute-start.8 = (bf16[480,128]{1,0:T(8,128)(2,1)S(1)}, bf16[480,128]{1,0:T(8,128)(2,1)S(1)}, u32[]{:S(2)}, u32[]{:S(2)}) collective-permute-start(bf16[480,128]{1,0:T(8,128)(2,1)S(1)} %get-tuple-element.44), channel_id=1, source_target_pairs={{0,4},{4,0},{8,12},{12,8},{16,20},{20,16},{24,28},{28,24},{1,5},{5... | collective-permute-start | bytes 368648 | tf_op jit(solution)/shard_map/ppermute | solution.py:359
  32.7 3.7 %collective-permute-start.12 = (bf16[288,128]{1,0:T(8,128)(2,1)S(1)}, bf16[288,128]{1,0:T(8,128)(2,1)S(1)}, u32[]{:S(2)}, u32[]{:S(2)}) collective-permute-start(bf16[288,128]{1,0:T(8,128)(2,1)S(1)} %get-tuple-element.50), channel_id=1, source_target_pairs={{0,1},{1,0},{2,3},{3,2},{4,5},{5,4},{6,7},{7,6},{8,9},{9,8},{10,11... | collective-permute-start | bytes 221192 | tf_op jit(solution)/shard_map/ppermute | solution.py:359
  32.8 6.9 %collective-permute-start.13 = (bf16[480,128]{1,0:T(8,128)(2,1)S(1)}, bf16[480,128]{1,0:T(8,128)(2,1)S(1)}, u32[]{:S(2)}, u32[]{:S(2)}) collective-permute-start(bf16[480,128]{1,0:T(8,128)(2,1)S(1)} %get-tuple-element.52), channel_id=1, source_target_pairs={{0,4},{4,0},{8,12},{12,8},{16,20},{20,16},{24,28},{28,24},{1,5},{5... | collective-permute-start | bytes 368648 | tf_op jit(solution)/shard_map/ppermute | solution.py:359
  38.5 5.4 %collective-permute-start.14 = (bf16[96,480]{1,0:T(8,128)(2,1)S(1)}, bf16[96,480]{1,0:T(8,128)(2,1)S(1)}, u32[]{:S(2)}, u32[]{:S(2)}) collective-permute-start(bf16[96,480]{1,0:T(8,128)(2,1)S(1)} %get-tuple-element.54), channel_id=1, source_target_pairs={{0,8},{4,12},{8,0},{12,4},{16,24},{20,28},{24,16},{28,20},{1,9},{5... | collective-permute-start | bytes 276488 | tf_op jit(solution)/shard_map/ppermute | solution.py:359
  40.0 4.8 %collective-permute-start.15 = (bf16[96,480]{1,0:T(8,128)(2,1)S(1)}, bf16[96,480]{1,0:T(8,128)(2,1)S(1)}, u32[]{:S(2)}, u32[]{:S(2)}) collective-permute-start(bf16[96,480]{1,0:T(8,128)(2,1)S(1)} %get-tuple-element.55), channel_id=1, source_target_pairs={{0,8},{4,12},{8,0},{12,4},{16,24},{20,28},{24,16},{28,20},{1,9},{5... | collective-permute-start | bytes 276488 | tf_op jit(solution)/shard_map/ppermute | solution.py:359

commit v10 on v9

--- a/solution.py
+++ b/solution.py
@@ -174,12 +174,11 @@
 def attention_kernel(pool, order, tok_rows, near_rels, late, *refs):
     blocks = len(order)
     parts, refs = refs[:blocks], refs[blocks:]
-    (wq, wk, wv_hbm, wo_hbm), refs = refs[:4], refs[4:]
+    (wq, wk, wv, wo), refs = refs[:4], refs[4:]
     g_out, refs = refs[0], refs[1:]
     gts, refs = refs[: len(near_rels)], refs[len(near_rels) :]
     p_buf, c_buf, q_buf, k_buf, v_buf, ga_buf, gq_buf, gk_buf, gv_buf = refs[:9]
-    probs_buf, turn, ends, wv, wo, sems = refs[9:]
-    copies = start_copies(((wv_hbm, wv), (wo_hbm, wo)), sems)
+    probs_buf, turn, ends = refs[9:]
     padded = parts[0].shape[0] - tok_rows - 8
     befores, afters, firsts, lasts = [], [], [], []
     for part in parts:
@@ -206,9 +205,7 @@
     for h, score in enumerate(scores):
         expo = jnp.exp(score - jnp.max(score, axis=0, keepdims=True))
         probs_buf[h] = expo / jnp.sum(expo, axis=0, keepdims=True)
-    copies[0].wait()
     v_buf[...] = dot_nn(p_buf[...], wv[...]).astype(BF16)
-    copies[1].wait()
     ga_buf[...] = dot_nt(wo[...], c_buf[...]).astype(BF16)
     probs_b = [probs_buf[h].astype(BF16) for h in range(HEADS)]
     outs = [dot_tn(v_buf[:, cols], p).astype(BF16) for cols, p in zip(heads, probs_b)]
@@ -475,7 +472,7 @@
 
     g_all, *gts = call(
         functools.partial(attention_kernel, pool, order, tok_rows, near_rels, late),
-        [*rows, w_query, w_key] + outside(w_value, w_out),
+        (*rows, w_query, w_key, w_value, w_out),
         [pltpu.VMEM((channels, tokens), BF16), pltpu.VMEM((len(late) * narrow, tokens), BF16)]
         + [pltpu.VMEM((len(late) // 2 * narrow, tokens), BF16)] * (len(near_rels) - 1),
         [pltpu.VMEM((tokens, channels), BF16)] * 5
@@ -485,11 +482,7 @@
             pltpu.VMEM((HEADS, tokens, tokens), F32),
             pltpu.VMEM((n_dp, narrow, tokens), BF16),
             pltpu.VMEM((n_ctx + 2, 8, channels), F32),
-            pltpu.VMEM(w_value.shape, BF16),
-            pltpu.VMEM(w_out.shape, BF16),
-            pltpu.SemaphoreType.DMA((2,)),
         ],
-        in_specs=[WHOLE] * (n_ctx + 2) + [hbm] * 2,
         micros=5,
     )
 

time: 46 us -> 46 us (level)
  waiting for transfers between devices: 12.1 us -> 13 us
  Pallas kernels: 15.2 us -> 14.3 us
    pallas_call x12, Pallas kernels: 15.2 us -> 14.3 us  [call(): pl.pallas_call(body, out_shape=list(outs), scratch_shapes=list(scratch),...]
    ppermute x16, waiting for transfers between devices: 12.1 us -> 13 us  [swap(): return lax.ppermute(value, axis, [(i, i ^ bit) for i in range(count)])]
  transfers between devices with their start and end apart: 16 -> 16, of which waited for: 7 -> 7; matrix products, arithmetic and copies ran while one was open for 0% -> 0% of each run, Pallas kernels for 22% -> 20%
where the time goes in v10:
time: 46 us; the launch traced here: 45.8 us
  starting transfers between devices  17.6 us (38%)
  Pallas kernels  14.3 us (31%)
  waiting for transfers between devices  13 us (28%)
  between operations  0.8 us (2%)
    ppermute x16, starting transfers between devices, swap(): return lax.ppermute(value, axis, [(i, i ^ bit) for i in range(count)])  17.6 us
    pallas_call x12, Pallas kernels, call(): pl.pallas_call(body, out_shape=list(outs), scratch_shapes=list(scratch),...  14.3 us
    ppermute x16, waiting for transfers between devices, swap(): return lax.ppermute(value, axis, [(i, i ^ bit) for i in range(count)])  13 us
  transfers between devices with their start and end apart: 16, of which 7 were waited for; matrix products, arithmetic and copies ran while one was open for 0% of the time, Pallas kernels for 20%

profile of v10, /device:TPU:0, one launch (start us, length us, event | category | flops | bytes accessed | tf_op | source)
XLA Modules:
  0.0 45.8 jit_solution(3591633472216222070)
XLA Ops:
  0.6 0.0 slice-start
  0.6 0.0 slice-start.1
  0.7 2.8 %shard_map.113 = (f32[200,768]{1,0:T(8,128)S(1)}, f32[40,768]{1,0:T(8,128)S(1)}, f32[512,768]{1,0:T(8,128)S(1)}, f32[512,128]{1,0:T(8,128)S(1)}, bf16[768]{0:T(1...) custom-call(bf16[512,768]{1,0:T(8,128)(2,1)} %bitcast.6, s32[1,512]{1,0:T(1,128)} %base_hbm.1, bf16[4,768]{1,0:T(4,128)(2,1)} %table_hbm.1, ...), custom_call_target="tpu_custom_call" | custom-call | flops 3449999872 | tf_op jit(solution)/shard_map/pallas_call | solution.py:365
  3.5 0.2 shard_map.114
  3.7 0.1 slice-done.1
  3.8 1.2 %shard_map.115.refs_0_ = bf16[80,768]{1,0:T(8,128)(2,1)S(1)} custom-call(bf16[5,80,768]{2,1,0:T(8,128)(2,1)S(1)} %get-tuple-element.30.pairs, f32[40,768]{1,0:T(8,128)S(1)} %get-tuple-element.31.sums, bf16[5,768,768]{2,1,0:T(8,128)(2,1)S(1)} %bitcast.5, bf16[32,768]{1,0:T(8,128)(2,1)S(1)} %get-tuple-element.32.cot), custom_call_target="tpu_custom_call" | custom-call | flops 1150000000 | tf_op jit(solution)/shard_map/pallas_call | solution.py:365
  4.9 3.1 %collective-permute-start = (bf16[80,768]{1,0:T(8,128)(2,1)S(1)}, bf16[80,768]{1,0:T(8,128)(2,1)S(1)}, u32[]{:S(2)}, u32[]{:S(2)}) collective-permute-start(bf16[80,768]{1,0:T(8,128)(2,1)S(1)} %shard_map.115.refs_0_), channel_id=1, source_target_pairs={{0,2},{1,3},{2,0},{3,1},{4,6},{5,7},{6,4},{7,5},{8,10},{9,11},{10,... | collective-permute-start | bytes 368648 | tf_op jit(solution)/shard_map/ppermute | solution.py:356
  8.0 0.1 collective-permute-start.3
  8.1 0.0 collective-permute-start.4
  8.1 2.1 %collective-permute-start.5 = (bf16[40,960]{1,0:T(8,128)(2,1)S(1)}, bf16[40,960]{1,0:T(8,128)(2,1)S(1)}, u32[]{:S(2)}, u32[]{:S(2)}) collective-permute-start(bf16[40,960]{1,0:T(8,128)(2,1)S(1)} %get-tuple-element.43), channel_id=1, source_target_pairs={{0,3},{1,2},{2,1},{3,0},{4,7},{5,6},{6,5},{7,4},{8,11},{9,10},{10,... | collective-permute-start | bytes 230408 | tf_op jit(solution)/shard_map/ppermute | solution.py:356
  10.1 0.0 collective-permute-start.1
  10.1 2.0 %collective-permute-done.refs_1_ = bf16[80,768]{1,0:T(8,128)(2,1)S(1)} collective-permute-done((bf16[80,768]{1,0:T(8,128)(2,1)S(1)}, bf16[80,768]{1,0:T(8,128)(2,1)S(1)}, u32[]{:S(2)}, u32[]{:S(2)}) %collective-permute-start) | collective-permute-done | bytes 122912 | tf_op jit(solution)/shard_map/ppermute | solution.py:356
  12.2 0.0 collective-permute-start.2
  12.2 1.8 %collective-permute-done.3.refs_1_ = bf16[40,960]{1,0:T(8,128)(2,1)S(1)} collective-permute-done((bf16[40,960]{1,0:T(8,128)(2,1)S(1)}, bf16[40,960]{1,0:T(8,128)(2,1)S(1)}, u32[]{:S(2)}, u32[]{:S(2)}) %collective-permute-start.3) | collective-permute-done | bytes 76832 | tf_op jit(solution)/shard_map/ppermute | solution.py:356
  13.9 0.0 collective-permute-done.4.refs_2_
  13.9 0.2 collective-permute-done.5.refs_3_
  14.1 0.3 shard_map.119.refs_0_
  14.4 1.7 %collective-permute-start.6 = (bf16[960,128]{1,0:T(8,128)(2,1)S(1)}, bf16[960,128]{1,0:T(8,128)(2,1)S(1)}, u32[]{:S(2)}, u32[]{:S(2)}) collective-permute-start(bf16[960,128]{1,0:T(8,128)(2,1)S(1)} %shard_map.119.refs_0_), channel_id=1, source_target_pairs={{0,4},{4,0},{8,12},{12,8},{16,20},{20,16},{24,28},{28,24},{1,5},{5... | collective-permute-start | bytes 737288 | tf_op jit(solution)/shard_map/ppermute | solution.py:356
  16.1 2.6 %collective-permute-start.7 = (bf16[960,128]{1,0:T(8,128)(2,1)S(1)}, bf16[960,128]{1,0:T(8,128)(2,1)S(1)}, u32[]{:S(2)}, u32[]{:S(2)}) collective-permute-start(bf16[960,128]{1,0:T(8,128)(2,1)S(1)} %shard_map.119.refs_0_), channel_id=1, source_target_pairs={{0,16},{4,20},{8,24},{12,28},{16,0},{20,4},{24,8},{28,12},{1,17},{... | collective-permute-start | bytes 737288 | tf_op jit(solution)/shard_map/ppermute | solution.py:356
  18.6 0.0 collective-permute-done.1.refs_2_
  18.7 0.0 collective-permute-done.2.refs_3_
  18.7 0.0 copy-done.3
  18.7 0.0 copy-done
  18.7 3.2 %shard_map.116 = (bf16[768,128]{1,0:T(8,128)(2,1)S(1)}, bf16[192,128]{1,0:T(8,128)(2,1)S(1)}, bf16[96,128]{1,0:T(8,128)(2,1)S(1)}, bf16[96,128]{1,0:T(8,128)(2,1)S(1)}, bf16[96,128]{1,0:T(8,128)(2,1)S(1)}) custom-call(bf16[80,768]{1,0:T(8,128)(2,1)S(1)} %shard_map.115.refs_0_, bf16[80,768]{1,0:T(8,128)(2,1)S(1)} %collective-permute-done.refs_1_, ...), custom_call_target="tpu_custom_call" | custom-call | flops 5750000128 | tf_op jit(solution)/shard_map/pallas_call | solution.py:365
  21.9 0.6 %collective-permute-start.9 = (bf16[96,128]{1,0:T(8,128)(2,1)S(1)}, bf16[96,128]{1,0:T(8,128)(2,1)S(1)}, u32[]{:S(2)}, u32[]{:S(2)}) collective-permute-start(bf16[96,128]{1,0:T(8,128)(2,1)S(1)} %get-tuple-element.46), channel_id=1, source_target_pairs={{0,4},{4,0},{8,12},{12,8},{16,20},{20,16},{24,28},{28,24},{1,5},{5... | collective-permute-start | bytes 73736 | tf_op jit(solution)/shard_map/ppermute | solution.py:356
  22.5 1.0 %collective-permute-start.10 = (bf16[96,128]{1,0:T(8,128)(2,1)S(1)}, bf16[96,128]{1,0:T(8,128)(2,1)S(1)}, u32[]{:S(2)}, u32[]{:S(2)}) collective-permute-start(bf16[96,128]{1,0:T(8,128)(2,1)S(1)} %get-tuple-element.47), channel_id=1, source_target_pairs={{0,16},{4,20},{8,24},{12,28},{16,0},{20,4},{24,8},{28,12},{1,17},{... | collective-permute-start | bytes 73736 | tf_op jit(solution)/shard_map/ppermute | solution.py:356
  23.5 2.8 %collective-permute-start.11 = (bf16[96,128]{1,0:T(8,128)(2,1)S(1)}, bf16[96,128]{1,0:T(8,128)(2,1)S(1)}, u32[]{:S(2)}, u32[]{:S(2)}) collective-permute-start(bf16[96,128]{1,0:T(8,128)(2,1)S(1)} %get-tuple-element.48), channel_id=1, source_target_pairs={{0,20},{4,16},{8,28},{12,24},{16,4},{20,0},{24,12},{28,8},{1,21},{... | collective-permute-start | bytes 73736 | tf_op jit(solution)/shard_map/ppermute | solution.py:356
  26.3 5.7 %collective-permute-done.7.value.refs_2_ = bf16[960,128]{1,0:T(8,128)(2,1)S(1)} collective-permute-done((bf16[960,128]{1,0:T(8,128)(2,1)S(1)}, bf16[960,128]{1,0:T(8,128)(2,1)S(1)}, u32[]{:S(2)}, u32[]{:S(2)}) %collective-permute-start.7) | collective-permute-done | bytes 245792 | tf_op jit(solution)/shard_map/ppermute | solution.py:356
  32.1 0.5 %collective-permute-start.8 = (bf16[480,128]{1,0:T(8,128)(2,1)S(1)}, bf16[480,128]{1,0:T(8,128)(2,1)S(1)}, u32[]{:S(2)}, u32[]{:S(2)}) collective-permute-start(bf16[480,128]{1,0:T(8,128)(2,1)S(1)} %get-tuple-element.44), channel_id=1, source_target_pairs={{0,4},{4,0},{8,12},{12,8},{16,20},{20,16},{24,28},{28,24},{1,5},{5... | collective-permute-start | bytes 368648 | tf_op jit(solution)/shard_map/ppermute | solution.py:356
  32.6 0.0 collective-permute-done.9.refs_0_
  32.6 0.0 collective-permute-done.10.refs_1_
  32.6 0.0 collective-permute-done.11.refs_2_
  32.6 0.1 shard_map.121
  32.7 0.1 collective-permute-start.12
  32.8 1.6 %collective-permute-start.13 = (bf16[480,128]{1,0:T(8,128)(2,1)S(1)}, bf16[480,128]{1,0:T(8,128)(2,1)S(1)}, u32[]{:S(2)}, u32[]{:S(2)}) collective-permute-start(bf16[480,128]{1,0:T(8,128)(2,1)S(1)} %get-tuple-element.52), channel_id=1, source_target_pairs={{0,4},{4,0},{8,12},{12,8},{16,20},{20,16},{24,28},{28,24},{1,5},{5... | collective-permute-start | bytes 368648 | tf_op jit(solution)/shard_map/ppermute | solution.py:356
  34.4 1.9 %shard_map.117 = (bf16[200,768]{1,0:T(8,128)(2,1)S(1)}, bf16[200,768]{1,0:T(8,128)(2,1)S(1)}, bf16[40,768]{1,0:T(8,128)(2,1)S(1)}) custom-call(bf16[768,128]{1,0:T(8,128)(2,1)S(1)} %get-tuple-element.33.g_ref, bf16[5,768,768]{2,1,0:T(8,128)(2,1)S(1)} %bitcast.5), custom_call_target="tpu_custom_call" | custom-call | flops 1150000000 | tf_op jit(solution)/shard_map/pallas_call | solution.py:365
  36.4 0.0 collective-permute-done.6.refs_1_
  36.4 0.0 collective-permute-done.12.refs_6_
  36.4 1.8 %collective-permute-done.8.refs_3_ = bf16[480,128]{1,0:T(8,128)(2,1)S(1)} collective-permute-done((bf16[480,128]{1,0:T(8,128)(2,1)S(1)}, bf16[480,128]{1,0:T(8,128)(2,1)S(1)}, u32[]{:S(2)}, u32[]{:S(2)}) %collective-permute-start.8) | collective-permute-done | bytes 122912 | tf_op jit(solution)/shard_map/ppermute | solution.py:356
  38.2 0.4 shard_map.122
  38.5 0.4 collective-permute-start.14
  39.0 0.7 %collective-permute-done.13.refs_3_ = bf16[480,128]{1,0:T(8,128)(2,1)S(1)} collective-permute-done((bf16[480,128]{1,0:T(8,128)(2,1)S(1)}, bf16[480,128]{1,0:T(8,128)(2,1)S(1)}, u32[]{:S(2)}, u32[]{:S(2)}) %collective-permute-start.13) | collective-permute-done | bytes 122912 | tf_op jit(solution)/shard_map/ppermute | solution.py:356
  39.7 0.4 shard_map.123
  40.0 1.1 %collective-permute-start.15 = (bf16[96,480]{1,0:T(8,128)(2,1)S(1)}, bf16[96,480]{1,0:T(8,128)(2,1)S(1)}, u32[]{:S(2)}, u32[]{:S(2)}) collective-permute-start(bf16[96,480]{1,0:T(8,128)(2,1)S(1)} %get-tuple-element.55), channel_id=1, source_target_pairs={{0,8},{4,12},{8,0},{12,4},{16,24},{20,28},{24,16},{28,20},{1,9},{5... | collective-permute-start | bytes 276488 | tf_op jit(solution)/shard_map/ppermute | solution.py:356
  41.1 2.9 %shard_map.118 = bf16[512,768]{1,0:T(8,128)(2,1)} custom-call(bf16[200,768]{1,0:T(8,128)(2,1)S(1)} %get-tuple-element.34.highs, bf16[200,768]{1,0:T(8,128)(2,1)S(1)} %get-tuple-element.35.lows, bf16[40,768]{1,0:T(8,128)(2,1)S(1)} %get-tuple-element.36.near, f32[512,768]{1,0:T(8,128)S(1)} %get-tuple-element.37.normed_ref, ...), custom_call_target="tpu_custom_call" | custom-call | flops 1150000000 | tf_op jit(solution)/shard_map/pallas_call | solution.py:365
  44.0 0.0 collective-permute-done.14.refs_2_
  44.0 0.9 %collective-permute-done.15.refs_3_ = bf16[96,480]{1,0:T(8,128)(2,1)S(1)} collective-permute-done((bf16[96,480]{1,0:T(8,128)(2,1)S(1)}, bf16[96,480]{1,0:T(8,128)(2,1)S(1)}, u32[]{:S(2)}, u32[]{:S(2)}) %collective-permute-start.15) | collective-permute-done | bytes 92192 | tf_op jit(solution)/shard_map/ppermute | solution.py:356
  44.8 1.0 %shard_map.124 = f32[5,192,96]{2,1,0:T(8,128)} custom-call(f32[96,480]{1,0:T(8,128)S(1)} %get-tuple-element.51.refs_0_, f32[96,480]{1,0:T(8,128)S(1)} %get-tuple-element.53.refs_1_, bf16[96,480]{1,0:T(8,128)(2,1)S(1)} %collective-permute-done.14.refs_2_, bf16[96,480]{1,0:T(8,128)(2,1)S(1)} %collective-permute-done.15.refs_3_), custom_call_target="tpu_custom_call" | custom-call | flops 1150000000 | tf_op jit(solution)/shard_map/pallas_call | solution.py:365
  (9 shorter events, 0.0 us)
Async XLA Ops:
  0.6 3.0 %slice-start = ((s8[5898240]{0:T(1024)(128)(4,1)}), s8[4194304]{0:T(1024)(128)(4,1)S(1)}, s32[]{:S(2)}) async-start(s8[5898240]{0:T(1024)(128)(4,1)} %bitcast.4), calls=%async_computation | async-start | bytes 8388608
  0.6 3.1 %slice-start.1 = ((s8[5898240]{0:T(1024)(128)(4,1)}), s8[1703936]{0:T(1024)(128)(4,1)S(1)}, s32[]{:S(2)}) async-start(s8[5898240]{0:T(1024)(128)(4,1)} %bitcast.4), calls=%async_computation.1 | async-start | bytes 3407872
  3.8 14.9 %copy-start.3 = (bf16[768,768]{1,0:T(8,128)(2,1)S(1)}, bf16[768,768]{1,0:T(8,128)(2,1)}, u32[]{:S(2)}) copy-start(bf16[768,768]{1,0:T(8,128)(2,1)} %refs_7_.1) | copy-start | bytes 3538948
  4.9 7.2 %collective-permute-start = (bf16[80,768]{1,0:T(8,128)(2,1)S(1)}, bf16[80,768]{1,0:T(8,128)(2,1)S(1)}, u32[]{:S(2)}, u32[]{:S(2)}) collective-permute-start(bf16[80,768]{1,0:T(8,128)(2,1)S(1)} %shard_map.115.refs_0_), channel_id=1, source_target_pairs={{0,2},{1,3},{2,0},{3,1},{4,6},{5,7},{6,4},{7,5},{8,10},{9,11},{10,... | collective-permute-start | bytes 368648 | tf_op jit(solution)/shard_map/ppermute | solution.py:356
  8.0 5.9 %collective-permute-start.3 = (bf16[40,960]{1,0:T(8,128)(2,1)S(1)}, bf16[40,960]{1,0:T(8,128)(2,1)S(1)}, u32[]{:S(2)}, u32[]{:S(2)}) collective-permute-start(bf16[40,960]{1,0:T(8,128)(2,1)S(1)} %get-tuple-element.41), channel_id=1, source_target_pairs={{0,2},{1,3},{2,0},{3,1},{4,6},{5,7},{6,4},{7,5},{8,10},{9,11},{10,... | collective-permute-start | bytes 230408 | tf_op jit(solution)/shard_map/ppermute | solution.py:356
  8.1 5.9 %collective-permute-start.4 = (bf16[40,960]{1,0:T(8,128)(2,1)S(1)}, bf16[40,960]{1,0:T(8,128)(2,1)S(1)}, u32[]{:S(2)}, u32[]{:S(2)}) collective-permute-start(bf16[40,960]{1,0:T(8,128)(2,1)S(1)} %get-tuple-element.42), channel_id=1, source_target_pairs={{0,1},{1,0},{2,3},{3,2},{4,5},{5,4},{6,7},{7,6},{8,9},{9,8},{10,11... | collective-permute-start | bytes 230408 | tf_op jit(solution)/shard_map/ppermute | solution.py:356
  8.1 6.0 %collective-permute-start.5 = (bf16[40,960]{1,0:T(8,128)(2,1)S(1)}, bf16[40,960]{1,0:T(8,128)(2,1)S(1)}, u32[]{:S(2)}, u32[]{:S(2)}) collective-permute-start(bf16[40,960]{1,0:T(8,128)(2,1)S(1)} %get-tuple-element.43), channel_id=1, source_target_pairs={{0,3},{1,2},{2,1},{3,0},{4,7},{5,6},{6,5},{7,4},{8,11},{9,10},{10,... | collective-permute-start | bytes 230408 | tf_op jit(solution)/shard_map/ppermute | solution.py:356
  10.1 8.5 %collective-permute-start.1 = (bf16[80,768]{1,0:T(8,128)(2,1)S(1)}, bf16[80,768]{1,0:T(8,128)(2,1)S(1)}, u32[]{:S(2)}, u32[]{:S(2)}) collective-permute-start(bf16[80,768]{1,0:T(8,128)(2,1)S(1)} %shard_map.115.refs_0_), channel_id=1, source_target_pairs={{0,1},{1,0},{2,3},{3,2},{4,5},{5,4},{6,7},{7,6},{8,9},{9,8},{10,11... | collective-permute-start | bytes 368648 | tf_op jit(solution)/shard_map/ppermute | solution.py:356
  12.2 6.5 %collective-permute-start.2 = (bf16[80,768]{1,0:T(8,128)(2,1)S(1)}, bf16[80,768]{1,0:T(8,128)(2,1)S(1)}, u32[]{:S(2)}, u32[]{:S(2)}) collective-permute-start(bf16[80,768]{1,0:T(8,128)(2,1)S(1)} %collective-permute-done.refs_1_), channel_id=1, source_target_pairs={{0,1},{1,0},{2,3},{3,2},{4,5},{5,4},{6,7},{7,6},{8,9},{9,8},{10,11... | collective-permute-start | bytes 368648 | tf_op jit(solution)/shard_map/ppermute | solution.py:356
  14.1 4.6 %copy-start = (bf16[768,768]{1,0:T(8,128)(2,1)S(1)}, bf16[768,768]{1,0:T(8,128)(2,1)}, u32[]{:S(2)}) copy-start(bf16[768,768]{1,0:T(8,128)(2,1)} %refs_4_.1) | copy-start | bytes 3538948
  14.1 4.6 %copy-start.1 = (bf16[768,768]{1,0:T(8,128)(2,1)S(1)}, bf16[768,768]{1,0:T(8,128)(2,1)}, u32[]{:S(2)}) copy-start(bf16[768,768]{1,0:T(8,128)(2,1)} %refs_5_.1) | copy-start | bytes 3538948
  14.1 4.6 %copy-start.2 = (bf16[768,768]{1,0:T(8,128)(2,1)S(1)}, bf16[768,768]{1,0:T(8,128)(2,1)}, u32[]{:S(2)}) copy-start(bf16[768,768]{1,0:T(8,128)(2,1)} %refs_6_.1) | copy-start | bytes 3538948
  14.4 22.0 %collective-permute-start.6 = (bf16[960,128]{1,0:T(8,128)(2,1)S(1)}, bf16[960,128]{1,0:T(8,128)(2,1)S(1)}, u32[]{:S(2)}, u32[]{:S(2)}) collective-permute-start(bf16[960,128]{1,0:T(8,128)(2,1)S(1)} %shard_map.119.refs_0_), channel_id=1, source_target_pairs={{0,4},{4,0},{8,12},{12,8},{16,20},{20,16},{24,28},{28,24},{1,5},{5... | collective-permute-start | bytes 737288 | tf_op jit(solution)/shard_map/ppermute | solution.py:356
  16.1 16.0 %collective-permute-start.7 = (bf16[960,128]{1,0:T(8,128)(2,1)S(1)}, bf16[960,128]{1,0:T(8,128)(2,1)S(1)}, u32[]{:S(2)}, u32[]{:S(2)}) collective-permute-start(bf16[960,128]{1,0:T(8,128)(2,1)S(1)} %shard_map.119.refs_0_), channel_id=1, source_target_pairs={{0,16},{4,20},{8,24},{12,28},{16,0},{20,4},{24,8},{28,12},{1,17},{... | collective-permute-start | bytes 737288 | tf_op jit(solution)/shard_map/ppermute | solution.py:356
  21.9 10.8 %collective-permute-start.9 = (bf16[96,128]{1,0:T(8,128)(2,1)S(1)}, bf16[96,128]{1,0:T(8,128)(2,1)S(1)}, u32[]{:S(2)}, u32[]{:S(2)}) collective-permute-start(bf16[96,128]{1,0:T(8,128)(2,1)S(1)} %get-tuple-element.46), channel_id=1, source_target_pairs={{0,4},{4,0},{8,12},{12,8},{16,20},{20,16},{24,28},{28,24},{1,5},{5... | collective-permute-start | bytes 73736 | tf_op jit(solution)/shard_map/ppermute | solution.py:356
  22.5 10.2 %collective-permute-start.10 = (bf16[96,128]{1,0:T(8,128)(2,1)S(1)}, bf16[96,128]{1,0:T(8,128)(2,1)S(1)}, u32[]{:S(2)}, u32[]{:S(2)}) collective-permute-start(bf16[96,128]{1,0:T(8,128)(2,1)S(1)} %get-tuple-element.47), channel_id=1, source_target_pairs={{0,16},{4,20},{8,24},{12,28},{16,0},{20,4},{24,8},{28,12},{1,17},{... | collective-permute-start | bytes 73736 | tf_op jit(solution)/shard_map/ppermute | solution.py:356
  23.5 9.1 %collective-permute-start.11 = (bf16[96,128]{1,0:T(8,128)(2,1)S(1)}, bf16[96,128]{1,0:T(8,128)(2,1)S(1)}, u32[]{:S(2)}, u32[]{:S(2)}) collective-permute-start(bf16[96,128]{1,0:T(8,128)(2,1)S(1)} %get-tuple-element.48), channel_id=1, source_target_pairs={{0,20},{4,16},{8,28},{12,24},{16,4},{20,0},{24,12},{28,8},{1,21},{... | collective-permute-start | bytes 73736 | tf_op jit(solution)/shard_map/ppermute | solution.py:356
  32.1 6.1 %collective-permute-start.8 = (bf16[480,128]{1,0:T(8,128)(2,1)S(1)}, bf16[480,128]{1,0:T(8,128)(2,1)S(1)}, u32[]{:S(2)}, u32[]{:S(2)}) collective-permute-start(bf16[480,128]{1,0:T(8,128)(2,1)S(1)} %get-tuple-element.44), channel_id=1, source_target_pairs={{0,4},{4,0},{8,12},{12,8},{16,20},{20,16},{24,28},{28,24},{1,5},{5... | collective-permute-start | bytes 368648 | tf_op jit(solution)/shard_map/ppermute | solution.py:356
  32.7 3.7 %collective-permute-start.12 = (bf16[288,128]{1,0:T(8,128)(2,1)S(1)}, bf16[288,128]{1,0:T(8,128)(2,1)S(1)}, u32[]{:S(2)}, u32[]{:S(2)}) collective-permute-start(bf16[288,128]{1,0:T(8,128)(2,1)S(1)} %get-tuple-element.50), channel_id=1, source_target_pairs={{0,1},{1,0},{2,3},{3,2},{4,5},{5,4},{6,7},{7,6},{8,9},{9,8},{10,11... | collective-permute-start | bytes 221192 | tf_op jit(solution)/shard_map/ppermute | solution.py:356
  32.8 6.9 %collective-permute-start.13 = (bf16[480,128]{1,0:T(8,128)(2,1)S(1)}, bf16[480,128]{1,0:T(8,128)(2,1)S(1)}, u32[]{:S(2)}, u32[]{:S(2)}) collective-permute-start(bf16[480,128]{1,0:T(8,128)(2,1)S(1)} %get-tuple-element.52), channel_id=1, source_target_pairs={{0,4},{4,0},{8,12},{12,8},{16,20},{20,16},{24,28},{28,24},{1,5},{5... | collective-permute-start | bytes 368648 | tf_op jit(solution)/shard_map/ppermute | solution.py:356
  38.5 5.4 %collective-permute-start.14 = (bf16[96,480]{1,0:T(8,128)(2,1)S(1)}, bf16[96,480]{1,0:T(8,128)(2,1)S(1)}, u32[]{:S(2)}, u32[]{:S(2)}) collective-permute-start(bf16[96,480]{1,0:T(8,128)(2,1)S(1)} %get-tuple-element.54), channel_id=1, source_target_pairs={{0,8},{4,12},{8,0},{12,4},{16,24},{20,28},{24,16},{28,20},{1,9},{5... | collective-permute-start | bytes 276488 | tf_op jit(solution)/shard_map/ppermute | solution.py:356
  40.0 4.8 %collective-permute-start.15 = (bf16[96,480]{1,0:T(8,128)(2,1)S(1)}, bf16[96,480]{1,0:T(8,128)(2,1)S(1)}, u32[]{:S(2)}, u32[]{:S(2)}) collective-permute-start(bf16[96,480]{1,0:T(8,128)(2,1)S(1)} %get-tuple-element.55), channel_id=1, source_target_pairs={{0,8},{4,12},{8,0},{12,4},{16,24},{20,28},{24,16},{28,20},{1,9},{5... | collective-permute-start | bytes 276488 | tf_op jit(solution)/shard_map/ppermute | solution.py:356

commit v11 on v10

--- a/solution.py
+++ b/solution.py
@@ -171,12 +171,12 @@
     out[...] = dot_tn(buf[...], eye).astype(BF16)
 
 
-def attention_kernel(pool, order, tok_rows, near_rels, late, *refs):
+def attention_kernel(pool, order, tok_rows, late, *refs):
     blocks = len(order)
     parts, refs = refs[:blocks], refs[blocks:]
     (wq, wk, wv, wo), refs = refs[:4], refs[4:]
     g_out, refs = refs[0], refs[1:]
-    gts, refs = refs[: len(near_rels)], refs[len(near_rels) :]
+    gts, refs = refs[:3], refs[3:]
     p_buf, c_buf, q_buf, k_buf, v_buf, ga_buf, gq_buf, gk_buf, gv_buf = refs[:9]
     probs_buf, turn, ends = refs[9:]
     padded = parts[0].shape[0] - tok_rows - 8
@@ -233,10 +233,12 @@
         gts[0][at * span : (at + 1) * span, :] = turn[rel]
     half = len(late) // 2
     core = lax.axis_index("ctx") % 2
-    for gt, base in zip(gts[1:], near_rels[1:]):
-        for at in range(half):
-            rel = pick(core, [late[at], late[half + at]])
-            gt[at * span : (at + 1) * span, :] = turn[base ^ rel]
+    for gt, bases in zip(gts[1:], ((X_BIT, X_BIT + Z_BIT), (Z_BIT,))):
+        for step, base in enumerate(bases):
+            for at in range(half):
+                rel = pick(core, [late[at], late[half + at]])
+                begin = (step * half + at) * span
+                gt[begin : begin + span, :] = turn[base ^ rel]
 
 
 def spread_kernel(kernel, tok_rows, befores, afters, g_ref, weights, highs, lows, near):
@@ -292,14 +294,18 @@
         at += out.shape[0]
 
 
-def merge_kernel(*refs):
-    *parts, out, turned = refs
+def relay_kernel(own, received, out):
+    half = own.shape[0]
+    out[:half, :] = own[...]
+    out[half:, :] = received[half:, :]
+
+
+def merge_kernel(from_x, from_z, out, turned):
     at = 0
-    for part in parts:
+    for part in (from_x[: from_x.shape[0] // 2, :], from_z[...]):
         here = slice(at, at + part.shape[0])
-        value = part[...]
-        out[here, :] = value
-        turned[here, :] = pltpu.roll(value.astype(F32), value.shape[1] // 2, axis=1).astype(BF16)
+        out[here, :] = part
+        turned[here, :] = pltpu.roll(part.astype(F32), part.shape[1] // 2, axis=1).astype(BF16)
         at += part.shape[0]
 
 
@@ -401,7 +407,6 @@
     tokens = n_ctx * tok_rows
     width = channels // n_ctx
     narrow = channels // n_dp
-    near_rels = [0, X_BIT, Z_BIT, X_BIT + Z_BIT]
     late = sums_of([bit for bit in bits_of(n_dp) if bit not in (X_BIT, Z_BIT)])
 
     order = xor_order(n_ctx)
@@ -471,10 +476,10 @@
     act_x = swap(act, "dp", X_BIT)
 
     g_all, *gts = call(
-        functools.partial(attention_kernel, pool, order, tok_rows, near_rels, late),
+        functools.partial(attention_kernel, pool, order, tok_rows, late),
         (*rows, w_query, w_key, w_value, w_out),
         [pltpu.VMEM((channels, tokens), BF16), pltpu.VMEM((len(late) * narrow, tokens), BF16)]
-        + [pltpu.VMEM((len(late) // 2 * narrow, tokens), BF16)] * (len(near_rels) - 1),
+        + [pltpu.VMEM((len(late) // 2 * narrow * steps, tokens), BF16) for steps in (2, 1)],
         [pltpu.VMEM((tokens, channels), BF16)] * 5
         + [pltpu.VMEM((channels, tokens), BF16)]
         + [pltpu.VMEM((tokens, channels), BF16)] * 3
@@ -493,13 +498,11 @@
     act_zx = list(act_zx)
     for at, value in enumerate(act_zx):
         act_zx[at] = swap(value, "dp", X_BIT)
-    swapped = []
-    for at, rel in enumerate(near_rels[1:], 1):
-        swapped.append(swap(gts[at], "dp", rel))
+    from_x = swap(gts[1], "dp", X_BIT)
+    to_z = call(relay_kernel, (gts[2], from_x), [pltpu.VMEM(gts[1].shape, BF16)])[0]
+    from_z = swap(to_z, "dp", Z_BIT)
     merged, turned = call(
-        merge_kernel,
-        swapped,
-        [pltpu.VMEM((sum(value.shape[0] for value in swapped), tokens), BF16)] * 2,
+        merge_kernel, (from_x, from_z), [pltpu.VMEM((3 * gts[2].shape[0], tokens), BF16)] * 2
     )
     shared = swap(turned, "ctx", 1)
 

time: 46 us -> 44 us (0.957)
  starting transfers between devices: 17.6 us -> 16.5 us
  waiting for transfers between devices: 13 us -> 12.2 us
    ppermute x16 -> x15, starting transfers between devices: 17.6 us -> 16.5 us  [swap(): return lax.ppermute(value, axis, [(i, i ^ bit) for i in range(count)])]
    ppermute x16 -> x15, waiting for transfers between devices: 13 us -> 12.2 us  [swap(): return lax.ppermute(value, axis, [(i, i ^ bit) for i in range(count)])]
    pallas_call x12 -> x13, Pallas kernels: 14.3 us -> 14.3 us  [call(): pl.pallas_call(body, out_shape=list(outs), scratch_shapes=list(scratch),...]
  transfers between devices with their start and end apart: 16 -> 15, of which waited for: 7 -> 7; matrix products, arithmetic and copies ran while one was open for 0% -> 0% of each run, Pallas kernels for 20% -> 21%
where the time goes in v11:
time: 44 us; the launch traced here: 43.8 us
  starting transfers between devices  16.5 us (38%)
  Pallas kernels  14.3 us (32%)
  waiting for transfers between devices  12.2 us (28%)
  between operations  0.79 us (2%)
    ppermute x15, starting transfers between devices, swap(): return lax.ppermute(value, axis, [(i, i ^ bit) for i in range(count)])  16.5 us
    pallas_call x13, Pallas kernels, call(): pl.pallas_call(body, out_shape=list(outs), scratch_shapes=list(scratch),...  14.3 us
    ppermute x15, waiting for transfers between devices, swap(): return lax.ppermute(value, axis, [(i, i ^ bit) for i in range(count)])  12.2 us
  transfers between devices with their start and end apart: 15, of which 7 were waited for; matrix products, arithmetic and copies ran while one was open for 0% of the time, Pallas kernels for 21%

profile of v11, /device:TPU:0, one launch (start us, length us, event | category | flops | bytes accessed | tf_op | source)
XLA Modules:
  0.0 43.8 jit_solution(13512458206272595927)
XLA Ops:
  0.6 0.0 slice-start
  0.6 0.0 slice-start.1
  0.7 2.8 %shard_map.113 = (f32[200,768]{1,0:T(8,128)S(1)}, f32[40,768]{1,0:T(8,128)S(1)}, f32[512,768]{1,0:T(8,128)S(1)}, f32[512,128]{1,0:T(8,128)S(1)}, bf16[768]{0:T(1...) custom-call(bf16[512,768]{1,0:T(8,128)(2,1)} %bitcast.6, s32[1,512]{1,0:T(1,128)} %base_hbm.1, bf16[4,768]{1,0:T(4,128)(2,1)} %table_hbm.1, ...), custom_call_target="tpu_custom_call" | custom-call | flops 3449999872 | tf_op jit(solution)/shard_map/pallas_call | solution.py:371
  3.5 0.2 shard_map.114
  3.7 0.0 slice-done
  3.7 0.1 slice-done.1
  3.8 1.2 %shard_map.115.refs_0_ = bf16[80,768]{1,0:T(8,128)(2,1)S(1)} custom-call(bf16[5,80,768]{2,1,0:T(8,128)(2,1)S(1)} %get-tuple-element.29.pairs, f32[40,768]{1,0:T(8,128)S(1)} %get-tuple-element.30.sums, bf16[5,768,768]{2,1,0:T(8,128)(2,1)S(1)} %bitcast.5, bf16[32,768]{1,0:T(8,128)(2,1)S(1)} %get-tuple-element.31.cot), custom_call_target="tpu_custom_call" | custom-call | flops 1150000000 | tf_op jit(solution)/shard_map/pallas_call | solution.py:371
  4.9 3.1 %collective-permute-start = (bf16[80,768]{1,0:T(8,128)(2,1)S(1)}, bf16[80,768]{1,0:T(8,128)(2,1)S(1)}, u32[]{:S(2)}, u32[]{:S(2)}) collective-permute-start(bf16[80,768]{1,0:T(8,128)(2,1)S(1)} %shard_map.115.refs_0_), channel_id=1, source_target_pairs={{0,2},{1,3},{2,0},{3,1},{4,6},{5,7},{6,4},{7,5},{8,10},{9,11},{10,... | collective-permute-start | bytes 368648 | tf_op jit(solution)/shard_map/ppermute | solution.py:362
  8.0 0.1 collective-permute-start.3
  8.1 0.0 collective-permute-start.4
  8.1 2.1 %collective-permute-start.5 = (bf16[40,960]{1,0:T(8,128)(2,1)S(1)}, bf16[40,960]{1,0:T(8,128)(2,1)S(1)}, u32[]{:S(2)}, u32[]{:S(2)}) collective-permute-start(bf16[40,960]{1,0:T(8,128)(2,1)S(1)} %get-tuple-element.42), channel_id=1, source_target_pairs={{0,3},{1,2},{2,1},{3,0},{4,7},{5,6},{6,5},{7,4},{8,11},{9,10},{10,... | collective-permute-start | bytes 230408 | tf_op jit(solution)/shard_map/ppermute | solution.py:362
  10.1 0.0 collective-permute-start.1
  10.1 2.0 %collective-permute-done.refs_1_ = bf16[80,768]{1,0:T(8,128)(2,1)S(1)} collective-permute-done((bf16[80,768]{1,0:T(8,128)(2,1)S(1)}, bf16[80,768]{1,0:T(8,128)(2,1)S(1)}, u32[]{:S(2)}, u32[]{:S(2)}) %collective-permute-start) | collective-permute-done | bytes 122912 | tf_op jit(solution)/shard_map/ppermute | solution.py:362
  12.2 0.0 collective-permute-start.2
  12.2 1.8 %collective-permute-done.3.refs_1_ = bf16[40,960]{1,0:T(8,128)(2,1)S(1)} collective-permute-done((bf16[40,960]{1,0:T(8,128)(2,1)S(1)}, bf16[40,960]{1,0:T(8,128)(2,1)S(1)}, u32[]{:S(2)}, u32[]{:S(2)}) %collective-permute-start.3) | collective-permute-done | bytes 76832 | tf_op jit(solution)/shard_map/ppermute | solution.py:362
  13.9 0.0 collective-permute-done.4.refs_2_
  13.9 0.2 collective-permute-done.5.refs_3_
  14.1 0.3 shard_map.119.refs_0_
  14.4 2.8 %collective-permute-start.7 = (bf16[960,128]{1,0:T(8,128)(2,1)S(1)}, bf16[960,128]{1,0:T(8,128)(2,1)S(1)}, u32[]{:S(2)}, u32[]{:S(2)}) collective-permute-start(bf16[960,128]{1,0:T(8,128)(2,1)S(1)} %shard_map.119.refs_0_), channel_id=1, source_target_pairs={{0,16},{4,20},{8,24},{12,28},{16,0},{20,4},{24,8},{28,12},{1,17},{... | collective-permute-start | bytes 737288 | tf_op jit(solution)/shard_map/ppermute | solution.py:362
  17.2 0.0 collective-permute-done.1.refs_2_
  17.2 0.0 collective-permute-done.2.refs_3_
  17.2 0.0 copy-done.3
  17.2 0.0 copy-done
  17.2 0.0 copy-done.1
  17.2 3.2 %shard_map.116 = (bf16[768,128]{1,0:T(8,128)(2,1)S(1)}, bf16[192,128]{1,0:T(8,128)(2,1)S(1)}, bf16[192,128]{1,0:T(8,128)(2,1)S(1)}, bf16[96,128]{1,0:T(8,128)(2,1)S(1)}) custom-call(bf16[80,768]{1,0:T(8,128)(2,1)S(1)} %shard_map.115.refs_0_, bf16[80,768]{1,0:T(8,128)(2,1)S(1)} %collective-permute-done.refs_1_, ...), custom_call_target="tpu_custom_call" | custom-call | flops 5750000128 | tf_op jit(solution)/shard_map/pallas_call | solution.py:371
  20.4 1.6 %collective-permute-start.9 = (bf16[192,128]{1,0:T(8,128)(2,1)S(1)}, bf16[192,128]{1,0:T(8,128)(2,1)S(1)}, u32[]{:S(2)}, u32[]{:S(2)}) collective-permute-start(bf16[192,128]{1,0:T(8,128)(2,1)S(1)} %get-tuple-element.45), channel_id=1, source_target_pairs={{0,4},{4,0},{8,12},{12,8},{16,20},{20,16},{24,28},{28,24},{1,5},{5... | collective-permute-start | bytes 147464 | tf_op jit(solution)/shard_map/ppermute | solution.py:362
  21.9 0.5 %collective-permute-start.6 = (bf16[960,128]{1,0:T(8,128)(2,1)S(1)}, bf16[960,128]{1,0:T(8,128)(2,1)S(1)}, u32[]{:S(2)}, u32[]{:S(2)}) collective-permute-start(bf16[960,128]{1,0:T(8,128)(2,1)S(1)} %shard_map.119.refs_0_), channel_id=1, source_target_pairs={{0,4},{4,0},{8,12},{12,8},{16,20},{20,16},{24,28},{28,24},{1,5},{5... | collective-permute-start | bytes 737288 | tf_op jit(solution)/shard_map/ppermute | solution.py:362
  22.5 2.1 %collective-permute-done.9.received.from_x = bf16[192,128]{1,0:T(8,128)(2,1)S(1)} collective-permute-done((bf16[192,128]{1,0:T(8,128)(2,1)S(1)}, bf16[192,128]{1,0:T(8,128)(2,1)S(1)}, u32[]{:S(2)}, u32[]{:S(2)}) %collective-permute-start.9) | collective-permute-done | bytes 49184 | tf_op jit(solution)/shard_map/ppermute | solution.py:362
  24.5 1.8 %collective-permute-start.10 = (bf16[192,128]{1,0:T(8,128)(2,1)S(1)}, bf16[192,128]{1,0:T(8,128)(2,1)S(1)}, u32[]{:S(2)}, u32[]{:S(2)}) collective-permute-start(bf16[192,128]{1,0:T(8,128)(2,1)S(1)} %shard_map.121), channel_id=1, source_target_pairs={{0,16},{4,20},{8,24},{12,28},{16,0},{20,4},{24,8},{28,12},{1,17},{... | collective-permute-start | bytes 147464 | tf_op jit(solution)/shard_map/ppermute | solution.py:362
  26.3 3.6 %collective-permute-done.7.value.refs_2_ = bf16[960,128]{1,0:T(8,128)(2,1)S(1)} collective-permute-done((bf16[960,128]{1,0:T(8,128)(2,1)S(1)}, bf16[960,128]{1,0:T(8,128)(2,1)S(1)}, u32[]{:S(2)}, u32[]{:S(2)}) %collective-permute-start.7) | collective-permute-done | bytes 245792 | tf_op jit(solution)/shard_map/ppermute | solution.py:362
  30.0 1.7 %collective-permute-start.8 = (bf16[480,128]{1,0:T(8,128)(2,1)S(1)}, bf16[480,128]{1,0:T(8,128)(2,1)S(1)}, u32[]{:S(2)}, u32[]{:S(2)}) collective-permute-start(bf16[480,128]{1,0:T(8,128)(2,1)S(1)} %get-tuple-element.43), channel_id=1, source_target_pairs={{0,4},{4,0},{8,12},{12,8},{16,20},{20,16},{24,28},{28,24},{1,5},{5... | collective-permute-start | bytes 368648 | tf_op jit(solution)/shard_map/ppermute | solution.py:362
  31.7 0.4 collective-permute-start.12
  32.1 0.0 collective-permute-done.10.from_z
  32.1 0.1 shard_map.122
  32.2 0.1 collective-permute-start.11
  32.3 2.0 %shard_map.117 = (bf16[200,768]{1,0:T(8,128)(2,1)S(1)}, bf16[200,768]{1,0:T(8,128)(2,1)S(1)}, bf16[40,768]{1,0:T(8,128)(2,1)S(1)}) custom-call(bf16[768,128]{1,0:T(8,128)(2,1)S(1)} %get-tuple-element.32.g_ref, bf16[5,768,768]{2,1,0:T(8,128)(2,1)S(1)} %bitcast.5), custom_call_target="tpu_custom_call" | custom-call | flops 1150000000 | tf_op jit(solution)/shard_map/pallas_call | solution.py:371
  34.2 0.0 collective-permute-done.6.refs_1_
  34.2 0.0 collective-permute-done.11.refs_6_
  34.2 2.0 %collective-permute-done.8.refs_3_ = bf16[480,128]{1,0:T(8,128)(2,1)S(1)} collective-permute-done((bf16[480,128]{1,0:T(8,128)(2,1)S(1)}, bf16[480,128]{1,0:T(8,128)(2,1)S(1)}, u32[]{:S(2)}, u32[]{:S(2)}) %collective-permute-start.8) | collective-permute-done | bytes 122912 | tf_op jit(solution)/shard_map/ppermute | solution.py:362
  36.2 0.4 shard_map.123
  36.6 1.1 %collective-permute-start.13 = (bf16[96,480]{1,0:T(8,128)(2,1)S(1)}, bf16[96,480]{1,0:T(8,128)(2,1)S(1)}, u32[]{:S(2)}, u32[]{:S(2)}) collective-permute-start(bf16[96,480]{1,0:T(8,128)(2,1)S(1)} %get-tuple-element.52), channel_id=1, source_target_pairs={{0,8},{4,12},{8,0},{12,4},{16,24},{20,28},{24,16},{28,20},{1,9},{5... | collective-permute-start | bytes 276488 | tf_op jit(solution)/shard_map/ppermute | solution.py:362
  37.7 0.0 collective-permute-done.12.refs_3_
  37.7 0.4 shard_map.124
  38.1 1.3 %collective-permute-start.14 = (bf16[96,480]{1,0:T(8,128)(2,1)S(1)}, bf16[96,480]{1,0:T(8,128)(2,1)S(1)}, u32[]{:S(2)}, u32[]{:S(2)}) collective-permute-start(bf16[96,480]{1,0:T(8,128)(2,1)S(1)} %get-tuple-element.53), channel_id=1, source_target_pairs={{0,8},{4,12},{8,0},{12,4},{16,24},{20,28},{24,16},{28,20},{1,9},{5... | collective-permute-start | bytes 276488 | tf_op jit(solution)/shard_map/ppermute | solution.py:362
  39.5 2.9 %shard_map.118 = bf16[512,768]{1,0:T(8,128)(2,1)} custom-call(bf16[200,768]{1,0:T(8,128)(2,1)S(1)} %get-tuple-element.33.highs, bf16[200,768]{1,0:T(8,128)(2,1)S(1)} %get-tuple-element.34.lows, bf16[40,768]{1,0:T(8,128)(2,1)S(1)} %get-tuple-element.35.near, f32[512,768]{1,0:T(8,128)S(1)} %get-tuple-element.36.normed_ref, ...), custom_call_target="tpu_custom_call" | custom-call | flops 1150000000 | tf_op jit(solution)/shard_map/pallas_call | solution.py:371
  42.3 0.0 collective-permute-done.13.refs_2_
  42.3 0.5 %collective-permute-done.14.refs_3_ = bf16[96,480]{1,0:T(8,128)(2,1)S(1)} collective-permute-done((bf16[96,480]{1,0:T(8,128)(2,1)S(1)}, bf16[96,480]{1,0:T(8,128)(2,1)S(1)}, u32[]{:S(2)}, u32[]{:S(2)}) %collective-permute-start.14) | collective-permute-done | bytes 92192 | tf_op jit(solution)/shard_map/ppermute | solution.py:362
  42.8 1.0 %shard_map.125 = f32[5,192,96]{2,1,0:T(8,128)} custom-call(f32[96,480]{1,0:T(8,128)S(1)} %get-tuple-element.49.refs_0_, f32[96,480]{1,0:T(8,128)S(1)} %get-tuple-element.51.refs_1_, bf16[96,480]{1,0:T(8,128)(2,1)S(1)} %collective-permute-done.13.refs_2_, bf16[96,480]{1,0:T(8,128)(2,1)S(1)} %collective-permute-done.14.refs_3_), custom_call_target="tpu_custom_call" | custom-call | flops 1150000000 | tf_op jit(solution)/shard_map/pallas_call | solution.py:371
  (8 shorter events, 0.0 us)
Async XLA Ops:
  0.6 3.0 %slice-start = ((s8[5898240]{0:T(1024)(128)(4,1)}), s8[4194304]{0:T(1024)(128)(4,1)S(1)}, s32[]{:S(2)}) async-start(s8[5898240]{0:T(1024)(128)(4,1)} %bitcast.4), calls=%async_computation | async-start | bytes 8388608
  0.6 3.1 %slice-start.1 = ((s8[5898240]{0:T(1024)(128)(4,1)}), s8[1703936]{0:T(1024)(128)(4,1)S(1)}, s32[]{:S(2)}) async-start(s8[5898240]{0:T(1024)(128)(4,1)} %bitcast.4), calls=%async_computation.1 | async-start | bytes 3407872
  3.8 13.4 %copy-start.3 = (bf16[768,768]{1,0:T(8,128)(2,1)S(1)}, bf16[768,768]{1,0:T(8,128)(2,1)}, u32[]{:S(2)}) copy-start(bf16[768,768]{1,0:T(8,128)(2,1)} %refs_7_.1) | copy-start | bytes 3538948
  4.9 7.2 %collective-permute-start = (bf16[80,768]{1,0:T(8,128)(2,1)S(1)}, bf16[80,768]{1,0:T(8,128)(2,1)S(1)}, u32[]{:S(2)}, u32[]{:S(2)}) collective-permute-start(bf16[80,768]{1,0:T(8,128)(2,1)S(1)} %shard_map.115.refs_0_), channel_id=1, source_target_pairs={{0,2},{1,3},{2,0},{3,1},{4,6},{5,7},{6,4},{7,5},{8,10},{9,11},{10,... | collective-permute-start | bytes 368648 | tf_op jit(solution)/shard_map/ppermute | solution.py:362
  8.0 5.9 %collective-permute-start.3 = (bf16[40,960]{1,0:T(8,128)(2,1)S(1)}, bf16[40,960]{1,0:T(8,128)(2,1)S(1)}, u32[]{:S(2)}, u32[]{:S(2)}) collective-permute-start(bf16[40,960]{1,0:T(8,128)(2,1)S(1)} %get-tuple-element.40), channel_id=1, source_target_pairs={{0,2},{1,3},{2,0},{3,1},{4,6},{5,7},{6,4},{7,5},{8,10},{9,11},{10,... | collective-permute-start | bytes 230408 | tf_op jit(solution)/shard_map/ppermute | solution.py:362
  8.1 5.9 %collective-permute-start.4 = (bf16[40,960]{1,0:T(8,128)(2,1)S(1)}, bf16[40,960]{1,0:T(8,128)(2,1)S(1)}, u32[]{:S(2)}, u32[]{:S(2)}) collective-permute-start(bf16[40,960]{1,0:T(8,128)(2,1)S(1)} %get-tuple-element.41), channel_id=1, source_target_pairs={{0,1},{1,0},{2,3},{3,2},{4,5},{5,4},{6,7},{7,6},{8,9},{9,8},{10,11... | collective-permute-start | bytes 230408 | tf_op jit(solution)/shard_map/ppermute | solution.py:362
  8.1 6.0 %collective-permute-start.5 = (bf16[40,960]{1,0:T(8,128)(2,1)S(1)}, bf16[40,960]{1,0:T(8,128)(2,1)S(1)}, u32[]{:S(2)}, u32[]{:S(2)}) collective-permute-start(bf16[40,960]{1,0:T(8,128)(2,1)S(1)} %get-tuple-element.42), channel_id=1, source_target_pairs={{0,3},{1,2},{2,1},{3,0},{4,7},{5,6},{6,5},{7,4},{8,11},{9,10},{10,... | collective-permute-start | bytes 230408 | tf_op jit(solution)/shard_map/ppermute | solution.py:362
  10.1 7.0 %collective-permute-start.1 = (bf16[80,768]{1,0:T(8,128)(2,1)S(1)}, bf16[80,768]{1,0:T(8,128)(2,1)S(1)}, u32[]{:S(2)}, u32[]{:S(2)}) collective-permute-start(bf16[80,768]{1,0:T(8,128)(2,1)S(1)} %shard_map.115.refs_0_), channel_id=1, source_target_pairs={{0,1},{1,0},{2,3},{3,2},{4,5},{5,4},{6,7},{7,6},{8,9},{9,8},{10,11... | collective-permute-start | bytes 368648 | tf_op jit(solution)/shard_map/ppermute | solution.py:362
  12.2 5.0 %collective-permute-start.2 = (bf16[80,768]{1,0:T(8,128)(2,1)S(1)}, bf16[80,768]{1,0:T(8,128)(2,1)S(1)}, u32[]{:S(2)}, u32[]{:S(2)}) collective-permute-start(bf16[80,768]{1,0:T(8,128)(2,1)S(1)} %collective-permute-done.refs_1_), channel_id=1, source_target_pairs={{0,1},{1,0},{2,3},{3,2},{4,5},{5,4},{6,7},{7,6},{8,9},{9,8},{10,11... | collective-permute-start | bytes 368648 | tf_op jit(solution)/shard_map/ppermute | solution.py:362
  14.1 3.1 %copy-start = (bf16[768,768]{1,0:T(8,128)(2,1)S(1)}, bf16[768,768]{1,0:T(8,128)(2,1)}, u32[]{:S(2)}) copy-start(bf16[768,768]{1,0:T(8,128)(2,1)} %refs_4_.1) | copy-start | bytes 3538948
  14.1 3.1 %copy-start.1 = (bf16[768,768]{1,0:T(8,128)(2,1)S(1)}, bf16[768,768]{1,0:T(8,128)(2,1)}, u32[]{:S(2)}) copy-start(bf16[768,768]{1,0:T(8,128)(2,1)} %refs_5_.1) | copy-start | bytes 3538948
  14.1 3.1 %copy-start.2 = (bf16[768,768]{1,0:T(8,128)(2,1)S(1)}, bf16[768,768]{1,0:T(8,128)(2,1)}, u32[]{:S(2)}) copy-start(bf16[768,768]{1,0:T(8,128)(2,1)} %refs_6_.1) | copy-start | bytes 3538948
  14.4 15.6 %collective-permute-start.7 = (bf16[960,128]{1,0:T(8,128)(2,1)S(1)}, bf16[960,128]{1,0:T(8,128)(2,1)S(1)}, u32[]{:S(2)}, u32[]{:S(2)}) collective-permute-start(bf16[960,128]{1,0:T(8,128)(2,1)S(1)} %shard_map.119.refs_0_), channel_id=1, source_target_pairs={{0,16},{4,20},{8,24},{12,28},{16,0},{20,4},{24,8},{28,12},{1,17},{... | collective-permute-start | bytes 737288 | tf_op jit(solution)/shard_map/ppermute | solution.py:362
  20.4 4.2 %collective-permute-start.9 = (bf16[192,128]{1,0:T(8,128)(2,1)S(1)}, bf16[192,128]{1,0:T(8,128)(2,1)S(1)}, u32[]{:S(2)}, u32[]{:S(2)}) collective-permute-start(bf16[192,128]{1,0:T(8,128)(2,1)S(1)} %get-tuple-element.45), channel_id=1, source_target_pairs={{0,4},{4,0},{8,12},{12,8},{16,20},{20,16},{24,28},{28,24},{1,5},{5... | collective-permute-start | bytes 147464 | tf_op jit(solution)/shard_map/ppermute | solution.py:362
  21.9 12.3 %collective-permute-start.6 = (bf16[960,128]{1,0:T(8,128)(2,1)S(1)}, bf16[960,128]{1,0:T(8,128)(2,1)S(1)}, u32[]{:S(2)}, u32[]{:S(2)}) collective-permute-start(bf16[960,128]{1,0:T(8,128)(2,1)S(1)} %shard_map.119.refs_0_), channel_id=1, source_target_pairs={{0,4},{4,0},{8,12},{12,8},{16,20},{20,16},{24,28},{28,24},{1,5},{5... | collective-permute-start | bytes 737288 | tf_op jit(solution)/shard_map/ppermute | solution.py:362
  24.5 7.6 %collective-permute-start.10 = (bf16[192,128]{1,0:T(8,128)(2,1)S(1)}, bf16[192,128]{1,0:T(8,128)(2,1)S(1)}, u32[]{:S(2)}, u32[]{:S(2)}) collective-permute-start(bf16[192,128]{1,0:T(8,128)(2,1)S(1)} %shard_map.121), channel_id=1, source_target_pairs={{0,16},{4,20},{8,24},{12,28},{16,0},{20,4},{24,8},{28,12},{1,17},{... | collective-permute-start | bytes 147464 | tf_op jit(solution)/shard_map/ppermute | solution.py:362
  30.0 6.3 %collective-permute-start.8 = (bf16[480,128]{1,0:T(8,128)(2,1)S(1)}, bf16[480,128]{1,0:T(8,128)(2,1)S(1)}, u32[]{:S(2)}, u32[]{:S(2)}) collective-permute-start(bf16[480,128]{1,0:T(8,128)(2,1)S(1)} %get-tuple-element.43), channel_id=1, source_target_pairs={{0,4},{4,0},{8,12},{12,8},{16,20},{20,16},{24,28},{28,24},{1,5},{5... | collective-permute-start | bytes 368648 | tf_op jit(solution)/shard_map/ppermute | solution.py:362
  31.7 6.1 %collective-permute-start.12 = (bf16[480,128]{1,0:T(8,128)(2,1)S(1)}, bf16[480,128]{1,0:T(8,128)(2,1)S(1)}, u32[]{:S(2)}, u32[]{:S(2)}) collective-permute-start(bf16[480,128]{1,0:T(8,128)(2,1)S(1)} %get-tuple-element.50), channel_id=1, source_target_pairs={{0,4},{4,0},{8,12},{12,8},{16,20},{20,16},{24,28},{28,24},{1,5},{5... | collective-permute-start | bytes 368648 | tf_op jit(solution)/shard_map/ppermute | solution.py:362
  32.2 2.1 %collective-permute-start.11 = (bf16[288,128]{1,0:T(8,128)(2,1)S(1)}, bf16[288,128]{1,0:T(8,128)(2,1)S(1)}, u32[]{:S(2)}, u32[]{:S(2)}) collective-permute-start(bf16[288,128]{1,0:T(8,128)(2,1)S(1)} %get-tuple-element.48), channel_id=1, source_target_pairs={{0,1},{1,0},{2,3},{3,2},{4,5},{5,4},{6,7},{7,6},{8,9},{9,8},{10,11... | collective-permute-start | bytes 221192 | tf_op jit(solution)/shard_map/ppermute | solution.py:362
  36.6 5.7 %collective-permute-start.13 = (bf16[96,480]{1,0:T(8,128)(2,1)S(1)}, bf16[96,480]{1,0:T(8,128)(2,1)S(1)}, u32[]{:S(2)}, u32[]{:S(2)}) collective-permute-start(bf16[96,480]{1,0:T(8,128)(2,1)S(1)} %get-tuple-element.52), channel_id=1, source_target_pairs={{0,8},{4,12},{8,0},{12,4},{16,24},{20,28},{24,16},{28,20},{1,9},{5... | collective-permute-start | bytes 276488 | tf_op jit(solution)/shard_map/ppermute | solution.py:362
  38.1 4.7 %collective-permute-start.14 = (bf16[96,480]{1,0:T(8,128)(2,1)S(1)}, bf16[96,480]{1,0:T(8,128)(2,1)S(1)}, u32[]{:S(2)}, u32[]{:S(2)}) collective-permute-start(bf16[96,480]{1,0:T(8,128)(2,1)S(1)} %get-tuple-element.53), channel_id=1, source_target_pairs={{0,8},{4,12},{8,0},{12,4},{16,24},{20,28},{24,16},{28,20},{1,9},{5... | collective-permute-start | bytes 276488 | tf_op jit(solution)/shard_map/ppermute | solution.py:362
